TPU v7x, 32 devices: a whole 2x2x4 slice. The times are simulated.
32 devices in a mesh: dp: 4 (over y, x), expert: 4 (over z), tok: 2 (over core).
Axes of the slice: x: 2, y: 2, z: 4, core: 2. Of those that a mesh axis runs over, the one named last changes fastest.
Arguments:
- tokens: bfloat16 [32768, 512], P(('dp', 'expert', 'tok')), may hold values from -6 to 6
- out_grad: bfloat16 [32768, 512], P(('dp', 'expert', 'tok')), may hold values from -6 to 6
- expert_ids: int32 [32768, 2], P(('dp', 'expert', 'tok')), may hold values from 0 to 3, all different within a row; in each aligned block of 1024 rows (0 to 1023, 1024 to 2047, ...) at most 768 rows name the same one
- sentence_ids: int32 [32, 1024], P(('dp', 'expert', 'tok')), may hold values from 0 to 15, never falling along the last dimension, each value on 1 to 128 neighbouring positions
- ln_attn: float32 [512], replicated, may hold values from 0.25 to 1.75
- w_kv: bfloat16 [512, 128], replicated, may hold values from -0.25 to 0.25
- w_router: bfloat16 [512, 4], replicated, may hold values from -0.1875 to 0.1875
- w_query: bfloat16 [4, 512, 64], P('expert'), may hold values from -0.25 to 0.25
- w_output: bfloat16 [4, 64, 512], P('expert'), may hold values from -4 to 4
- ln_ffn: float32 [512], replicated, may hold values from 0.25 to 1.75
- w_in: bfloat16 [512, 2048], replicated, may hold values from -0.25 to 0.25
- w_out: bfloat16 [2048, 512], replicated, may hold values from -0.1875 to 0.1875
Outputs:
- output: bfloat16 [32768, 512], P(('dp', 'expert', 'tok'))
- grad_tokens: bfloat16 [32768, 512], P(('dp', 'expert', 'tok'))
- grad_ln_attn: float32 [512], replicated
- grad_kv: float32 [512, 128], replicated
- grad_router: float32 [512, 4], replicated
- grad_query: float32 [4, 512, 64], P('expert')
- grad_output: float32 [4, 64, 512], P('expert')
- grad_ln_ffn: float32 [512], replicated
- grad_in: float32 [512, 2048], replicated
- grad_out: float32 [2048, 512], replicated
Inputs may be any that keep to these rules, and one draw needn't show every extreme that they name: `expert_ids`: among the 1024 rows of one device no expert is named more than 768 times, a bound that some block reaches; a token's 2 ids differ. `sentence_ids`: in each device's row the ids never fall; each id covers 1 to 128 consecutive positions, one exactly 128.
All inputs are finite; a program needn't handle non-finite values.
Results may differ from a plain program's by a relative error of at most 0.017.
Values may be sent and summed in bfloat16 or wider, within the bound.
No kernel may reach another device: no remote copies, remote signals or barrier semaphores. Data moves between devices by JAX's collectives and lax.ppermute only.
A program may use at most 128 MiB of HBM per device.

v0:
```python
import jax
import jax.numpy as jnp
from jax import lax
from jax.sharding import PartitionSpec as P


def product(left, right):
    return jnp.dot(left, right, preferred_element_type=jnp.float32)


def product_tn(left, right):
    return lax.dot_general(
        left, right, (((0,), (0,)), ((), ())), preferred_element_type=jnp.float32
    )


def product_nt(left, right):
    return lax.dot_general(
        left, right, (((1,), (1,)), ((), ())), preferred_element_type=jnp.float32
    )


def layer_norm_parts(values, gain):
    centre = values - jnp.mean(values, axis=-1, keepdims=True)
    spread = jnp.mean(centre * centre, axis=-1, keepdims=True)
    inverse = lax.rsqrt(spread + 1e-05)
    normalized = centre * inverse
    return (normalized * gain, normalized, inverse)


def layer_norm_back(upstream, normalized, inverse, gain):
    scaled = upstream * gain
    gain_grad = jnp.sum(upstream * normalized, axis=0)
    inner = (
        scaled
        - jnp.mean(scaled, axis=-1, keepdims=True)
        - normalized * jnp.mean(scaled * normalized, axis=-1, keepdims=True)
    )
    return (inner * inverse, gain_grad)


def gelu_exact(values):
    return 0.5 * values * (1.0 + jax.scipy.special.erf(values * 0.7071067811865476))


def gelu_slope(values):
    cumulative = 0.5 * (1.0 + jax.scipy.special.erf(values * 0.7071067811865476))
    density = jnp.exp(-0.5 * values * values) * 0.3989422804014327
    return cumulative + values * density


def head_forward(rows, row_ids, shared, key_ids, query_weight, output_weight):
    head_size = query_weight.shape[1]
    queries = product(rows, query_weight).astype(jnp.bfloat16)
    scores = product_nt(queries, shared[:, :head_size]) * 0.125
    scores = jnp.where(row_ids[:, None] == key_ids[None, :], scores, -30000.0)
    largest = jnp.max(scores, axis=-1, keepdims=True)
    raised = jnp.exp(scores - largest)
    total = jnp.sum(raised, axis=-1, keepdims=True)
    weights = (raised / total).astype(jnp.bfloat16)
    attended = product(weights, shared[:, head_size:]).astype(jnp.bfloat16)
    result = product(attended, output_weight).astype(jnp.bfloat16)
    log_total = largest[:, 0] + jnp.log(total[:, 0])
    return (result, queries, attended, log_total)


def head_backward(
    rows,
    row_ids,
    shared,
    key_ids,
    query_weight,
    output_weight,
    queries,
    attended,
    log_total,
    result_grad,
):
    head_size = query_weight.shape[1]
    output_grad = product_tn(attended, result_grad)
    attended_grad = product_nt(result_grad, output_weight).astype(jnp.bfloat16)
    scores = product_nt(queries, shared[:, :head_size]) * 0.125
    scores = jnp.where(row_ids[:, None] == key_ids[None, :], scores, -30000.0)
    probs = jnp.exp(scores - log_total[:, None])
    prob_low = probs.astype(jnp.bfloat16)
    prob_grad = product_nt(attended_grad, shared[:, head_size:])
    score_grad = (probs * (prob_grad - jnp.sum(probs * prob_grad, axis=-1, keepdims=True))).astype(
        jnp.bfloat16
    )
    query_grad = (product(score_grad, shared[:, :head_size]) * 0.125).astype(jnp.bfloat16)
    key_grad = product_tn(score_grad, queries) * 0.125
    value_grad = product_tn(prob_low, attended_grad)
    shared_grad = jnp.concatenate([key_grad, value_grad], axis=1)
    query_weight_grad = product_tn(rows, query_grad)
    rows_grad = product_nt(query_grad, query_weight).astype(jnp.bfloat16)
    return (rows_grad, shared_grad, query_weight_grad, output_grad)


def body(
    tokens,
    out_grad,
    expert_ids,
    sentence_ids,
    ln_attn,
    w_kv,
    w_router,
    w_query,
    w_output,
    ln_ffn,
    w_in,
    w_out,
):
    length = tokens.shape[0]
    width = tokens.shape[1]
    choose = expert_ids.shape[1]
    head_size = w_query.shape[2]
    experts = lax.axis_size("expert")
    capacity = 3 * length // experts
    sentence = sentence_ids[0]
    inputs = tokens.astype(jnp.float32)
    normed, norm_one, inverse_one = layer_norm_parts(inputs, ln_attn)
    normed_low = normed.astype(jnp.bfloat16)
    shared = product(normed_low, w_kv).astype(jnp.bfloat16)
    logits = product(normed_low, w_router)
    expert_range = jnp.arange(experts, dtype=jnp.int32)
    selector = (expert_ids[:, :, None] == expert_range[None, None, :]).astype(jnp.float32)
    picked = jnp.sum(selector * logits[:, None, :], axis=2)
    picked_top = jnp.max(picked, axis=-1, keepdims=True)
    picked_raised = jnp.exp(picked - picked_top)
    gates = picked_raised / jnp.sum(picked_raised, axis=-1, keepdims=True)
    flat_expert = expert_ids.reshape(length * choose)
    member = (flat_expert[:, None] == expert_range[None, :]).astype(jnp.int32)
    earlier = jnp.cumsum(member, axis=0) - member
    position = jnp.sum(earlier * member, axis=1)
    slot_index = flat_expert * capacity + position
    routed_rows = jnp.broadcast_to(normed_low[:, None, :], (length, choose, width)).reshape(
        length * choose, width
    )
    routed_ids = jnp.broadcast_to(sentence[:, None], (length, choose)).reshape(length * choose)
    dispatch_rows = (
        jnp.zeros((experts * capacity, width), jnp.bfloat16)
        .at[slot_index]
        .set(routed_rows)
        .reshape(experts, capacity, width)
    )
    dispatch_ids = (
        jnp.full((experts * capacity,), -1, jnp.int32)
        .at[slot_index]
        .set(routed_ids)
        .reshape(experts, capacity)
    )
    arrived, arrived_ids = (
        lax.all_to_all(dispatch_rows, "expert", split_axis=0, concat_axis=0, tiled=True),
        lax.all_to_all(dispatch_ids, "expert", split_axis=0, concat_axis=0, tiled=True),
    )
    all_shared, all_ids = (
        lax.all_gather(shared, "expert", axis=0, tiled=True),
        lax.all_gather(sentence, "expert", axis=0, tiled=True),
    )
    all_shared = all_shared.reshape(experts, length, 2 * head_size)
    all_ids = all_ids.reshape(experts, length)
    own_query = w_query[0]
    own_output = w_output[0]

    def forward_item(item):
        rows, row_ids, item_shared, key_ids = item
        return head_forward(rows, row_ids, item_shared, key_ids, own_query, own_output)

    results, kept_queries, kept_attended, kept_totals = lax.map(
        forward_item, (arrived, arrived_ids, all_shared, all_ids)
    )
    returned = lax.all_to_all(results, "expert", split_axis=0, concat_axis=0, tiled=True)
    returned_rows = (
        returned.reshape(experts * capacity, width)[slot_index]
        .astype(jnp.float32)
        .reshape(length, choose, width)
    )
    mixed = jnp.sum(gates[:, :, None] * returned_rows, axis=1)
    hidden_in = inputs + mixed
    normed_two, norm_two, inverse_two = layer_norm_parts(hidden_in, ln_ffn)
    normed_two_low = normed_two.astype(jnp.bfloat16)
    before = product(normed_two_low, w_in)
    activated = gelu_exact(before).astype(jnp.bfloat16)
    output = (hidden_in + product(activated, w_out)).astype(jnp.bfloat16)
    out_weight_grad = product_tn(activated, out_grad)
    activated_grad = product_nt(out_grad, w_out)
    before_grad = (activated_grad * gelu_slope(before)).astype(jnp.bfloat16)
    in_weight_grad = product_tn(normed_two_low, before_grad)
    normed_two_grad = product_nt(before_grad, w_in)
    hidden_back, ln_ffn_grad = layer_norm_back(normed_two_grad, norm_two, inverse_two, ln_ffn)
    hidden_grad = out_grad.astype(jnp.float32) + hidden_back
    gate_grad = jnp.sum(hidden_grad[:, None, :] * returned_rows, axis=2)
    picked_grad = gates * (gate_grad - jnp.sum(gates * gate_grad, axis=-1, keepdims=True))
    logits_grad = jnp.sum(selector * picked_grad[:, :, None], axis=1).astype(jnp.bfloat16)
    router_grad = product_tn(normed_low, logits_grad)
    route_grad = (
        (gates[:, :, None] * hidden_grad[:, None, :])
        .astype(jnp.bfloat16)
        .reshape(length * choose, width)
    )
    route_dispatch = (
        jnp.zeros((experts * capacity, width), jnp.bfloat16)
        .at[slot_index]
        .set(route_grad)
        .reshape(experts, capacity, width)
    )
    arrived_grad = lax.all_to_all(route_dispatch, "expert", split_axis=0, concat_axis=0, tiled=True)

    def backward_item(item):
        rows, row_ids, item_shared, key_ids, queries, attended, totals, result_grad = item
        return head_backward(
            rows,
            row_ids,
            item_shared,
            key_ids,
            own_query,
            own_output,
            queries,
            attended,
            totals,
            result_grad,
        )

    rows_grad, shared_parts, query_parts, output_parts = lax.map(
        backward_item,
        (
            arrived,
            arrived_ids,
            all_shared,
            all_ids,
            kept_queries,
            kept_attended,
            kept_totals,
            arrived_grad,
        ),
    )
    back_rows = lax.all_to_all(rows_grad, "expert", split_axis=0, concat_axis=0, tiled=True)
    shared_grad = lax.psum_scatter(
        shared_parts.reshape(experts * length, 2 * head_size).astype(jnp.bfloat16),
        "expert",
        scatter_dimension=0,
        tiled=True,
    )
    query_grad_sum = jnp.sum(query_parts, axis=0)[None]
    output_grad_sum = jnp.sum(output_parts, axis=0)[None]
    query_total, output_total = (
        lax.psum(query_grad_sum.astype(jnp.bfloat16), ("dp", "tok")).astype(jnp.float32),
        lax.psum(output_grad_sum.astype(jnp.bfloat16), ("dp", "tok")).astype(jnp.float32),
    )
    kv_weight_grad = product_tn(normed_low, shared_grad)
    routes_back = (
        back_rows.reshape(experts * capacity, width)[slot_index]
        .astype(jnp.float32)
        .reshape(length, choose, width)
    )
    normed_grad = (
        product_nt(shared_grad, w_kv)
        + product_nt(logits_grad, w_router)
        + jnp.sum(routes_back, axis=1)
    )
    input_back, ln_attn_grad = layer_norm_back(normed_grad, norm_one, inverse_one, ln_attn)
    input_grad = (hidden_grad + input_back).astype(jnp.bfloat16)
    summed = lax.psum(
        (ln_attn_grad, kv_weight_grad, router_grad, in_weight_grad, out_weight_grad, ln_ffn_grad),
        ("dp", "expert", "tok"),
    )
    return (
        output,
        input_grad,
        summed[0],
        summed[1],
        summed[2],
        query_total,
        output_total,
        summed[5],
        summed[3],
        summed[4],
    )


def solution(mesh):
    return jax.shard_map(
        body,
        mesh=mesh,
        in_specs=(
            P(("dp", "expert", "tok"), None),
            P(("dp", "expert", "tok"), None),
            P(("dp", "expert", "tok"), None),
            P(("dp", "expert", "tok"), None),
            P(),
            P(),
            P(),
            P("expert", None, None),
            P("expert", None, None),
            P(),
            P(),
            P(),
        ),
        out_specs=(
            P(("dp", "expert", "tok"), None),
            P(("dp", "expert", "tok"), None),
            P(),
            P(),
            P(),
            P("expert", None, None),
            P("expert", None, None),
            P(),
            P(),
            P(),
        ),
        check_vma=False,
    )
```

profile of v0, /device:TPU:0, one launch (start us, length us, event | category | flops | bytes accessed | tf_op | source)
XLA Modules:
  0.0 818.7 jit_solution(17089918963078222424)
XLA Ops:
  19.5 8.6 %scatter_custom_fusion = s32[3072]{0:T(1024)} fusion(s32[2048]{0:T(1024)S(1)} %bitcast.203, s32[2048]{0:T(1024)S(1)} %reshape.331, s32[]{:T(128)} %constant.101.clone.1), kind=kCustom, calls=%fused_computation.137 | custom fusion | bytes 12292 | tf_op jit(solution)/shard_map/scatter | solution.py:149
  28.2 6.3 all-to-all-start
  37.6 2.4 broadcast_in_dim.56
  40.0 4.1 reshape.339
  44.1 12.1 %scatter_custom_fusion.1 = bf16[3072,512]{1,0:T(8,128)(2,1)} fusion(s32[2048]{0:T(1024)S(1)} %bitcast.204, bf16[2048,512]{1,0:T(8,128)(2,1)} %reshape.339, bf16[]{:T(256)} %constant.98.clone.1), kind=kCustom, calls=%fused_computation.115 | custom fusion | bytes 3146240 | tf_op jit(solution)/shard_map/scatter | solution.py:143
  56.1 5.2 all-to-all-start.1
  62.6 91.3 %all-gather = s32[1,4096]{1,0:T(1,128)S(1)} all-gather(s32[1,1024]{1,0:T(1,128)S(1)} %copy-done.35), channel_id=2, replica_groups=mesh['dp'=4,'expert'=4,'tok'=2] {'expert'}, dimensions={1}, use_global_device_ids=true | all-gather | bytes 20480 | tf_op jit(solution)/shard_map/all_gather | solution.py:158
  157.8 41.3 %while.32 = (s32[]{:T(128)}, bf16[4,768,512]{2,1,0:T(8,128)(2,1)}, bf16[4,768,64]{1,2,0:T(8,128)(2,1)}, bf16[4,768,64]{1,2,0:T(8,128)(2,1)}, f32[4,768]{1,0:T(4,...) while((s32[]{:T(128)}, bf16[4,768,512]{2,1,0:T(8,128)(2,1)}, ...), condition=%wide.region_13.14_spmd, body=%wide.region_10.13_spmd.sunk | while | flops 314277120 | bytes 12918941 | solution.py:169
  158.8 2.1 bitcast_dynamic-update-slice_fusion.4
  162.7 1.9 bitcast_dynamic-update-slice_fusion.5
  166.0 2.1 fusion.155
  169.1 2.2 bitcast_dynamic-update-slice_fusion.4
  173.1 1.9 bitcast_dynamic-update-slice_fusion.5
  176.3 2.1 fusion.155
  179.4 2.1 bitcast_dynamic-update-slice_fusion.4
  183.4 1.9 bitcast_dynamic-update-slice_fusion.5
  186.6 2.1 fusion.155
  189.8 2.2 bitcast_dynamic-update-slice_fusion.4
  193.7 1.9 bitcast_dynamic-update-slice_fusion.5
  197.0 2.1 fusion.155
  199.1 4.8 all-to-all-start.2
  204.9 66.7 %all-to-all-done.2 = bf16[4,768,512]{2,1,0:T(8,128)(2,1)} async-done(((bf16[4,768,512]{2,1,0:T(8,128)(2,1)}), bf16[4,768,512]{2,1,0:T(8,128)(2,1)}, u32[]{:S(2)}, u32[]{:S(2)}) %all-to-all-start.2) | async-done | bytes 3145760 | tf_op jit(solution)/shard_map/all_to_all | solution.py:172
  271.6 11.6 %gather_fusion = bf16[2048,512]{1,0:T(8,128)(2,1)} fusion(bf16[3072,512]{1,0:T(8,128)(2,1)} %bitcast.25, s32[2048]{0:T(1024)S(1)} %broadcast_clamp_fusion), kind=kCustom, calls=%fused_computation | custom fusion | bytes 4202496 | tf_op jit(solution)/shard_map/gather | solution.py:174
  283.2 5.4 reshape.309
  288.6 7.7 multiply_reduce_fusion.2
  297.1 4.7 multiply_convert_fusion.1
  301.8 5.0 fusion.47
  306.9 3.4 multiply_reduce_fusion.3
  312.8 3.4 mul.256
  316.2 6.2 mul.257
  322.4 13.1 %scatter_custom_fusion.2 = bf16[3072,512]{1,0:T(8,128)(2,1)} fusion(s32[2048]{0:T(1024)S(1)} %bitcast.206, f32[2048,512]{1,0:T(8,128)} %mul.257, f32[2048]{0:T(1024)S(1)} %div.59, bf16[]{:T(256)} %constant.98.clone.1), kind=kCustom, calls=%fused_computation.102 | custom fusion | flops 2097152 | bytes 7348226 | tf_op jit(solution)/shard_map/scatter | solution.py:204
  335.5 3.7 all-to-all-start.3
  339.3 70.0 %all-to-all-done.3 = bf16[4,768,512]{2,1,0:T(8,128)(2,1)S(1)} async-done(((bf16[4,768,512]{2,1,0:T(8,128)(2,1)}), bf16[4,768,512]{2,1,0:T(8,128)(2,1)S(1)}, u32[]{:S(2)}, u32[]{:S(2)}) %all-to-all-start.3) | async-done | bytes 3145760 | tf_op jit(solution)/shard_map/all_to_all | solution.py:207
  411.3 68.2 %while.33 = (s32[]{:T(128)}, bf16[4,768,512]{2,1,0:T(8,128)(2,1)}, bf16[4,1024,128]{2,1,0:T(8,128)(2,1)}, f32[4,512,64]{1,2,0:T(8,128)}, f32[4,64,512]{2,1,0:T(8...) while((s32[]{:T(128)}, bf16[4,768,512]{2,1,0:T(8,128)(2,1)}, ...), condition=%wide.region_22.23_spmd, body=%wide.region_20.22_spmd.sunk | while | flops 713702656 | bytes 31267520 | solution.py:224
  416.7 2.2 multiply_reduce_fusion.10
  423.4 2.0 fusion.176
  426.2 2.2 fusion.174
  433.7 2.2 multiply_reduce_fusion.10
  440.4 2.0 fusion.176
  443.2 2.2 fusion.174
  450.8 2.2 multiply_reduce_fusion.10
  457.5 2.0 fusion.176
  460.3 2.2 fusion.174
  467.9 2.2 multiply_reduce_fusion.10
  474.6 2.0 fusion.176
  477.3 2.2 fusion.174
  479.6 3.7 all-to-all-start.4
  483.6 7.2 fusion.84
  490.8 4.6 fusion.78
  498.9 31.1 %reduce-scatter.2.cloned.1.call-done = bf16[1024,128]{1,0:T(8,128)(2,1)} async-done(((bf16[4096,128]{1,0:T(8,128)(2,1)}), bf16[1024,128]{1,0:T(8,128)(2,1)}) %reduce-scatter.2.cloned.1.call-update) | async-done | bytes 262160 | tf_op jit(solution)/shard_map/reduce_scatter | solution.py:238
  529.9 2.4 fusion.83
  532.4 5.9 multiply_reduce_fusion.1
  539.7 2.1 fusion.85
  541.8 6.8 add_convert_fusion
  548.6 64.8 %all-reduce.8.cloned.1.call-done = (bf16[1,512,64]{1,2,0:T(8,128)(2,1)}, bf16[1,64,512]{2,1,0:T(8,128)(2,1)}) async-done(((bf16[1,512,64]{1,2,0:T(8,128)(2,1)}, bf16[1,64,512]{2,1,0:T(8,128)(2,1)}), (bf16[1,512,64]{1,2,0:T(8,128)(2,1)}, bf16[1,64,512]{2,1,0:T(8,128)(2,1)})) %all-reduce.8.cloned.1.call-update) | async-done | bytes 131088 | tf_op jit(solution)/shard_map/psum | solution.py:247
  618.2 9.5 %gather_fusion.1 = bf16[2048,512]{1,0:T(8,128)(2,1)} fusion(bf16[3072,512]{1,0:T(8,128)(2,1)S(1)} %bitcast.191, s32[2048]{0:T(1024)S(1)} %copy-done.22), kind=kCustom, calls=%fused_computation.1 | custom fusion | bytes 4202496 | tf_op jit(solution)/shard_map/gather | solution.py:252
  627.7 5.5 reshape.310
  633.2 8.7 %reduce_sum.214 = f32[1024,512]{1,0:T(8,128)} reduce(f32[1024,2,512]{2,1,0:T(2,128)} %reshape.310, f32[]{:T(128)} %constant.71.clone.1), dimensions={1}, to_apply=%region_27.28 | reduce | flops 524288 | bytes 6291460 | tf_op jit(solution)/shard_map/reduce_sum | solution.py:259
  642.0 4.8 fusion.60
  646.8 40.0 %all-reduce = (f32[512]{0:T(512)}, f32[512,4]{0,1:T(4,128)}, f32[512]{0:T(512)}) all-reduce(f32[512]{0:T(512)S(1)} %get-tuple-element.235, f32[512,4]{0,1:T(4,128)S(1)} %copy-done.28, f32[512]{0:T(512)S(1)} %copy-done.36), channel_id=1, replica_groups=mesh['dp'=4,'expert'=4,'tok'=2] {'dp','expert','tok'}, use_global_device_ids=true, to_apply=%region_31.32 | all-reduce | flops 3072 | bytes 24576 | tf_op jit(solution)/shard_map/psum | solution.py:263
  686.9 3.0 fusion.59
  689.9 113.2 %all-reduce.6.cloned.1.call-done = (f32[512,128]{1,0:T(8,128)}, f32[512,2048]{1,0:T(8,128)}, f32[2048,512]{1,0:T(8,128)}) async-done(((f32[512,128]{1,0:T(8,128)}, f32[512,2048]{1,0:T(8,128)}, f32[2048,512]{1,0:T(8,128)}), (f32[512,128]{1,0:T(8,128)}, f32[512,2048]{1,0:T(8,128)}, f32[2048,512]{1,0:T(8,128)})) %all-reduce.6.cloned.1.call-update) | async-done | bytes 8650768 | tf_op jit(solution)/shard_map/psum | solution.py:263
  804.8 4.8 copy.166
  809.7 2.0 copy.167
  (236 shorter events, 97.1 us)
Async XLA Ops:
  7.2 289.8 %copy-start = (bf16[512,2048]{1,0:T(8,128)(2,1)S(1)}, bf16[512,2048]{1,0:T(8,128)(2,1)}, u32[]{:S(2)}) copy-start(bf16[512,2048]{1,0:T(8,128)(2,1)} %param.26) | copy-start | bytes 6291460
  7.2 27.3 %copy-start.5 = (bf16[1024,512]{1,0:T(8,128)(2,1)S(1)}, bf16[1024,512]{1,0:T(8,128)(2,1)}, u32[]{:S(2)}) copy-start(bf16[1024,512]{1,0:T(8,128)(2,1)} %param.16) | copy-start | bytes 3145732
  7.2 28.7 %copy-start.29 = (f32[512]{0:T(512)S(1)}, f32[512]{0:T(512)}, u32[]{:S(2)}) copy-start(f32[512]{0:T(512)} %param.20) | copy-start | bytes 6148
  28.2 28.0 %all-to-all-start = ((s32[4,1,768]{2,1,0:T(1,128)}), s32[4,1,768]{2,1,0:T(1,128)S(1)}, u32[]{:S(2)}, u32[]{:S(2)}) async-start(s32[4,1,768]{2,1,0:T(1,128)} %bitcast.20), calls=%async_computation | async-start | bytes 24576 | tf_op jit(solution)/shard_map/all_to_all | solution.py:154
  34.7 0.6 copy-start.19
  35.3 0.6 copy-start.23
  37.5 166.3 %copy-start.4 = (bf16[1024,512]{1,0:T(8,128)(2,1)}, bf16[1024,512]{1,0:T(8,128)(2,1)S(1)}, u32[]{:S(2)}) copy-start(bf16[1024,512]{1,0:T(8,128)(2,1)S(1)} %fusion.54) | copy-start | bytes 3145732
  56.1 5.3 copy-start.15
  56.1 6.4 copy-start.35
  56.1 99.0 %copy-start.25 = (bf16[1,512,64]{1,2,0:T(8,128)(2,1)S(1)}, bf16[1,512,64]{1,2,0:T(8,128)(2,1)}, u32[]{:S(2)}) copy-start(bf16[1,512,64]{1,2,0:T(8,128)(2,1)} %param.23) | copy-start | bytes 196612
  56.1 99.7 %all-to-all-start.1 = ((bf16[4,768,512]{2,1,0:T(8,128)(2,1)}), bf16[4,768,512]{2,1,0:T(8,128)(2,1)}, u32[]{:S(2)}, u32[]{:S(2)}) async-start(bf16[4,768,512]{2,1,0:T(8,128)(2,1)} %bitcast.192), calls=%async_computation.1 | async-start | bytes 6291456 | tf_op jit(solution)/shard_map/all_to_all | solution.py:153
  61.4 94.5 %all-gather.3.cloned.1.call-start = ((), (), s32[]{:S(2)}) async-start(), calls=%async_computation.6 | async-start | bytes 1310720 | tf_op jit(solution)/shard_map/all_gather | solution.py:157
  199.1 4.8 copy-start.33
  199.1 5.2 copy-start.17
  199.1 72.5 %all-to-all-start.2 = ((bf16[4,768,512]{2,1,0:T(8,128)(2,1)}), bf16[4,768,512]{2,1,0:T(8,128)(2,1)}, u32[]{:S(2)}, u32[]{:S(2)}) async-start(bf16[4,768,512]{2,1,0:T(8,128)(2,1)} %get-tuple-element.150), calls=%async_computation.2 | async-start | bytes 6291456 | tf_op jit(solution)/shard_map/all_to_all | solution.py:172
  204.4 78.8 %copy-start.26 = (f32[1024]{0:T(1024)}, f32[1024]{0:T(1024)S(1)}, u32[]{:S(2)}) copy-start(f32[1024]{0:T(1024)S(1)} %fusion.74) | copy-start | bytes 12292
  204.9 78.2 %copy-start.21 = (s32[2048]{0:T(1024)}, s32[2048]{0:T(1024)S(1)}, u32[]{:S(2)}) copy-start(s32[2048]{0:T(1024)S(1)} %broadcast_clamp_fusion) | copy-start | bytes 24580
  288.6 7.7 copy-start.6
  296.3 0.8 copy-start.31
  296.6 13.7 %copy-start.2 = (f32[1024,512]{1,0:T(8,128)}, f32[1024,512]{1,0:T(8,128)S(1)}, u32[]{:S(2)}) copy-start(f32[1024,512]{1,0:T(8,128)S(1)} %get-tuple-element.300) | copy-start | bytes 6291460
  297.0 4.8 copy-start.14
  297.0 4.7 copy-start.37
  306.8 3.4 copy-start.10
  311.4 1.4 copy-start.8
  335.5 73.8 %all-to-all-start.3 = ((bf16[4,768,512]{2,1,0:T(8,128)(2,1)}), bf16[4,768,512]{2,1,0:T(8,128)(2,1)S(1)}, u32[]{:S(2)}, u32[]{:S(2)}) async-start(bf16[4,768,512]{2,1,0:T(8,128)(2,1)} %bitcast.193), calls=%async_computation.3 | async-start | bytes 6291456 | tf_op jit(solution)/shard_map/all_to_all | solution.py:207
  339.3 190.7 %reduce-scatter.2.cloned.1.call-start = ((), (), s32[]{:S(2)}) async-start(), calls=%async_computation.7 | async-start | bytes 1310720 | tf_op jit(solution)/shard_map/reduce_scatter | solution.py:238
  479.6 138.7 %all-to-all-start.4 = ((bf16[4,768,512]{2,1,0:T(8,128)(2,1)}), bf16[4,768,512]{2,1,0:T(8,128)(2,1)S(1)}, u32[]{:S(2)}, u32[]{:S(2)}) async-start(bf16[4,768,512]{2,1,0:T(8,128)(2,1)} %get-tuple-element.155), calls=%async_computation.5 | async-start | bytes 6291456 | tf_op jit(solution)/shard_map/all_to_all | solution.py:237
  483.3 130.1 %all-reduce.8.cloned.1.call-start = ((), (), s32[]{:S(2)}) async-start(), calls=%async_computation.9 | async-start | bytes 262144 | tf_op jit(solution)/shard_map/psum | solution.py:247
  483.5 7.2 copy-start.3
  483.5 7.2 copy-start.11
  483.6 7.2 copy-start.32
  498.8 304.3 %all-reduce.6.cloned.1.call-start = ((), (), s32[]{:S(2)}) async-start(), calls=%async_computation.8 | async-start | bytes 17301504 | tf_op jit(solution)/shard_map/psum | solution.py:263
  532.4 7.2 copy-start.27
  532.4 7.2 copy-start.18
  541.8 74.6 %copy-start.13 = (bf16[1024,128]{1,0:T(8,128)(2,1)S(1)}, bf16[1024,128]{1,0:T(8,128)(2,1)}, u32[]{:S(2)}) copy-start(bf16[1024,128]{1,0:T(8,128)(2,1)} %reduce-scatter.2.cloned.1.call-done) | copy-start | bytes 786436
  541.8 74.6 %copy-start.16 = (bf16[512,128]{1,0:T(8,128)(2,1)S(1)}, bf16[512,128]{1,0:T(8,128)(2,1)}, u32[]{:S(2)}) copy-start(bf16[512,128]{1,0:T(8,128)(2,1)} %param.21) | copy-start | bytes 393220
  541.8 76.4 %copy-start.22 = (s32[2048]{0:T(1024)S(1)}, s32[2048]{0:T(1024)}, u32[]{:S(2)}) copy-start(s32[2048]{0:T(1024)} %copy-done.21) | copy-start | bytes 24580
  633.2 8.7 %copy-start.7 = (bf16[1024,512]{1,0:T(8,128)(2,1)S(1)}, bf16[1024,512]{1,0:T(8,128)(2,1)}, u32[]{:S(2)}) copy-start(bf16[1024,512]{1,0:T(8,128)(2,1)} %param.16) | copy-start | bytes 3145732
  633.2 8.7 %copy-start.20 = (f32[1024]{0:T(1024)S(1)}, f32[1024]{0:T(1024)}, u32[]{:S(2)}) copy-start(f32[1024]{0:T(1024)} %copy-done.19) | copy-start | bytes 12292
  633.2 8.7 %copy-start.24 = (f32[1024]{0:T(1024)S(1)}, f32[1024]{0:T(1024)}, u32[]{:S(2)}) copy-start(f32[1024]{0:T(1024)} %copy-done.23) | copy-start | bytes 12292
  633.2 8.7 %copy-start.30 = (f32[512]{0:T(512)S(1)}, f32[512]{0:T(512)}, u32[]{:S(2)}) copy-start(f32[512]{0:T(512)} %param.20) | copy-start | bytes 6148
  633.2 8.7 %copy-start.34 = (bf16[512,4]{0,1:T(4,128)(2,1)S(1)}, bf16[512,4]{0,1:T(4,128)(2,1)}, u32[]{:S(2)}) copy-start(bf16[512,4]{0,1:T(4,128)(2,1)} %param.22) | copy-start | bytes 12292
  641.9 4.9 copy-start.28
  641.9 4.9 copy-start.36
  642.0 44.9 %copy-start.9 = (f32[1024,512]{1,0:T(8,128)S(1)}, f32[1024,512]{1,0:T(8,128)}, u32[]{:S(2)}) copy-start(f32[1024,512]{1,0:T(8,128)} %copy-done.8) | copy-start | bytes 6291460
  804.8 4.9 copy-start.12
  804.8 6.9 copy-start.1
Sparse Core Ops, SparseCore 0:
  64.3 43.4 all-gather.2
  479.7 50.2 reduce-scatter.1
  533.9 79.4 all-reduce.7
  620.0 183.1 all-reduce.5
where the time goes:
time: 829 us; the launch traced here: 819 us
  waiting for transfers between devices  346 us (42%)
  blocking collectives  131 us (16%)
  matrix products  122 us (15%)
  local copies, waits for them, and re-layouts  120 us (14%)
  other arithmetic  60.4 us (7%)
  starting transfers between devices  24.1 us (3%)
  between operations  14.8 us (2%)
    psum x1, waiting for transfers between devices, body(): lax.psum((ln_attn_grad, kv_weight_grad, router_grad, in_weight_grad, out_...  113 us
    all_gather x1, blocking collectives, body(): lax.all_gather(sentence, 'expert', axis=0, tiled=True)  91.3 us
    all_to_all x1, waiting for transfers between devices, body(): lax.all_to_all(route_dispatch, 'expert', split_axis=0, concat_axis=0, til...  70 us
    all_to_all x1, waiting for transfers between devices, body(): lax.all_to_all(results, 'expert', split_axis=0, concat_axis=0, tiled=True)  66.7 us
    psum x1, waiting for transfers between devices, body(): lax.psum(query_grad_sum.astype(jnp.bfloat16), ('dp', 'tok'))  64.8 us
    dot_general x24, matrix products, product_nt(): lax.dot_general(left, right, (((1,), (1,)), ((), ())), preferred_element_...  43.4 us
    dot_general x20, matrix products, product(): return jnp.dot(left, right, preferred_element_type=jnp.float32)  40.2 us
    psum x1, blocking collectives, body(): lax.psum((ln_attn_grad, kv_weight_grad, router_grad, in_weight_grad, out_...  40 us
  transfers between devices with their start and end apart: 9, of which 5 were waited for; matrix products, arithmetic and copies ran while one was open for 12% of the time, Pallas kernels for 0%

commit v1 on v0

v1 whole, which is shorter than its diff:
```python
import functools
import jax
import jax.numpy as jnp
from jax import lax
from jax.experimental import pallas as pl
from jax.experimental.pallas import tpu as pltpu
from jax.sharding import PartitionSpec as P

BF = jnp.bfloat16
F32 = jnp.float32
MASKED = -1e30
BAND = 128
ROWS = 256
VMEM_LIMIT = 56 * 1024 * 1024


def nn(left, right):
    return lax.dot_general(left, right, (((1,), (0,)), ((), ())), preferred_element_type=F32)


def nt(left, right):
    return lax.dot_general(left, right, (((1,), (1,)), ((), ())), preferred_element_type=F32)


def tn(left, right):
    return lax.dot_general(left, right, (((0,), (0,)), ((), ())), preferred_element_type=F32)


def normalize(values):
    centre = values - jnp.mean(values, axis=-1, keepdims=True)
    spread = jnp.mean(centre * centre, axis=-1, keepdims=True)
    inverse = lax.rsqrt(spread + 1e-05)
    return centre * inverse, inverse


def normalize_back(upstream, normalized, inverse, gain):
    scaled = upstream * gain
    inner = (
        scaled
        - jnp.mean(scaled, axis=-1, keepdims=True)
        - normalized * jnp.mean(scaled * normalized, axis=-1, keepdims=True)
    )
    return inner * inverse


def vmem(count):
    return [pl.BlockSpec(memory_space=pltpu.VMEM)] * count


def call(kernel, operands, outs, scratch=(), flops=0, **extra):
    moved = sum(a.size * a.dtype.itemsize for a in operands)
    moved += sum(o.size * jnp.dtype(o.dtype).itemsize for o in outs)
    return pl.pallas_call(
        kernel,
        out_shape=outs,
        in_specs=vmem(len(operands)),
        out_specs=vmem(len(outs)),
        scratch_shapes=list(scratch),
        compiler_params=pltpu.CompilerParams(vmem_limit_bytes=VMEM_LIMIT),
        cost_estimate=pl.CostEstimate(flops=flops, bytes_accessed=moved, transcendentals=0),
        **extra,
    )(*operands)


def sds(shape, dtype):
    return jax.ShapeDtypeStruct(shape, dtype)


def prepare_kernel(x_ref, g_ref, ids_ref, ln_ref, small_ref, xn_ref, kv_ref, kvt_ref, gates_ref, gt_ref, *, experts, pair):
    length = x_ref.shape[0]
    gain = ln_ref[...]
    for start in range(0, length, ROWS):
        rows = pl.ds(start, ROWS)
        normalized, _ = normalize(x_ref[rows, :].astype(F32))
        xn_ref[rows, :] = (normalized * gain).astype(BF)
    normed = xn_ref[...]
    small = small_ref[...]
    both = nt(small, normed)
    kvt_ref[...] = both[:pair].astype(BF)
    kv_ref[...] = nt(normed, small[:pair]).astype(BF)
    choose = ids_ref.shape[0]
    picked = []
    for route in range(choose):
        ids = ids_ref[route : route + 1, :]
        value = jnp.zeros((1, length), F32)
        for expert in range(experts):
            value = jnp.where(ids == expert, both[pair + expert : pair + expert + 1], value)
        picked.append(value)
    top = functools.reduce(jnp.maximum, picked)
    raised = [jnp.exp(value - top) for value in picked]
    total = functools.reduce(lambda a, b: a + b, raised)
    for route in range(choose):
        gates_ref[route : route + 1, :] = raised[route] / total
    gt_ref[...] = g_ref[...].T


def column_ids(sent_ref, keyid_ref):
    length = sent_ref.shape[1]
    for start in range(0, length, BAND):
        row = jnp.broadcast_to(sent_ref[:, start : start + BAND].astype(F32), (BAND, BAND))
        keyid_ref[pl.ds(start, BAND), :] = row.T


def masked_scores(kv_ref, keyid_ref, sent_ref, queries, start, low, high, head, choose):
    padded = jnp.concatenate([queries, jnp.zeros_like(queries)], axis=0)
    scores = nn(kv_ref[low:high, :], padded) * 0.125
    same = keyid_ref[low:high, :] == sent_ref[:, start : start + BAND].astype(F32)
    parts = [
        jnp.where(same, scores[:, route * BAND : (route + 1) * BAND], MASKED)
        for route in range(choose)
    ]
    return jnp.concatenate(parts, axis=1)


def window(start, length):
    return max(start - BAND, 0), min(start + 2 * BAND, length)


def attend_kernel(
    x_ref, xn_ref, kv_ref, kvt_ref, ids_ref, sent_ref, gates_ref, wq_ref, wo_ref, ln_ref,
    qt_ref, at_ref, lse_ref, gat_ref, h_ref, hn_ref, hnt_ref, all_ref, keyid_ref, *, experts, head,
):
    length = x_ref.shape[0]
    choose = ids_ref.shape[0]
    column_ids(sent_ref, keyid_ref)
    all_ref[...] = nt(wq_ref[...], xn_ref[...])
    for start in range(0, length, BAND):
        lanes = slice(start, start + BAND)
        block = slice(start * choose, (start + BAND) * choose)
        low, high = window(start, length)
        chosen = []
        for route in range(choose):
            ids = ids_ref[route : route + 1, lanes]
            value = jnp.zeros((head, BAND), F32)
            for expert in range(experts):
                value = jnp.where(
                    ids == expert, all_ref[expert * head : (expert + 1) * head, lanes], value
                )
            chosen.append(value)
        queries = jnp.concatenate(chosen, axis=1).astype(BF)
        qt_ref[:, block] = queries
        scores = masked_scores(kv_ref, keyid_ref, sent_ref, queries, start, low, high, head, choose)
        largest = jnp.max(scores, axis=0, keepdims=True)
        raised = jnp.exp(scores - largest)
        total = jnp.sum(raised, axis=0, keepdims=True)
        probs = (raised * (1.0 / total)).astype(BF)
        lse_ref[:, block] = largest + jnp.log(total)
        attended = nn(kvt_ref[head:, low:high], probs).astype(BF)
        at_ref[:, block] = attended
        spread = [jnp.zeros((head, BAND), F32) for _ in range(experts)]
        for route in range(choose):
            ids = ids_ref[route : route + 1, lanes]
            gated = attended[:, route * BAND : (route + 1) * BAND].astype(F32) * gates_ref[
                route : route + 1, lanes
            ]
            for expert in range(experts):
                spread[expert] = jnp.where(ids == expert, gated, spread[expert])
        for expert in range(experts):
            gat_ref[expert * head : (expert + 1) * head, lanes] = spread[expert].astype(BF)
    gain = ln_ref[...]
    for start in range(0, length, ROWS):
        rows = slice(start, start + ROWS)
        mixed = tn(gat_ref[:, rows], wo_ref[...])
        hidden = x_ref[rows, :].astype(F32) + mixed
        h_ref[rows, :] = hidden
        normalized, _ = normalize(hidden)
        low_value = (normalized * gain).astype(BF)
        hn_ref[rows, :] = low_value
        hnt_ref[:, rows] = low_value.T


def gelu_both(values):
    bell = jnp.exp(-0.5 * values * values)
    t = 1.0 / (1.0 + 0.23164188 * jnp.abs(values))
    poly = 0.5 * t * (
        0.254829592
        + t * (-0.284496736 + t * (1.421413741 + t * (-1.453152027 + t * 1.061405429)))
    )
    tail = poly * bell
    cumulative = jnp.where(values >= 0.0, 1.0 - tail, tail)
    return values * cumulative, cumulative + values * bell * 0.3989422804014327


def ffn_kernel(hn_ref, hnt_ref, g_ref, gt_ref, win_ref, wout_ref, u_ref, dpre_ref, gin_ref, gout_ref):
    length = hn_ref.shape[0]
    win = win_ref[...]
    wout = wout_ref[...]
    for start in range(0, length, ROWS):
        rows = slice(start, start + ROWS)
        before = nn(hn_ref[rows, :], win)
        upstream = nt(g_ref[rows, :], wout)
        activated, slope = gelu_both(before)
        u_ref[rows, :] = activated.astype(BF)
        dpre_ref[rows, :] = (upstream * slope).astype(BF)
    gin_ref[...] = nn(hnt_ref[...], dpre_ref[...]).astype(gin_ref.dtype)
    gout_ref[...] = nn(gt_ref[...], u_ref[...]).T.astype(gout_ref.dtype)


def finish_kernel(h_ref, g_ref, u_ref, dpre_ref, win_ref, wout_ref, ln_ref, out_ref, dh_ref, gain_ref):
    hidden = h_ref[...]
    out_ref[...] = (hidden + nn(u_ref[...], wout_ref[...])).astype(BF)
    upstream = nt(dpre_ref[...], win_ref[...])
    normalized, inverse = normalize(hidden)
    dh_ref[...] = g_ref[...].astype(F32) + normalize_back(upstream, normalized, inverse, ln_ref[...])

    @pl.when(pl.program_id(0) == 0)
    def _():
        gain_ref[...] = jnp.zeros_like(gain_ref)

    gain_ref[...] += jnp.sum(upstream * normalized, axis=0, keepdims=True)


def back_kernel(
    x_ref, xn_ref, kv_ref, kvt_ref, ids_ref, sent_ref, gates_ref, wcat_ref, wo_ref, ln_ref,
    qt_ref, at_ref, lse_ref, gat_ref, dh_ref,
    dx_ref, grads_ref, gout_ref, gain_ref, all_ref, keyid_ref, z_ref, dkv_ref, *, experts, head,
):
    length = x_ref.shape[0]
    choose = ids_ref.shape[0]
    wide = experts * head
    column_ids(sent_ref, keyid_ref)
    dh_low = dh_ref[...].astype(BF)
    all_ref[...] = nt(wo_ref[...], dh_low)
    gout_ref[...] = nn(gat_ref[...], dh_low).astype(gout_ref.dtype)
    dkv_ref[...] = jnp.zeros_like(dkv_ref)
    z_ref[...] = jnp.zeros_like(z_ref)
    for start in range(0, length, BAND):
        lanes = slice(start, start + BAND)
        block = slice(start * choose, (start + BAND) * choose)
        low, high = window(start, length)
        raw, gate_grads = [], []
        for route in range(choose):
            ids = ids_ref[route : route + 1, lanes]
            value = jnp.zeros((head, BAND), F32)
            for expert in range(experts):
                value = jnp.where(
                    ids == expert, all_ref[expert * head : (expert + 1) * head, lanes], value
                )
            raw.append(value)
            attended = at_ref[:, start * choose + route * BAND : start * choose + (route + 1) * BAND]
            gate_grads.append(jnp.sum(value * attended.astype(F32), axis=0, keepdims=True))
        gates = [gates_ref[route : route + 1, lanes] for route in range(choose)]
        common = functools.reduce(
            lambda a, b: a + b, [gate * grad for gate, grad in zip(gates, gate_grads)]
        )
        logit_rows = [jnp.zeros((1, BAND), F32) for _ in range(experts)]
        for route in range(choose):
            ids = ids_ref[route : route + 1, lanes]
            picked = gates[route] * (gate_grads[route] - common)
            for expert in range(experts):
                logit_rows[expert] = jnp.where(ids == expert, picked, logit_rows[expert])
        logit_pad = jnp.concatenate(
            logit_rows + [jnp.zeros((16 - experts, BAND), F32)], axis=0
        )
        z_ref[wide + 2 * head :, lanes] = logit_pad.astype(BF)
        queries = qt_ref[:, block]
        scores = masked_scores(kv_ref, keyid_ref, sent_ref, queries, start, low, high, head, choose)
        probs = jnp.exp(scores - lse_ref[:, block])
        prob_low = probs.astype(BF)
        upstream = jnp.concatenate(
            [gate * value for gate, value in zip(gates, raw)], axis=1
        ).astype(BF)
        padded = jnp.concatenate([jnp.zeros_like(upstream), upstream], axis=0)
        prob_grad = nn(kv_ref[low:high, :], padded)
        mean = jnp.sum(probs * prob_grad, axis=0, keepdims=True)
        score_grad = (probs * (prob_grad - mean)).astype(BF)
        query_grad = (nn(kvt_ref[:head, low:high], score_grad) * 0.125).astype(BF)
        spread = [jnp.zeros((head, BAND), BF) for _ in range(experts)]
        for route in range(choose):
            ids = ids_ref[route : route + 1, lanes]
            piece = query_grad[:, route * BAND : (route + 1) * BAND]
            for expert in range(experts):
                spread[expert] = jnp.where(ids == expert, piece, spread[expert])
        for expert in range(experts):
            z_ref[expert * head : (expert + 1) * head, lanes] = spread[expert]
        dkv_ref[:head, low:high] += nt(queries, score_grad) * 0.125
        dkv_ref[head:, low:high] += nt(upstream, prob_low)
    z_ref[wide : wide + 2 * head, :] = dkv_ref[...].astype(BF)
    grads_ref[...] = nn(z_ref[...], xn_ref[...]).astype(grads_ref.dtype)
    gain = ln_ref[...]
    total = jnp.zeros_like(gain)
    for start in range(0, length, ROWS):
        rows = slice(start, start + ROWS)
        normed_grad = tn(z_ref[:, rows], wcat_ref[...])
        normalized, inverse = normalize(x_ref[rows, :].astype(F32))
        total = total + jnp.sum(normed_grad * normalized, axis=0, keepdims=True)
        back = normalize_back(normed_grad, normalized, inverse, gain)
        dx_ref[rows, :] = (dh_ref[rows, :] + back).astype(BF)
    gain_ref[...] = total


def transposed_weights(w_kv, w_router):
    pad = jnp.zeros((16 - w_router.shape[1], w_router.shape[0]), BF)
    return jnp.concatenate([w_kv.T, w_router.T, pad], axis=0)


def local_prepare(tokens, out_grad, ids, ln, small, experts, pair):
    length, width = tokens.shape
    kernel = functools.partial(prepare_kernel, experts=experts, pair=pair)
    return call(
        kernel,
        (tokens, out_grad, ids, ln, small),
        [
            sds((length, width), BF),
            sds((length, pair), BF),
            sds((pair, length), BF),
            sds(ids.shape, F32),
            sds((width, length), BF),
        ],
        flops=2 * length * width * 2 * pair,
    )


def local_attend(tokens, normed, kv, kvt, ids, sent, gates, wq, wo, ln, experts, head):
    length, width = tokens.shape
    choose = ids.shape[0]
    kernel = functools.partial(attend_kernel, experts=experts, head=head)
    return call(
        kernel,
        (tokens, normed, kv, kvt, ids, sent, gates, wq, wo, ln),
        [
            sds((head, choose * length), BF),
            sds((head, choose * length), BF),
            sds((1, choose * length), F32),
            sds((experts * head, length), BF),
            sds((length, width), F32),
            sds((length, width), BF),
            sds((width, length), BF),
        ],
        scratch=(pltpu.VMEM((experts * head, length), F32), pltpu.VMEM((length, BAND), F32)),
        flops=4 * length * width * experts * head,
    )


def local_ffn(hn, hnt, g, gt, w_in, w_out, chunk, chunks):
    length, width = hn.shape
    hidden = w_in.shape[1] // chunks
    whole = pl.BlockSpec((length, width), lambda i: (0, 0))
    turned = pl.BlockSpec((width, length), lambda i: (0, 0))
    return pl.pallas_call(
        ffn_kernel,
        grid=(1,),
        out_shape=[
            sds((length, hidden), BF),
            sds((length, hidden), BF),
            sds((width, hidden), BF),
            sds((hidden, width), BF),
        ],
        in_specs=[
            whole, turned, whole, turned,
            pl.BlockSpec((width, hidden), lambda i: (0, chunk)),
            pl.BlockSpec((hidden, width), lambda i: (chunk, 0)),
        ],
        out_specs=[
            pl.BlockSpec((length, hidden), lambda i: (0, 0)),
            pl.BlockSpec((length, hidden), lambda i: (0, 0)),
            pl.BlockSpec((width, hidden), lambda i: (0, 0)),
            pl.BlockSpec((hidden, width), lambda i: (0, 0)),
        ],
        compiler_params=pltpu.CompilerParams(vmem_limit_bytes=VMEM_LIMIT),
        cost_estimate=pl.CostEstimate(
            flops=8 * length * width * hidden, bytes_accessed=8 << 20, transcendentals=0
        ),
    )(hn, hnt, g, gt, w_in, w_out)


def local_finish(h, g, us, dpres, w_in, w_out, ln):
    length, width = h.shape
    chunks = len(us)
    hidden = us[0].shape[1]

    def kernel(h_ref, g_ref, *refs):
        u_refs, dpre_refs = refs[:chunks], refs[chunks : 2 * chunks]
        win_ref, wout_ref, ln_ref, out_ref, dh_ref, gain_ref = refs[2 * chunks :]
        value = h_ref[...]
        total, upstream = value, None
        for c in range(chunks):
            total = total + nn(u_refs[c][...], wout_ref[c * hidden : (c + 1) * hidden, :])
            part = nt(dpre_refs[c][...], win_ref[:, c * hidden : (c + 1) * hidden])
            upstream = part if upstream is None else upstream + part
        out_ref[...] = total.astype(BF)
        normalized, inverse = normalize(value)
        dh_ref[...] = g_ref[...].astype(F32) + normalize_back(
            upstream, normalized, inverse, ln_ref[...]
        )

        @pl.when(pl.program_id(0) == 0)
        def _():
            gain_ref[...] = jnp.zeros_like(gain_ref)

        gain_ref[...] += jnp.sum(upstream * normalized, axis=0, keepdims=True)

    row = pl.BlockSpec((ROWS, width), lambda i: (i, 0))
    part = pl.BlockSpec((ROWS, hidden), lambda i: (i, 0))
    fixed = lambda a: pl.BlockSpec(a.shape, lambda i: (0, 0))
    return pl.pallas_call(
        kernel,
        grid=(length // ROWS,),
        out_shape=[sds((length, width), BF), sds((length, width), F32), sds((1, width), F32)],
        in_specs=[row, row] + [part] * (2 * chunks) + [fixed(w_in), fixed(w_out), fixed(ln)],
        out_specs=[row, row, pl.BlockSpec((1, width), lambda i: (0, 0))],
        compiler_params=pltpu.CompilerParams(vmem_limit_bytes=VMEM_LIMIT),
        cost_estimate=pl.CostEstimate(
            flops=4 * length * width * hidden * chunks, bytes_accessed=20 << 20, transcendentals=0
        ),
    )(h, g, *us, *dpres, w_in, w_out, ln)


def local_back(tokens, normed, kv, kvt, ids, sent, gates, wcat, wo, ln, kept, dh, experts, head):
    length, width = tokens.shape
    rows = experts * head + 2 * head + 16
    kernel = functools.partial(back_kernel, experts=experts, head=head)
    qt, at, lse, gat = kept
    return call(
        kernel,
        (tokens, normed, kv, kvt, ids, sent, gates, wcat, wo, ln, qt, at, lse, gat, dh),
        [
            sds((length, width), BF),
            sds((rows, width), BF),
            sds((experts * head, width), BF),
            sds((1, width), F32),
        ],
        scratch=(
            pltpu.VMEM((experts * head, length), F32),
            pltpu.VMEM((length, BAND), F32),
            pltpu.VMEM((rows, length), BF),
            pltpu.VMEM((2 * head, length), F32),
        ),
        flops=8 * length * width * experts * head,
    )


CHUNKS = 4
AXES = ("dp", "expert", "tok")


def body(tokens, out_grad, expert_ids, sentence_ids, ln_attn, w_kv, w_router, w_query, w_output, ln_ffn, w_in, w_out):
    width = tokens.shape[1]
    head = w_query.shape[2]
    pair = w_kv.shape[1]
    experts = lax.axis_size("expert")
    wq = lax.all_gather(w_query[0].T, "expert", axis=0, tiled=True)
    wo = lax.all_gather(w_output[0], "expert", axis=0, tiled=True)
    ids = expert_ids.T
    ln_one = ln_attn.reshape(1, width)
    ln_two = ln_ffn.reshape(1, width)
    small = transposed_weights(w_kv, w_router)
    normed, kv, kvt, gates, gt = local_prepare(tokens, out_grad, ids, ln_one, small, experts, pair)
    qt, at, lse, gat, h, hn, hnt = local_attend(
        tokens, normed, kv, kvt, ids, sentence_ids, gates, wq, wo, ln_two, experts, head
    )
    us, dpres, gins, gouts = [], [], [], []
    for chunk in range(CHUNKS):
        u, dpre, gin, gout = local_ffn(hn, hnt, out_grad, gt, w_in, w_out, chunk, CHUNKS)
        us.append(u)
        dpres.append(dpre)
        gins.append(gin)
        gouts.append(gout)
    output, dh, ln_two_grad = local_finish(h, out_grad, us, dpres, w_in, w_out, ln_two)
    wcat = jnp.concatenate([wq, small], axis=0)
    dx, grads, wo_grad, ln_one_grad = local_back(
        tokens, normed, kv, kvt, ids, sentence_ids, gates, wcat, wo, ln_one, (qt, at, lse, gat), dh, experts, head
    )
    wide = experts * head
    gin, gout, small_grad, gain_grads = lax.psum(
        (
            jnp.concatenate(gins, axis=1),
            jnp.concatenate(gouts, axis=0),
            grads[wide:],
            jnp.concatenate([ln_one_grad, ln_two_grad], axis=0),
        ),
        AXES,
    )
    experts_grad = jnp.concatenate([grads[:wide].reshape(experts, head, width), wo_grad.reshape(experts, head, width)], axis=1)
    own = lax.psum(lax.psum_scatter(experts_grad, "expert", scatter_dimension=0, tiled=True), ("dp", "tok"))[0].astype(F32)
    return (
        output,
        dx,
        gain_grads[0],
        small_grad[:pair].T.astype(F32),
        small_grad[pair : pair + experts].T.astype(F32),
        own[:head].T[None],
        own[head:][None],
        gain_grads[1],
        gin.astype(F32),
        gout.astype(F32),
    )


def solution(mesh):
    rows = P(AXES, None)
    heads = P("expert", None, None)
    return jax.shard_map(
        body,
        mesh=mesh,
        in_specs=(rows, rows, rows, rows, P(), P(), P(), heads, heads, P(), P(), P()),
        out_specs=(rows, rows, P(), P(), P(), heads, heads, P(), P(), P()),
        check_vma=False,
    )
```

time: 829 us -> 351 us (0.42); the launches traced: 819 us -> 351 us
  waiting for transfers between devices: 346 us -> 179 us
  matrix products: 122 us -> 0 us
  local copies, waits for them, and re-layouts: 120 us -> 7.94 us
  blocking collectives: 131 us -> 70.6 us
  Pallas kernels: 0 us -> 60.2 us
  other arithmetic: 60.4 us -> 19.1 us
  starting transfers between devices: 24.1 us -> 0.12 us
    all_to_all x5 -> x0, waiting for transfers between devices: 137 us -> none  [the longest x1 70 us: body(): lax.all_to_all(route_dispatch, 'expert', split_axis=0, concat_axis=0, til...]
    dot_general x64 -> x0, matrix products: 122 us -> none  [the longest x24 43.4 us: product_nt(): lax.dot_general(left, right, (((1,), (1,)), ((), ())), preferred_element_...]
    pallas_call x0 -> x8, Pallas kernels: none -> 60.2 us  [the longest x4 27.6 us: local_ffn(): pl.pallas_call(ffn_kernel, grid=(1,), out_shape=[sds((length, hidden), BF...]
    all_gather x1 -> x2, blocking collectives: 91.3 us -> 32.1 us  [the longest x1 16.3 us: body(): wo = lax.all_gather(w_output[0], 'expert', axis=0, tiled=True)]
    reduce_sum x18 -> x0, other arithmetic: 31.1 us -> none  [the longest x1 8.71 us: body(): jnp.sum(routes_back, axis=1)]
    all_to_all x5 -> x0, starting transfers between devices: 23.7 us -> none  [the longest x1 6.32 us: body(): lax.all_to_all(dispatch_ids, 'expert', split_axis=0, concat_axis=0, tiled...]
    gather x2 -> x0, local copies, waits for them, and re-layouts: 21 us -> none  [the longest x1 11.6 us: body(): returned.reshape(experts * capacity, width)[slot_index].astype(jnp.float32)]
    scatter x2 -> x0, local copies, waits for them, and re-layouts: 20.7 us -> none  [the longest x1 12.1 us: body(): dispatch_rows = jnp.zeros((experts * capacity, width), jnp.bfloat16).at[s...]
  transfers between devices with their start and end apart: 9 -> 3, of which waited for: 5 -> 3; matrix products, arithmetic and copies ran while one was open for 12% -> 3% of each run, Pallas kernels for 0% -> 0%
where the time goes in v1:
time: 351 us
  waiting for transfers between devices  179 us (51%)
  blocking collectives  70.6 us (20%)
  Pallas kernels  60.2 us (17%)
  other arithmetic  19.1 us (5%)
  between operations  13.9 us (4%)
  local copies, waits for them, and re-layouts  7.94 us (2%)
    psum x1, waiting for transfers between devices, body(): lax.psum((jnp.concatenate(gins, axis=1), jnp.concatenate(gouts, axis=0),...  149 us
    psum x1, blocking collectives, body(): lax.psum((jnp.concatenate(gins, axis=1), jnp.concatenate(gouts, axis=0),...  38.5 us
    pallas_call x4, Pallas kernels, local_ffn(): pl.pallas_call(ffn_kernel, grid=(1,), out_shape=[sds((length, hidden), BF...  27.6 us
    pallas_call x3, Pallas kernels, call(): pl.pallas_call(kernel, out_shape=outs, in_specs=vmem(len(operands)), out_...  21.8 us
    reduce_scatter x1, waiting for transfers between devices, body(): lax.psum_scatter(experts_grad, 'expert', scatter_dimension=0, tiled=True)  18.9 us
    all_gather x1, blocking collectives, body(): wo = lax.all_gather(w_output[0], 'expert', axis=0, tiled=True)  16.3 us
    all_gather x1, blocking collectives, body(): wq = lax.all_gather(w_query[0].T, 'expert', axis=0, tiled=True)  15.8 us
    psum x1, waiting for transfers between devices, body(): lax.psum(lax.psum_scatter(experts_grad, 'expert', scatter_dimension=0, ti...  11.2 us
  transfers between devices with their start and end apart: 3, of which 3 were waited for; matrix products, arithmetic and copies ran while one was open for 3% of the time, Pallas kernels for 0%

profile of v1, /device:TPU:0, one launch (start us, length us, event | category | flops | bytes accessed | tf_op | source)
XLA Modules:
  0.0 350.7 jit_solution(1476033130232489341)
XLA Ops:
  7.2 0.0 reduce-scatter.2.cloned.1.call-start
  7.2 1.0 copy.22
  8.2 15.8 %all_gather.6.wq_ref = bf16[256,512]{1,0:T(8,128)(2,1)S(1)} all-gather(bf16[64,512]{1,0:T(8,128)(2,1)} %bitcast.32), channel_id=1, replica_groups=mesh['dp'=4,'expert'=4,'tok'=2] {'expert'}, dimensions={0}, use_global_device_ids=true | all-gather | bytes 327680 | tf_op jit(solution)/shard_map/all_gather | solution.py:442
  24.1 0.0 copy-start
  24.1 1.4 pad_maximum_fusion.4.small_ref
  25.5 1.5 pad_maximum_fusion.3.wcat_ref
  26.9 16.3 %all-gather = bf16[1,256,512]{2,1,0:T(8,128)(2,1)} all-gather(bf16[1,64,512]{2,1,0:T(8,128)(2,1)} %param.20), channel_id=2, replica_groups=mesh['dp'=4,'expert'=4,'tok'=2] {'expert'}, dimensions={1}, use_global_device_ids=true | all-gather | bytes 327680 | tf_op jit(solution)/shard_map/all_gather | solution.py:443
  43.2 3.9 %shard_map.195 = (bf16[1024,512]{1,0:T(8,128)(2,1)}, bf16[1024,128]{1,0:T(8,128)(2,1)}, bf16[128,1024]{1,0:T(8,128)(2,1)}, f32[2,1024]{1,0:T(2,128)}, bf16[512,1024]{1,0:T(8,128)(2,1)}) custom-call(bf16[1024,512]{1,0:T(8,128)(2,1)} %x_ref.5, bf16[1024,512]{1,0:T(8,128)(2,1)} %g_ref.11, s32[2,1024]{1,0:T(2,128)} %bitcast.29, f32[1,512]{1,0:T(1,128)} %bitcast.35, ...), custom_call_target="tpu_custom_call" | custom-call | flops 268435456 | bytes 4884480 | tf_op jit(solution)/shard_map/pallas_call | solution.py:53
  47.1 0.0 copy-done
  47.1 8.2 %shard_map.196 = (bf16[64,2048]{1,0:T(8,128)(2,1)}, bf16[64,2048]{1,0:T(8,128)(2,1)}, f32[1,2048]{1,0:T(1,128)}, bf16[256,1024]{1,0:T(8,128)(2,1)}, f32[1024,512...) custom-call(bf16[1024,512]{1,0:T(8,128)(2,1)} %x_ref.5, ...), custom_call_target="tpu_custom_call" | custom-call | flops 536870912 | bytes 8419328 | tf_op jit(solution)/shard_map/pallas_call | solution.py:53
  55.3 6.9 %shard_map.200 = (bf16[1024,512]{1,0:T(8,128)(2,1)}, bf16[1024,512]{1,0:T(8,128)(2,1)}, bf16[512,512]{1,0:T(8,128)(2,1)}, bf16[512,512]{1,0:T(8,128)(2,1)}) custom-call(bf16[1024,512]{1,0:T(8,128)(2,1)} %get-tuple-element.50.hn_ref, bf16[512,1024]{1,0:T(8,128)(2,1)} %get-tuple-element.51.hnt_ref, bf16[1024,512]{1,0:T(8,128)(2,1)} %g_ref.11, ...), custom_call_target="tpu_custom_call" | custom-call | flops 2147483648 | bytes 8388608 | tf_op jit(solution)/shard_map/pallas_call | solution.py:340
  62.2 6.9 %shard_map.199 = (bf16[1024,512]{1,0:T(8,128)(2,1)}, bf16[1024,512]{1,0:T(8,128)(2,1)}, bf16[512,512]{1,0:T(8,128)(2,1)}, bf16[512,512]{1,0:T(8,128)(2,1)}) custom-call(bf16[1024,512]{1,0:T(8,128)(2,1)} %get-tuple-element.50.hn_ref, bf16[512,1024]{1,0:T(8,128)(2,1)} %get-tuple-element.51.hnt_ref, bf16[1024,512]{1,0:T(8,128)(2,1)} %g_ref.11, ...), custom_call_target="tpu_custom_call" | custom-call | flops 2147483648 | bytes 8388608 | tf_op jit(solution)/shard_map/pallas_call | solution.py:340
  69.0 7.0 %shard_map.198 = (bf16[1024,512]{1,0:T(8,128)(2,1)}, bf16[1024,512]{1,0:T(8,128)(2,1)}, bf16[512,512]{1,0:T(8,128)(2,1)}, bf16[512,512]{1,0:T(8,128)(2,1)}) custom-call(bf16[1024,512]{1,0:T(8,128)(2,1)} %get-tuple-element.50.hn_ref, bf16[512,1024]{1,0:T(8,128)(2,1)} %get-tuple-element.51.hnt_ref, bf16[1024,512]{1,0:T(8,128)(2,1)} %g_ref.11, ...), custom_call_target="tpu_custom_call" | custom-call | flops 2147483648 | bytes 8388608 | tf_op jit(solution)/shard_map/pallas_call | solution.py:340
  76.1 6.9 %shard_map.197 = (bf16[1024,512]{1,0:T(8,128)(2,1)}, bf16[1024,512]{1,0:T(8,128)(2,1)}, bf16[512,512]{1,0:T(8,128)(2,1)}, bf16[512,512]{1,0:T(8,128)(2,1)}) custom-call(bf16[1024,512]{1,0:T(8,128)(2,1)} %get-tuple-element.50.hn_ref, bf16[512,1024]{1,0:T(8,128)(2,1)} %get-tuple-element.51.hnt_ref, bf16[1024,512]{1,0:T(8,128)(2,1)} %g_ref.11, ...), custom_call_target="tpu_custom_call" | custom-call | flops 2147483648 | bytes 8388608 | tf_op jit(solution)/shard_map/pallas_call | solution.py:340
  82.9 10.8 %shard_map.201 = (bf16[1024,512]{1,0:T(8,128)(2,1)}, f32[1024,512]{1,0:T(8,128)}, f32[1,512]{1,0:T(1,128)}) custom-call(f32[1024,512]{1,0:T(8,128)} %get-tuple-element.49.h_ref, bf16[1024,512]{1,0:T(8,128)(2,1)} %g_ref.11, bf16[1024,512]{1,0:T(8,128)(2,1)} %get-tuple-element.53.refs_0_, bf16[1024,512]{1,0:T(8,128)(2,1)} %get-tuple-element.54.refs_1_, ...), custom_call_target="tpu_custom_call" | custom-call | flops 4294967296 | bytes 20971520 | tf_op jit(solution)/shard_map/pallas_call | solution.py:396
  93.7 9.7 %shard_map.202 = (bf16[1024,512]{1,0:T(8,128)(2,1)}, bf16[400,512]{1,0:T(8,128)(2,1)}, bf16[256,512]{1,0:T(8,128)(2,1)}, f32[1,512]{1,0:T(1,128)}) custom-call(bf16[1024,512]{1,0:T(8,128)(2,1)} %x_ref.5, bf16[1024,512]{1,0:T(8,128)(2,1)} %get-tuple-element.45.xn_ref, bf16[1024,128]{1,0:T(8,128)(2,1)} %get-tuple-element.46.kv_ref, ...), custom_call_target="tpu_custom_call" | custom-call | flops 1073741824 | bytes 8192000 | tf_op jit(solution)/shard_map/pallas_call | solution.py:53
  103.4 0.0 copy-start.6
  103.4 0.0 copy-start.7
  103.4 1.1 slice.32
  104.4 1.8 pad_maximum_fusion.2
  106.2 0.0 reduce-scatter.2.cloned.1.call-update
  106.3 0.0 all-reduce.4.cloned.1.call-start
  106.3 0.0 copy-done.6
  106.3 0.0 copy-done.7
  106.3 0.0 copy-start.2
  106.3 0.0 copy-start.3
  106.3 0.0 copy-start.4
  106.4 0.0 copy-start.5
  106.4 2.9 pad_maximum_fusion
  109.3 18.9 %reduce-scatter.2.cloned.1.call-done = bf16[1,128,512]{2,1,0:T(8,128)(2,1)} async-done(((bf16[4,128,512]{2,1,0:T(8,128)(2,1)}), bf16[1,128,512]{2,1,0:T(8,128)(2,1)}) %reduce-scatter.2.cloned.1.call-update) | async-done | bytes 131088 | tf_op jit(solution)/shard_map/reduce_scatter | solution.py:475
  128.2 0.0 all-reduce.4.cloned.1.call-update
  128.2 0.0 all-reduce.6.cloned.1.call-start
  128.2 0.0 copy-done.2
  128.2 0.0 copy-done.3
  128.3 0.0 copy-done.4
  128.3 0.0 copy-done.5
  128.3 1.5 pad_maximum_fusion.1
  129.7 1.6 slice.29
  131.3 0.0 copy-start.8
  131.3 0.0 copy-start.9
  131.3 0.0 all-reduce.6.cloned.1.call-update
  131.3 0.7 copy-done.8
  132.0 0.0 copy-done.9
  132.0 38.5 %psum.35 = f32[2,512]{1,0:T(2,128)S(1)} all-reduce(f32[2,512]{1,0:T(2,128)S(1)} %pad_maximum_fusion.5), channel_id=1, replica_groups=mesh['dp'=4,'expert'=4,'tok'=2] {'dp','expert','tok'}, use_global_device_ids=true, to_apply=%region_0.0 | all-reduce | flops 1024 | bytes 8192 | tf_op jit(solution)/shard_map/psum | solution.py:465
  170.6 0.6 fusion
  171.2 11.2 %all-reduce.4.cloned.1.call-done = bf16[1,128,512]{2,1,0:T(8,128)(2,1)} async-done(((bf16[1,128,512]{2,1,0:T(8,128)(2,1)}), bf16[1,128,512]{2,1,0:T(8,128)(2,1)}) %all-reduce.4.cloned.1.call-update) | async-done | bytes 131088 | tf_op jit(solution)/shard_map/psum | solution.py:475
  182.4 1.5 slice.41
  183.9 0.9 convert_element_type.26
  184.8 0.7 slice_bitcast_fusion
  185.5 148.7 %all-reduce.6.cloned.1.call-done = (bf16[144,512]{1,0:T(8,128)(2,1)}, bf16[512,2048]{1,0:T(8,128)(2,1)}, bf16[2048,512]{1,0:T(8,128)(2,1)}) async-done(((bf16[144,512]{1,0:T(8,128)(2,1)}, bf16[512,2048]{1,0:T(8,128)(2,1)}, bf16[2048,512]{1,0:T(8,128)(2,1)}), (bf16[144,512]{1,0:T(8,128)(2,1)}, bf16[512,2048]{1,0:T(8,128)(2,1)}, bf16[2048,512]{1,0:T(8,128)(2,1)})) %all-reduce.6.cloned.1.call-update) | async-done | bytes 4341776 | tf_op jit(solution)/shard_map/psum | solution.py:465
  334.2 1.3 convert_bitcast_fusion.1
  335.5 0.9 convert_bitcast_fusion
  336.4 0.8 copy.23
  337.3 0.0 copy-start.1
  337.3 4.3 %convert_element_type.27 = f32[512,2048]{1,0:T(8,128)} convert(bf16[512,2048]{1,0:T(8,128)(2,1)} %get-tuple-element.91) | non-fusion elementwise | flops 1048576 | bytes 6291456 | tf_op jit(solution)/shard_map/convert_element_type | solution.py:485
  341.5 0.0 copy-done.1
  341.5 2.6 convert_element_type.28
  (2 shorter events, 0.0 us)
Async XLA Ops:
  7.2 121.0 %reduce-scatter.2.cloned.1.call-start = ((), (), s32[]{:S(2)}) async-start(), calls=%async_computation.1 | async-start | bytes 655360 | tf_op jit(solution)/shard_map/reduce_scatter | solution.py:475
  24.1 23.0 %copy-start = (bf16[256,512]{1,0:T(8,128)(2,1)}, bf16[256,512]{1,0:T(8,128)(2,1)S(1)}, u32[]{:S(2)}) copy-start(bf16[256,512]{1,0:T(8,128)(2,1)S(1)} %all_gather.6.wq_ref) | copy-start | bytes 786436
  103.4 2.9 copy-start.6
  103.4 2.9 copy-start.7
  106.3 76.1 %all-reduce.4.cloned.1.call-start = ((), (), s32[]{:S(2)}) async-start(), calls=%async_computation.2 | async-start | bytes 262144 | tf_op jit(solution)/shard_map/psum | solution.py:475
  106.3 21.9 %copy-start.2 = (bf16[512,512]{1,0:T(8,128)(2,1)S(1)}, bf16[512,512]{1,0:T(8,128)(2,1)}, u32[]{:S(2)}) copy-start(bf16[512,512]{1,0:T(8,128)(2,1)} %get-tuple-element.79) | copy-start | bytes 1572868
  106.3 21.9 %copy-start.3 = (bf16[512,512]{1,0:T(8,128)(2,1)S(1)}, bf16[512,512]{1,0:T(8,128)(2,1)}, u32[]{:S(2)}) copy-start(bf16[512,512]{1,0:T(8,128)(2,1)} %get-tuple-element.78) | copy-start | bytes 1572868
  106.3 21.9 %copy-start.4 = (bf16[512,512]{1,0:T(8,128)(2,1)S(1)}, bf16[512,512]{1,0:T(8,128)(2,1)}, u32[]{:S(2)}) copy-start(bf16[512,512]{1,0:T(8,128)(2,1)} %get-tuple-element.77) | copy-start | bytes 1572868
  106.4 21.9 %copy-start.5 = (bf16[512,512]{1,0:T(8,128)(2,1)S(1)}, bf16[512,512]{1,0:T(8,128)(2,1)}, u32[]{:S(2)}) copy-start(bf16[512,512]{1,0:T(8,128)(2,1)} %get-tuple-element.76) | copy-start | bytes 1572868
  128.2 206.0 %all-reduce.6.cloned.1.call-start = ((), (), s32[]{:S(2)}) async-start(), calls=%async_computation.3 | async-start | bytes 8683520 | tf_op jit(solution)/shard_map/psum | solution.py:465
  131.3 0.7 copy-start.8
  131.3 0.7 copy-start.9
  337.3 4.3 %copy-start.1 = (bf16[2048,512]{1,0:T(8,128)(2,1)S(1)}, bf16[2048,512]{1,0:T(8,128)(2,1)}, u32[]{:S(2)}) copy-start(bf16[2048,512]{1,0:T(8,128)(2,1)} %get-tuple-element.92) | copy-start | bytes 6291460
Sparse Core Ops, SparseCore 0:
  106.4 21.7 reduce-scatter.1
  131.2 51.1 all-reduce.3
  190.6 143.5 all-reduce.5

commit v2 on v1

v2 whole, which is shorter than its diff:
```python
import functools

import jax
import jax.numpy as jnp
from jax import lax
from jax.experimental import pallas as pl
from jax.experimental.pallas import tpu as pltpu
from jax.sharding import PartitionSpec as P

BF = jnp.bfloat16
F32 = jnp.float32
MASKED = -1e30
BAND = 128
ROWS = 256
AXES = ("dp", "expert", "tok")


def nn(left, right):
    return lax.dot_general(left, right, (((1,), (0,)), ((), ())), preferred_element_type=F32)


def nt(left, right):
    return lax.dot_general(left, right, (((1,), (1,)), ((), ())), preferred_element_type=F32)


def tn(left, right):
    return lax.dot_general(left, right, (((0,), (0,)), ((), ())), preferred_element_type=F32)


def normalize(values):
    centre = values - jnp.mean(values, axis=-1, keepdims=True)
    spread = jnp.mean(centre * centre, axis=-1, keepdims=True)
    inverse = lax.rsqrt(spread + 1e-05)
    return centre * inverse, inverse


def normalize_back(upstream, normalized, inverse, gain):
    scaled = upstream * gain
    inner = (
        scaled
        - jnp.mean(scaled, axis=-1, keepdims=True)
        - normalized * jnp.mean(scaled * normalized, axis=-1, keepdims=True)
    )
    return inner * inverse


def sds(shape, dtype):
    return jax.ShapeDtypeStruct(shape, dtype)


def size_of(array):
    lanes = -(-array.shape[-1] // 128) * 128
    rows = -(-array.shape[-2] // 16) * 16
    lead = 1
    for extent in array.shape[:-2]:
        lead = lead * extent
    return lead * rows * lanes * jnp.dtype(array.dtype).itemsize


class Line:
    def __init__(self):
        self.last = None

    def call(self, kernel, operands, outs, fetched=(), scalars=(), scratch=(), room=2 << 20, flops=0):
        n, f, s = len(operands), len(fetched), len(scalars)
        late = () if self.last is None else (self.last,)
        skip = len(late)

        def wrapped(*refs):
            ins = refs[:n]
            sources = refs[n : n + f]
            smem = refs[n + f : n + f + s]
            rest = refs[n + f + s + skip :]
            body = rest[: len(rest) - f - (1 if f else 0)] if f else rest
            waits = []
            if f:
                buffers, sems = rest[len(body) : len(body) + f], rest[-1]
                for i in range(f):
                    copy = pltpu.make_async_copy(sources[i], buffers[i], sems.at[i])
                    copy.start()

                    def wait(copy=copy, buffer=buffers[i]):
                        copy.wait()
                        return buffer

                    waits.append(wait)
            kernel(*ins, *waits, *smem, *body)

        need = sum(size_of(a) for a in (*operands, *fetched, *outs)) + sum(
            size_of(a) for a in scratch
        )
        moved = sum(a.size * jnp.dtype(a.dtype).itemsize for a in (*operands, *fetched, *outs))
        extra = [pltpu.VMEM(a.shape, a.dtype) for a in fetched]
        if f:
            extra.append(pltpu.SemaphoreType.DMA((f,)))
        results = pl.pallas_call(
            wrapped,
            out_shape=list(outs),
            in_specs=[pl.BlockSpec(memory_space=pltpu.VMEM)] * n
            + [pl.BlockSpec(memory_space=pltpu.HBM)] * f
            + [pl.BlockSpec(memory_space=pltpu.SMEM)] * s
            + [pl.BlockSpec(memory_space=pl.ANY)] * skip,
            out_specs=[pl.BlockSpec(memory_space=pltpu.VMEM)] * len(outs),
            scratch_shapes=[pltpu.VMEM(a.shape, a.dtype) for a in scratch] + extra,
            compiler_params=pltpu.CompilerParams(vmem_limit_bytes=need + room),
            cost_estimate=pl.CostEstimate(flops=flops, bytes_accessed=moved, transcendentals=0),
        )(*operands, *fetched, *scalars, *late)
        self.last = min(results, key=lambda a: a.size)
        return results


def prepare_kernel(
    x_wait, g_wait, ids_wait, ln_wait, wkv_wait, wr_wait,
    xn_ref, kv_ref, kvt_ref, gates_ref, gt_ref, small_ref,
):
    ln_ref, x_ref = ln_wait(), x_wait()
    length = x_ref.shape[0]
    gain = ln_ref[...]
    for start in range(0, length, ROWS):
        rows = pl.ds(start, ROWS)
        normalized, _ = normalize(x_ref[rows, :].astype(F32))
        xn_ref[rows, :] = (normalized * gain).astype(BF)
    normed = xn_ref[...]
    wkv_ref, wr_ref, ids_ref = wkv_wait(), wr_wait(), ids_wait()
    pair = wkv_ref.shape[1]
    experts = wr_ref.shape[0]
    small_ref[:pair, :] = wkv_ref[...].T
    small_ref[pair:, :] = jnp.concatenate(
        [wr_ref[...].astype(F32), jnp.zeros((16 - experts, wr_ref.shape[1]), F32)], axis=0
    ).astype(BF)
    small = small_ref[...]
    both = nt(small, normed)
    kvt_ref[...] = both[:pair].astype(BF)
    kv_ref[...] = nn(normed, wkv_ref[...]).astype(BF)
    choose = ids_ref.shape[0]
    picked = []
    for route in range(choose):
        ids = ids_ref[route : route + 1, :]
        value = jnp.zeros((1, length), F32)
        for expert in range(experts):
            value = jnp.where(ids == expert, both[pair + expert : pair + expert + 1], value)
        picked.append(value)
    top = functools.reduce(jnp.maximum, picked)
    raised = [jnp.exp(value - top) for value in picked]
    total = functools.reduce(lambda a, b: a + b, raised)
    for route in range(choose):
        gates_ref[route : route + 1, :] = raised[route] / total
    g_ref = g_wait()
    gt_ref[...] = g_ref[...].T


def upstream_kernel(g_ref, wout_ref, ag_ref):
    for start in range(0, g_ref.shape[0], ROWS):
        rows = slice(start, start + ROWS)
        ag_ref[rows, :] = nt(g_ref[rows, :], wout_ref[...]).astype(BF)


def column_ids(sent_ref, keyid_ref):
    length = sent_ref.shape[1]
    for start in range(0, length, BAND):
        row = jnp.broadcast_to(sent_ref[:, start : start + BAND].astype(F32), (BAND, BAND))
        keyid_ref[pl.ds(start, BAND), :] = row.T


def masked_scores(kv_ref, keyid_ref, sent_ref, queries, start, low, high, choose):
    padded = jnp.concatenate([queries, jnp.zeros_like(queries)], axis=0)
    scores = nn(kv_ref[low:high, :], padded) * 0.125
    same = keyid_ref[low:high, :] == sent_ref[:, start : start + BAND].astype(F32)
    parts = [
        jnp.where(same, scores[:, route * BAND : (route + 1) * BAND], MASKED)
        for route in range(choose)
    ]
    return jnp.concatenate(parts, axis=1)


def window(start, length):
    return max(start - BAND, 0), min(start + 2 * BAND, length)


def attend_kernel(*refs, experts, head):
    piece_refs, refs = refs[:experts], refs[experts:]
    (
        xn_ref, kv_ref, kvt_ref, gates_ref, x_wait, ids_wait, sent_wait, ln_wait, place_ref,
        wq_ref, wo_ref, qt_ref, at_ref, lse_ref, gat_ref, h_ref, hn_ref, hnt_ref, all_ref, keyid_ref,
    ) = refs
    for k in range(experts):
        rows = pl.ds((place_ref[1] ^ k) * head, head)
        wq_ref[rows, :] = piece_refs[k][:head, :]
        wo_ref[rows, :] = piece_refs[k][head:, :]
    length = xn_ref.shape[0]
    sent_ref, ids_ref = sent_wait(), ids_wait()
    choose = ids_ref.shape[0]
    column_ids(sent_ref, keyid_ref)
    all_ref[...] = nt(wq_ref[...], xn_ref[...])
    for start in range(0, length, BAND):
        lanes = slice(start, start + BAND)
        block = slice(start * choose, (start + BAND) * choose)
        low, high = window(start, length)
        chosen = []
        for route in range(choose):
            ids = ids_ref[route : route + 1, lanes]
            value = jnp.zeros((head, BAND), F32)
            for expert in range(experts):
                value = jnp.where(
                    ids == expert, all_ref[expert * head : (expert + 1) * head, lanes], value
                )
            chosen.append(value)
        queries = jnp.concatenate(chosen, axis=1).astype(BF)
        qt_ref[:, block] = queries
        scores = masked_scores(kv_ref, keyid_ref, sent_ref, queries, start, low, high, choose)
        largest = jnp.max(scores, axis=0, keepdims=True)
        raised = jnp.exp(scores - largest)
        total = jnp.sum(raised, axis=0, keepdims=True)
        probs = (raised * (1.0 / total)).astype(BF)
        lse_ref[:, block] = largest + jnp.log(total)
        attended = nn(kvt_ref[head:, low:high], probs).astype(BF)
        at_ref[:, block] = attended
        spread = [jnp.zeros((head, BAND), F32) for _ in range(experts)]
        for route in range(choose):
            ids = ids_ref[route : route + 1, lanes]
            gated = attended[:, route * BAND : (route + 1) * BAND].astype(F32) * gates_ref[
                route : route + 1, lanes
            ]
            for expert in range(experts):
                spread[expert] = jnp.where(ids == expert, gated, spread[expert])
        for expert in range(experts):
            gat_ref[expert * head : (expert + 1) * head, lanes] = spread[expert].astype(BF)
    x_ref, ln_ref = x_wait(), ln_wait()
    gain = ln_ref[...]
    for start in range(0, length, ROWS):
        rows = slice(start, start + ROWS)
        mixed = tn(gat_ref[:, rows], wo_ref[...])
        hidden = x_ref[rows, :].astype(F32) + mixed
        h_ref[rows, :] = hidden
        normalized, _ = normalize(hidden)
        low_value = (normalized * gain).astype(BF)
        hn_ref[rows, :] = low_value
        hnt_ref[:, rows] = low_value.T


def gelu_both(values):
    bell = jnp.exp(-0.5 * values * values)
    t = 1.0 / (1.0 + 0.23164188 * jnp.abs(values))
    poly = t * (
        0.127414796
        + t * (-0.142248368 + t * (0.7107068705 + t * (-0.7265760135 + t * 0.5307027145)))
    )
    tail = poly * bell
    cumulative = jnp.where(values >= 0.0, 1.0 - tail, tail)
    return values * cumulative, cumulative + values * bell * 0.3989422804014327


def ffn_kernel(*refs, first, hidden, peers):
    hn_ref, hnt_ref, gt_ref, ag_ref, win_ref, place_ref, u_ref, dpre_ref = refs[:8]
    part_refs, sum_ref = refs[8 : 8 + peers], refs[8 + peers]
    length, width = hn_ref.shape
    for column in range(0, hidden, width):
        span = slice(column, column + width)
        far = slice(first + column, first + column + width)
        for start in range(0, length, ROWS):
            rows = slice(start, start + ROWS)
            activated, slope = gelu_both(nn(hn_ref[rows, :], win_ref[:, far]))
            u_ref[rows, span] = activated.astype(BF)
            dpre_ref[rows, span] = (ag_ref[rows, far].astype(F32) * slope).astype(BF)
        sum_ref[hidden + column : hidden + column + width, :] = nn(
            hnt_ref[...], dpre_ref[:, span]
        ).astype(BF)
        sum_ref[span, :] = nn(gt_ref[...], u_ref[:, span]).astype(BF).T
    rows = 2 * hidden // peers
    for k in range(peers):
        part_refs[k][...] = sum_ref[pl.ds((place_ref[0] ^ k) * rows, rows), :]


def finish_kernel(*refs, chunks):
    h_ref, g_ref, win_ref, wout_ref = refs[:4]
    u_refs, dpre_refs = refs[4 : 4 + chunks], refs[4 + chunks : 4 + 2 * chunks]
    ln_wait, out_ref, dh_ref, gain_ref = refs[4 + 2 * chunks :]
    ln_ref = ln_wait()
    gain = ln_ref[...]
    length = h_ref.shape[0]
    gain_sum = jnp.zeros_like(gain)
    for start in range(0, length, ROWS):
        rows = slice(start, start + ROWS)
        hidden = h_ref[rows, :]
        total, upstream, first = hidden, None, 0
        for c in range(chunks):
            size = u_refs[c].shape[1]
            total = total + nn(u_refs[c][rows, :], wout_ref[first : first + size, :])
            part = nt(dpre_refs[c][rows, :], win_ref[:, first : first + size])
            upstream = part if upstream is None else upstream + part
            first = first + size
        out_ref[rows, :] = total.astype(BF)
        normalized, inverse = normalize(hidden)
        dh_ref[rows, :] = g_ref[rows, :].astype(F32) + normalize_back(
            upstream, normalized, inverse, gain
        )
        gain_sum = gain_sum + jnp.sum(upstream * normalized, axis=0, keepdims=True)
    gain_ref[...] = gain_sum


def back_kernel(*refs, experts, head, peers, misc):
    (
        xn_ref, kv_ref, kvt_ref, gates_ref, small_ref, wq_ref, wo_ref, qt_ref, at_ref, lse_ref, gat_ref,
        dh_ref, gain_two_ref, x_wait, ids_wait, sent_wait, ln_wait, place_ref, dx_ref,
    ) = refs[:19]
    part_refs = refs[19 : 19 + peers]
    all_ref, keyid_ref, z_ref, dkv_ref, grads_ref, pair_ref, misc_ref = refs[19 + peers :]
    length = xn_ref.shape[0]
    wide, pair = experts * head, 2 * head
    sent_ref, ids_ref = sent_wait(), ids_wait()
    choose = ids_ref.shape[0]
    column_ids(sent_ref, keyid_ref)
    dh_low = dh_ref[...].astype(BF)
    all_ref[...] = nt(wo_ref[...], dh_low)
    out_grads = nn(gat_ref[...], dh_low)
    for expert in range(experts):
        pair_ref[expert * pair + head : (expert + 1) * pair, :] = out_grads[
            expert * head : (expert + 1) * head
        ]
    dkv_ref[...] = jnp.zeros_like(dkv_ref)
    for start in range(0, length, BAND):
        lanes = slice(start, start + BAND)
        block = slice(start * choose, (start + BAND) * choose)
        low, high = window(start, length)
        raw, gate_grads = [], []
        for route in range(choose):
            ids = ids_ref[route : route + 1, lanes]
            value = jnp.zeros((head, BAND), F32)
            for expert in range(experts):
                value = jnp.where(
                    ids == expert, all_ref[expert * head : (expert + 1) * head, lanes], value
                )
            raw.append(value)
            attended = at_ref[:, start * choose + route * BAND : start * choose + (route + 1) * BAND]
            gate_grads.append(jnp.sum(value * attended.astype(F32), axis=0, keepdims=True))
        gates = [gates_ref[route : route + 1, lanes] for route in range(choose)]
        common = functools.reduce(
            lambda a, b: a + b, [gate * grad for gate, grad in zip(gates, gate_grads)]
        )
        logit_rows = [jnp.zeros((1, BAND), F32) for _ in range(experts)]
        for route in range(choose):
            ids = ids_ref[route : route + 1, lanes]
            picked = gates[route] * (gate_grads[route] - common)
            for expert in range(experts):
                logit_rows[expert] = jnp.where(ids == expert, picked, logit_rows[expert])
        logit_pad = jnp.concatenate(
            logit_rows + [jnp.zeros((16 - experts, BAND), F32)], axis=0
        )
        z_ref[wide + pair :, lanes] = logit_pad.astype(BF)
        queries = qt_ref[:, block]
        scores = masked_scores(kv_ref, keyid_ref, sent_ref, queries, start, low, high, choose)
        probs = jnp.exp(scores - lse_ref[:, block])
        upstream = jnp.concatenate(
            [gate * value for gate, value in zip(gates, raw)], axis=1
        ).astype(BF)
        padded = jnp.concatenate([jnp.zeros_like(upstream), upstream], axis=0)
        prob_grad = nn(kv_ref[low:high, :], padded)
        mean = jnp.sum(probs * prob_grad, axis=0, keepdims=True)
        score_grad = (probs * (prob_grad - mean)).astype(BF)
        query_grad = (nn(kvt_ref[:head, low:high], score_grad) * 0.125).astype(BF)
        spread = [jnp.zeros((head, BAND), BF) for _ in range(experts)]
        for route in range(choose):
            ids = ids_ref[route : route + 1, lanes]
            piece = query_grad[:, route * BAND : (route + 1) * BAND]
            for expert in range(experts):
                spread[expert] = jnp.where(ids == expert, piece, spread[expert])
        for expert in range(experts):
            z_ref[expert * head : (expert + 1) * head, lanes] = spread[expert]
        dkv_ref[:head, low:high] += nt(queries, score_grad) * 0.125
        dkv_ref[head:, low:high] += nt(upstream, probs.astype(BF))
    z_ref[wide : wide + pair, :] = dkv_ref[...].astype(BF)
    grads_ref[...] = nn(z_ref[...], xn_ref[...])
    for expert in range(experts):
        pair_ref[expert * pair : expert * pair + head, :] = grads_ref[
            expert * head : (expert + 1) * head, :
        ]
    x_ref, ln_ref = x_wait(), ln_wait()
    gain = ln_ref[...]
    total = jnp.zeros_like(gain)
    for start in range(0, length, ROWS):
        rows = slice(start, start + ROWS)
        normed_grad = tn(z_ref[:wide, rows], wq_ref[...]) + tn(z_ref[wide:, rows], small_ref[...])
        normalized, inverse = normalize(x_ref[rows, :].astype(F32))
        total = total + jnp.sum(normed_grad * normalized, axis=0, keepdims=True)
        back = normalize_back(normed_grad, normalized, inverse, gain)
        dx_ref[rows, :] = (dh_ref[rows, :] + back).astype(BF)
    misc_ref[...] = jnp.zeros_like(misc_ref)
    misc_ref[:pair, :] = grads_ref[wide : wide + pair, :]
    misc_ref[pair : pair + 16, :] = jnp.concatenate(
        [
            grads_ref[wide + pair : wide + pair + experts, :],
            total,
            gain_two_ref[...],
            jnp.zeros((14 - experts, total.shape[1]), F32),
        ],
        axis=0,
    )
    each, share = pair // peers, misc // peers
    for k in range(peers):
        part = place_ref[0] ^ k
        for expert in range(experts):
            rows = pl.ds(expert * pair + part * each, each)
            part_refs[k][expert * each : (expert + 1) * each, :] = pair_ref[rows, :].astype(BF)
        part_refs[k][experts * each :, :] = misc_ref[pl.ds(part * share, share), :].astype(BF)


def added(refs, span):
    total = refs[0][span, :].astype(F32)
    for ref in refs[1:]:
        total = total + ref[span, :].astype(F32)
    return total.astype(BF)


def exchange(parts, axis):
    size = len(parts)
    return [
        lax.ppermute(parts[k], axis, [(i, i ^ k) for i in range(size)]) for k in range(1, size)
    ]


def bits(size):
    return size.bit_length() - 1


def dp_bit(stage, parity):
    count = bits(lax.axis_size("dp"))
    return (stage + parity) % count


def swap_dp(array, stage):
    dp, expert, tok = (lax.axis_size(axis) for axis in AXES)
    pairs = []
    for d in range(dp):
        for e in range(expert):
            for t in range(tok):
                other = d ^ (1 << dp_bit(stage, t % 2))
                pairs.append(((d * expert + e) * tok + t, (other * expert + e) * tok + t))
    return lax.ppermute(array, AXES, pairs)


def swap_expert(array, stage):
    size = lax.axis_size("expert")
    return lax.ppermute(array, "expert", [(i, i ^ (1 << stage)) for i in range(size)])


def split_step(line, place, arrays, row):
    rows, width = arrays[0].shape
    half, count = rows // 2, len(arrays)

    def kernel(*refs):
        place_ref, keep_ref, send_ref = refs[count:]
        bit = place_ref[row]
        keep_ref[...] = added(refs[:count], pl.ds(bit * half, half))
        send_ref[...] = added(refs[:count], pl.ds((1 - bit) * half, half))

    return line.call(kernel, arrays, [sds((half, width), BF)] * 2, scalars=(place,))


def add_step(line, arrays):
    count = len(arrays)

    def kernel(*refs):
        refs[count][...] = added(refs[:count], slice(None))

    return line.call(kernel, arrays, [sds(arrays[0].shape, BF)])[0]


def join_step(line, place, own, other, row):
    half, width = own.shape

    def kernel(own_ref, other_ref, place_ref, out_ref):
        bit = place_ref[row]
        out_ref[pl.ds(bit * half, half), :] = own_ref[...]
        out_ref[pl.ds((1 - bit) * half, half), :] = other_ref[...]

    return line.call(kernel, (own, other), [sds((2 * half, width), BF)], scalars=(place,))[0]


def tail_step(line, place, arrays, row, count, each):
    rows, width = arrays[0].shape
    rest = rows - count * each
    half, many = count // 2 * each, len(arrays)

    def kernel(*refs):
        place_ref, keep_ref, send_ref = refs[many:]
        bit = place_ref[row]
        for q in range(count // 2):
            span = slice(q * each, (q + 1) * each)
            keep_ref[span, :] = added(refs[:many], pl.ds((2 * q + bit) * each, each))
            send_ref[span, :] = added(refs[:many], pl.ds((2 * q + 1 - bit) * each, each))
        small = added(refs[:many], slice(count * each, rows))
        keep_ref[half:, :] = small
        send_ref[half:, :] = small

    return line.call(kernel, arrays, [sds((half + rest, width), BF)] * 2, scalars=(place,))


def chunk_steps(line, place, parts):
    arrays = [parts[0]] + exchange(parts, "tok")
    yield
    stages = bits(lax.axis_size("dp"))
    for stage in range(stages):
        keep, send = split_step(line, place, arrays, 2 + stage)
        arrays = [keep, swap_dp(send, stage)]
        yield
    for stage in range(bits(lax.axis_size("expert"))):
        own = add_step(line, arrays)
        arrays = [own, swap_expert(own, stage)]
        yield
    own = add_step(line, arrays)
    for stage in reversed(range(stages)):
        other = swap_dp(own, stage)
        yield
        own = join_step(line, place, own, other, 2 + stage)
    others = exchange([own] * lax.axis_size("tok"), "tok")
    yield
    return [own] + others


def place_chunk(line, place, parts, first, hidden, full, before):
    peers = len(parts)
    rows, width = parts[0].shape
    block = width

    def kernel(*refs):
        part_refs, place_ref = refs[:peers], refs[peers]
        gin_ref, gout_ref, sum_ref = refs[-3:]
        for k in range(peers):
            sum_ref[pl.ds((place_ref[0] ^ k) * rows, rows), :] = part_refs[k][...]
        for column in range(0, hidden, block):
            span = slice(column, column + block)
            gout_ref[span, :] = sum_ref[span, :].astype(F32)
            gin_ref[:, span] = sum_ref[hidden + column : hidden + column + block, :].astype(F32)

    late = () if line.last is None else (line.last,)
    operands = [*parts, place, *late, *before]
    base = peers + 1 + len(late)
    results = pl.pallas_call(
        kernel,
        grid=(1,),
        out_shape=[sds((width, full), F32), sds((full, width), F32)],
        in_specs=[pl.BlockSpec((rows, width), lambda i: (0, 0), pipeline_mode=pl.Buffered(1))] * peers
        + [pl.BlockSpec(memory_space=pltpu.SMEM)]
        + [pl.BlockSpec(memory_space=pl.ANY)] * (len(late) + len(before)),
        out_specs=[
            pl.BlockSpec((width, hidden), lambda i: (0, first // hidden), pipeline_mode=pl.Buffered(1)),
            pl.BlockSpec((hidden, width), lambda i: (first // hidden, 0), pipeline_mode=pl.Buffered(1)),
        ],
        scratch_shapes=[pltpu.VMEM((2 * hidden, width), BF)],
        input_output_aliases={base + n: n for n in range(len(before))},
        compiler_params=pltpu.CompilerParams(vmem_limit_bytes=20 << 20),
        cost_estimate=pl.CostEstimate(flops=0, bytes_accessed=6 << 20, transcendentals=0),
    )(*operands)
    return results


def tail_steps(line, place, parts, experts, head, misc):
    peers = len(parts)
    pair = 2 * head
    each, share = pair // peers, misc // peers
    width = parts[0].shape[1]
    arrays = [parts[0]] + exchange(parts, "tok")
    yield
    stages = bits(lax.axis_size("dp"))
    for stage in range(bits(experts)):
        keep, send = tail_step(line, place, arrays, 2 + stages + stage, experts >> stage, each)
        arrays = [keep, swap_expert(send, stage)]
        yield
    for stage in range(stages):
        own = add_step(line, arrays)
        arrays = [own, swap_dp(own, stage)]
        yield
    own = add_step(line, arrays)
    arrays = [own] + exchange([own] * peers, "tok")
    yield

    def last(*refs):
        part_refs, place_ref = refs[:peers], refs[peers]
        query_ref, output_ref, kv_ref, router_ref, one_ref, two_ref, pair_ref, misc_ref = refs[
            peers + 1 :
        ]
        for k in range(peers):
            part = place_ref[0] ^ k
            pair_ref[pl.ds(part * each, each), :] = part_refs[k][:each, :].astype(F32)
            misc_ref[pl.ds(part * share, share), :] = part_refs[k][each:, :].astype(F32)
        query_ref[0] = pair_ref[:head, :]
        output_ref[0] = pair_ref[head:, :]
        kv_ref[...] = misc_ref[:pair, :].T
        router_ref[...] = misc_ref[pair : pair + experts, :]
        one_ref[...] = misc_ref[pair + experts : pair + experts + 1, :]
        two_ref[...] = misc_ref[pair + experts + 1 : pair + experts + 2, :]

    return line.call(
        last,
        arrays,
        [
            sds((1, head, width), F32),
            sds((1, head, width), F32),
            sds((width, pair), F32),
            sds((experts, width), F32),
            sds((1, width), F32),
            sds((1, width), F32),
        ],
        scalars=(place,),
        scratch=(sds((pair, width), F32), sds((misc, width), F32)),
    )


def step(walk):
    try:
        next(walk)
    except StopIteration as end:
        return end.value
    return None


def body(
    tokens, out_grad, expert_ids, sentence_ids, ln_attn, w_kv, w_router, w_query, w_output, ln_ffn, w_in, w_out
):
    length, width = tokens.shape
    head = w_query.shape[2]
    pair = w_kv.shape[1]
    full = w_in.shape[1]
    experts = lax.axis_size("expert")
    peers = lax.axis_size("tok")
    choose = expert_ids.shape[1]
    tok, dp, expert = lax.axis_index("tok"), lax.axis_index("dp"), lax.axis_index("expert")
    odd = tok % 2
    stages = bits(lax.axis_size("dp"))
    dp_bits = [
        jnp.where(odd == 1, (dp >> dp_bit(s, 1)) & 1, (dp >> dp_bit(s, 0)) & 1) for s in range(stages)
    ]
    place = jnp.stack(
        [tok, expert] + dp_bits + [(expert >> s) & 1 for s in range(bits(experts))]
    ).astype(jnp.int32)
    weights = jnp.concatenate([w_query[0].T, w_output[0]], axis=0)
    pieces = [weights] + exchange([weights] * experts, "expert")
    ids = expert_ids.T
    ln_one = ln_attn.reshape(1, width)
    ln_two = ln_ffn.reshape(1, width)
    line = Line()
    normed, kv, kvt, gates, gt, small = line.call(
        prepare_kernel,
        (),
        [
            sds((length, width), BF),
            sds((length, pair), BF),
            sds((pair, length), BF),
            sds((choose, length), F32),
            sds((width, length), BF),
            sds((pair + 16, width), BF),
        ],
        fetched=(tokens, out_grad, ids, ln_one, w_kv, w_router.T),
        room=8 << 20,
        flops=4 * length * width * pair,
    )
    [ag] = line.call(
        upstream_kernel, (out_grad, w_out), [sds((length, full), BF)], room=8 << 20,
        flops=2 * length * width * full,
    )
    wq, wo, qt, at, lse, gat, h, hn, hnt = line.call(
        functools.partial(attend_kernel, experts=experts, head=head),
        (*pieces, normed, kv, kvt, gates),
        [
            sds((experts * head, width), BF),
            sds((experts * head, width), BF),
            sds((head, choose * length), BF),
            sds((head, choose * length), BF),
            sds((1, choose * length), F32),
            sds((experts * head, length), BF),
            sds((length, width), F32),
            sds((length, width), BF),
            sds((width, length), BF),
        ],
        fetched=(tokens, ids, sentence_ids, ln_two),
        scalars=(place,),
        scratch=(sds((experts * head, length), F32), sds((length, BAND), F32)),
        room=8 << 20,
        flops=8 * length * width * experts * head,
    )

    def ffn(first, hidden):
        u, dpre, *parts = line.call(
            functools.partial(ffn_kernel, first=first, hidden=hidden, peers=peers),
            (hn, hnt, gt, ag, w_in),
            [sds((length, hidden), BF)] * 2 + [sds((2 * hidden // peers, width), BF)] * peers,
            scalars=(place,),
            scratch=(sds((2 * hidden, width), BF),),
            room=8 << 20,
            flops=6 * length * width * hidden,
        )
        return u, dpre, chunk_steps(line, place, parts)

    half = full // 2
    u_one, dpre_one, walk_one = ffn(0, half)
    step(walk_one)
    u_two, dpre_two, walk_two = ffn(half, half)
    step(walk_one)
    step(walk_two)
    output, dh, gain_two = line.call(
        functools.partial(finish_kernel, chunks=2),
        (h, out_grad, w_in, w_out, u_one, u_two, dpre_one, dpre_two),
        [sds((length, width), BF), sds((length, width), F32), sds((1, width), F32)],
        fetched=(ln_two,),
        room=8 << 20,
        flops=4 * length * width * full,
    )
    step(walk_one)
    step(walk_two)
    misc = -(-(pair + 16) // (16 * peers)) * 16 * peers
    dx, *parts = line.call(
        functools.partial(back_kernel, experts=experts, head=head, peers=peers, misc=misc),
        (normed, kv, kvt, gates, small, wq, wo, qt, at, lse, gat, dh, gain_two),
        [sds((length, width), BF)] + [sds(((experts * pair + misc) // peers, width), BF)] * peers,
        fetched=(tokens, ids, sentence_ids, ln_one),
        scalars=(place,),
        scratch=(
            sds((experts * head, length), F32),
            sds((length, BAND), F32),
            sds((experts * head + pair + 16, length), BF),
            sds((pair, length), F32),
            sds((experts * head + pair + 16, width), F32),
            sds((experts * pair, width), F32),
            sds((misc, width), F32),
        ),
        room=8 << 20,
        flops=12 * length * width * experts * head,
    )
    walk_three = tail_steps(line, place, parts, experts, head, misc)
    step(walk_three)
    walks = {1: walk_one, 2: walk_two, 3: walk_three}
    done = {}
    while walks:
        for name in list(walks):
            result = step(walks[name])
            if result is not None:
                done[name] = result
                del walks[name]
    query, outp, kv_grad, router, one, two = done[3]
    both = place_chunk(line, place, done[1], 0, half, full, ())
    both = place_chunk(line, place, done[2], half, half, full, both)
    return (
        output,
        dx,
        one.reshape(width),
        kv_grad,
        router.T,
        jnp.swapaxes(query, 1, 2),
        outp,
        two.reshape(width),
        both[0],
        both[1],
    )


def solution(mesh):
    rows = P(AXES, None)
    heads = P("expert", None, None)
    return jax.shard_map(
        body,
        mesh=mesh,
        in_specs=(rows, rows, rows, rows, P(), P(), P(), heads, heads, P(), P(), P()),
        out_specs=(rows, rows, P(), P(), P(), heads, heads, P(), P(), P()),
        check_vma=False,
    )
```

time: 351 us -> 141 us (0.40)
  waiting for transfers between devices: 179 us -> 49.9 us
  blocking collectives: 70.6 us -> 0 us
  starting transfers between devices: 0.12 us -> 27.2 us
  other arithmetic: 19.1 us -> 0.88 us
  between operations: 13.9 us -> 1.01 us
  Pallas kernels: 60.2 us -> 53.9 us
    psum x2 -> x0, waiting for transfers between devices: 160 us -> none  [the longest x1 149 us: body(): lax.psum((jnp.concatenate(gins, axis=1), jnp.concatenate(gouts, axis=0),...]
    ppermute x0 -> x25, waiting for transfers between devices: none -> 49.9 us  [the longest x6 35 us: swap_expert(): lax.ppermute(array, 'expert', [(i, i ^ 1 << stage) for i in range(size)])]
    psum x1 -> x0, blocking collectives: 38.5 us -> none  [body(): lax.psum((jnp.concatenate(gins, axis=1), jnp.concatenate(gouts, axis=0),...]
    all_gather x2 -> x0, blocking collectives: 32.1 us -> none  [the longest x1 16.3 us: body(): wo = lax.all_gather(w_output[0], 'expert', axis=0, tiled=True)]
    ppermute x0 -> x25, starting transfers between devices: none -> 27.2 us  [the longest x10 13.5 us: swap_dp(): return lax.ppermute(array, AXES, pairs)]
    reduce_scatter x1 -> x0, waiting for transfers between devices: 18.9 us -> none  [body(): lax.psum_scatter(experts_grad, 'expert', scatter_dimension=0, tiled=True)]
    convert_element_type x5 -> x0, other arithmetic: 10 us -> none  [the longest x1 4.28 us: body(): gin.astype(F32)]
    concatenate x6 -> x1, other arithmetic: 9.04 us -> 0.88 us  [body(): weights = jnp.concatenate([w_query[0].T, w_output[0]], axis=0)]
  transfers between devices with their start and end apart: 3 -> 25, of which waited for: 3 -> 11; matrix products, arithmetic and copies ran while one was open for 3% -> 0% of each run, Pallas kernels for 0% -> 26%
where the time goes in v2:
time: 141 us
  Pallas kernels  53.9 us (38%)
  waiting for transfers between devices  49.9 us (35%)
  starting transfers between devices  27.2 us (19%)
  local copies, waits for them, and re-layouts  7.8 us (6%)
    pallas_call x27, Pallas kernels, call(): pl.pallas_call(wrapped, out_shape=list(outs), in_specs=[pl.BlockSpec(memo...  48.1 us
    ppermute x6, waiting for transfers between devices, swap_expert(): lax.ppermute(array, 'expert', [(i, i ^ 1 << stage) for i in range(size)])  35 us
    ppermute x10, starting transfers between devices, swap_dp(): return lax.ppermute(array, AXES, pairs)  13.5 us
    ppermute x10, waiting for transfers between devices, swap_dp(): return lax.ppermute(array, AXES, pairs)  12.5 us
    unnamed x32, local copies, waits for them, and re-layouts  7.72 us
    ppermute x9, starting transfers between devices, exchange(): lax.ppermute(parts[k], axis, [(i, i ^ k) for i in range(size)])  7.03 us
    ppermute x6, starting transfers between devices, swap_expert(): lax.ppermute(array, 'expert', [(i, i ^ 1 << stage) for i in range(size)])  6.69 us
    pallas_call x2, Pallas kernels, place_chunk(): pl.pallas_call(kernel, grid=(1,), out_shape=[sds((width, full), F32), sds...  5.79 us
  transfers between devices with their start and end apart: 25, of which 11 were waited for; matrix products, arithmetic and copies ran while one was open for 0% of the time, Pallas kernels for 26%

profile of v2, /device:TPU:0, one launch (start us, length us, event | category | flops | bytes accessed | tf_op | source)
XLA Modules:
  0.0 140.7 jit_solution(12833613662771818671)
XLA Ops:
  0.6 0.9 pad_maximum_fusion.refs_0_
  1.5 5.1 %collective-permute-start.2 = (bf16[128,512]{1,0:T(8,128)(2,1)S(1)}, bf16[128,512]{1,0:T(8,128)(2,1)S(1)}, u32[]{:S(2)}, u32[]{:S(2)}) collective-permute-start(bf16[128,512]{1,0:T(8,128)(2,1)S(1)} %pad_maximum_fusion.refs_0_), channel_id=1, source_target_pairs={{0,6},{2,4},{4,2},{6,0},{1,7},{3,5},{5,3},{7,1},{8,14},{10,12},{12... | collective-permute-start | bytes 393224 | tf_op jit(solution)/shard_map/ppermute | solution.py:417
  6.6 0.6 collective-permute-start
  7.3 0.1 stack.27.refs_12_.refs_5_.refs_2_.refs_17_
  7.4 1.2 copy-done
  8.6 1.2 copy-done.2
  9.8 0.9 copy-done.7
  10.7 0.7 copy-done.8
  11.4 0.7 copy-done.11
  12.1 0.7 copy-done.15
  12.8 2.2 %shard_map.195 = (bf16[1024,512]{1,0:T(8,128)(2,1)S(1)}, bf16[1024,128]{1,0:T(8,128)(2,1)S(1)}, bf16[128,1024]{1,0:T(8,128)(2,1)S(1)}, f32[2,1024]{1,0:T(2,128)S...) custom-call(bf16[1024,512]{1,0:T(8,128)(2,1)S(1)} %copy-done, bf16[1024,512]{1,0:T(8,128)(2,1)S(1)} %copy-done.2, ...), custom_call_target="tpu_custom_call" | custom-call | flops 268435456 | bytes 5019648 | tf_op jit(solution)/shard_map/pallas_call | solution.py:96
  15.0 1.6 %copy-done.4 = bf16[2048,512]{1,0:T(8,128)(2,1)S(1)} copy-done((bf16[2048,512]{1,0:T(8,128)(2,1)S(1)}, bf16[2048,512]{1,0:T(8,128)(2,1)}, u32[]{:S(2)}) %copy-start.4) | copy-done | bytes 2097176
  16.6 2.4 %shard_map.196.refs_13_.refs_3_ = bf16[1024,2048]{1,0:T(8,128)(2,1)S(1)} custom-call(bf16[1024,512]{1,0:T(8,128)(2,1)S(1)} %copy-done.3, bf16[2048,512]{1,0:T(8,128)(2,1)S(1)} %copy-done.4, f32[2,1024]{1,0:T(2,128)S(1)} %get-tuple-element.64.refs_2_.refs_7_.refs_3_), custom_call_target="tpu_custom_call" | custom-call | flops 2147483648 | bytes 7340032 | tf_op jit(solution)/shard_map/pallas_call | solution.py:96
  19.0 5.6 %shard_map.197 = (bf16[256,512]{1,0:T(8,128)(2,1)S(1)}, bf16[256,512]{1,0:T(8,128)(2,1)S(1)}, bf16[64,2048]{1,0:T(8,128)(2,1)S(1)}, bf16[64,2048]{1,0:T(8,128)(2...) custom-call(bf16[128,512]{1,0:T(8,128)(2,1)S(1)} %pad_maximum_fusion, ...), custom_call_target="tpu_custom_call" | custom-call | flops 1073741824 | bytes 8943616 | tf_op jit(solution)/shard_map/pallas_call | solution.py:96
  24.6 7.3 %shard_map.198 = (bf16[1024,1024]{1,0:T(8,128)(2,1)S(1)}, bf16[1024,1024]{1,0:T(8,128)(2,1)S(1)}, bf16[1024,512]{1,0:T(8,128)(2,1)S(1)}, bf16[1024,512]{1,0:T(8,128)(2,1)S(1)}) custom-call(bf16[1024,512]{1,0:T(8,128)(2,1)S(1)} %get-tuple-element.66.refs_0_, bf16[512,1024]{1,0:T(8,128)(2,1)S(1)} %get-tuple-element.67.refs_1_, ...), custom_call_target="tpu_custom_call" | custom-call | flops 3221225472 | bytes 15728640 | tf_op jit(solution)/shard_map/pallas_call | solution.py:96
  32.0 0.1 collective-permute-start.3
  32.0 7.5 %shard_map.199 = (bf16[1024,1024]{1,0:T(8,128)(2,1)S(1)}, bf16[1024,1024]{1,0:T(8,128)(2,1)S(1)}, bf16[1024,512]{1,0:T(8,128)(2,1)S(1)}, bf16[1024,512]{1,0:T(8,128)(2,1)S(1)}) custom-call(bf16[1024,512]{1,0:T(8,128)(2,1)S(1)} %get-tuple-element.66.refs_0_, bf16[512,1024]{1,0:T(8,128)(2,1)S(1)} %get-tuple-element.67.refs_1_, ...), custom_call_target="tpu_custom_call" | custom-call | flops 3221225472 | bytes 15728640 | tf_op jit(solution)/shard_map/pallas_call | solution.py:96
  39.6 0.6 collective-permute-start.4
  40.1 0.8 shard_map.200
  40.9 1.7 %collective-permute-start.5 = (bf16[512,512]{1,0:T(8,128)(2,1)S(1)}, bf16[512,512]{1,0:T(8,128)(2,1)S(1)}, u32[]{:S(2)}, u32[]{:S(2)}) collective-permute-start(bf16[512,512]{1,0:T(8,128)(2,1)S(1)} %get-tuple-element.88), channel_id=1, source_target_pairs={{0,8},{1,17},{2,10},{3,19},{4,12},{5,21},{6,14},{7,23},{8,0},{9,25... | collective-permute-start | bytes 1572872 | tf_op jit(solution)/shard_map/ppermute | solution.py:438
  42.6 6.2 %shard_map.201 = (bf16[1024,512]{1,0:T(8,128)(2,1)}, f32[1024,512]{1,0:T(8,128)S(1)}, f32[1,512]{1,0:T(1,128)S(1)}) custom-call(f32[1024,512]{1,0:T(8,128)S(1)} %get-tuple-element.65.refs_0_, bf16[1024,512]{1,0:T(8,128)(2,1)S(1)} %copy-done.3, bf16[512,2048]{1,0:T(8,128)(2,1)S(1)} %copy-done.6, bf16[2048,512]{1,0:T(8,128)(2,1)S(1)} %copy-done.5, ...), custom_call_target="tpu_custom_call" | custom-call | flops 4294967296 | bytes 18878464 | tf_op jit(solution)/shard_map/pallas_call | solution.py:96
  48.8 1.4 collective-permute-done.5.refs_1_
  50.2 0.7 shard_map.202
  50.9 0.8 shard_map.203
  51.7 1.7 %collective-permute-start.7 = (bf16[512,512]{1,0:T(8,128)(2,1)S(1)}, bf16[512,512]{1,0:T(8,128)(2,1)S(1)}, u32[]{:S(2)}, u32[]{:S(2)}) collective-permute-start(bf16[512,512]{1,0:T(8,128)(2,1)S(1)} %get-tuple-element.94), channel_id=1, source_target_pairs={{0,8},{1,17},{2,10},{3,19},{4,12},{5,21},{6,14},{7,23},{8,0},{9,25... | collective-permute-start | bytes 1572872 | tf_op jit(solution)/shard_map/ppermute | solution.py:438
  53.4 1.5 %collective-permute-start.8 = (bf16[256,512]{1,0:T(8,128)(2,1)S(1)}, bf16[256,512]{1,0:T(8,128)(2,1)S(1)}, u32[]{:S(2)}, u32[]{:S(2)}) collective-permute-start(bf16[256,512]{1,0:T(8,128)(2,1)S(1)} %get-tuple-element.95), channel_id=1, source_target_pairs={{0,16},{1,9},{2,18},{3,11},{4,20},{5,13},{6,22},{7,15},{8,24},{9,1... | collective-permute-start | bytes 786440 | tf_op jit(solution)/shard_map/ppermute | solution.py:438
  54.9 8.5 %shard_map.204 = (bf16[1024,512]{1,0:T(8,128)(2,1)}, bf16[336,512]{1,0:T(8,128)(2,1)S(1)}, bf16[336,512]{1,0:T(8,128)(2,1)S(1)}) custom-call(bf16[1024,512]{1,0:T(8,128)(2,1)S(1)} %get-tuple-element.61.refs_4_.refs_0_, bf16[1024,128]{1,0:T(8,128)(2,1)S(1)} %get-tuple-element.62.refs_5_.refs_1_, bf16[128,1024]{1,0:T(8,128)(2,1)S(1)} %get-tuple-element.63.refs_6_.refs_2_, ...), custom_call_target="tpu_custom_call" | custom-call | flops 1610612736 | bytes 8208384 | tf_op jit(solution)/shard_map/pallas_call | solution.py:96
  63.4 0.1 collective-permute-start.6
  63.5 0.1 shard_map.205.refs_3_.refs_0_
  63.6 1.3 collective-permute-start.11
  64.9 0.7 shard_map.206
  65.6 0.6 collective-permute-start.10
  66.1 0.6 shard_map.207
  66.8 5.6 %collective-permute-done.11.refs_1_ = bf16[256,512]{1,0:T(8,128)(2,1)S(1)} collective-permute-done((bf16[256,512]{1,0:T(8,128)(2,1)S(1)}, bf16[256,512]{1,0:T(8,128)(2,1)S(1)}, u32[]{:S(2)}, u32[]{:S(2)}) %collective-permute-start.11) | collective-permute-done | bytes 262176 | tf_op jit(solution)/shard_map/ppermute | solution.py:443
  72.4 2.5 %collective-permute-start.14 = (bf16[256,512]{1,0:T(8,128)(2,1)S(1)}, bf16[256,512]{1,0:T(8,128)(2,1)S(1)}, u32[]{:S(2)}, u32[]{:S(2)}) collective-permute-start(bf16[256,512]{1,0:T(8,128)(2,1)S(1)} %shard_map.208.refs_2_.refs_0_), channel_id=1, source_target_pairs={{0,4},{2,6},{4,0},{6,2},{1,5},{3,7},{5,1},{7,3},{8,12},{10,14},{12... | collective-permute-start | bytes 786440 | tf_op jit(solution)/shard_map/ppermute | solution.py:443
  74.9 1.7 %collective-permute-start.9 = (bf16[208,512]{1,0:T(8,128)(2,1)S(1)}, bf16[208,512]{1,0:T(8,128)(2,1)S(1)}, u32[]{:S(2)}, u32[]{:S(2)}) collective-permute-start(bf16[208,512]{1,0:T(8,128)(2,1)S(1)} %get-tuple-element.98), channel_id=1, source_target_pairs={{0,2},{2,0},{4,6},{6,4},{1,3},{3,1},{5,7},{7,5},{8,10},{10,8},{12,... | collective-permute-start | bytes 638984 | tf_op jit(solution)/shard_map/ppermute | solution.py:443
  76.7 0.4 collective-permute-start.13
  77.1 10.5 %collective-permute-done.9.refs_1_ = bf16[208,512]{1,0:T(8,128)(2,1)S(1)} collective-permute-done((bf16[208,512]{1,0:T(8,128)(2,1)S(1)}, bf16[208,512]{1,0:T(8,128)(2,1)S(1)}, u32[]{:S(2)}, u32[]{:S(2)}) %collective-permute-start.9) | collective-permute-done | bytes 213024 | tf_op jit(solution)/shard_map/ppermute | solution.py:443
  87.6 0.6 shard_map.210
  88.3 0.6 collective-permute-start.17
  88.9 0.8 collective-permute-start.12
  89.6 3.8 %collective-permute-done.13.refs_1_ = bf16[256,512]{1,0:T(8,128)(2,1)S(1)} collective-permute-done((bf16[256,512]{1,0:T(8,128)(2,1)S(1)}, bf16[256,512]{1,0:T(8,128)(2,1)S(1)}, u32[]{:S(2)}, u32[]{:S(2)}) %collective-permute-start.13) | collective-permute-done | bytes 262176 | tf_op jit(solution)/shard_map/ppermute | solution.py:443
  93.5 3.7 %collective-permute-done.12.refs_1_ = bf16[144,512]{1,0:T(8,128)(2,1)S(1)} collective-permute-done((bf16[144,512]{1,0:T(8,128)(2,1)S(1)}, bf16[144,512]{1,0:T(8,128)(2,1)S(1)}, u32[]{:S(2)}, u32[]{:S(2)}) %collective-permute-start.12) | collective-permute-done | bytes 147488 | tf_op jit(solution)/shard_map/ppermute | solution.py:443
  97.3 0.6 shard_map.214.refs_2_.refs_0_
  97.9 0.8 collective-permute-start.20
  98.7 11.3 %collective-permute-done.16.refs_1_ = bf16[256,512]{1,0:T(8,128)(2,1)S(1)} collective-permute-done((bf16[256,512]{1,0:T(8,128)(2,1)S(1)}, bf16[256,512]{1,0:T(8,128)(2,1)S(1)}, u32[]{:S(2)}, u32[]{:S(2)}) %collective-permute-start.16) | collective-permute-done | bytes 262176 | tf_op jit(solution)/shard_map/ppermute | solution.py:443
  110.1 1.7 %collective-permute-start.19 = (bf16[256,512]{1,0:T(8,128)(2,1)S(1)}, bf16[256,512]{1,0:T(8,128)(2,1)S(1)}, u32[]{:S(2)}, u32[]{:S(2)}) collective-permute-start(bf16[256,512]{1,0:T(8,128)(2,1)S(1)} %shard_map.215.refs_2_.refs_0_), channel_id=1, source_target_pairs={{0,16},{1,9},{2,18},{3,11},{4,20},{5,13},{6,22},{7,15},{8,24},{9,1... | collective-permute-start | bytes 786440 | tf_op jit(solution)/shard_map/ppermute | solution.py:438
  111.8 1.6 %collective-permute-start.15 = (bf16[144,512]{1,0:T(8,128)(2,1)S(1)}, bf16[144,512]{1,0:T(8,128)(2,1)S(1)}, u32[]{:S(2)}, u32[]{:S(2)}) collective-permute-start(bf16[144,512]{1,0:T(8,128)(2,1)S(1)} %shard_map.213.refs_3_.refs_0_), channel_id=1, source_target_pairs={{0,8},{1,17},{2,10},{3,19},{4,12},{5,21},{6,14},{7,23},{8,0},{9,25... | collective-permute-start | bytes 442376 | tf_op jit(solution)/shard_map/ppermute | solution.py:438
  113.4 3.6 %collective-permute-done.15.refs_1_ = bf16[144,512]{1,0:T(8,128)(2,1)S(1)} collective-permute-done((bf16[144,512]{1,0:T(8,128)(2,1)S(1)}, bf16[144,512]{1,0:T(8,128)(2,1)S(1)}, u32[]{:S(2)}, u32[]{:S(2)}) %collective-permute-start.15) | collective-permute-done | bytes 147488 | tf_op jit(solution)/shard_map/ppermute | solution.py:438
  117.0 0.6 shard_map.217.refs_3_.refs_0_
  117.6 1.7 %collective-permute-done.19.refs_1_ = bf16[256,512]{1,0:T(8,128)(2,1)S(1)} collective-permute-done((bf16[256,512]{1,0:T(8,128)(2,1)S(1)}, bf16[256,512]{1,0:T(8,128)(2,1)S(1)}, u32[]{:S(2)}, u32[]{:S(2)}) %collective-permute-start.19) | collective-permute-done | bytes 262176 | tf_op jit(solution)/shard_map/ppermute | solution.py:438
  119.3 0.6 shard_map.218.refs_2_.refs_0_
  119.9 1.7 %collective-permute-start.22 = (bf16[512,512]{1,0:T(8,128)(2,1)S(1)}, bf16[512,512]{1,0:T(8,128)(2,1)S(1)}, u32[]{:S(2)}, u32[]{:S(2)}) collective-permute-start(bf16[512,512]{1,0:T(8,128)(2,1)S(1)} %shard_map.218.refs_2_.refs_0_), channel_id=1, source_target_pairs={{0,8},{1,17},{2,10},{3,19},{4,12},{5,21},{6,14},{7,23},{8,0},{9,25... | collective-permute-start | bytes 1572872 | tf_op jit(solution)/shard_map/ppermute | solution.py:438
  121.6 1.7 %collective-permute-start.18 = (bf16[144,512]{1,0:T(8,128)(2,1)S(1)}, bf16[144,512]{1,0:T(8,128)(2,1)S(1)}, u32[]{:S(2)}, u32[]{:S(2)}) collective-permute-start(bf16[144,512]{1,0:T(8,128)(2,1)S(1)} %shard_map.216.refs_3_.refs_0_), channel_id=1, source_target_pairs={{0,16},{1,9},{2,18},{3,11},{4,20},{5,13},{6,22},{7,15},{8,24},{9,1... | collective-permute-start | bytes 442376 | tf_op jit(solution)/shard_map/ppermute | solution.py:438
  123.3 3.5 %collective-permute-done.18.refs_1_ = bf16[144,512]{1,0:T(8,128)(2,1)S(1)} collective-permute-done((bf16[144,512]{1,0:T(8,128)(2,1)S(1)}, bf16[144,512]{1,0:T(8,128)(2,1)S(1)}, u32[]{:S(2)}, u32[]{:S(2)}) %collective-permute-start.18) | collective-permute-done | bytes 147488 | tf_op jit(solution)/shard_map/ppermute | solution.py:438
  126.8 2.4 %collective-permute-done.22.refs_1_ = bf16[512,512]{1,0:T(8,128)(2,1)S(1)} collective-permute-done((bf16[512,512]{1,0:T(8,128)(2,1)S(1)}, bf16[512,512]{1,0:T(8,128)(2,1)S(1)}, u32[]{:S(2)}, u32[]{:S(2)}) %collective-permute-start.22) | collective-permute-done | bytes 524320 | tf_op jit(solution)/shard_map/ppermute | solution.py:438
  129.2 0.6 shard_map.220.refs_3_.refs_0_
  129.8 0.1 collective-permute-start.23
  129.9 0.5 collective-permute-start.21
  130.4 2.4 %collective-permute-done.21.refs_1_ = bf16[144,512]{1,0:T(8,128)(2,1)S(1)} collective-permute-done((bf16[144,512]{1,0:T(8,128)(2,1)S(1)}, bf16[144,512]{1,0:T(8,128)(2,1)S(1)}, u32[]{:S(2)}, u32[]{:S(2)}) %collective-permute-start.21) | collective-permute-done | bytes 147488 | tf_op jit(solution)/shard_map/ppermute | solution.py:417
  132.7 1.4 %shard_map.221 = (f32[1,64,512]{2,1,0:T(8,128)}, f32[1,64,512]{2,1,0:T(8,128)}, f32[512,128]{1,0:T(8,128)}, f32[4,512]{1,0:T(4,128)}, f32[1,512]{1,0:T(1,128)}, /*index=5*/f32[1,512]{1,0:T(1,128)}) custom-call(bf16[144,512]{1,0:T(8,128)(2,1)S(1)} %shard_map.219.refs_3_.refs_0_, bf16[144,512]{1,0:T(8,128)(2,1)S(1)} %collective-permute-done.21.refs_1_, ...), custom_call_target="tpu_custom_call" | custom-call | bytes 831488 | tf_op jit(solution)/shard_map/pallas_call | solution.py:96
  134.2 0.7 copy-done.13
  134.9 2.9 %shard_map.222 = (f32[512,2048]{1,0:T(8,128)}, f32[2048,512]{1,0:T(8,128)}) custom-call(bf16[1024,512]{1,0:T(8,128)(2,1)S(1)} %shard_map.217.refs_3_.refs_0_, bf16[1024,512]{1,0:T(8,128)(2,1)S(1)} %collective-permute-done.24.refs_1_, s32[6]{0:T(128)S(1)} %stack.27.refs_12_.refs_5_.refs_2_.refs_17_, f32[1,512]{1,0:T(1,128)S(1)} %copy-done.13), custom_call_target="tpu_custom_call" | custom-call | bytes 6291456 | tf_op jit(solution)/shard_map/pallas_call | solution.py:538
  137.8 2.9 %shard_map.223 = (f32[512,2048]{1,0:T(8,128)}, f32[2048,512]{1,0:T(8,128)}) custom-call(bf16[1024,512]{1,0:T(8,128)(2,1)S(1)} %shard_map.220.refs_3_.refs_0_, bf16[1024,512]{1,0:T(8,128)(2,1)S(1)} %collective-permute-done.23.refs_1_, s32[6]{0:T(128)S(1)} %stack.27.refs_12_.refs_5_.refs_2_.refs_17_, ...), custom_call_target="tpu_custom_call", output_to_operand_aliasing={{0}: (4, {}), {1}: (5, {})} | custom-call | bytes 6291456 | tf_op jit(solution)/shard_map/pallas_call | solution.py:538
  (49 shorter events, 0.5 us)
Async XLA Ops:
  1.5 17.4 %collective-permute-start.2 = (bf16[128,512]{1,0:T(8,128)(2,1)S(1)}, bf16[128,512]{1,0:T(8,128)(2,1)S(1)}, u32[]{:S(2)}, u32[]{:S(2)}) collective-permute-start(bf16[128,512]{1,0:T(8,128)(2,1)S(1)} %pad_maximum_fusion.refs_0_), channel_id=1, source_target_pairs={{0,6},{2,4},{4,2},{6,0},{1,7},{3,5},{5,3},{7,1},{8,14},{10,12},{12... | collective-permute-start | bytes 393224 | tf_op jit(solution)/shard_map/ppermute | solution.py:417
  6.6 12.3 %collective-permute-start.1 = (bf16[128,512]{1,0:T(8,128)(2,1)S(1)}, bf16[128,512]{1,0:T(8,128)(2,1)S(1)}, u32[]{:S(2)}, u32[]{:S(2)}) collective-permute-start(bf16[128,512]{1,0:T(8,128)(2,1)S(1)} %pad_maximum_fusion.refs_0_), channel_id=1, source_target_pairs={{0,4},{2,6},{4,0},{6,2},{1,5},{3,7},{5,1},{7,3},{8,12},{10,14},{12... | collective-permute-start | bytes 393224 | tf_op jit(solution)/shard_map/ppermute | solution.py:417
  6.6 12.3 %collective-permute-start = (bf16[128,512]{1,0:T(8,128)(2,1)S(1)}, bf16[128,512]{1,0:T(8,128)(2,1)S(1)}, u32[]{:S(2)}, u32[]{:S(2)}) collective-permute-start(bf16[128,512]{1,0:T(8,128)(2,1)S(1)} %pad_maximum_fusion.refs_0_), channel_id=1, source_target_pairs={{0,2},{2,0},{4,6},{6,4},{1,3},{3,1},{5,7},{7,5},{8,10},{10,8},{12,... | collective-permute-start | bytes 393224 | tf_op jit(solution)/shard_map/ppermute | solution.py:417
  7.4 1.2 copy-start
  8.6 1.2 copy-start.2
  9.8 0.9 copy-start.7
  10.7 0.7 copy-start.8
  11.4 0.7 copy-start.11
  12.1 0.7 copy-start.15
  12.8 2.2 %copy-start.3 = (bf16[1024,512]{1,0:T(8,128)(2,1)S(1)}, bf16[1024,512]{1,0:T(8,128)(2,1)}, u32[]{:S(2)}) copy-start(bf16[1024,512]{1,0:T(8,128)(2,1)} %refs_1_.5) | copy-start | bytes 3145732
  15.0 1.6 %copy-start.4 = (bf16[2048,512]{1,0:T(8,128)(2,1)S(1)}, bf16[2048,512]{1,0:T(8,128)(2,1)}, u32[]{:S(2)}) copy-start(bf16[2048,512]{1,0:T(8,128)(2,1)} %refs_3_.1) | copy-start | bytes 6291460
  16.6 2.4 %copy-start.1 = (bf16[1024,512]{1,0:T(8,128)(2,1)S(1)}, bf16[1024,512]{1,0:T(8,128)(2,1)}, u32[]{:S(2)}) copy-start(bf16[1024,512]{1,0:T(8,128)(2,1)} %refs_13_.1) | copy-start | bytes 3145732
  16.6 2.4 %copy-start.9 = (s32[1024,2]{0,1:T(2,128)S(1)}, s32[1024,2]{0,1:T(2,128)}, u32[]{:S(2)}) copy-start(s32[1024,2]{0,1:T(2,128)} %param.14) | copy-start | bytes 24580
  16.6 2.4 %copy-start.10 = (s32[1,1024]{1,0:T(1,128)S(1)}, s32[1,1024]{1,0:T(1,128)}, u32[]{:S(2)}) copy-start(s32[1,1024]{1,0:T(1,128)} %refs_15_.1) | copy-start | bytes 12292
  16.6 2.5 %copy-start.14 = (f32[512]{0:T(512)S(1)}, f32[512]{0:T(512)}, u32[]{:S(2)}) copy-start(f32[512]{0:T(512)} %param.21) | copy-start | bytes 6148
  19.0 5.6 %copy-start.6 = (bf16[512,2048]{1,0:T(8,128)(2,1)S(1)}, bf16[512,2048]{1,0:T(8,128)(2,1)}, u32[]{:S(2)}) copy-start(bf16[512,2048]{1,0:T(8,128)(2,1)} %refs_2_.1) | copy-start | bytes 6291460
  32.0 8.2 %collective-permute-start.3 = (bf16[1024,512]{1,0:T(8,128)(2,1)S(1)}, bf16[1024,512]{1,0:T(8,128)(2,1)S(1)}, u32[]{:S(2)}, u32[]{:S(2)}) collective-permute-start(bf16[1024,512]{1,0:T(8,128)(2,1)S(1)} %get-tuple-element.75), channel_id=1, source_target_pairs={{0,1},{1,0},{2,3},{3,2},{4,5},{5,4},{6,7},{7,6},{8,9},{9,8},{10,11... | collective-permute-start | bytes 3145736 | tf_op jit(solution)/shard_map/ppermute | solution.py:417
  39.6 3.1 %copy-start.5 = (bf16[2048,512]{1,0:T(8,128)(2,1)S(1)}, bf16[2048,512]{1,0:T(8,128)(2,1)}, u32[]{:S(2)}) copy-start(bf16[2048,512]{1,0:T(8,128)(2,1)} %refs_3_.1) | copy-start | bytes 6291460
  39.6 11.3 %collective-permute-start.4 = (bf16[1024,512]{1,0:T(8,128)(2,1)S(1)}, bf16[1024,512]{1,0:T(8,128)(2,1)S(1)}, u32[]{:S(2)}, u32[]{:S(2)}) collective-permute-start(bf16[1024,512]{1,0:T(8,128)(2,1)S(1)} %get-tuple-element.87), channel_id=1, source_target_pairs={{0,1},{1,0},{2,3},{3,2},{4,5},{5,4},{6,7},{7,6},{8,9},{9,8},{10,11... | collective-permute-start | bytes 3145736 | tf_op jit(solution)/shard_map/ppermute | solution.py:417
  40.9 9.2 %collective-permute-start.5 = (bf16[512,512]{1,0:T(8,128)(2,1)S(1)}, bf16[512,512]{1,0:T(8,128)(2,1)S(1)}, u32[]{:S(2)}, u32[]{:S(2)}) collective-permute-start(bf16[512,512]{1,0:T(8,128)(2,1)S(1)} %get-tuple-element.88), channel_id=1, source_target_pairs={{0,8},{1,17},{2,10},{3,19},{4,12},{5,21},{6,14},{7,23},{8,0},{9,25... | collective-permute-start | bytes 1572872 | tf_op jit(solution)/shard_map/ppermute | solution.py:438
  48.8 6.1 %copy-start.12 = (f32[512]{0:T(512)S(1)}, f32[512]{0:T(512)}, u32[]{:S(2)}) copy-start(f32[512]{0:T(512)} %param.16) | copy-start | bytes 6148
  51.7 13.2 %collective-permute-start.7 = (bf16[512,512]{1,0:T(8,128)(2,1)S(1)}, bf16[512,512]{1,0:T(8,128)(2,1)S(1)}, u32[]{:S(2)}, u32[]{:S(2)}) collective-permute-start(bf16[512,512]{1,0:T(8,128)(2,1)S(1)} %get-tuple-element.94), channel_id=1, source_target_pairs={{0,8},{1,17},{2,10},{3,19},{4,12},{5,21},{6,14},{7,23},{8,0},{9,25... | collective-permute-start | bytes 1572872 | tf_op jit(solution)/shard_map/ppermute | solution.py:438
  53.4 10.1 %collective-permute-start.8 = (bf16[256,512]{1,0:T(8,128)(2,1)S(1)}, bf16[256,512]{1,0:T(8,128)(2,1)S(1)}, u32[]{:S(2)}, u32[]{:S(2)}) collective-permute-start(bf16[256,512]{1,0:T(8,128)(2,1)S(1)} %get-tuple-element.95), channel_id=1, source_target_pairs={{0,16},{1,9},{2,18},{3,11},{4,20},{5,13},{6,22},{7,15},{8,24},{9,1... | collective-permute-start | bytes 786440 | tf_op jit(solution)/shard_map/ppermute | solution.py:438
  63.4 2.7 %collective-permute-start.6 = (bf16[336,512]{1,0:T(8,128)(2,1)S(1)}, bf16[336,512]{1,0:T(8,128)(2,1)S(1)}, u32[]{:S(2)}, u32[]{:S(2)}) collective-permute-start(bf16[336,512]{1,0:T(8,128)(2,1)S(1)} %get-tuple-element.93), channel_id=1, source_target_pairs={{0,1},{1,0},{2,3},{3,2},{4,5},{5,4},{6,7},{7,6},{8,9},{9,8},{10,11... | collective-permute-start | bytes 1032200 | tf_op jit(solution)/shard_map/ppermute | solution.py:417
  63.6 8.8 %collective-permute-start.11 = (bf16[256,512]{1,0:T(8,128)(2,1)S(1)}, bf16[256,512]{1,0:T(8,128)(2,1)S(1)}, u32[]{:S(2)}, u32[]{:S(2)}) collective-permute-start(bf16[256,512]{1,0:T(8,128)(2,1)S(1)} %shard_map.205.refs_3_.refs_0_), channel_id=1, source_target_pairs={{0,2},{2,0},{4,6},{6,4},{1,3},{3,1},{5,7},{7,5},{8,10},{10,8},{12,... | collective-permute-start | bytes 786440 | tf_op jit(solution)/shard_map/ppermute | solution.py:443
  65.6 11.1 %collective-permute-start.10 = (bf16[256,512]{1,0:T(8,128)(2,1)S(1)}, bf16[256,512]{1,0:T(8,128)(2,1)S(1)}, u32[]{:S(2)}, u32[]{:S(2)}) collective-permute-start(bf16[256,512]{1,0:T(8,128)(2,1)S(1)} %get-tuple-element.99), channel_id=1, source_target_pairs={{0,16},{1,9},{2,18},{3,11},{4,20},{5,13},{6,22},{7,15},{8,24},{9,1... | collective-permute-start | bytes 786440 | tf_op jit(solution)/shard_map/ppermute | solution.py:438
  72.4 15.8 %collective-permute-start.14 = (bf16[256,512]{1,0:T(8,128)(2,1)S(1)}, bf16[256,512]{1,0:T(8,128)(2,1)S(1)}, u32[]{:S(2)}, u32[]{:S(2)}) collective-permute-start(bf16[256,512]{1,0:T(8,128)(2,1)S(1)} %shard_map.208.refs_2_.refs_0_), channel_id=1, source_target_pairs={{0,4},{2,6},{4,0},{6,2},{1,5},{3,7},{5,1},{7,3},{8,12},{10,14},{12... | collective-permute-start | bytes 786440 | tf_op jit(solution)/shard_map/ppermute | solution.py:443
  74.9 12.7 %collective-permute-start.9 = (bf16[208,512]{1,0:T(8,128)(2,1)S(1)}, bf16[208,512]{1,0:T(8,128)(2,1)S(1)}, u32[]{:S(2)}, u32[]{:S(2)}) collective-permute-start(bf16[208,512]{1,0:T(8,128)(2,1)S(1)} %get-tuple-element.98), channel_id=1, source_target_pairs={{0,2},{2,0},{4,6},{6,4},{1,3},{3,1},{5,7},{7,5},{8,10},{10,8},{12,... | collective-permute-start | bytes 638984 | tf_op jit(solution)/shard_map/ppermute | solution.py:443
  76.7 16.7 %collective-permute-start.13 = (bf16[256,512]{1,0:T(8,128)(2,1)S(1)}, bf16[256,512]{1,0:T(8,128)(2,1)S(1)}, u32[]{:S(2)}, u32[]{:S(2)}) collective-permute-start(bf16[256,512]{1,0:T(8,128)(2,1)S(1)} %shard_map.209.refs_3_.refs_0_), channel_id=1, source_target_pairs={{0,2},{2,0},{4,6},{6,4},{1,3},{3,1},{5,7},{7,5},{8,10},{10,8},{12,... | collective-permute-start | bytes 786440 | tf_op jit(solution)/shard_map/ppermute | solution.py:443
  88.3 9.0 %collective-permute-start.17 = (bf16[256,512]{1,0:T(8,128)(2,1)S(1)}, bf16[256,512]{1,0:T(8,128)(2,1)S(1)}, u32[]{:S(2)}, u32[]{:S(2)}) collective-permute-start(bf16[256,512]{1,0:T(8,128)(2,1)S(1)} %shard_map.211.refs_2_.refs_0_), channel_id=1, source_target_pairs={{0,16},{1,9},{2,18},{3,11},{4,20},{5,13},{6,22},{7,15},{8,24},{9,1... | collective-permute-start | bytes 786440 | tf_op jit(solution)/shard_map/ppermute | solution.py:438
  88.9 8.4 %collective-permute-start.12 = (bf16[144,512]{1,0:T(8,128)(2,1)S(1)}, bf16[144,512]{1,0:T(8,128)(2,1)S(1)}, u32[]{:S(2)}, u32[]{:S(2)}) collective-permute-start(bf16[144,512]{1,0:T(8,128)(2,1)S(1)} %get-tuple-element.101), channel_id=1, source_target_pairs={{0,4},{2,6},{4,0},{6,2},{1,5},{3,7},{5,1},{7,3},{8,12},{10,14},{12... | collective-permute-start | bytes 442376 | tf_op jit(solution)/shard_map/ppermute | solution.py:443
  97.9 19.1 %collective-permute-start.20 = (bf16[512,512]{1,0:T(8,128)(2,1)S(1)}, bf16[512,512]{1,0:T(8,128)(2,1)S(1)}, u32[]{:S(2)}, u32[]{:S(2)}) collective-permute-start(bf16[512,512]{1,0:T(8,128)(2,1)S(1)} %shard_map.214.refs_2_.refs_0_), channel_id=1, source_target_pairs={{0,8},{1,17},{2,10},{3,19},{4,12},{5,21},{6,14},{7,23},{8,0},{9,25... | collective-permute-start | bytes 1572872 | tf_op jit(solution)/shard_map/ppermute | solution.py:438
  98.7 11.3 %collective-permute-start.16 = (bf16[256,512]{1,0:T(8,128)(2,1)S(1)}, bf16[256,512]{1,0:T(8,128)(2,1)S(1)}, u32[]{:S(2)}, u32[]{:S(2)}) collective-permute-start(bf16[256,512]{1,0:T(8,128)(2,1)S(1)} %shard_map.212.refs_2_.refs_0_), channel_id=1, source_target_pairs={{0,4},{2,6},{4,0},{6,2},{1,5},{3,7},{5,1},{7,3},{8,12},{10,14},{12... | collective-permute-start | bytes 786440 | tf_op jit(solution)/shard_map/ppermute | solution.py:443
  110.1 9.3 %collective-permute-start.19 = (bf16[256,512]{1,0:T(8,128)(2,1)S(1)}, bf16[256,512]{1,0:T(8,128)(2,1)S(1)}, u32[]{:S(2)}, u32[]{:S(2)}) collective-permute-start(bf16[256,512]{1,0:T(8,128)(2,1)S(1)} %shard_map.215.refs_2_.refs_0_), channel_id=1, source_target_pairs={{0,16},{1,9},{2,18},{3,11},{4,20},{5,13},{6,22},{7,15},{8,24},{9,1... | collective-permute-start | bytes 786440 | tf_op jit(solution)/shard_map/ppermute | solution.py:438
  111.8 5.1 %collective-permute-start.15 = (bf16[144,512]{1,0:T(8,128)(2,1)S(1)}, bf16[144,512]{1,0:T(8,128)(2,1)S(1)}, u32[]{:S(2)}, u32[]{:S(2)}) collective-permute-start(bf16[144,512]{1,0:T(8,128)(2,1)S(1)} %shard_map.213.refs_3_.refs_0_), channel_id=1, source_target_pairs={{0,8},{1,17},{2,10},{3,19},{4,12},{5,21},{6,14},{7,23},{8,0},{9,25... | collective-permute-start | bytes 442376 | tf_op jit(solution)/shard_map/ppermute | solution.py:438
  119.9 9.2 %collective-permute-start.22 = (bf16[512,512]{1,0:T(8,128)(2,1)S(1)}, bf16[512,512]{1,0:T(8,128)(2,1)S(1)}, u32[]{:S(2)}, u32[]{:S(2)}) collective-permute-start(bf16[512,512]{1,0:T(8,128)(2,1)S(1)} %shard_map.218.refs_2_.refs_0_), channel_id=1, source_target_pairs={{0,8},{1,17},{2,10},{3,19},{4,12},{5,21},{6,14},{7,23},{8,0},{9,25... | collective-permute-start | bytes 1572872 | tf_op jit(solution)/shard_map/ppermute | solution.py:438
  121.6 5.1 %collective-permute-start.18 = (bf16[144,512]{1,0:T(8,128)(2,1)S(1)}, bf16[144,512]{1,0:T(8,128)(2,1)S(1)}, u32[]{:S(2)}, u32[]{:S(2)}) collective-permute-start(bf16[144,512]{1,0:T(8,128)(2,1)S(1)} %shard_map.216.refs_3_.refs_0_), channel_id=1, source_target_pairs={{0,16},{1,9},{2,18},{3,11},{4,20},{5,13},{6,22},{7,15},{8,24},{9,1... | collective-permute-start | bytes 442376 | tf_op jit(solution)/shard_map/ppermute | solution.py:438
  123.3 10.9 %collective-permute-start.24 = (bf16[1024,512]{1,0:T(8,128)(2,1)S(1)}, bf16[1024,512]{1,0:T(8,128)(2,1)S(1)}, u32[]{:S(2)}, u32[]{:S(2)}) collective-permute-start(bf16[1024,512]{1,0:T(8,128)(2,1)S(1)} %shard_map.217.refs_3_.refs_0_), channel_id=1, source_target_pairs={{0,1},{1,0},{2,3},{3,2},{4,5},{5,4},{6,7},{7,6},{8,9},{9,8},{10,11... | collective-permute-start | bytes 3145736 | tf_op jit(solution)/shard_map/ppermute | solution.py:417
  129.8 8.0 %collective-permute-start.23 = (bf16[1024,512]{1,0:T(8,128)(2,1)S(1)}, bf16[1024,512]{1,0:T(8,128)(2,1)S(1)}, u32[]{:S(2)}, u32[]{:S(2)}) collective-permute-start(bf16[1024,512]{1,0:T(8,128)(2,1)S(1)} %shard_map.220.refs_3_.refs_0_), channel_id=1, source_target_pairs={{0,1},{1,0},{2,3},{3,2},{4,5},{5,4},{6,7},{7,6},{8,9},{9,8},{10,11... | collective-permute-start | bytes 3145736 | tf_op jit(solution)/shard_map/ppermute | solution.py:417
  129.9 2.9 %collective-permute-start.21 = (bf16[144,512]{1,0:T(8,128)(2,1)S(1)}, bf16[144,512]{1,0:T(8,128)(2,1)S(1)}, u32[]{:S(2)}, u32[]{:S(2)}) collective-permute-start(bf16[144,512]{1,0:T(8,128)(2,1)S(1)} %shard_map.219.refs_3_.refs_0_), channel_id=1, source_target_pairs={{0,1},{1,0},{2,3},{3,2},{4,5},{5,4},{6,7},{7,6},{8,9},{9,8},{10,11... | collective-permute-start | bytes 442376 | tf_op jit(solution)/shard_map/ppermute | solution.py:417
  134.2 0.7 copy-start.13

commit v3 on v2

v3 whole, which is shorter than its diff:
```python
import functools

import jax
import jax.numpy as jnp
from jax import lax
from jax.experimental import pallas as pl
from jax.experimental.pallas import tpu as pltpu
from jax.sharding import PartitionSpec as P

BF = jnp.bfloat16
F32 = jnp.float32
MASKED = -1e30
BAND = 128
ROWS = 256
PIECE = 256
AXES = ("dp", "expert", "tok")
GLUE = 23 * 10**9
COPIES = 8
WORK = 1
ORDER = (
    "f", "A", "f", "a", "B", "ab", "n", "h", "a", "b", "r", "a", "t", "b", "t", "a", "b", "o", "t",
    "a", "b", "t", "a", "bt", "a", "P", "bt", "p", "bt", "Q", "T", "q",
)


def nn(left, right):
    return lax.dot_general(left, right, (((1,), (0,)), ((), ())), preferred_element_type=F32)


def nt(left, right):
    return lax.dot_general(left, right, (((1,), (1,)), ((), ())), preferred_element_type=F32)


def tn(left, right):
    return lax.dot_general(left, right, (((0,), (0,)), ((), ())), preferred_element_type=F32)


def normalize(values):
    centre = values - jnp.mean(values, axis=-1, keepdims=True)
    spread = jnp.mean(centre * centre, axis=-1, keepdims=True)
    inverse = lax.rsqrt(spread + 1e-05)
    return centre * inverse, inverse


def normalize_back(upstream, normalized, inverse, gain):
    scaled = upstream * gain
    inner = (
        scaled
        - jnp.mean(scaled, axis=-1, keepdims=True)
        - normalized * jnp.mean(scaled * normalized, axis=-1, keepdims=True)
    )
    return inner * inverse


def sds(shape, dtype):
    return jax.ShapeDtypeStruct(shape, dtype)


def size_of(array):
    lanes = -(-array.shape[-1] // 128) * 128
    rows = -(-array.shape[-2] // 16) * 16
    lead = 1
    for extent in array.shape[:-2]:
        lead = lead * extent
    return lead * rows * lanes * jnp.dtype(array.dtype).itemsize


class Place:
    def __init__(self, ref):
        self.ref = ref

    def __getitem__(self, row):
        return self.ref[row, 0]


class Line:
    def __init__(self):
        self.last = None

    def call(
        self, kernel, operands, outs, fetched=(), scalars=(), scratch=(), room=2 << 20, weight=WORK,
        sent=(), aliased=(), kept=(), numbers=(),
    ):
        n, f, s = len(operands), len(fetched) + len(kept), len(scalars)
        late = () if self.last is None else (self.last,)
        skip = len(late) + len(aliased)
        outs = list(outs)
        h = len(sent)
        if not outs:
            outs = [sds((8, 128), F32)]
        outs = outs + [sds(a.shape, a.dtype) for a in kept]
        scratch_copies, fetched = len(fetched), (*fetched, *kept)

        def wrapped(*refs):
            ins = refs[:n]
            sources = refs[n : n + f]
            smem = [Place(ref) for ref in refs[n + f : n + f + s]] + list(
                refs[n + f + s : n + f + s + len(numbers)]
            )
            rest = list(refs[n + f + s + len(numbers) + skip :])
            far = rest[len(outs) : len(outs) + h]
            del rest[len(outs) : len(outs) + h]
            open_copies, send_sem = [], rest.pop() if h else None
            sems = rest.pop() if f else None
            buffers = rest[len(rest) - scratch_copies :] if scratch_copies else []
            del rest[len(rest) - scratch_copies :]
            first = len(outs) - len(kept)
            buffers = buffers + rest[first : len(outs)]
            del rest[first : len(outs)]
            body, waits, waiting = rest, [], {}
            for i in range(f):
                copy = pltpu.make_async_copy(sources[i], buffers[i], sems.at[i])
                copy.start()
                waiting[i] = copy

                def wait(i=i):
                    if i in waiting:
                        waiting.pop(i).wait()
                    return buffers[i]

                waits.append(wait)
            def send(source, target, other=None, near=None):
                sem = send_sem.at[len(open_copies)]
                copy = pltpu.make_async_copy(source, target, sem)
                open_copies.append(copy)
                if other is None:
                    copy.start()
                    return
                pl.when(near)(copy.start)
                pl.when(jnp.logical_not(near))(pltpu.make_async_copy(source, other, sem).start)

            if h:
                kernel(*ins, *waits, *smem, *body, send, *far)
                for copy in open_copies:
                    copy.wait()
            else:
                kernel(*ins, *waits, *smem, *body)
            for copy in waiting.values():
                copy.wait()

        need = sum(size_of(a) for a in (*fetched[:scratch_copies], *scratch))
        extra = [pltpu.VMEM(a.shape, a.dtype) for a in fetched[:scratch_copies]]
        if f:
            extra.append(pltpu.SemaphoreType.DMA((f,)))
        if h:
            extra.append(pltpu.SemaphoreType.DMA((COPIES,)))
        results = pl.pallas_call(
            wrapped,
            out_shape=outs + list(sent),
            in_specs=[pl.BlockSpec(memory_space=pltpu.VMEM)] * n
            + [pl.BlockSpec(memory_space=pltpu.HBM)] * f
            + [pl.BlockSpec(memory_space=pltpu.VMEM)] * s
            + [pl.BlockSpec(memory_space=pltpu.SMEM)] * len(numbers)
            + [pl.BlockSpec(memory_space=pl.ANY)] * skip,
            out_specs=[pl.BlockSpec(memory_space=pltpu.VMEM)] * len(outs)
            + [pl.BlockSpec(memory_space=pltpu.HBM)] * h,
            input_output_aliases={
                n + f + s + len(numbers) + len(late) + i: len(outs) + i for i in range(len(aliased))
            },
            scratch_shapes=[pltpu.VMEM(a.shape, a.dtype) for a in scratch] + extra,
            compiler_params=pltpu.CompilerParams(vmem_limit_bytes=need + room),
            cost_estimate=pl.CostEstimate(flops=weight, bytes_accessed=1024, transcendentals=0),
        )(
            *operands,
            *[pltpu.with_memory_space_constraint(a, pltpu.HBM) for a in fetched],
            *scalars,
            *numbers,
            *late,
            *aliased,
        )
        self.last = min(results[: len(outs)], key=lambda a: a.size)
        return results


def prepare_kernel(
    ln_wait, wkv_wait, wr_wait, sent_wait, ln_two_wait, x_wait, g_wait, ids_wait, win_wait, wout_wait,
    wq_wait, wo_wait, spots_ref, xn_ref, kv_ref, kvt_ref, gates_ref, gt_ref, small_ref, sent_keep, gains_keep, keyid_ref,
    place_ref,
):
    for i in range(spots_ref.shape[0]):
        place_ref[i : i + 1, :] = jnp.full((1, place_ref.shape[1]), spots_ref[i], jnp.int32)
    ln_ref, x_ref = ln_wait(), x_wait()
    length = x_ref.shape[0]
    gain = ln_ref[...]
    gains_keep[0:1, :] = gain
    for start in range(0, length, ROWS):
        rows = pl.ds(start, ROWS)
        normalized, _ = normalize(x_ref[rows, :].astype(F32))
        xn_ref[rows, :] = (normalized * gain).astype(BF)
    normed = xn_ref[...]
    wkv_ref, wr_ref, ids_ref = wkv_wait(), wr_wait(), ids_wait()
    pair = wkv_ref.shape[1]
    experts = wr_ref.shape[0]
    small_ref[:pair, :] = wkv_ref[...].T
    small_ref[pair:, :] = jnp.concatenate(
        [wr_ref[...].astype(F32), jnp.zeros((16 - experts, wr_ref.shape[1]), F32)], axis=0
    ).astype(BF)
    small = small_ref[...]
    both = nt(small, normed)
    kvt_ref[...] = both[:pair].astype(BF)
    kv_ref[...] = nn(normed, wkv_ref[...]).astype(BF)
    choose = ids_ref.shape[0]
    picked = []
    for route in range(choose):
        ids = ids_ref[route : route + 1, :]
        value = jnp.zeros((1, length), F32)
        for expert in range(experts):
            value = jnp.where(ids == expert, both[pair + expert : pair + expert + 1], value)
        picked.append(value)
    top = functools.reduce(jnp.maximum, picked)
    raised = [jnp.exp(value - top) for value in picked]
    total = functools.reduce(lambda a, b: a + b, raised)
    for route in range(choose):
        gates_ref[route : route + 1, :] = raised[route] / total
    gains_keep[1:2, :] = ln_two_wait()[...]
    sent_ref = sent_wait()
    sent_keep[...] = sent_ref[...].astype(F32)
    column_ids(sent_keep, keyid_ref)
    g_ref = g_wait()
    gt_ref[...] = g_ref[...].T


def upstream_kernel(g_ref, wout_ref, ag_ref):
    for start in range(0, g_ref.shape[0], ROWS):
        rows = slice(start, start + ROWS)
        ag_ref[rows, :] = nt(g_ref[rows, :], wout_ref[...]).astype(BF)


def column_ids(sent_ref, keyid_ref):
    length = sent_ref.shape[1]
    for start in range(0, length, BAND):
        row = jnp.broadcast_to(sent_ref[:, start : start + BAND], (BAND, BAND))
        keyid_ref[pl.ds(start, BAND), :] = row.T


def masked_scores(kv_ref, keyid_ref, sent_ref, queries, start, low, high, choose):
    padded = jnp.concatenate([queries, jnp.zeros_like(queries)], axis=0)
    scores = nn(kv_ref[low:high, :], padded) * 0.125
    same = keyid_ref[low:high, :] == sent_ref[:, start : start + BAND]
    parts = [
        jnp.where(same, scores[:, route * BAND : (route + 1) * BAND], MASKED)
        for route in range(choose)
    ]
    return jnp.concatenate(parts, axis=1)


def window(start, length):
    return max(start - BAND, 0), min(start + 2 * BAND, length)


def attend_kernel(*refs, experts, head, peers):
    slab_refs, refs = refs[:peers], refs[peers:]
    (
        xn_ref, kv_ref, kvt_ref, gates_ref, x_ref, ids_ref, sent_ref, ln_ref, keyid_ref, wq_own, wo_own,
        place_ref, wq_ref, wo_ref, qt_ref, at_ref, lse_ref, gat_ref, h_ref, hn_ref, hnt_ref, all_ref,
        pair_ref,
    ) = refs
    own = place_ref[1]
    each = 2 * head // peers
    wq_ref[pl.ds(own * head, head), :] = wq_own[...]
    wo_ref[pl.ds(own * head, head), :] = wo_own[...]
    for k in range(1, experts):
        for j in range(peers):
            rows = pl.ds((place_ref[0] ^ j) * each, each)
            pair_ref[rows, :] = slab_refs[j][(k - 1) * each : k * each, :]
        rows = pl.ds((own ^ k) * head, head)
        wq_ref[rows, :] = pair_ref[:head, :]
        wo_ref[rows, :] = pair_ref[head:, :]
    length = xn_ref.shape[0]
    choose = ids_ref.shape[0]
    all_ref[...] = nt(wq_ref[...], xn_ref[...])
    for start in range(0, length, BAND):
        lanes = slice(start, start + BAND)
        block = slice(start * choose, (start + BAND) * choose)
        low, high = window(start, length)
        chosen = []
        for route in range(choose):
            ids = ids_ref[route : route + 1, lanes]
            value = jnp.zeros((head, BAND), F32)
            for expert in range(experts):
                value = jnp.where(
                    ids == expert, all_ref[expert * head : (expert + 1) * head, lanes], value
                )
            chosen.append(value)
        queries = jnp.concatenate(chosen, axis=1).astype(BF)
        qt_ref[:, block] = queries
        scores = masked_scores(kv_ref, keyid_ref, sent_ref, queries, start, low, high, choose)
        largest = jnp.max(scores, axis=0, keepdims=True)
        raised = jnp.exp(scores - largest)
        total = jnp.sum(raised, axis=0, keepdims=True)
        probs = (raised * (1.0 / total)).astype(BF)
        lse_ref[:, block] = largest + jnp.log(total)
        attended = nn(kvt_ref[head:, low:high], probs).astype(BF)
        at_ref[:, block] = attended
        spread = [jnp.zeros((head, BAND), F32) for _ in range(experts)]
        for route in range(choose):
            ids = ids_ref[route : route + 1, lanes]
            gated = attended[:, route * BAND : (route + 1) * BAND].astype(F32) * gates_ref[
                route : route + 1, lanes
            ]
            for expert in range(experts):
                spread[expert] = jnp.where(ids == expert, gated, spread[expert])
        for expert in range(experts):
            gat_ref[expert * head : (expert + 1) * head, lanes] = spread[expert].astype(BF)
    gain = ln_ref[1:2, :]
    for start in range(0, length, ROWS):
        rows = slice(start, start + ROWS)
        mixed = tn(gat_ref[:, rows], wo_ref[...])
        hidden = x_ref[rows, :].astype(F32) + mixed
        h_ref[rows, :] = hidden
        normalized, _ = normalize(hidden)
        low_value = (normalized * gain).astype(BF)
        hn_ref[rows, :] = low_value
        hnt_ref[:, rows] = low_value.T


def gelu_both(values):
    bell = jnp.exp2(values * values * -0.7213475204444817)
    t = 1.0 / (1.0 + 0.23164188 * jnp.abs(values))
    poly = t * (
        0.127414796
        + t * (-0.142248368 + t * (0.7107068705 + t * (-0.7265760135 + t * 0.5307027145)))
    )
    tail = poly * bell
    cumulative = jnp.where(values >= 0.0, 1.0 - tail, tail)
    return values * cumulative, cumulative + values * (bell * 0.3989422804014327)


def ffn_block(refs, first):
    hn_ref, hnt_ref, gt_ref, ag_ref, win_ref, u_ref, dpre_ref = refs
    length, width = hn_ref.shape
    far = slice(first, first + width)
    out_grad = in_grad = None
    for start in range(0, length, 2 * ROWS):
        rows = slice(start, start + 2 * ROWS)
        activated, slope = gelu_both(nn(hn_ref[rows, :], win_ref[:, far]))
        activated = activated.astype(BF)
        before = (ag_ref[rows, far].astype(F32) * slope).astype(BF)
        u_ref[rows, :], dpre_ref[rows, :] = activated, before
        out_part, in_part = nn(gt_ref[:, rows], activated), nn(hnt_ref[:, rows], before)
        out_grad = out_part if out_grad is None else out_grad + out_part
        in_grad = in_part if in_grad is None else in_grad + in_part
    return out_grad.astype(BF).T, in_grad.astype(BF)


def ffn_kernel(*refs, first, peers):
    place_ref, part_refs = refs[5], list(refs[8:])
    width = refs[0].shape[1]
    tok = place_ref[0]
    out_grad, in_grad = ffn_block((*refs[:5], *refs[6:8]), first)
    if peers == 2:
        pieces = len(part_refs) // 2
        size = part_refs[0].shape[0]
        for i in range(pieces):
            span = slice(i * size, (i + 1) * size)
            one, two = out_grad[span, :], in_grad[span, :]
            part_refs[i][...] = jnp.where(tok == 0, one, two)
            part_refs[pieces + i][...] = jnp.where(tok == 0, two, one)
        return
    sum_ref = part_refs.pop()
    sum_ref[:width, :], sum_ref[width:, :] = out_grad, in_grad
    size = part_refs[0].shape[0]
    pieces = len(part_refs) // peers
    for k in range(peers):
        for i in range(pieces):
            start = (tok ^ k) * size * pieces + i * size
            part_refs[k * pieces + i][...] = sum_ref[pl.ds(start, size), :]


def output_kernel(*refs):
    h_ref, wout_ref = refs[:2]
    out_ref, send, far_ref = refs[-3:]
    u_refs = refs[2:-4]
    for start in range(0, h_ref.shape[0], ROWS):
        rows = slice(start, start + ROWS)
        total, first = h_ref[rows, :], 0
        for ref in u_refs:
            size = ref.shape[1]
            total = total + nn(ref[rows, :], wout_ref[first : first + size, :])
            first = first + size
        out_ref[rows, :] = total.astype(BF)
        send(out_ref.at[rows, :], far_ref.at[rows, :])


def hidden_kernel(*refs):
    h_ref, g_ref, win_ref, ln_ref = refs[:4]
    dh_ref, low_ref, gain_ref = refs[-3:]
    dpre_refs = refs[4:-3]
    gain = ln_ref[1:2, :]
    gain_sum = jnp.zeros_like(gain)
    for start in range(0, h_ref.shape[0], ROWS):
        rows = slice(start, start + ROWS)
        upstream, first = None, 0
        for ref in dpre_refs:
            size = ref.shape[1]
            part = nt(ref[rows, :], win_ref[:, first : first + size])
            upstream = part if upstream is None else upstream + part
            first = first + size
        normalized, inverse = normalize(h_ref[rows, :])
        value = g_ref[rows, :].astype(F32) + normalize_back(upstream, normalized, inverse, gain)
        dh_ref[rows, :] = value
        low_ref[rows, :] = value.astype(BF)
        gain_sum = gain_sum + jnp.sum(upstream * normalized, axis=0, keepdims=True)
    gain_ref[...] = gain_sum


def heads_back_kernel(
    kv_ref, kvt_ref, gates_ref, wo_ref, qt_ref, at_ref, lse_ref, gat_ref, low_ref, ids_ref, sent_ref,
    keyid_ref, z_ref, gout_ref, all_ref, dkv_ref, *, experts, head,
):
    length = kv_ref.shape[0]
    wide, pair = experts * head, 2 * head
    choose = ids_ref.shape[0]
    all_ref[...] = nt(wo_ref[...], low_ref[...])
    gout_ref[...] = nn(gat_ref[...], low_ref[...]).astype(BF)
    dkv_ref[...] = jnp.zeros_like(dkv_ref)
    for start in range(0, length, BAND):
        lanes = slice(start, start + BAND)
        block = slice(start * choose, (start + BAND) * choose)
        low, high = window(start, length)
        raw, gate_grads = [], []
        for route in range(choose):
            ids = ids_ref[route : route + 1, lanes]
            value = jnp.zeros((head, BAND), F32)
            for expert in range(experts):
                value = jnp.where(
                    ids == expert, all_ref[expert * head : (expert + 1) * head, lanes], value
                )
            raw.append(value)
            attended = at_ref[:, start * choose + route * BAND : start * choose + (route + 1) * BAND]
            gate_grads.append(jnp.sum(value * attended.astype(F32), axis=0, keepdims=True))
        gates = [gates_ref[route : route + 1, lanes] for route in range(choose)]
        common = functools.reduce(
            lambda a, b: a + b, [gate * grad for gate, grad in zip(gates, gate_grads)]
        )
        logit_rows = [jnp.zeros((1, BAND), F32) for _ in range(experts)]
        for route in range(choose):
            ids = ids_ref[route : route + 1, lanes]
            picked = gates[route] * (gate_grads[route] - common)
            for expert in range(experts):
                logit_rows[expert] = jnp.where(ids == expert, picked, logit_rows[expert])
        logit_pad = jnp.concatenate(
            logit_rows + [jnp.zeros((16 - experts, BAND), F32)], axis=0
        )
        z_ref[wide + pair :, lanes] = logit_pad.astype(BF)
        queries = qt_ref[:, block]
        scores = masked_scores(kv_ref, keyid_ref, sent_ref, queries, start, low, high, choose)
        probs = jnp.exp(scores - lse_ref[:, block])
        upstream = jnp.concatenate(
            [gate * value for gate, value in zip(gates, raw)], axis=1
        ).astype(BF)
        padded = jnp.concatenate([jnp.zeros_like(upstream), upstream], axis=0)
        prob_grad = nn(kv_ref[low:high, :], padded)
        mean = jnp.sum(probs * prob_grad, axis=0, keepdims=True)
        score_grad = (probs * (prob_grad - mean)).astype(BF)
        query_grad = (nn(kvt_ref[:head, low:high], score_grad) * 0.125).astype(BF)
        spread = [jnp.zeros((head, BAND), BF) for _ in range(experts)]
        for route in range(choose):
            ids = ids_ref[route : route + 1, lanes]
            piece = query_grad[:, route * BAND : (route + 1) * BAND]
            for expert in range(experts):
                spread[expert] = jnp.where(ids == expert, piece, spread[expert])
        for expert in range(experts):
            z_ref[expert * head : (expert + 1) * head, lanes] = spread[expert]
        dkv_ref[:head, low:high] += nt(queries, score_grad) * 0.125
        dkv_ref[head:, low:high] += nt(upstream, probs.astype(BF))
    z_ref[wide : wide + pair, :] = dkv_ref[...].astype(BF)


def rows_back_kernel(*refs, experts, head, peers, misc):
    (
        z_ref, gout_ref, xn_ref, wq_ref, small_ref, dh_ref, gain_two_ref, x_ref, ln_ref, place_ref,
    ) = refs[:10]
    pieces = experts // 2 + 1
    part_refs = refs[10 : 10 + peers * pieces]
    grads_ref, pair_ref, misc_ref, dx_ref, send, far_ref = refs[10 + peers * pieces :]
    length = xn_ref.shape[0]
    wide, pair = experts * head, 2 * head
    grads_ref[...] = nn(z_ref[...], xn_ref[...])
    for expert in range(experts):
        rows = slice(expert * head, (expert + 1) * head)
        pair_ref[expert * pair : expert * pair + head, :] = grads_ref[rows, :].astype(BF)
        pair_ref[expert * pair + head : (expert + 1) * pair, :] = gout_ref[rows, :]
    gain = ln_ref[0:1, :]
    total = jnp.zeros_like(gain)
    for start in range(0, length, ROWS):
        rows = slice(start, start + ROWS)
        normed_grad = tn(z_ref[:wide, rows], wq_ref[...]) + tn(z_ref[wide:, rows], small_ref[...])
        normalized, inverse = normalize(x_ref[rows, :].astype(F32))
        total = total + jnp.sum(normed_grad * normalized, axis=0, keepdims=True)
        back = normalize_back(normed_grad, normalized, inverse, gain)
        dx_ref[rows, :] = (dh_ref[rows, :] + back).astype(BF)
        send(dx_ref.at[rows, :], far_ref.at[rows, :])
    misc_ref[...] = jnp.zeros_like(misc_ref)
    misc_ref[:pair, :] = grads_ref[wide : wide + pair, :]
    misc_ref[pair : pair + 16, :] = jnp.concatenate(
        [
            grads_ref[wide + pair : wide + pair + experts, :],
            total,
            gain_two_ref[...],
            jnp.zeros((14 - experts, total.shape[1]), F32),
        ],
        axis=0,
    )
    each, share = pair // peers, misc // peers
    for k in range(peers):
        part = place_ref[0] ^ k
        for expert in range(experts):
            rows = pl.ds(expert * pair + part * each, each)
            low = expert % 2 * each
            part_refs[k * pieces + expert // 2][low : low + each, :] = pair_ref[rows, :]
        part_refs[(k + 1) * pieces - 1][...] = misc_ref[pl.ds(part * share, share), :].astype(BF)


def exchange(parts, axis):
    size = len(parts)
    return [
        lax.ppermute(parts[k], axis, [(i, i ^ k) for i in range(size)]) for k in range(1, size)
    ]


def tok_views(parts, peers):
    pieces = len(parts) // peers
    others = [exchange(parts[i::pieces], "tok") for i in range(pieces)]
    own = [View(parts[0], more=parts[1:pieces])]
    return own + [View(others[0][k], more=[o[k] for o in others[1:]]) for k in range(peers - 1)]


def bits(size):
    return size.bit_length() - 1


def swap(array, key):
    kind, stage = key
    if kind == "expert":
        size = lax.axis_size("expert")
        return lax.ppermute(array, "expert", [(i, i ^ (1 << stage)) for i in range(size)])
    dp, expert, tok = (lax.axis_size(axis) for axis in AXES)
    pairs = []
    for d in range(dp):
        for e in range(expert):
            for t in range(tok):
                other = d ^ (1 << ((stage + t) % bits(dp)))
                pairs.append(((d * expert + e) * tok + t, (other * expert + e) * tok + t))
    return lax.ppermute(array, AXES, pairs)


def place_row(key):
    kind, stage = key
    return 2 + stage if kind == "dp" else 2 + bits(lax.axis_size("dp")) + stage


class View:
    def __init__(self, array, start=0, rows=None, more=()):
        self.arrays, self.start = [array, *more], start
        self.rows = sum(a.shape[0] for a in self.arrays) if rows is None else rows
        self.array = array

    def read(self, refs, base, stride, bit, rows):
        if len(self.arrays) == 1:
            return refs[0][pl.ds(self.start + base + bit * stride, rows), :].astype(F32)
        size = self.arrays[0].shape[0]
        if stride == 0:
            at = min(base // size, len(self.arrays) - 1)
            return refs[at][base - at * size : base - at * size + rows, :].astype(F32)
        near, far = base // size, (base + stride) // size
        if near == far:
            return refs[near][pl.ds(base - near * size + bit * stride, rows), :].astype(F32)
        if rows > size:
            parts = [
                self.read(refs, base + i * size, stride, bit, size) for i in range(rows // size)
            ]
            return jnp.concatenate(parts, axis=0)
        one = refs[near][base - near * size : base - near * size + rows, :]
        two = refs[far][base + stride - far * size : base + stride - far * size + rows, :]
        return jnp.where(bit == 0, one.astype(F32), two.astype(F32))


class Job:
    def __init__(self, kind, views, key, row=0, count=0, each=0):
        self.kind, self.views, self.key, self.row = kind, views, key, row
        self.count, self.each = count, each
        rows = views[0].rows
        self.kept = rows // 2
        if kind == "add":
            self.sent = rows
        elif kind == "join":
            self.sent = 2 * rows
        elif kind == "weave":
            self.sent = 2 * rows
        elif kind in ("split", "halve"):
            self.sent = rows // 2
        else:
            self.sent = self.kept = count // 2 * each + rows - count * each
        self.keeps = kind in ("split", "pick", "halve")


def glue(line, place, jobs):
    arrays = []
    for job in jobs:
        for view in job.views:
            for array in view.arrays:
                if not any(array is a for a in arrays):
                    arrays.append(array)
    width = arrays[0].shape[1]
    offsets, total = [], 0
    for job in jobs:
        offsets.append(total)
        total += job.sent
    n = len(arrays)

    def kernel(*refs):
        place_ref, send_ref, keep_refs = refs[n], refs[n + 1], list(refs[n + 2 :])

        def ref_of(array):
            return refs[[array is a for a in arrays].index(True)]

        def added(job, base, rows, stride=0, bit=0):
            value = None
            for view in job.views:
                part = view.read([ref_of(a) for a in view.arrays], base, stride, bit, rows)
                value = part if value is None else value + part
            return value.astype(BF)

        for job, offset in zip(jobs, offsets):
            rows, bit = job.views[0].rows, place_ref[job.row]
            if job.kind == "add":
                send_ref[offset : offset + rows, :] = added(job, 0, rows)
            elif job.kind == "join":
                for view, turn in zip(job.views, (bit, 1 - bit)):
                    send_ref[pl.ds(offset + turn * rows, rows), :] = ref_of(view.array)[
                        view.start : view.start + rows, :
                    ]
            elif job.kind == "weave":
                spans = [(q * job.each, job.each) for q in range(job.count)]
                if rows > job.count * job.each:
                    spans.append((job.count * job.each, rows - job.count * job.each))
                for view, turn in zip(job.views, (bit, 1 - bit)):
                    ref = ref_of(view.array)
                    for base, size in spans:
                        send_ref[pl.ds(offset + 2 * base + turn * size, size), :] = ref[
                            view.start + base : view.start + base + size, :
                        ]
            elif job.kind == "halve":
                keep_ref, to = keep_refs.pop(0), 0
                spans = [(q * job.each, job.each) for q in range(job.count)]
                if rows > job.count * job.each:
                    spans.append((job.count * job.each, rows - job.count * job.each))
                for base, size in spans:
                    half = size // 2
                    keep_ref[to : to + half, :] = added(job, base, half, half, bit)
                    send_ref[offset + to : offset + to + half, :] = added(job, base, half, half, 1 - bit)
                    to += half
            elif job.kind == "split":
                half, keep_ref = job.sent, keep_refs.pop(0)
                keep_ref[...] = added(job, 0, half, half, bit)
                send_ref[offset : offset + half, :] = added(job, 0, half, half, 1 - bit)
            else:
                keep_ref, each = keep_refs.pop(0), job.each
                for q in range(job.count // 2):
                    keep_ref[q * each : (q + 1) * each, :] = added(job, 2 * q * each, each, each, bit)
                    send_ref[offset + q * each : offset + (q + 1) * each, :] = added(
                        job, 2 * q * each, each, each, 1 - bit
                    )
                done, base = job.count // 2 * each, job.count * each
                rest = added(job, base, rows - base)
                keep_ref[done:, :] = rest
                send_ref[offset + done : offset + job.sent, :] = rest

    outs = [sds((total, width), BF)] + [sds((job.kept, width), BF) for job in jobs if job.keeps]
    send, *keeps = line.call(kernel, arrays, outs, scalars=(place,), weight=GLUE)
    owns = []
    for job, offset in zip(jobs, offsets):
        owns.append(View(keeps.pop(0)) if job.keeps else View(send, offset, job.sent))
    return send, owns, offsets


class Chains:
    def __init__(self, line, place):
        self.line, self.place = line, place
        self.walks, self.jobs, self.done = {}, {}, {}

    def take(self, name, value):
        try:
            self.jobs[name] = self.walks[name].send(value)
        except StopIteration as end:
            self.done[name] = end.value
            del self.walks[name]

    def begin(self, name, walk):
        self.walks[name] = walk
        self.take(name, None)

    def advance(self, *names):
        names = [name for name in names if name in self.walks]
        while names:
            key = self.jobs[names[0]].key
            group = [name for name in names if self.jobs[name].key == key]
            names = [name for name in names if name not in group]
            jobs = [self.jobs[name] for name in group]
            send, owns, offsets = glue(self.line, self.place, jobs)
            if key[0] == "tok":
                others = exchange([send] * lax.axis_size("tok"), "tok")
            else:
                others = [swap(send, key)]
            for name, job, own, offset in zip(group, jobs, owns, offsets):
                self.take(name, [own] + [View(other, offset, job.sent) for other in others])

    def finish(self, name):
        while name in self.walks:
            self.advance(name)
        return self.done[name]


def chunk_walk(views, mirror, count, each):
    order = [("dp", (s + mirror) % 2) for s in range(bits(lax.axis_size("dp")))]
    experts = [("expert", s) for s in range(bits(lax.axis_size("expert")))]
    halved = []
    for key in order + experts[:-1]:
        if each < 32:
            break
        views = yield Job("halve", views, key, place_row(key), count, each)
        each //= 2
        halved.append(key)
    for key in (order + experts)[len(halved) :]:
        views = yield Job("add", views, key)
    views = [views]
    for key in reversed(halved):
        if len(views) == 1:
            views = yield Job("add", views[0], key)
        else:
            views = yield Job("weave", views, key, place_row(before), count, each)
            each *= 2
        before = key
    views = yield Job("weave", views, ("tok", 0), place_row(before), count, each)
    return views


def tail_walk(views, experts, each, mirror):
    stages = bits(lax.axis_size("dp"))
    order = [("dp", (s + mirror) % 2) for s in range(stages)]
    halves = each >> stages >= 16
    for key in order if halves else ():
        views = yield Job("halve", views, key, place_row(key), experts, each)
        each //= 2
    for stage in range(bits(experts)):
        key = ("expert", stage)
        views = yield Job("pick", views, key, place_row(key), experts >> stage, each)
    before = None
    for key in reversed(order):
        if before is None or not halves:
            views = yield Job("add", views, key)
        else:
            views = yield Job("weave", views, key, place_row(before), 1, each)
            each *= 2
        before = key
    if halves:
        views = yield Job("weave", views, ("tok", 0), place_row(before), 1, each)
    else:
        views = yield Job("add", views, ("tok", 0))
    return views


def place_part(line, place, view, turn, first, hidden, full, before):
    rows, width = view.rows, view.array.shape[1]
    many = hidden // width
    block = rows // many

    def kernel(part_ref, place_ref, _, wide_ref, send, gin_ref, gout_ref):
        part = place_ref[0] ^ turn
        for i in range(many):
            span = slice(i * block, (i + 1) * block)
            wide_ref[span, :] = part_ref[
                view.start + i * block : view.start + (i + 1) * block, :
            ].astype(F32)
            column, at = first + i * width, part * block
            to = pl.multiple_of(column + jnp.minimum(at, width - block), block)
            row = pl.multiple_of(jnp.maximum(at - width, 0), block)
            send(
                wide_ref.at[span, :],
                gout_ref.at[pl.ds(to, block), :],
                gin_ref.at[pl.ds(row, block), column : column + width],
                at < width,
            )

    _, *grads = line.call(
        kernel,
        (view.array,),
        (),
        scalars=(place,),
        scratch=(sds((rows, width), F32),),
        sent=(sds((width, full), F32), sds((full, width), F32)),
        aliased=before,
    )
    return tuple(grads)


def place_tail(line, place, views, experts, head, misc):
    peers = len(views)
    parts = [view.array for view in views]
    pair, width = 2 * head, parts[0].shape[1]
    each, share = pair // peers, misc // peers

    def last(*refs):
        part_refs, place_ref = refs[:peers], refs[peers]
        query_ref, output_ref, kv_ref, router_ref, one_ref, two_ref, pair_ref, misc_ref = refs[
            peers + 1 :
        ]
        for k, view in enumerate(views):
            part, start = place_ref[0] ^ k, view.start
            pair_ref[pl.ds(part * each, each), :] = part_refs[k][start : start + each, :].astype(F32)
            misc_ref[pl.ds(part * share, share), :] = part_refs[k][
                start + each : start + view.rows, :
            ].astype(F32)
        query_ref[0] = pair_ref[:head, :]
        output_ref[0] = pair_ref[head:, :]
        kv_ref[...] = misc_ref[:pair, :].T
        router_ref[...] = misc_ref[pair : pair + experts, :]
        one_ref[...] = misc_ref[pair + experts : pair + experts + 1, :]
        two_ref[...] = misc_ref[pair + experts + 1 : pair + experts + 2, :]

    return line.call(
        last,
        parts,
        [
            sds((1, head, width), F32),
            sds((1, head, width), F32),
            sds((width, pair), F32),
            sds((experts, width), F32),
            sds((1, width), F32),
            sds((1, width), F32),
        ],
        scalars=(place,),
        scratch=(sds((pair, width), F32), sds((misc, width), F32)),
    )


def join_all(line, arrays):
    rows, width = arrays[0].shape
    count = len(arrays)

    def kernel(*refs):
        for k in range(count):
            refs[count][k * rows : (k + 1) * rows, :] = refs[k][...]

    return line.call(kernel, arrays, [sds((count * rows, width), BF)])[0]


def body(
    tokens, out_grad, expert_ids, sentence_ids, ln_attn, w_kv, w_router, w_query, w_output, ln_ffn, w_in, w_out
):
    length, width = tokens.shape
    head = w_query.shape[2]
    pair = w_kv.shape[1]
    full = w_in.shape[1]
    experts = lax.axis_size("expert")
    peers = lax.axis_size("tok")
    choose = expert_ids.shape[1]
    tok, dp, expert = lax.axis_index("tok"), lax.axis_index("dp"), lax.axis_index("expert")
    stages = bits(lax.axis_size("dp"))
    dp_bits = [(dp >> ((s + tok) % stages)) & 1 for s in range(stages)]
    spots = jnp.stack(
        [tok, expert] + dp_bits + [(expert >> s) & 1 for s in range(bits(experts))]
    ).astype(jnp.int32)
    weights = jnp.concatenate([w_query[0].T, w_output[0]], axis=0)
    each = weights.shape[0] // peers
    weights = lax.dynamic_slice_in_dim(weights, tok * each, each, axis=0)
    pieces = exchange([weights] * experts, "expert")
    ids = expert_ids.T
    ln_one = ln_attn.reshape(1, width)
    ln_two = ln_ffn.reshape(1, width)
    line = Line()
    line.last = spots
    (
        normed, kv, kvt, gates, gt, small, sent, gains, keyid, place, x, g, ids, in_weight, out_weight, own_query,
        own_output,
    ) = line.call(
        prepare_kernel,
        (),
        [
            sds((length, width), BF),
            sds((length, pair), BF),
            sds((pair, length), BF),
            sds((choose, length), F32),
            sds((width, length), BF),
            sds((pair + 16, width), BF),
            sds((1, length), F32),
            sds((2, width), F32),
            sds((length, BAND), F32),
            sds((8, 128), jnp.int32),
        ],
        fetched=(ln_one, w_kv, w_router.T, sentence_ids, ln_two),
        numbers=(spots,),
        kept=(tokens, out_grad, ids, w_in, w_out, w_query[0].T, w_output[0]),
        room=8 << 20,
    )
    [ag] = line.call(
        upstream_kernel, (g, out_weight), [sds((length, full), BF)], room=8 << 20,
    )
    slab = join_all(line, pieces)
    slabs = [slab] + exchange([slab] * peers, "tok")
    wq, wo, qt, at, lse, gat, h, hn, hnt = line.call(
        functools.partial(attend_kernel, experts=experts, head=head, peers=peers),
        (*slabs, normed, kv, kvt, gates, x, ids, sent, gains, keyid, own_query, own_output),
        [
            sds((experts * head, width), BF),
            sds((experts * head, width), BF),
            sds((head, choose * length), BF),
            sds((head, choose * length), BF),
            sds((1, choose * length), F32),
            sds((experts * head, length), BF),
            sds((length, width), F32),
            sds((length, width), BF),
            sds((width, length), BF),
        ],
        scalars=(place,),
        scratch=(
            sds((experts * head, length), F32),
            sds((2 * head, width), BF),
        ),
        room=8 << 20,
    )

    chains = Chains(line, place)
    us, dpres, sums = [], [], []

    def ffn(last=None, mirror=0):
        rows = 2 * width // peers
        pieces = max(1, rows // PIECE)
        rows = rows // pieces
        u, dpre, *parts = line.call(
            functools.partial(ffn_kernel, first=len(us) * width, peers=peers),
            (hn, hnt, gt, ag, in_weight),
            [sds((length, width), BF)] * 2 + [sds((rows, width), BF)] * (peers * pieces),
            scalars=(place,),
            scratch=() if peers == 2 else (sds((2 * width, width), BF),),
            room=6 << 20,
        )
        us.append(u)
        dpres.append(dpre)
        for i in range(pieces):
            sums.append([parts[i]] + exchange(parts[i::pieces], "tok"))
        if last is not None:
            views = [View(same[0], more=same[1:]) for same in zip(*sums)]
            chains.begin(last, chunk_walk(views, mirror, len(sums), rows))
            sums.clear()

    misc = -(-(pair + 16) // (64 * peers)) * 64 * peers
    half = full // 2

    def hidden():
        made["dh"], made["low"], made["gain"] = line.call(
            hidden_kernel,
            (h, g, in_weight, gains, *dpres),
            [sds((length, width), F32), sds((length, width), BF), sds((1, width), F32)],
            room=6 << 20,
        )

    def heads_back():
        made["z"], made["gout"] = line.call(
            functools.partial(heads_back_kernel, experts=experts, head=head),
            (kv, kvt, gates, wo, qt, at, lse, gat, made["low"], ids, sent, keyid),
            [sds((experts * head + pair + 16, length), BF), sds((experts * head, width), BF)],
            scratch=(sds((experts * head, length), F32), sds((pair, length), F32)),
            room=6 << 20,
        )

    def rows_back():
        *parts, made["dx"] = line.call(
            functools.partial(rows_back_kernel, experts=experts, head=head, peers=peers, misc=misc),
            (made["z"], made["gout"], normed, wq, small, made["dh"], made["gain"], x, gains),
            ([sds((2 * pair // peers, width), BF)] * (experts // 2) + [sds((misc // peers, width), BF)])
            * peers,
            sent=(sds((length, width), BF),),
            scalars=(place,),
            scratch=(
                sds((experts * head + pair + 16, width), F32),
                sds((experts * pair, width), BF),
                sds((misc, width), F32),
                sds((length, width), BF),
            ),
            room=6 << 20,
        )
        chains.begin("t", tail_walk(tok_views(parts, peers), experts, pair // peers, 1))

    def out():
        _, made["output"] = line.call(
            output_kernel,
            (h, out_weight, *us),
            (),
            sent=(sds((length, width), BF),),
            scratch=(sds((length, width), BF),),
            room=6 << 20,
        )

    def place_one(name, first, turn):
        if turn == 0:
            made[name] = chains.finish(name)
            views = made[name][:1]
        else:
            views = made[name][1:]
        for view in views:
            made["both"] = place_part(
                line, place, view, turn, first, half, full, made.get("both", ())
            )
            turn += 1

    def last():
        made["t"] = place_tail(line, place, chains.finish("t"), experts, head, misc)

    made = {}
    acts = {
        "f": ffn,
        "A": lambda: ffn("a"),
        "B": lambda: ffn("b", 1),
        "n": hidden,
        "h": heads_back,
        "r": rows_back,
        "o": out,
        "P": lambda: place_one("a", 0, 0),
        "p": lambda: place_one("a", 0, 1),
        "Q": lambda: place_one("b", half, 0),
        "q": lambda: place_one("b", half, 1),
        "T": last,
    }
    for word in ORDER:
        if word in acts:
            acts[word]()
        else:
            chains.advance(*word)
    query, outp, kv_grad, router, one, two = made["t"]
    output, dx, both = made["output"], made["dx"], made["both"]
    return (
        output,
        dx,
        one.reshape(width),
        kv_grad,
        router.T,
        jnp.swapaxes(query, 1, 2),
        outp,
        two.reshape(width),
        both[0],
        both[1],
    )


def solution(mesh):
    rows = P(AXES, None)
    heads = P("expert", None, None)
    return jax.shard_map(
        body,
        mesh=mesh,
        in_specs=(rows, rows, rows, rows, P(), P(), P(), heads, heads, P(), P(), P()),
        out_specs=(rows, rows, P(), P(), P(), heads, heads, P(), P(), P()),
        check_vma=False,
    )
```

time: 141 us -> 114 us (0.81)
  waiting for transfers between devices: 49.9 us -> 33.2 us
  Pallas kernels: 53.9 us -> 47.4 us
  local copies, waits for them, and re-layouts: 7.8 us -> 1.47 us
  starting transfers between devices: 27.2 us -> 29.7 us
    ppermute x16 -> x17, waiting for transfers between devices: 47.5 us -> 28.9 us  [the longest x9 21.4 us: swap(): return lax.ppermute(array, AXES, pairs)]
    pallas_call x29 -> x36, Pallas kernels: 53.9 us -> 47.4 us  [call(): pl.pallas_call(wrapped, out_shape=outs + list(sent), in_specs=[pl.BlockSp...]
    unnamed x32 -> x6, local copies, waits for them, and re-layouts: 7.72 us -> 1.39 us
    ppermute x9 -> x17, waiting for transfers between devices: 2.38 us -> 4.31 us  [exchange(): lax.ppermute(parts[k], axis, [(i, i ^ k) for i in range(size)])]
    ppermute x9 -> x17, starting transfers between devices: 7.03 us -> 8.78 us  [exchange(): lax.ppermute(parts[k], axis, [(i, i ^ k) for i in range(size)])]
    ppermute x16 -> x17, starting transfers between devices: 20.2 us -> 20.9 us  [the longest x9 13.2 us: swap(): return lax.ppermute(array, AXES, pairs)]
  transfers between devices with their start and end apart: 25 -> 34, of which waited for: 11 -> 16; matrix products, arithmetic and copies ran while one was open for 0% -> 0% of each run, Pallas kernels for 26% -> 31%
where the time goes in v3:
time: 114 us
  Pallas kernels  47.4 us (42%)
  waiting for transfers between devices  33.2 us (29%)
  starting transfers between devices  29.7 us (26%)
  local copies, waits for them, and re-layouts  1.47 us (1%)
  between operations  1.2 us (1%)
    pallas_call x36, Pallas kernels, call(): pl.pallas_call(wrapped, out_shape=outs + list(sent), in_specs=[pl.BlockSp...  47.4 us
    ppermute x9, waiting for transfers between devices, swap(): return lax.ppermute(array, AXES, pairs)  21.4 us
    ppermute x9, starting transfers between devices, swap(): return lax.ppermute(array, AXES, pairs)  13.2 us
    ppermute x17, starting transfers between devices, exchange(): lax.ppermute(parts[k], axis, [(i, i ^ k) for i in range(size)])  8.78 us
    ppermute x8, starting transfers between devices, swap(): lax.ppermute(array, 'expert', [(i, i ^ 1 << stage) for i in range(size)])  7.72 us
    ppermute x8, waiting for transfers between devices, swap(): lax.ppermute(array, 'expert', [(i, i ^ 1 << stage) for i in range(size)])  7.44 us
    ppermute x17, waiting for transfers between devices, exchange(): lax.ppermute(parts[k], axis, [(i, i ^ k) for i in range(size)])  4.31 us
  transfers between devices with their start and end apart: 34, of which 16 were waited for; matrix products, arithmetic and copies ran while one was open for 0% of the time, Pallas kernels for 31%

profile of v3, /device:TPU:0, one launch (start us, length us, event | category | flops | bytes accessed | tf_op | source)
XLA Modules:
  0.0 113.8 jit_solution(13172877195087285331)
XLA Ops:
  0.6 0.9 fusion
  1.5 4.1 %collective-permute-start.1 = (bf16[64,512]{1,0:T(8,128)(2,1)S(1)}, bf16[64,512]{1,0:T(8,128)(2,1)S(1)}, u32[]{:S(2)}, u32[]{:S(2)}) collective-permute-start(bf16[64,512]{1,0:T(8,128)(2,1)S(1)} %fusion), channel_id=1, source_target_pairs={{0,4},{2,6},{4,0},{6,2},{1,5},{3,7},{5,1},{7,3},{8,12},{10,14},{12... | collective-permute-start | bytes 196616 | tf_op jit(solution)/shard_map/ppermute | solution.py:518
  5.6 1.6 %collective-permute-start = (bf16[64,512]{1,0:T(8,128)(2,1)S(1)}, bf16[64,512]{1,0:T(8,128)(2,1)S(1)}, u32[]{:S(2)}, u32[]{:S(2)}) collective-permute-start(bf16[64,512]{1,0:T(8,128)(2,1)S(1)} %fusion), channel_id=1, source_target_pairs={{0,2},{2,0},{4,6},{6,4},{1,3},{3,1},{5,7},{7,5},{8,10},{10,8},{12,... | collective-permute-start | bytes 196616 | tf_op jit(solution)/shard_map/ppermute | solution.py:518
  7.3 4.1 %shard_map.195 = (bf16[1024,512]{1,0:T(8,128)(2,1)S(1)}, bf16[1024,128]{1,0:T(8,128)(2,1)S(1)}, bf16[128,1024]{1,0:T(8,128)(2,1)S(1)}, f32[2,1024]{1,0:T(2,128)S...) custom-call(f32[1,512]{1,0:T(1,128)} %bitcast.25, ...), custom_call_target="tpu_custom_call" | custom-call | flops 1 | bytes 1024 | tf_op jit(solution)/shard_map/pallas_call | solution.py:147
  11.4 2.6 %shard_map.196.refs_3_ = bf16[1024,2048]{1,0:T(8,128)(2,1)S(1)} custom-call(bf16[1024,512]{1,0:T(8,128)(2,1)S(1)} %get-tuple-element.110.refs_0_.refs_1_, bf16[2048,512]{1,0:T(8,128)(2,1)S(1)} %get-tuple-element.111.refs_1_, f32[1,1024]{1,0:T(1,128)S(1)} %get-tuple-element.112.refs_2_.refs_8_.refs_10_), custom_call_target="tpu_custom_call" | custom-call | flops 1 | bytes 1024 | tf_op jit(solution)/shard_map/pallas_call | solution.py:147
  14.1 1.4 %collective-permute-done.3.refs_1_ = bf16[192,512]{1,0:T(8,128)(2,1)S(1)} collective-permute-done((bf16[192,512]{1,0:T(8,128)(2,1)S(1)}, bf16[192,512]{1,0:T(8,128)(2,1)S(1)}, u32[]{:S(2)}, u32[]{:S(2)}) %collective-permute-start.3) | collective-permute-done | bytes 196640 | tf_op jit(solution)/shard_map/ppermute | solution.py:518
  15.6 4.6 %shard_map.198 = (bf16[256,512]{1,0:T(8,128)(2,1)S(1)}, bf16[256,512]{1,0:T(8,128)(2,1)S(1)}, bf16[64,2048]{1,0:T(8,128)(2,1)S(1)}, bf16[64,2048]{1,0:T(8,128)(2...) custom-call(bf16[192,512]{1,0:T(8,128)(2,1)S(1)} %shard_map.197.refs, ...), custom_call_target="tpu_custom_call" | custom-call | flops 1 | bytes 1024 | tf_op jit(solution)/shard_map/pallas_call | solution.py:147
  20.2 3.2 %shard_map.199 = (bf16[1024,512]{1,0:T(8,128)(2,1)S(1)}, bf16[1024,512]{1,0:T(8,128)(2,1)S(1)}, bf16[256,512]{1,0:T(8,128)(2,1)S(1)}, bf16[256,512]{1,0:T(8,128)...) custom-call(bf16[1024,512]{1,0:T(8,128)(2,1)S(1)} %get-tuple-element.125.refs_0_, ...), custom_call_target="tpu_custom_call" | custom-call | flops 1 | bytes 1024 | tf_op jit(solution)/shard_map/pallas_call | solution.py:147
  23.4 0.2 collective-permute-start.4
  23.6 0.4 collective-permute-start.5
  23.9 3.4 %shard_map.200 = (bf16[1024,512]{1,0:T(8,128)(2,1)S(1)}, bf16[1024,512]{1,0:T(8,128)(2,1)S(1)}, bf16[256,512]{1,0:T(8,128)(2,1)S(1)}, bf16[256,512]{1,0:T(8,128)...) custom-call(bf16[1024,512]{1,0:T(8,128)(2,1)S(1)} %get-tuple-element.125.refs_0_, ...), custom_call_target="tpu_custom_call" | custom-call | flops 1 | bytes 1024 | tf_op jit(solution)/shard_map/pallas_call | solution.py:147
  27.3 0.2 collective-permute-start.6
  27.5 0.4 collective-permute-start.7
  27.9 3.2 %shard_map.201 = (bf16[1024,512]{1,0:T(8,128)(2,1)S(1)}, bf16[1024,512]{1,0:T(8,128)(2,1)S(1)}, bf16[256,512]{1,0:T(8,128)(2,1)S(1)}, bf16[256,512]{1,0:T(8,128)...) custom-call(bf16[1024,512]{1,0:T(8,128)(2,1)S(1)} %get-tuple-element.125.refs_0_, ...), custom_call_target="tpu_custom_call" | custom-call | flops 1 | bytes 1024 | tf_op jit(solution)/shard_map/pallas_call | solution.py:147
  31.1 0.4 shard_map.202
  31.5 1.8 %collective-permute-start.8 = (bf16[512,512]{1,0:T(8,128)(2,1)S(1)}, bf16[512,512]{1,0:T(8,128)(2,1)S(1)}, u32[]{:S(2)}, u32[]{:S(2)}) collective-permute-start(bf16[512,512]{1,0:T(8,128)(2,1)S(1)} %get-tuple-element.142.refs_6_), channel_id=1, source_target_pairs={{0,8},{1,17},{2,10},{3,19},{4,12},{5,21},{6,14},{7,23},{8,0},{9,25... | collective-permute-start | bytes 1572872 | tf_op jit(solution)/shard_map/ppermute | solution.py:545
  33.3 0.5 collective-permute-start.10
  33.8 3.2 %shard_map.203 = (bf16[1024,512]{1,0:T(8,128)(2,1)S(1)}, bf16[1024,512]{1,0:T(8,128)(2,1)S(1)}, bf16[256,512]{1,0:T(8,128)(2,1)S(1)}, bf16[256,512]{1,0:T(8,128)...) custom-call(bf16[1024,512]{1,0:T(8,128)(2,1)S(1)} %get-tuple-element.125.refs_0_, ...), custom_call_target="tpu_custom_call" | custom-call | flops 1 | bytes 1024 | tf_op jit(solution)/shard_map/pallas_call | solution.py:147
  37.1 0.5 collective-permute-start.12
  37.6 1.0 collective-permute-done.11.refs_8_
  38.6 0.4 collective-permute-done.12.refs_9_
  39.0 1.8 %collective-permute-done.8.refs_1_ = bf16[512,512]{1,0:T(8,128)(2,1)S(1)} collective-permute-done((bf16[512,512]{1,0:T(8,128)(2,1)S(1)}, bf16[512,512]{1,0:T(8,128)(2,1)S(1)}, u32[]{:S(2)}, u32[]{:S(2)}) %collective-permute-start.8) | collective-permute-done | bytes 524320 | tf_op jit(solution)/shard_map/ppermute | solution.py:545
  40.8 0.5 shard_map.204
  41.3 1.8 %collective-permute-start.13 = (bf16[768,512]{1,0:T(8,128)(2,1)S(1)}, bf16[768,512]{1,0:T(8,128)(2,1)S(1)}, u32[]{:S(2)}, u32[]{:S(2)}) collective-permute-start(bf16[768,512]{1,0:T(8,128)(2,1)S(1)} %get-tuple-element.153), channel_id=1, source_target_pairs={{0,16},{1,9},{2,18},{3,11},{4,20},{5,13},{6,22},{7,15},{8,24},{9,1... | collective-permute-start | bytes 2359304 | tf_op jit(solution)/shard_map/ppermute | solution.py:545
  43.1 3.2 %shard_map.205 = (f32[1024,512]{1,0:T(8,128)S(1)}, bf16[1024,512]{1,0:T(8,128)(2,1)S(1)}, f32[1,512]{1,0:T(1,128)S(1)}) custom-call(f32[1024,512]{1,0:T(8,128)S(1)} %get-tuple-element.124.refs_0_, bf16[1024,512]{1,0:T(8,128)(2,1)S(1)} %get-tuple-element.110.refs_0_.refs_1_, bf16[512,2048]{1,0:T(8,128)(2,1)S(1)} %get-tuple-element.128.refs_4_.refs_2_, ...), custom_call_target="tpu_custom_call" | custom-call | flops 1 | bytes 1024 | tf_op jit(solution)/shard_map/pallas_call | solution.py:147
  46.3 4.3 %shard_map.206 = (bf16[400,1024]{1,0:T(8,128)(2,1)S(1)}, bf16[256,512]{1,0:T(8,128)(2,1)S(1)}) custom-call(bf16[1024,128]{1,0:T(8,128)(2,1)S(1)} %get-tuple-element.114.refs_3_.refs_0_, bf16[128,1024]{1,0:T(8,128)(2,1)S(1)} %get-tuple-element.115.refs_4_.refs_1_, f32[2,1024]{1,0:T(2,128)S(1)} %get-tuple-element.116.refs_5_.refs_2_, ...), custom_call_target="tpu_custom_call" | custom-call | flops 1 | bytes 1024 | tf_op jit(solution)/shard_map/pallas_call | solution.py:147
  50.6 2.7 %collective-permute-done.13.refs_1_ = bf16[768,512]{1,0:T(8,128)(2,1)S(1)} collective-permute-done((bf16[768,512]{1,0:T(8,128)(2,1)S(1)}, bf16[768,512]{1,0:T(8,128)(2,1)S(1)}, u32[]{:S(2)}, u32[]{:S(2)}) %collective-permute-start.13) | collective-permute-done | bytes 786464 | tf_op jit(solution)/shard_map/ppermute | solution.py:545
  53.4 1.0 collective-permute-start.18
  54.4 0.2 shard_map.208
  54.6 1.6 %collective-permute-start.14 = (bf16[256,512]{1,0:T(8,128)(2,1)S(1)}, bf16[256,512]{1,0:T(8,128)(2,1)S(1)}, u32[]{:S(2)}, u32[]{:S(2)}) collective-permute-start(bf16[256,512]{1,0:T(8,128)(2,1)S(1)} %get-tuple-element.168.refs_10_), channel_id=1, source_target_pairs={{0,8},{1,17},{2,10},{3,19},{4,12},{5,21},{6,14},{7,23},{8,0},{9,25... | collective-permute-start | bytes 786440 | tf_op jit(solution)/shard_map/ppermute | solution.py:545
  56.1 3.0 %shard_map.209 = (bf16[128,512]{1,0:T(8,128)(2,1)S(1)}, bf16[128,512]{1,0:T(8,128)(2,1)S(1)}, bf16[128,512]{1,0:T(8,128)(2,1)S(1)}, bf16[128,512]{1,0:T(8,128)(2...) custom-call(bf16[400,1024]{1,0:T(8,128)(2,1)S(1)} %get-tuple-element.169.refs_0_, ...), custom_call_target="tpu_custom_call" | custom-call | flops 1 | bytes 1024 | tf_op jit(solution)/shard_map/pallas_call | solution.py:147
  59.1 0.5 collective-permute-start.16
  59.8 3.6 %collective-permute-start.20 = (bf16[128,512]{1,0:T(8,128)(2,1)S(1)}, bf16[128,512]{1,0:T(8,128)(2,1)S(1)}, u32[]{:S(2)}, u32[]{:S(2)}) collective-permute-start(bf16[128,512]{1,0:T(8,128)(2,1)S(1)} %shard_map.210.refs_7_.refs_0_), channel_id=1, source_target_pairs={{0,4},{2,6},{4,0},{6,2},{1,5},{3,7},{5,1},{7,3},{8,12},{10,14},{12... | collective-permute-start | bytes 393224 | tf_op jit(solution)/shard_map/ppermute | solution.py:537
  63.3 0.1 shard_map.211
  63.5 1.6 %collective-permute-start.21 = (bf16[192,512]{1,0:T(8,128)(2,1)S(1)}, bf16[192,512]{1,0:T(8,128)(2,1)S(1)}, u32[]{:S(2)}, u32[]{:S(2)}) collective-permute-start(bf16[192,512]{1,0:T(8,128)(2,1)S(1)} %get-tuple-element.180.refs_3_), channel_id=1, source_target_pairs={{0,16},{1,9},{2,18},{3,11},{4,20},{5,13},{6,22},{7,15},{8,24},{9,1... | collective-permute-start | bytes 589832 | tf_op jit(solution)/shard_map/ppermute | solution.py:545
  65.2 4.0 %collective-permute-done.21.refs_1_ = bf16[192,512]{1,0:T(8,128)(2,1)S(1)} collective-permute-done((bf16[192,512]{1,0:T(8,128)(2,1)S(1)}, bf16[192,512]{1,0:T(8,128)(2,1)S(1)}, u32[]{:S(2)}, u32[]{:S(2)}) %collective-permute-start.21) | collective-permute-done | bytes 196640 | tf_op jit(solution)/shard_map/ppermute | solution.py:545
  69.3 0.6 collective-permute-start.24
  69.9 0.4 collective-permute-done.20.refs_1_
  70.3 0.3 collective-permute-start.23
  70.6 1.6 %collective-permute-done.19.refs_1_ = bf16[128,512]{1,0:T(8,128)(2,1)S(1)} collective-permute-done((bf16[128,512]{1,0:T(8,128)(2,1)S(1)}, bf16[128,512]{1,0:T(8,128)(2,1)S(1)}, u32[]{:S(2)}, u32[]{:S(2)}) %collective-permute-start.19) | collective-permute-done | bytes 131104 | tf_op jit(solution)/shard_map/ppermute | solution.py:537
  72.2 0.9 collective-permute-start.22
  73.1 0.7 copy-done.1
  73.8 3.1 %shard_map.216 = (f32[8,128]{1,0:T(8,128)S(1)}, bf16[1024,512]{1,0:T(8,128)(2,1)}) custom-call(f32[1024,512]{1,0:T(8,128)S(1)} %get-tuple-element.124.refs_0_, bf16[2048,512]{1,0:T(8,128)(2,1)S(1)} %copy-done.1, bf16[1024,512]{1,0:T(8,128)(2,1)S(1)} %get-tuple-element.130.refs_2_, bf16[1024,512]{1,0:T(8,128)(2,1)S(1)} %get-tuple-element.132.refs_3_, ...), custom_call_target="tpu_custom_call" | custom-call | flops 1 | bytes 1024 | tf_op jit(solution)/shard_map/pallas_call | solution.py:147
  77.0 0.2 collective-permute-start.26
  77.3 1.6 %collective-permute-start.28 = (bf16[256,512]{1,0:T(8,128)(2,1)S(1)}, bf16[256,512]{1,0:T(8,128)(2,1)S(1)}, u32[]{:S(2)}, u32[]{:S(2)}) collective-permute-start(bf16[256,512]{1,0:T(8,128)(2,1)S(1)} %shard_map.218.refs_3_.refs_0_), channel_id=1, source_target_pairs={{0,16},{1,9},{2,18},{3,11},{4,20},{5,13},{6,22},{7,15},{8,24},{9,1... | collective-permute-start | bytes 786440 | tf_op jit(solution)/shard_map/ppermute | solution.py:545
  78.9 1.8 %collective-permute-done.22.refs_1_ = bf16[128,512]{1,0:T(8,128)(2,1)S(1)} collective-permute-done((bf16[128,512]{1,0:T(8,128)(2,1)S(1)}, bf16[128,512]{1,0:T(8,128)(2,1)S(1)}, u32[]{:S(2)}, u32[]{:S(2)}) %collective-permute-start.22) | collective-permute-done | bytes 131104 | tf_op jit(solution)/shard_map/ppermute | solution.py:537
  80.8 0.1 collective-permute-start.25
  80.9 1.1 collective-permute-done.26.refs_1_
  82.0 1.6 %collective-permute-start.27 = (bf16[48,512]{1,0:T(8,128)(2,1)S(1)}, bf16[48,512]{1,0:T(8,128)(2,1)S(1)}, u32[]{:S(2)}, u32[]{:S(2)}) collective-permute-start(bf16[48,512]{1,0:T(8,128)(2,1)S(1)} %get-tuple-element.192.refs_3_), channel_id=1, source_target_pairs={{0,4},{2,6},{4,0},{6,2},{1,5},{3,7},{5,1},{7,3},{8,12},{10,14},{12... | collective-permute-start | bytes 147464 | tf_op jit(solution)/shard_map/ppermute | solution.py:537
  83.6 0.2 collective-permute-done.28.refs_1_
  83.9 1.2 %collective-permute-start.30 = (bf16[512,512]{1,0:T(8,128)(2,1)S(1)}, bf16[512,512]{1,0:T(8,128)(2,1)S(1)}, u32[]{:S(2)}, u32[]{:S(2)}) collective-permute-start(bf16[512,512]{1,0:T(8,128)(2,1)S(1)} %shard_map.221.refs_5_.refs_0_), channel_id=1, source_target_pairs={{0,8},{1,17},{2,10},{3,19},{4,12},{5,21},{6,14},{7,23},{8,0},{9,25... | collective-permute-start | bytes 1572872 | tf_op jit(solution)/shard_map/ppermute | solution.py:545
  85.0 2.5 %collective-permute-done.27.refs_3_ = bf16[48,512]{1,0:T(8,128)(2,1)S(1)} collective-permute-done((bf16[48,512]{1,0:T(8,128)(2,1)S(1)}, bf16[48,512]{1,0:T(8,128)(2,1)S(1)}, u32[]{:S(2)}, u32[]{:S(2)}) %collective-permute-start.27) | collective-permute-done | bytes 49184 | tf_op jit(solution)/shard_map/ppermute | solution.py:537
  87.7 1.5 %collective-permute-start.29 = (bf16[304,512]{1,0:T(8,128)(2,1)S(1)}, bf16[304,512]{1,0:T(8,128)(2,1)S(1)}, u32[]{:S(2)}, u32[]{:S(2)}) collective-permute-start(bf16[304,512]{1,0:T(8,128)(2,1)S(1)} %shard_map.222.refs_3_.refs_0_), channel_id=1, source_target_pairs={{0,8},{1,17},{2,10},{3,19},{4,12},{5,21},{6,14},{7,23},{8,0},{9,25... | collective-permute-start | bytes 933896 | tf_op jit(solution)/shard_map/ppermute | solution.py:545
  89.2 3.9 %collective-permute-done.30.refs_1_ = bf16[512,512]{1,0:T(8,128)(2,1)S(1)} collective-permute-done((bf16[512,512]{1,0:T(8,128)(2,1)S(1)}, bf16[512,512]{1,0:T(8,128)(2,1)S(1)}, u32[]{:S(2)}, u32[]{:S(2)}) %collective-permute-start.30) | collective-permute-done | bytes 524320 | tf_op jit(solution)/shard_map/ppermute | solution.py:545
  93.3 1.5 %shard_map.224 = (f32[8,128]{1,0:T(8,128)S(1)}, f32[512,2048]{1,0:T(8,128)}, f32[2048,512]{1,0:T(8,128)}) custom-call(bf16[1024,512]{1,0:T(8,128)(2,1)S(1)} %shard_map.223.refs_0_.refs_2_, s32[8,128]{1,0:T(8,128)S(1)} %get-tuple-element.123.refs_13_.refs_5_.refs_8_.refs_10_.refs_2_.refs_9_.refs_6_.refs_4_.refs_1_, ...), custom_call_target="tpu_custom_call" | custom-call | flops 1 | bytes 1024 | tf_op jit(solution)/shard_map/pallas_call | solution.py:147
  94.8 1.7 %collective-permute-done.29.refs_1_ = bf16[304,512]{1,0:T(8,128)(2,1)S(1)} collective-permute-done((bf16[304,512]{1,0:T(8,128)(2,1)S(1)}, bf16[304,512]{1,0:T(8,128)(2,1)S(1)}, u32[]{:S(2)}, u32[]{:S(2)}) %collective-permute-start.29) | collective-permute-done | bytes 311328 | tf_op jit(solution)/shard_map/ppermute | solution.py:545
  96.5 1.6 %collective-permute-start.31 = (bf16[608,512]{1,0:T(8,128)(2,1)S(1)}, bf16[608,512]{1,0:T(8,128)(2,1)S(1)}, u32[]{:S(2)}, u32[]{:S(2)}) collective-permute-start(bf16[608,512]{1,0:T(8,128)(2,1)S(1)} %shard_map.225.refs_2_.refs_0_), channel_id=1, source_target_pairs={{0,16},{1,9},{2,18},{3,11},{4,20},{5,13},{6,22},{7,15},{8,24},{9,1... | collective-permute-start | bytes 1867784 | tf_op jit(solution)/shard_map/ppermute | solution.py:545
  98.1 1.5 %shard_map.226 = (f32[8,128]{1,0:T(8,128)S(1)}, f32[512,2048]{1,0:T(8,128)}, f32[2048,512]{1,0:T(8,128)}) custom-call(bf16[1024,512]{1,0:T(8,128)(2,1)S(1)} %collective-permute-done.32.refs_0_, s32[8,128]{1,0:T(8,128)S(1)} %get-tuple-element.123.refs_13_.refs_5_.refs_8_.refs_10_.refs_2_.refs_9_.refs_6_.refs_4_.refs_1_, ...), custom_call_target="tpu_custom_call", output_to_operand_aliasing={{1}: (3, {}), {2}: (4, {})} | custom-call | flops 1 | bytes 1024 | tf_op jit(solution)/shard_map/pallas_call | solution.py:147
  99.6 7.2 %collective-permute-done.31.refs_1_ = bf16[608,512]{1,0:T(8,128)(2,1)S(1)} collective-permute-done((bf16[608,512]{1,0:T(8,128)(2,1)S(1)}, bf16[608,512]{1,0:T(8,128)(2,1)S(1)}, u32[]{:S(2)}, u32[]{:S(2)}) %collective-permute-start.31) | collective-permute-done | bytes 622624 | tf_op jit(solution)/shard_map/ppermute | solution.py:545
  107.0 1.5 %shard_map.228 = (f32[8,128]{1,0:T(8,128)S(1)}, f32[512,2048]{1,0:T(8,128)}, f32[2048,512]{1,0:T(8,128)}) custom-call(bf16[1216,512]{1,0:T(8,128)(2,1)S(1)} %shard_map.227.refs_0_.refs_2_, s32[8,128]{1,0:T(8,128)S(1)} %get-tuple-element.123.refs_13_.refs_5_.refs_8_.refs_10_.refs_2_.refs_9_.refs_6_.refs_4_.refs_1_, ...), custom_call_target="tpu_custom_call", output_to_operand_aliasing={{1}: (3, {}), {2}: (4, {})} | custom-call | flops 1 | bytes 1024 | tf_op jit(solution)/shard_map/pallas_call | solution.py:147
  108.5 1.5 %collective-permute-done.33.refs_1_.refs_0_ = bf16[1216,512]{1,0:T(8,128)(2,1)S(1)} collective-permute-done((bf16[1216,512]{1,0:T(8,128)(2,1)S(1)}, bf16[1216,512]{1,0:T(8,128)(2,1)S(1)}, u32[]{:S(2)}, u32[]{:S(2)}) %collective-permute-start.33) | collective-permute-done | bytes 1245216 | tf_op jit(solution)/shard_map/ppermute | solution.py:518
  110.0 0.9 shard_map.229
  110.9 0.7 copy-done.2
  111.6 2.0 %shard_map.230 = (f32[8,128]{1,0:T(8,128)}, f32[512,2048]{1,0:T(8,128)}, f32[2048,512]{1,0:T(8,128)}) custom-call(bf16[1216,512]{1,0:T(8,128)(2,1)S(1)} %collective-permute-done.33.refs_1_.refs_0_, ...), custom_call_target="tpu_custom_call", output_to_operand_aliasing={{1}: (3, {}), {2}: (4, {})} | custom-call | flops 1 | bytes 1024 | tf_op jit(solution)/shard_map/pallas_call | solution.py:147
  (48 shorter events, 1.7 us)
Async XLA Ops:
  1.5 12.5 %collective-permute-start.1 = (bf16[64,512]{1,0:T(8,128)(2,1)S(1)}, bf16[64,512]{1,0:T(8,128)(2,1)S(1)}, u32[]{:S(2)}, u32[]{:S(2)}) collective-permute-start(bf16[64,512]{1,0:T(8,128)(2,1)S(1)} %fusion), channel_id=1, source_target_pairs={{0,4},{2,6},{4,0},{6,2},{1,5},{3,7},{5,1},{7,3},{8,12},{10,14},{12... | collective-permute-start | bytes 196616 | tf_op jit(solution)/shard_map/ppermute | solution.py:518
  5.6 8.4 %collective-permute-start = (bf16[64,512]{1,0:T(8,128)(2,1)S(1)}, bf16[64,512]{1,0:T(8,128)(2,1)S(1)}, u32[]{:S(2)}, u32[]{:S(2)}) collective-permute-start(bf16[64,512]{1,0:T(8,128)(2,1)S(1)} %fusion), channel_id=1, source_target_pairs={{0,2},{2,0},{4,6},{6,4},{1,3},{3,1},{5,7},{7,5},{8,10},{10,8},{12,... | collective-permute-start | bytes 196616 | tf_op jit(solution)/shard_map/ppermute | solution.py:518
  7.2 6.8 %collective-permute-start.2 = (bf16[64,512]{1,0:T(8,128)(2,1)S(1)}, bf16[64,512]{1,0:T(8,128)(2,1)S(1)}, u32[]{:S(2)}, u32[]{:S(2)}) collective-permute-start(bf16[64,512]{1,0:T(8,128)(2,1)S(1)} %fusion), channel_id=1, source_target_pairs={{0,6},{2,4},{4,2},{6,0},{1,7},{3,5},{5,3},{7,1},{8,14},{10,12},{12... | collective-permute-start | bytes 196616 | tf_op jit(solution)/shard_map/ppermute | solution.py:518
  11.4 2.7 %copy-start = (bf16[2048,512]{1,0:T(8,128)(2,1)}, bf16[2048,512]{1,0:T(8,128)(2,1)S(1)}, u32[]{:S(2)}) copy-start(bf16[2048,512]{1,0:T(8,128)(2,1)S(1)} %get-tuple-element.111.refs_1_) | copy-start | bytes 6291460
  14.1 1.5 %collective-permute-start.3 = (bf16[192,512]{1,0:T(8,128)(2,1)S(1)}, bf16[192,512]{1,0:T(8,128)(2,1)S(1)}, u32[]{:S(2)}, u32[]{:S(2)}) collective-permute-start(bf16[192,512]{1,0:T(8,128)(2,1)S(1)} %shard_map.197.refs_0_.refs_14_), channel_id=1, source_target_pairs={{0,1},{1,0},{2,3},{3,2},{4,5},{5,4},{6,7},{7,6},{8,9},{9,8},{10,11... | collective-permute-start | bytes 589832 | tf_op jit(solution)/shard_map/ppermute | solution.py:518
  23.4 7.7 %collective-permute-start.4 = (bf16[256,512]{1,0:T(8,128)(2,1)S(1)}, bf16[256,512]{1,0:T(8,128)(2,1)S(1)}, u32[]{:S(2)}, u32[]{:S(2)}) collective-permute-start(bf16[256,512]{1,0:T(8,128)(2,1)S(1)} %get-tuple-element.137), channel_id=1, source_target_pairs={{0,1},{1,0},{2,3},{3,2},{4,5},{5,4},{6,7},{7,6},{8,9},{9,8},{10,11... | collective-permute-start | bytes 786440 | tf_op jit(solution)/shard_map/ppermute | solution.py:518
  23.6 7.5 %collective-permute-start.5 = (bf16[256,512]{1,0:T(8,128)(2,1)S(1)}, bf16[256,512]{1,0:T(8,128)(2,1)S(1)}, u32[]{:S(2)}, u32[]{:S(2)}) collective-permute-start(bf16[256,512]{1,0:T(8,128)(2,1)S(1)} %get-tuple-element.138), channel_id=1, source_target_pairs={{0,1},{1,0},{2,3},{3,2},{4,5},{5,4},{6,7},{7,6},{8,9},{9,8},{10,11... | collective-permute-start | bytes 786440 | tf_op jit(solution)/shard_map/ppermute | solution.py:518
  27.3 3.8 %collective-permute-start.6 = (bf16[256,512]{1,0:T(8,128)(2,1)S(1)}, bf16[256,512]{1,0:T(8,128)(2,1)S(1)}, u32[]{:S(2)}, u32[]{:S(2)}) collective-permute-start(bf16[256,512]{1,0:T(8,128)(2,1)S(1)} %get-tuple-element.139), channel_id=1, source_target_pairs={{0,1},{1,0},{2,3},{3,2},{4,5},{5,4},{6,7},{7,6},{8,9},{9,8},{10,11... | collective-permute-start | bytes 786440 | tf_op jit(solution)/shard_map/ppermute | solution.py:518
  27.5 3.6 %collective-permute-start.7 = (bf16[256,512]{1,0:T(8,128)(2,1)S(1)}, bf16[256,512]{1,0:T(8,128)(2,1)S(1)}, u32[]{:S(2)}, u32[]{:S(2)}) collective-permute-start(bf16[256,512]{1,0:T(8,128)(2,1)S(1)} %get-tuple-element.140), channel_id=1, source_target_pairs={{0,1},{1,0},{2,3},{3,2},{4,5},{5,4},{6,7},{7,6},{8,9},{9,8},{10,11... | collective-permute-start | bytes 786440 | tf_op jit(solution)/shard_map/ppermute | solution.py:518
  31.5 9.2 %collective-permute-start.8 = (bf16[512,512]{1,0:T(8,128)(2,1)S(1)}, bf16[512,512]{1,0:T(8,128)(2,1)S(1)}, u32[]{:S(2)}, u32[]{:S(2)}) collective-permute-start(bf16[512,512]{1,0:T(8,128)(2,1)S(1)} %get-tuple-element.142.refs_6_), channel_id=1, source_target_pairs={{0,8},{1,17},{2,10},{3,19},{4,12},{5,21},{6,14},{7,23},{8,0},{9,25... | collective-permute-start | bytes 1572872 | tf_op jit(solution)/shard_map/ppermute | solution.py:545
  33.3 4.3 %collective-permute-start.9 = (bf16[256,512]{1,0:T(8,128)(2,1)S(1)}, bf16[256,512]{1,0:T(8,128)(2,1)S(1)}, u32[]{:S(2)}, u32[]{:S(2)}) collective-permute-start(bf16[256,512]{1,0:T(8,128)(2,1)S(1)} %get-tuple-element.148), channel_id=1, source_target_pairs={{0,1},{1,0},{2,3},{3,2},{4,5},{5,4},{6,7},{7,6},{8,9},{9,8},{10,11... | collective-permute-start | bytes 786440 | tf_op jit(solution)/shard_map/ppermute | solution.py:518
  33.3 4.3 %collective-permute-start.10 = (bf16[256,512]{1,0:T(8,128)(2,1)S(1)}, bf16[256,512]{1,0:T(8,128)(2,1)S(1)}, u32[]{:S(2)}, u32[]{:S(2)}) collective-permute-start(bf16[256,512]{1,0:T(8,128)(2,1)S(1)} %get-tuple-element.149), channel_id=1, source_target_pairs={{0,1},{1,0},{2,3},{3,2},{4,5},{5,4},{6,7},{7,6},{8,9},{9,8},{10,11... | collective-permute-start | bytes 786440 | tf_op jit(solution)/shard_map/ppermute | solution.py:518
  37.0 1.6 %collective-permute-start.11 = (bf16[256,512]{1,0:T(8,128)(2,1)S(1)}, bf16[256,512]{1,0:T(8,128)(2,1)S(1)}, u32[]{:S(2)}, u32[]{:S(2)}) collective-permute-start(bf16[256,512]{1,0:T(8,128)(2,1)S(1)} %get-tuple-element.150), channel_id=1, source_target_pairs={{0,1},{1,0},{2,3},{3,2},{4,5},{5,4},{6,7},{7,6},{8,9},{9,8},{10,11... | collective-permute-start | bytes 786440 | tf_op jit(solution)/shard_map/ppermute | solution.py:518
  37.1 1.9 %collective-permute-start.12 = (bf16[256,512]{1,0:T(8,128)(2,1)S(1)}, bf16[256,512]{1,0:T(8,128)(2,1)S(1)}, u32[]{:S(2)}, u32[]{:S(2)}) collective-permute-start(bf16[256,512]{1,0:T(8,128)(2,1)S(1)} %get-tuple-element.151), channel_id=1, source_target_pairs={{0,1},{1,0},{2,3},{3,2},{4,5},{5,4},{6,7},{7,6},{8,9},{9,8},{10,11... | collective-permute-start | bytes 786440 | tf_op jit(solution)/shard_map/ppermute | solution.py:518
  41.3 12.1 %collective-permute-start.13 = (bf16[768,512]{1,0:T(8,128)(2,1)S(1)}, bf16[768,512]{1,0:T(8,128)(2,1)S(1)}, u32[]{:S(2)}, u32[]{:S(2)}) collective-permute-start(bf16[768,512]{1,0:T(8,128)(2,1)S(1)} %get-tuple-element.153), channel_id=1, source_target_pairs={{0,16},{1,9},{2,18},{3,11},{4,20},{5,13},{6,22},{7,15},{8,24},{9,1... | collective-permute-start | bytes 2359304 | tf_op jit(solution)/shard_map/ppermute | solution.py:545
  53.4 6.3 %collective-permute-start.18 = (bf16[128,512]{1,0:T(8,128)(2,1)S(1)}, bf16[128,512]{1,0:T(8,128)(2,1)S(1)}, u32[]{:S(2)}, u32[]{:S(2)}) collective-permute-start(bf16[128,512]{1,0:T(8,128)(2,1)S(1)} %get-tuple-element.166.refs_3_), channel_id=1, source_target_pairs={{0,2},{2,0},{4,6},{6,4},{1,3},{3,1},{5,7},{7,5},{8,10},{10,8},{12,... | collective-permute-start | bytes 393224 | tf_op jit(solution)/shard_map/ppermute | solution.py:537
  54.6 10.5 %collective-permute-start.14 = (bf16[256,512]{1,0:T(8,128)(2,1)S(1)}, bf16[256,512]{1,0:T(8,128)(2,1)S(1)}, u32[]{:S(2)}, u32[]{:S(2)}) collective-permute-start(bf16[256,512]{1,0:T(8,128)(2,1)S(1)} %get-tuple-element.168.refs_10_), channel_id=1, source_target_pairs={{0,8},{1,17},{2,10},{3,19},{4,12},{5,21},{6,14},{7,23},{8,0},{9,25... | collective-permute-start | bytes 786440 | tf_op jit(solution)/shard_map/ppermute | solution.py:545
  59.1 4.3 %collective-permute-start.15 = (bf16[128,512]{1,0:T(8,128)(2,1)S(1)}, bf16[128,512]{1,0:T(8,128)(2,1)S(1)}, u32[]{:S(2)}, u32[]{:S(2)}) collective-permute-start(bf16[128,512]{1,0:T(8,128)(2,1)S(1)} %get-tuple-element.176), channel_id=1, source_target_pairs={{0,1},{1,0},{2,3},{3,2},{4,5},{5,4},{6,7},{7,6},{8,9},{9,8},{10,11... | collective-permute-start | bytes 393224 | tf_op jit(solution)/shard_map/ppermute | solution.py:518
  59.1 4.2 %collective-permute-start.16 = (bf16[128,512]{1,0:T(8,128)(2,1)S(1)}, bf16[128,512]{1,0:T(8,128)(2,1)S(1)}, u32[]{:S(2)}, u32[]{:S(2)}) collective-permute-start(bf16[128,512]{1,0:T(8,128)(2,1)S(1)} %get-tuple-element.177), channel_id=1, source_target_pairs={{0,1},{1,0},{2,3},{3,2},{4,5},{5,4},{6,7},{7,6},{8,9},{9,8},{10,11... | collective-permute-start | bytes 393224 | tf_op jit(solution)/shard_map/ppermute | solution.py:518
  59.6 3.7 %collective-permute-start.17 = (bf16[128,512]{1,0:T(8,128)(2,1)S(1)}, bf16[128,512]{1,0:T(8,128)(2,1)S(1)}, u32[]{:S(2)}, u32[]{:S(2)}) collective-permute-start(bf16[128,512]{1,0:T(8,128)(2,1)S(1)} %get-tuple-element.178), channel_id=1, source_target_pairs={{0,1},{1,0},{2,3},{3,2},{4,5},{5,4},{6,7},{7,6},{8,9},{9,8},{10,11... | collective-permute-start | bytes 393224 | tf_op jit(solution)/shard_map/ppermute | solution.py:518
  59.8 10.5 %collective-permute-start.20 = (bf16[128,512]{1,0:T(8,128)(2,1)S(1)}, bf16[128,512]{1,0:T(8,128)(2,1)S(1)}, u32[]{:S(2)}, u32[]{:S(2)}) collective-permute-start(bf16[128,512]{1,0:T(8,128)(2,1)S(1)} %shard_map.210.refs_7_.refs_0_), channel_id=1, source_target_pairs={{0,4},{2,6},{4,0},{6,2},{1,5},{3,7},{5,1},{7,3},{8,12},{10,14},{12... | collective-permute-start | bytes 393224 | tf_op jit(solution)/shard_map/ppermute | solution.py:537
  63.5 5.7 %collective-permute-start.21 = (bf16[192,512]{1,0:T(8,128)(2,1)S(1)}, bf16[192,512]{1,0:T(8,128)(2,1)S(1)}, u32[]{:S(2)}, u32[]{:S(2)}) collective-permute-start(bf16[192,512]{1,0:T(8,128)(2,1)S(1)} %get-tuple-element.180.refs_3_), channel_id=1, source_target_pairs={{0,16},{1,9},{2,18},{3,11},{4,20},{5,13},{6,22},{7,15},{8,24},{9,1... | collective-permute-start | bytes 589832 | tf_op jit(solution)/shard_map/ppermute | solution.py:545
  65.2 7.0 %collective-permute-start.19 = (bf16[128,512]{1,0:T(8,128)(2,1)S(1)}, bf16[128,512]{1,0:T(8,128)(2,1)S(1)}, u32[]{:S(2)}, u32[]{:S(2)}) collective-permute-start(bf16[128,512]{1,0:T(8,128)(2,1)S(1)} %get-tuple-element.182.refs_3_), channel_id=1, source_target_pairs={{0,2},{2,0},{4,6},{6,4},{1,3},{3,1},{5,7},{7,5},{8,10},{10,8},{12,... | collective-permute-start | bytes 393224 | tf_op jit(solution)/shard_map/ppermute | solution.py:537
  69.3 7.7 %collective-permute-start.24 = (bf16[96,512]{1,0:T(8,128)(2,1)S(1)}, bf16[96,512]{1,0:T(8,128)(2,1)S(1)}, u32[]{:S(2)}, u32[]{:S(2)}) collective-permute-start(bf16[96,512]{1,0:T(8,128)(2,1)S(1)} %get-tuple-element.184.refs_3_), channel_id=1, source_target_pairs={{0,8},{1,17},{2,10},{3,19},{4,12},{5,21},{6,14},{7,23},{8,0},{9,25... | collective-permute-start | bytes 294920 | tf_op jit(solution)/shard_map/ppermute | solution.py:545
  70.3 7.0 %collective-permute-start.23 = (bf16[128,512]{1,0:T(8,128)(2,1)S(1)}, bf16[128,512]{1,0:T(8,128)(2,1)S(1)}, u32[]{:S(2)}, u32[]{:S(2)}) collective-permute-start(bf16[128,512]{1,0:T(8,128)(2,1)S(1)} %shard_map.214.refs_3_.refs_0_), channel_id=1, source_target_pairs={{0,2},{2,0},{4,6},{6,4},{1,3},{3,1},{5,7},{7,5},{8,10},{10,8},{12,... | collective-permute-start | bytes 393224 | tf_op jit(solution)/shard_map/ppermute | solution.py:537
  72.2 1.6 %copy-start.1 = (bf16[2048,512]{1,0:T(8,128)(2,1)S(1)}, bf16[2048,512]{1,0:T(8,128)(2,1)}, u32[]{:S(2)}) copy-start(bf16[2048,512]{1,0:T(8,128)(2,1)} %copy-done) | copy-start | bytes 6291460
  72.2 8.5 %collective-permute-start.22 = (bf16[128,512]{1,0:T(8,128)(2,1)S(1)}, bf16[128,512]{1,0:T(8,128)(2,1)S(1)}, u32[]{:S(2)}, u32[]{:S(2)}) collective-permute-start(bf16[128,512]{1,0:T(8,128)(2,1)S(1)} %shard_map.215.refs_6_.refs_0_), channel_id=1, source_target_pairs={{0,4},{2,6},{4,0},{6,2},{1,5},{3,7},{5,1},{7,3},{8,12},{10,14},{12... | collective-permute-start | bytes 393224 | tf_op jit(solution)/shard_map/ppermute | solution.py:537
  77.0 4.9 %collective-permute-start.26 = (bf16[64,512]{1,0:T(8,128)(2,1)S(1)}, bf16[64,512]{1,0:T(8,128)(2,1)S(1)}, u32[]{:S(2)}, u32[]{:S(2)}) collective-permute-start(bf16[64,512]{1,0:T(8,128)(2,1)S(1)} %get-tuple-element.189.refs_3_), channel_id=1, source_target_pairs={{0,2},{2,0},{4,6},{6,4},{1,3},{3,1},{5,7},{7,5},{8,10},{10,8},{12,... | collective-permute-start | bytes 196616 | tf_op jit(solution)/shard_map/ppermute | solution.py:537
  77.3 6.4 %collective-permute-start.28 = (bf16[256,512]{1,0:T(8,128)(2,1)S(1)}, bf16[256,512]{1,0:T(8,128)(2,1)S(1)}, u32[]{:S(2)}, u32[]{:S(2)}) collective-permute-start(bf16[256,512]{1,0:T(8,128)(2,1)S(1)} %shard_map.218.refs_3_.refs_0_), channel_id=1, source_target_pairs={{0,16},{1,9},{2,18},{3,11},{4,20},{5,13},{6,22},{7,15},{8,24},{9,1... | collective-permute-start | bytes 786440 | tf_op jit(solution)/shard_map/ppermute | solution.py:545
  80.8 6.8 %collective-permute-start.25 = (bf16[128,512]{1,0:T(8,128)(2,1)S(1)}, bf16[128,512]{1,0:T(8,128)(2,1)S(1)}, u32[]{:S(2)}, u32[]{:S(2)}) collective-permute-start(bf16[128,512]{1,0:T(8,128)(2,1)S(1)} %shard_map.219.refs_3_.refs_0_), channel_id=1, source_target_pairs={{0,2},{2,0},{4,6},{6,4},{1,3},{3,1},{5,7},{7,5},{8,10},{10,8},{12,... | collective-permute-start | bytes 393224 | tf_op jit(solution)/shard_map/ppermute | solution.py:537
  82.0 5.6 %collective-permute-start.27 = (bf16[48,512]{1,0:T(8,128)(2,1)S(1)}, bf16[48,512]{1,0:T(8,128)(2,1)S(1)}, u32[]{:S(2)}, u32[]{:S(2)}) collective-permute-start(bf16[48,512]{1,0:T(8,128)(2,1)S(1)} %get-tuple-element.192.refs_3_), channel_id=1, source_target_pairs={{0,4},{2,6},{4,0},{6,2},{1,5},{3,7},{5,1},{7,3},{8,12},{10,14},{12... | collective-permute-start | bytes 147464 | tf_op jit(solution)/shard_map/ppermute | solution.py:537
  83.9 9.2 %collective-permute-start.30 = (bf16[512,512]{1,0:T(8,128)(2,1)S(1)}, bf16[512,512]{1,0:T(8,128)(2,1)S(1)}, u32[]{:S(2)}, u32[]{:S(2)}) collective-permute-start(bf16[512,512]{1,0:T(8,128)(2,1)S(1)} %shard_map.221.refs_5_.refs_0_), channel_id=1, source_target_pairs={{0,8},{1,17},{2,10},{3,19},{4,12},{5,21},{6,14},{7,23},{8,0},{9,25... | collective-permute-start | bytes 1572872 | tf_op jit(solution)/shard_map/ppermute | solution.py:545
  87.7 8.8 %collective-permute-start.29 = (bf16[304,512]{1,0:T(8,128)(2,1)S(1)}, bf16[304,512]{1,0:T(8,128)(2,1)S(1)}, u32[]{:S(2)}, u32[]{:S(2)}) collective-permute-start(bf16[304,512]{1,0:T(8,128)(2,1)S(1)} %shard_map.222.refs_3_.refs_0_), channel_id=1, source_target_pairs={{0,8},{1,17},{2,10},{3,19},{4,12},{5,21},{6,14},{7,23},{8,0},{9,25... | collective-permute-start | bytes 933896 | tf_op jit(solution)/shard_map/ppermute | solution.py:545
  93.2 4.9 %collective-permute-start.32 = (bf16[1024,512]{1,0:T(8,128)(2,1)S(1)}, bf16[1024,512]{1,0:T(8,128)(2,1)S(1)}, u32[]{:S(2)}, u32[]{:S(2)}) collective-permute-start(bf16[1024,512]{1,0:T(8,128)(2,1)S(1)} %shard_map.223.refs_0_.refs_2_), channel_id=1, source_target_pairs={{0,1},{1,0},{2,3},{3,2},{4,5},{5,4},{6,7},{7,6},{8,9},{9,8},{10,11... | collective-permute-start | bytes 3145736 | tf_op jit(solution)/shard_map/ppermute | solution.py:518
  96.5 10.3 %collective-permute-start.31 = (bf16[608,512]{1,0:T(8,128)(2,1)S(1)}, bf16[608,512]{1,0:T(8,128)(2,1)S(1)}, u32[]{:S(2)}, u32[]{:S(2)}) collective-permute-start(bf16[608,512]{1,0:T(8,128)(2,1)S(1)} %shard_map.225.refs_2_.refs_0_), channel_id=1, source_target_pairs={{0,16},{1,9},{2,18},{3,11},{4,20},{5,13},{6,22},{7,15},{8,24},{9,1... | collective-permute-start | bytes 1867784 | tf_op jit(solution)/shard_map/ppermute | solution.py:545
  106.9 3.0 %collective-permute-start.33 = (bf16[1216,512]{1,0:T(8,128)(2,1)S(1)}, bf16[1216,512]{1,0:T(8,128)(2,1)S(1)}, u32[]{:S(2)}, u32[]{:S(2)}) collective-permute-start(bf16[1216,512]{1,0:T(8,128)(2,1)S(1)} %shard_map.227.refs_0_.refs_2_), channel_id=1, source_target_pairs={{0,1},{1,0},{2,3},{3,2},{4,5},{5,4},{6,7},{7,6},{8,9},{9,8},{10,11... | collective-permute-start | bytes 3735560 | tf_op jit(solution)/shard_map/ppermute | solution.py:518
  110.9 0.7 copy-start.2

commit v4 on v3

--- a/solution.py
+++ b/solution.py
@@ -18,8 +18,8 @@
 COPIES = 8
 WORK = 1
 ORDER = (
-    "f", "A", "f", "a", "B", "ab", "n", "h", "a", "b", "r", "a", "t", "b", "t", "a", "b", "o", "t",
-    "a", "b", "t", "a", "bt", "a", "P", "bt", "p", "bt", "Q", "T", "q",
+    "f", "A", "f", "a", "B", "n", "a", "b", "h", "a", "r", "b", "a", "o", "b", "t", "a", "b", "t",
+    "a", "t", "b", "a", "t", "b", "t", "a", "1", "b", "2", "t", "b", "3", "t", "4", "T",
 )
 
 
@@ -79,7 +79,7 @@
 
     def call(
         self, kernel, operands, outs, fetched=(), scalars=(), scratch=(), room=2 << 20, weight=WORK,
-        sent=(), aliased=(), kept=(), numbers=(),
+        sent=(), aliased=(), kept=(), numbers=(), delayed=0,
     ):
         n, f, s = len(operands), len(fetched) + len(kept), len(scalars)
         late = () if self.last is None else (self.last,)
@@ -94,10 +94,18 @@
         def wrapped(*refs):
             ins = refs[:n]
             sources = refs[n : n + f]
-            smem = [Place(ref) for ref in refs[n + f : n + f + s]] + list(
-                refs[n + f + s : n + f + s + len(numbers)]
-            )
+            smem = [Place(ref) for ref in refs[n + f : n + f + s]]
             rest = list(refs[n + f + s + len(numbers) + skip :])
+            if numbers:
+                number_sem, number_ref = rest.pop(), rest.pop()
+                number = pltpu.make_async_copy(refs[n + f + s], number_ref, number_sem.at[0])
+                number.start()
+
+                def number_wait():
+                    number.wait()
+                    return number_ref
+
+                smem = smem + [number_wait]
             far = rest[len(outs) : len(outs) + h]
             del rest[len(outs) : len(outs) + h]
             open_copies, send_sem = [], rest.pop() if h else None
@@ -110,12 +118,16 @@
             body, waits, waiting = rest, [], {}
             for i in range(f):
                 copy = pltpu.make_async_copy(sources[i], buffers[i], sems.at[i])
-                copy.start()
+                if i < f - delayed:
+                    copy.start()
                 waiting[i] = copy
 
                 def wait(i=i):
                     if i in waiting:
                         waiting.pop(i).wait()
+                        if i == f - delayed - 1:
+                            for j in range(f - delayed, f):
+                                waiting[j].start()
                     return buffers[i]
 
                 waits.append(wait)
@@ -144,13 +156,15 @@
             extra.append(pltpu.SemaphoreType.DMA((f,)))
         if h:
             extra.append(pltpu.SemaphoreType.DMA((COPIES,)))
+        if numbers:
+            extra += [pltpu.SMEM(numbers[0].shape, jnp.int32), pltpu.SemaphoreType.DMA((1,))]
         results = pl.pallas_call(
             wrapped,
             out_shape=outs + list(sent),
             in_specs=[pl.BlockSpec(memory_space=pltpu.VMEM)] * n
             + [pl.BlockSpec(memory_space=pltpu.HBM)] * f
             + [pl.BlockSpec(memory_space=pltpu.VMEM)] * s
-            + [pl.BlockSpec(memory_space=pltpu.SMEM)] * len(numbers)
+            + [pl.BlockSpec(memory_space=pl.ANY)] * len(numbers)
             + [pl.BlockSpec(memory_space=pl.ANY)] * skip,
             out_specs=[pl.BlockSpec(memory_space=pltpu.VMEM)] * len(outs)
             + [pl.BlockSpec(memory_space=pltpu.HBM)] * h,
@@ -173,12 +187,10 @@
 
 
 def prepare_kernel(
-    ln_wait, wkv_wait, wr_wait, sent_wait, ln_two_wait, x_wait, g_wait, ids_wait, win_wait, wout_wait,
-    wq_wait, wo_wait, spots_ref, xn_ref, kv_ref, kvt_ref, gates_ref, gt_ref, small_ref, sent_keep, gains_keep, keyid_ref,
+    ln_wait, wkv_wait, wr_wait, sent_wait, ln_two_wait, ids_wait, wq_wait, wo_wait, x_wait, g_wait, wout_wait,
+    spots_wait, xn_ref, kv_ref, kvt_ref, gates_ref, gt_ref, small_ref, sent_keep, gains_keep, keyid_ref,
     place_ref,
 ):
-    for i in range(spots_ref.shape[0]):
-        place_ref[i : i + 1, :] = jnp.full((1, place_ref.shape[1]), spots_ref[i], jnp.int32)
     ln_ref, x_ref = ln_wait(), x_wait()
     length = x_ref.shape[0]
     gain = ln_ref[...]
@@ -218,9 +230,12 @@
     column_ids(sent_keep, keyid_ref)
     g_ref = g_wait()
     gt_ref[...] = g_ref[...].T
-
-
-def upstream_kernel(g_ref, wout_ref, ag_ref):
+    spots_ref = spots_wait()
+    for i in range(spots_ref.shape[0]):
+        place_ref[i : i + 1, :] = jnp.full((1, place_ref.shape[1]), spots_ref[i], jnp.int32)
+
+
+def upstream_kernel(g_ref, wout_ref, win_wait, ag_ref):
     for start in range(0, g_ref.shape[0], ROWS):
         rows = slice(start, start + ROWS)
         ag_ref[rows, :] = nt(g_ref[rows, :], wout_ref[...]).astype(BF)
@@ -234,8 +249,8 @@
 
 
 def masked_scores(kv_ref, keyid_ref, sent_ref, queries, start, low, high, choose):
-    padded = jnp.concatenate([queries, jnp.zeros_like(queries)], axis=0)
-    scores = nn(kv_ref[low:high, :], padded) * 0.125
+    padded = jnp.concatenate([queries * 0.125, jnp.zeros_like(queries)], axis=0)
+    scores = nn(kv_ref[low:high, :], padded)
     same = keyid_ref[low:high, :] == sent_ref[:, start : start + BAND]
     parts = [
         jnp.where(same, scores[:, route * BAND : (route + 1) * BAND], MASKED)
@@ -253,7 +268,7 @@
     (
         xn_ref, kv_ref, kvt_ref, gates_ref, x_ref, ids_ref, sent_ref, ln_ref, keyid_ref, wq_own, wo_own,
         place_ref, wq_ref, wo_ref, qt_ref, at_ref, lse_ref, gat_ref, h_ref, hn_ref, hnt_ref, all_ref,
-        pair_ref,
+        pair_ref, score_ref, prob_ref,
     ) = refs
     own = place_ref[1]
     each = 2 * head // peers
@@ -269,35 +284,44 @@
     length = xn_ref.shape[0]
     choose = ids_ref.shape[0]
     all_ref[...] = nt(wq_ref[...], xn_ref[...])
-    for start in range(0, length, BAND):
+    starts = range(0, length, BAND)
+    spans = [slice(start * choose, (start + BAND) * choose) for start in starts]
+    bounds = [window(start, length) for start in starts]
+    for start, block in zip(starts, spans):
         lanes = slice(start, start + BAND)
-        block = slice(start * choose, (start + BAND) * choose)
-        low, high = window(start, length)
         chosen = []
         for route in range(choose):
             ids = ids_ref[route : route + 1, lanes]
-            value = jnp.zeros((head, BAND), F32)
-            for expert in range(experts):
+            value = all_ref[:head, lanes]
+            for expert in range(1, experts):
                 value = jnp.where(
                     ids == expert, all_ref[expert * head : (expert + 1) * head, lanes], value
                 )
             chosen.append(value)
-        queries = jnp.concatenate(chosen, axis=1).astype(BF)
-        qt_ref[:, block] = queries
-        scores = masked_scores(kv_ref, keyid_ref, sent_ref, queries, start, low, high, choose)
+        qt_ref[:, block] = jnp.concatenate(chosen, axis=1).astype(BF)
+    for i, start in enumerate(starts):
+        low, high = bounds[i]
+        score_ref[i, : high - low, :] = masked_scores(
+            kv_ref, keyid_ref, sent_ref, qt_ref[:, spans[i]], start, low, high, choose
+        )
+    for i, block in enumerate(spans):
+        size = bounds[i][1] - bounds[i][0]
+        scores = score_ref[i, :size, :]
         largest = jnp.max(scores, axis=0, keepdims=True)
         raised = jnp.exp(scores - largest)
         total = jnp.sum(raised, axis=0, keepdims=True)
-        probs = (raised * (1.0 / total)).astype(BF)
+        prob_ref[i, :size, :] = (raised * (1.0 / total)).astype(BF)
         lse_ref[:, block] = largest + jnp.log(total)
-        attended = nn(kvt_ref[head:, low:high], probs).astype(BF)
-        at_ref[:, block] = attended
+    for i, block in enumerate(spans):
+        low, high = bounds[i]
+        at_ref[:, block] = nn(kvt_ref[head:, low:high], prob_ref[i, : high - low, :]).astype(BF)
+    for start in starts:
+        lanes = slice(start, start + BAND)
         spread = [jnp.zeros((head, BAND), F32) for _ in range(experts)]
         for route in range(choose):
             ids = ids_ref[route : route + 1, lanes]
-            gated = attended[:, route * BAND : (route + 1) * BAND].astype(F32) * gates_ref[
-                route : route + 1, lanes
-            ]
+            first = start * choose + route * BAND
+            gated = at_ref[:, first : first + BAND].astype(F32) * gates_ref[route : route + 1, lanes]
             for expert in range(experts):
                 spread[expert] = jnp.where(ids == expert, gated, spread[expert])
         for expert in range(experts):
@@ -406,7 +430,8 @@
 
 def heads_back_kernel(
     kv_ref, kvt_ref, gates_ref, wo_ref, qt_ref, at_ref, lse_ref, gat_ref, low_ref, ids_ref, sent_ref,
-    keyid_ref, z_ref, gout_ref, all_ref, dkv_ref, *, experts, head,
+    keyid_ref, z_ref, gout_ref, all_ref, dkv_ref, up_ref, prob_ref, grad_ref, soft_ref, ds_ref, *, experts,
+    head,
 ):
     length = kv_ref.shape[0]
     wide, pair = experts * head, 2 * head
@@ -414,21 +439,23 @@
     all_ref[...] = nt(wo_ref[...], low_ref[...])
     gout_ref[...] = nn(gat_ref[...], low_ref[...]).astype(BF)
     dkv_ref[...] = jnp.zeros_like(dkv_ref)
-    for start in range(0, length, BAND):
+    starts = range(0, length, BAND)
+    spans = [slice(start * choose, (start + BAND) * choose) for start in starts]
+    bounds = [window(start, length) for start in starts]
+    for start, block in zip(starts, spans):
         lanes = slice(start, start + BAND)
-        block = slice(start * choose, (start + BAND) * choose)
-        low, high = window(start, length)
         raw, gate_grads = [], []
         for route in range(choose):
             ids = ids_ref[route : route + 1, lanes]
-            value = jnp.zeros((head, BAND), F32)
-            for expert in range(experts):
+            value = all_ref[:head, lanes]
+            for expert in range(1, experts):
                 value = jnp.where(
                     ids == expert, all_ref[expert * head : (expert + 1) * head, lanes], value
                 )
             raw.append(value)
-            attended = at_ref[:, start * choose + route * BAND : start * choose + (route + 1) * BAND]
-            gate_grads.append(jnp.sum(value * attended.astype(F32), axis=0, keepdims=True))
+            first = start * choose + route * BAND
+            attended = at_ref[:, first : first + BAND].astype(F32)
+            gate_grads.append(jnp.sum(value * attended, axis=0, keepdims=True))
         gates = [gates_ref[route : route + 1, lanes] for route in range(choose)]
         common = functools.reduce(
             lambda a, b: a + b, [gate * grad for gate, grad in zip(gates, gate_grads)]
@@ -443,16 +470,28 @@
             logit_rows + [jnp.zeros((16 - experts, BAND), F32)], axis=0
         )
         z_ref[wide + pair :, lanes] = logit_pad.astype(BF)
-        queries = qt_ref[:, block]
-        scores = masked_scores(kv_ref, keyid_ref, sent_ref, queries, start, low, high, choose)
-        probs = jnp.exp(scores - lse_ref[:, block])
-        upstream = jnp.concatenate(
+        up_ref[:, block] = jnp.concatenate(
             [gate * value for gate, value in zip(gates, raw)], axis=1
         ).astype(BF)
+    for i, start in enumerate(starts):
+        low, high = bounds[i]
+        prob_ref[i, : high - low, :] = masked_scores(
+            kv_ref, keyid_ref, sent_ref, qt_ref[:, spans[i]], start, low, high, choose
+        )
+        upstream = up_ref[:, spans[i]]
         padded = jnp.concatenate([jnp.zeros_like(upstream), upstream], axis=0)
-        prob_grad = nn(kv_ref[low:high, :], padded)
+        grad_ref[i, : high - low, :] = nn(kv_ref[low:high, :], padded)
+    for i, block in enumerate(spans):
+        size = bounds[i][1] - bounds[i][0]
+        probs = jnp.exp(prob_ref[i, :size, :] - lse_ref[:, block])
+        soft_ref[i, :size, :] = probs.astype(BF)
+        prob_grad = grad_ref[i, :size, :]
         mean = jnp.sum(probs * prob_grad, axis=0, keepdims=True)
-        score_grad = (probs * (prob_grad - mean)).astype(BF)
+        ds_ref[i, :size, :] = (probs * (prob_grad - mean)).astype(BF)
+    for i, start in enumerate(starts):
+        low, high = bounds[i]
+        lanes = slice(start, start + BAND)
+        score_grad = ds_ref[i, : high - low, :]
         query_grad = (nn(kvt_ref[:head, low:high], score_grad) * 0.125).astype(BF)
         spread = [jnp.zeros((head, BAND), BF) for _ in range(experts)]
         for route in range(choose):
@@ -462,8 +501,8 @@
                 spread[expert] = jnp.where(ids == expert, piece, spread[expert])
         for expert in range(experts):
             z_ref[expert * head : (expert + 1) * head, lanes] = spread[expert]
-        dkv_ref[:head, low:high] += nt(queries, score_grad) * 0.125
-        dkv_ref[head:, low:high] += nt(upstream, probs.astype(BF))
+        dkv_ref[:head, low:high] += nt(qt_ref[:, spans[i]], score_grad) * 0.125
+        dkv_ref[head:, low:high] += nt(up_ref[:, spans[i]], soft_ref[i, : high - low, :])
     z_ref[wide : wide + pair, :] = dkv_ref[...].astype(BF)
 
 
@@ -872,8 +911,7 @@
     line = Line()
     line.last = spots
     (
-        normed, kv, kvt, gates, gt, small, sent, gains, keyid, place, x, g, ids, in_weight, out_weight, own_query,
-        own_output,
+        normed, kv, kvt, gates, gt, small, sent, gains, keyid, place, ids, own_query, own_output, x, g, out_weight,
     ) = line.call(
         prepare_kernel,
         (),
@@ -891,11 +929,11 @@
         ],
         fetched=(ln_one, w_kv, w_router.T, sentence_ids, ln_two),
         numbers=(spots,),
-        kept=(tokens, out_grad, ids, w_in, w_out, w_query[0].T, w_output[0]),
+        kept=(ids, w_query[0].T, w_output[0], tokens, out_grad, w_out),
         room=8 << 20,
     )
-    [ag] = line.call(
-        upstream_kernel, (g, out_weight), [sds((length, full), BF)], room=8 << 20,
+    ag, in_weight = line.call(
+        upstream_kernel, (g, out_weight), [sds((length, full), BF)], kept=(w_in,), room=8 << 20,
     )
     slab = join_all(line, pieces)
     slabs = [slab] + exchange([slab] * peers, "tok")
@@ -917,12 +955,14 @@
         scratch=(
             sds((experts * head, length), F32),
             sds((2 * head, width), BF),
+            sds((length // BAND, 3 * BAND, choose * BAND), F32),
+            sds((length // BAND, 3 * BAND, choose * BAND), BF),
         ),
         room=8 << 20,
     )
 
     chains = Chains(line, place)
-    us, dpres, sums = [], [], []
+    us, dpres, sums, spans = [], [], [], {}
 
     def ffn(last=None, mirror=0):
         rows = 2 * width // peers
@@ -943,10 +983,11 @@
         if last is not None:
             views = [View(same[0], more=same[1:]) for same in zip(*sums)]
             chains.begin(last, chunk_walk(views, mirror, len(sums), rows))
+            hidden = len(sums) // pieces * width
+            spans[last] = (len(us) * width - hidden, hidden)
             sums.clear()
 
     misc = -(-(pair + 16) // (64 * peers)) * 64 * peers
-    half = full // 2
 
     def hidden():
         made["dh"], made["low"], made["gain"] = line.call(
@@ -961,7 +1002,12 @@
             functools.partial(heads_back_kernel, experts=experts, head=head),
             (kv, kvt, gates, wo, qt, at, lse, gat, made["low"], ids, sent, keyid),
             [sds((experts * head + pair + 16, length), BF), sds((experts * head, width), BF)],
-            scratch=(sds((experts * head, length), F32), sds((pair, length), F32)),
+            scratch=(
+                sds((experts * head, length), F32),
+                sds((pair, length), F32),
+                sds((head, choose * length), BF),
+                *[sds((length // BAND, 3 * BAND, choose * BAND), t) for t in (F32, F32, BF, BF)],
+            ),
             room=6 << 20,
         )
 
@@ -993,15 +1039,13 @@
             room=6 << 20,
         )
 
-    def place_one(name, first, turn):
+    def place_one(name, turn):
         if turn == 0:
             made[name] = chains.finish(name)
-            views = made[name][:1]
-        else:
-            views = made[name][1:]
+        views = made[name][:1] if turn == 0 else made[name][1:]
         for view in views:
             made["both"] = place_part(
-                line, place, view, turn, first, half, full, made.get("both", ())
+                line, place, view, turn, *spans[name], full, made.get("both", ())
             )
             turn += 1
 
@@ -1009,20 +1053,11 @@
         made["t"] = place_tail(line, place, chains.finish("t"), experts, head, misc)
 
     made = {}
-    acts = {
-        "f": ffn,
-        "A": lambda: ffn("a"),
-        "B": lambda: ffn("b", 1),
-        "n": hidden,
-        "h": heads_back,
-        "r": rows_back,
-        "o": out,
-        "P": lambda: place_one("a", 0, 0),
-        "p": lambda: place_one("a", 0, 1),
-        "Q": lambda: place_one("b", half, 0),
-        "q": lambda: place_one("b", half, 1),
-        "T": last,
-    }
+    acts = {"f": ffn, "n": hidden, "h": heads_back, "r": rows_back, "o": out, "T": last}
+    for i, name in enumerate("abc"):
+        acts[name.upper()] = functools.partial(ffn, name, i % 2)
+        acts[str(2 * i + 1)] = functools.partial(place_one, name, 0)
+        acts[str(2 * i + 2)] = functools.partial(place_one, name, 1)
     for word in ORDER:
         if word in acts:
             acts[word]()

time: 114 us -> 102 us (0.89)
  waiting for transfers between devices: 33.2 us -> 17.7 us
  starting transfers between devices: 29.7 us -> 38.1 us
  Pallas kernels: 47.4 us -> 43.7 us
  local copies, waits for them, and re-layouts: 1.47 us -> 0.09 us
    ppermute x9 -> x12, waiting for transfers between devices: 21.4 us -> 10.5 us  [swap(): return lax.ppermute(array, AXES, pairs)]
    ppermute x9 -> x12, starting transfers between devices: 13.2 us -> 18 us  [swap(): return lax.ppermute(array, AXES, pairs)]
    pallas_call x36 -> x40, Pallas kernels: 47.4 us -> 43.7 us  [call(): pl.pallas_call(wrapped, out_shape=outs + list(sent), in_specs=[pl.BlockSp...]
    ppermute x8, starting transfers between devices: 7.72 us -> 10.7 us  [swap(): lax.ppermute(array, 'expert', [(i, i ^ 1 << stage) for i in range(size)])]
    ppermute x17 -> x18, waiting for transfers between devices: 4.31 us -> 2.02 us  [exchange(): lax.ppermute(parts[k], axis, [(i, i ^ k) for i in range(size)])]
    ppermute x8, waiting for transfers between devices: 7.44 us -> 5.28 us  [swap(): lax.ppermute(array, 'expert', [(i, i ^ 1 << stage) for i in range(size)])]
    unnamed x6 -> x4, local copies, waits for them, and re-layouts: 1.39 us -> 0.01 us
    ppermute x17 -> x18, starting transfers between devices: 8.78 us -> 9.33 us  [exchange(): lax.ppermute(parts[k], axis, [(i, i ^ k) for i in range(size)])]
  transfers between devices with their start and end apart: 34 -> 38, of which waited for: 16 -> 12; matrix products, arithmetic and copies ran while one was open for 0% -> 0% of each run, Pallas kernels for 31% -> 36%
where the time goes in v4:
time: 102 us
  Pallas kernels  43.7 us (43%)
  starting transfers between devices  38.1 us (37%)
  waiting for transfers between devices  17.7 us (17%)
  between operations  1.1 us (1%)
    pallas_call x40, Pallas kernels, call(): pl.pallas_call(wrapped, out_shape=outs + list(sent), in_specs=[pl.BlockSp...  43.7 us
    ppermute x12, starting transfers between devices, swap(): return lax.ppermute(array, AXES, pairs)  18 us
    ppermute x8, starting transfers between devices, swap(): lax.ppermute(array, 'expert', [(i, i ^ 1 << stage) for i in range(size)])  10.7 us
    ppermute x12, waiting for transfers between devices, swap(): return lax.ppermute(array, AXES, pairs)  10.5 us
    ppermute x18, starting transfers between devices, exchange(): lax.ppermute(parts[k], axis, [(i, i ^ k) for i in range(size)])  9.33 us
    ppermute x8, waiting for transfers between devices, swap(): lax.ppermute(array, 'expert', [(i, i ^ 1 << stage) for i in range(size)])  5.28 us
  transfers between devices with their start and end apart: 38, of which 12 were waited for; matrix products, arithmetic and copies ran while one was open for 0% of the time, Pallas kernels for 36%

profile of v4, /device:TPU:0, one launch (start us, length us, event | category | flops | bytes accessed | tf_op | source)
XLA Modules:
  0.0 101.6 jit_solution(13219347504234498216)
XLA Ops:
  0.6 0.9 fusion
  1.5 4.1 %collective-permute-start.1 = (bf16[64,512]{1,0:T(8,128)(2,1)S(1)}, bf16[64,512]{1,0:T(8,128)(2,1)S(1)}, u32[]{:S(2)}, u32[]{:S(2)}) collective-permute-start(bf16[64,512]{1,0:T(8,128)(2,1)S(1)} %fusion), channel_id=1, source_target_pairs={{0,4},{2,6},{4,0},{6,2},{1,5},{3,7},{5,1},{7,3},{8,12},{10,14},{12... | collective-permute-start | bytes 196616 | tf_op jit(solution)/shard_map/ppermute | solution.py:557
  5.6 1.6 %collective-permute-start = (bf16[64,512]{1,0:T(8,128)(2,1)S(1)}, bf16[64,512]{1,0:T(8,128)(2,1)S(1)}, u32[]{:S(2)}, u32[]{:S(2)}) collective-permute-start(bf16[64,512]{1,0:T(8,128)(2,1)S(1)} %fusion), channel_id=1, source_target_pairs={{0,2},{2,0},{4,6},{6,4},{1,3},{3,1},{5,7},{7,5},{8,10},{10,8},{12,... | collective-permute-start | bytes 196616 | tf_op jit(solution)/shard_map/ppermute | solution.py:557
  7.3 3.6 %shard_map.195 = (bf16[1024,512]{1,0:T(8,128)(2,1)S(1)}, bf16[1024,128]{1,0:T(8,128)(2,1)S(1)}, bf16[128,1024]{1,0:T(8,128)(2,1)S(1)}, f32[2,1024]{1,0:T(2,128)S...) custom-call(f32[1,512]{1,0:T(1,128)} %bitcast.24, ...), custom_call_target="tpu_custom_call" | custom-call | flops 1 | bytes 1024 | tf_op jit(solution)/shard_map/pallas_call | solution.py:161
  10.9 2.6 %shard_map.196 = (bf16[1024,2048]{1,0:T(8,128)(2,1)S(1)}, bf16[512,2048]{1,0:T(8,128)(2,1)S(1)}) custom-call(bf16[1024,512]{1,0:T(8,128)(2,1)S(1)} %get-tuple-element.113.refs_0_.refs_1_, bf16[2048,512]{1,0:T(8,128)(2,1)S(1)} %get-tuple-element.114.refs_1_, bf16[512,2048]{1,0:T(8,128)(2,1)} %refs_2_.1, f32[1,1024]{1,0:T(1,128)S(1)} %get-tuple-element.115.refs_3_.refs_8_.refs_10_), custom_call_target="tpu_custom_call" | custom-call | flops 1 | bytes 1024 | tf_op jit(solution)/shard_map/pallas_call | solution.py:161
  13.7 1.4 %collective-permute-done.3.refs_1_ = bf16[192,512]{1,0:T(8,128)(2,1)S(1)} collective-permute-done((bf16[192,512]{1,0:T(8,128)(2,1)S(1)}, bf16[192,512]{1,0:T(8,128)(2,1)S(1)}, u32[]{:S(2)}, u32[]{:S(2)}) %collective-permute-start.3) | collective-permute-done | bytes 196640 | tf_op jit(solution)/shard_map/ppermute | solution.py:557
  15.1 3.0 %shard_map.198 = (bf16[256,512]{1,0:T(8,128)(2,1)S(1)}, bf16[256,512]{1,0:T(8,128)(2,1)S(1)}, bf16[64,2048]{1,0:T(8,128)(2,1)S(1)}, bf16[64,2048]{1,0:T(8,128)(2...) custom-call(bf16[192,512]{1,0:T(8,128)(2,1)S(1)} %shard_map.197.refs, ...), custom_call_target="tpu_custom_call" | custom-call | flops 1 | bytes 1024 | tf_op jit(solution)/shard_map/pallas_call | solution.py:161
  18.1 3.2 %shard_map.199 = (bf16[1024,512]{1,0:T(8,128)(2,1)S(1)}, bf16[1024,512]{1,0:T(8,128)(2,1)S(1)}, bf16[256,512]{1,0:T(8,128)(2,1)S(1)}, bf16[256,512]{1,0:T(8,128)...) custom-call(bf16[1024,512]{1,0:T(8,128)(2,1)S(1)} %get-tuple-element.129.refs_0_, ...), custom_call_target="tpu_custom_call" | custom-call | flops 1 | bytes 1024 | tf_op jit(solution)/shard_map/pallas_call | solution.py:161
  21.3 0.2 collective-permute-start.4
  21.6 0.4 collective-permute-start.5
  21.9 3.4 %shard_map.200 = (bf16[1024,512]{1,0:T(8,128)(2,1)S(1)}, bf16[1024,512]{1,0:T(8,128)(2,1)S(1)}, bf16[256,512]{1,0:T(8,128)(2,1)S(1)}, bf16[256,512]{1,0:T(8,128)...) custom-call(bf16[1024,512]{1,0:T(8,128)(2,1)S(1)} %get-tuple-element.129.refs_0_, ...), custom_call_target="tpu_custom_call" | custom-call | flops 1 | bytes 1024 | tf_op jit(solution)/shard_map/pallas_call | solution.py:161
  25.3 0.2 collective-permute-start.6
  25.5 0.4 collective-permute-start.7
  25.9 3.2 %shard_map.201 = (bf16[1024,512]{1,0:T(8,128)(2,1)S(1)}, bf16[1024,512]{1,0:T(8,128)(2,1)S(1)}, bf16[256,512]{1,0:T(8,128)(2,1)S(1)}, bf16[256,512]{1,0:T(8,128)...) custom-call(bf16[1024,512]{1,0:T(8,128)(2,1)S(1)} %get-tuple-element.129.refs_0_, ...), custom_call_target="tpu_custom_call" | custom-call | flops 1 | bytes 1024 | tf_op jit(solution)/shard_map/pallas_call | solution.py:161
  29.1 0.4 shard_map.202
  29.5 1.8 %collective-permute-start.8 = (bf16[512,512]{1,0:T(8,128)(2,1)S(1)}, bf16[512,512]{1,0:T(8,128)(2,1)S(1)}, u32[]{:S(2)}, u32[]{:S(2)}) collective-permute-start(bf16[512,512]{1,0:T(8,128)(2,1)S(1)} %get-tuple-element.146.refs_6_), channel_id=1, source_target_pairs={{0,8},{1,17},{2,10},{3,19},{4,12},{5,21},{6,14},{7,23},{8,0},{9,25... | collective-permute-start | bytes 1572872 | tf_op jit(solution)/shard_map/ppermute | solution.py:584
  31.3 0.5 collective-permute-start.11
  31.8 3.2 %shard_map.203 = (bf16[1024,512]{1,0:T(8,128)(2,1)S(1)}, bf16[1024,512]{1,0:T(8,128)(2,1)S(1)}, bf16[256,512]{1,0:T(8,128)(2,1)S(1)}, bf16[256,512]{1,0:T(8,128)...) custom-call(bf16[1024,512]{1,0:T(8,128)(2,1)S(1)} %get-tuple-element.129.refs_0_, ...), custom_call_target="tpu_custom_call" | custom-call | flops 1 | bytes 1024 | tf_op jit(solution)/shard_map/pallas_call | solution.py:161
  35.1 0.5 collective-permute-start.13
  35.6 3.2 %shard_map.204 = (f32[1024,512]{1,0:T(8,128)S(1)}, bf16[1024,512]{1,0:T(8,128)(2,1)S(1)}, f32[1,512]{1,0:T(1,128)S(1)}) custom-call(f32[1024,512]{1,0:T(8,128)S(1)} %get-tuple-element.128.refs_0_, bf16[1024,512]{1,0:T(8,128)(2,1)S(1)} %get-tuple-element.113.refs_0_.refs_1_, bf16[512,2048]{1,0:T(8,128)(2,1)S(1)} %get-tuple-element.116.refs_3_.refs_4_.refs_2_, ...), custom_call_target="tpu_custom_call" | custom-call | flops 1 | bytes 1024 | tf_op jit(solution)/shard_map/pallas_call | solution.py:161
  38.8 0.2 shard_map.205
  39.0 1.7 %collective-permute-start.9 = (bf16[256,512]{1,0:T(8,128)(2,1)S(1)}, bf16[256,512]{1,0:T(8,128)(2,1)S(1)}, u32[]{:S(2)}, u32[]{:S(2)}) collective-permute-start(bf16[256,512]{1,0:T(8,128)(2,1)S(1)} %get-tuple-element.156.refs_9_), channel_id=1, source_target_pairs={{0,16},{1,9},{2,18},{3,11},{4,20},{5,13},{6,22},{7,15},{8,24},{9,1... | collective-permute-start | bytes 786440 | tf_op jit(solution)/shard_map/ppermute | solution.py:584
  40.7 0.4 shard_map.206
  41.1 0.4 collective-permute-start.15
  41.5 3.1 %shard_map.207 = (bf16[400,1024]{1,0:T(8,128)(2,1)S(1)}, bf16[256,512]{1,0:T(8,128)(2,1)S(1)}) custom-call(bf16[1024,128]{1,0:T(8,128)(2,1)S(1)} %get-tuple-element.118.refs_3_.refs_0_, bf16[128,1024]{1,0:T(8,128)(2,1)S(1)} %get-tuple-element.119.refs_4_.refs_1_, f32[2,1024]{1,0:T(2,128)S(1)} %get-tuple-element.120.refs_5_.refs_2_, ...), custom_call_target="tpu_custom_call" | custom-call | flops 1 | bytes 1024 | tf_op jit(solution)/shard_map/pallas_call | solution.py:161
  44.6 0.8 collective-permute-done.9.refs_1_
  45.5 0.9 collective-permute-start.14
  46.4 2.9 %shard_map.209 = (bf16[128,512]{1,0:T(8,128)(2,1)S(1)}, bf16[128,512]{1,0:T(8,128)(2,1)S(1)}, bf16[128,512]{1,0:T(8,128)(2,1)S(1)}, bf16[128,512]{1,0:T(8,128)(2...) custom-call(bf16[400,1024]{1,0:T(8,128)(2,1)S(1)} %get-tuple-element.173.refs_0_, ...), custom_call_target="tpu_custom_call" | custom-call | flops 1 | bytes 1024 | tf_op jit(solution)/shard_map/pallas_call | solution.py:161
  49.4 0.5 collective-permute-start.17
  50.0 1.0 collective-permute-done.15.refs_1_
  51.0 0.2 shard_map.210
  51.2 1.7 %collective-permute-start.19 = (bf16[256,512]{1,0:T(8,128)(2,1)S(1)}, bf16[256,512]{1,0:T(8,128)(2,1)S(1)}, u32[]{:S(2)}, u32[]{:S(2)}) collective-permute-start(bf16[256,512]{1,0:T(8,128)(2,1)S(1)} %get-tuple-element.178.refs_3_), channel_id=1, source_target_pairs={{0,8},{1,17},{2,10},{3,19},{4,12},{5,21},{6,14},{7,23},{8,0},{9,25... | collective-permute-start | bytes 786440 | tf_op jit(solution)/shard_map/ppermute | solution.py:584
  52.9 2.4 %collective-permute-start.22 = (bf16[128,512]{1,0:T(8,128)(2,1)S(1)}, bf16[128,512]{1,0:T(8,128)(2,1)S(1)}, u32[]{:S(2)}, u32[]{:S(2)}) collective-permute-start(bf16[128,512]{1,0:T(8,128)(2,1)S(1)} %shard_map.211.refs_6_.refs_0_), channel_id=1, source_target_pairs={{0,4},{2,6},{4,0},{6,2},{1,5},{3,7},{5,1},{7,3},{8,12},{10,14},{12... | collective-permute-start | bytes 393224 | tf_op jit(solution)/shard_map/ppermute | solution.py:576
  55.3 3.1 %shard_map.212 = (f32[8,128]{1,0:T(8,128)S(1)}, bf16[1024,512]{1,0:T(8,128)(2,1)}) custom-call(f32[1024,512]{1,0:T(8,128)S(1)} %get-tuple-element.128.refs_0_, bf16[2048,512]{1,0:T(8,128)(2,1)S(1)} %copy-done.1, bf16[1024,512]{1,0:T(8,128)(2,1)S(1)} %get-tuple-element.134.refs_2_, bf16[1024,512]{1,0:T(8,128)(2,1)S(1)} %get-tuple-element.136.refs_3_, ...), custom_call_target="tpu_custom_call" | custom-call | flops 1 | bytes 1024 | tf_op jit(solution)/shard_map/pallas_call | solution.py:161
  58.6 1.9 %collective-permute-start.21 = (bf16[128,512]{1,0:T(8,128)(2,1)S(1)}, bf16[128,512]{1,0:T(8,128)(2,1)S(1)}, u32[]{:S(2)}, u32[]{:S(2)}) collective-permute-start(bf16[128,512]{1,0:T(8,128)(2,1)S(1)} %get-tuple-element.188.refs_7_), channel_id=1, source_target_pairs={{0,2},{2,0},{4,6},{6,4},{1,3},{3,1},{5,7},{7,5},{8,10},{10,8},{12,... | collective-permute-start | bytes 393224 | tf_op jit(solution)/shard_map/ppermute | solution.py:576
  60.5 0.1 shard_map.214
  60.7 1.6 %collective-permute-start.20 = (bf16[192,512]{1,0:T(8,128)(2,1)S(1)}, bf16[192,512]{1,0:T(8,128)(2,1)S(1)}, u32[]{:S(2)}, u32[]{:S(2)}) collective-permute-start(bf16[192,512]{1,0:T(8,128)(2,1)S(1)} %get-tuple-element.190.refs_3_), channel_id=1, source_target_pairs={{0,16},{1,9},{2,18},{3,11},{4,20},{5,13},{6,22},{7,15},{8,24},{9,1... | collective-permute-start | bytes 589832 | tf_op jit(solution)/shard_map/ppermute | solution.py:584
  62.3 0.3 collective-permute-start.24
  62.5 2.2 %collective-permute-done.21.refs_1_ = bf16[128,512]{1,0:T(8,128)(2,1)S(1)} collective-permute-done((bf16[128,512]{1,0:T(8,128)(2,1)S(1)}, bf16[128,512]{1,0:T(8,128)(2,1)S(1)}, u32[]{:S(2)}, u32[]{:S(2)}) %collective-permute-start.21) | collective-permute-done | bytes 131104 | tf_op jit(solution)/shard_map/ppermute | solution.py:576
  64.8 1.7 %collective-permute-start.27 = (bf16[128,512]{1,0:T(8,128)(2,1)S(1)}, bf16[128,512]{1,0:T(8,128)(2,1)S(1)}, u32[]{:S(2)}, u32[]{:S(2)}) collective-permute-start(bf16[128,512]{1,0:T(8,128)(2,1)S(1)} %shard_map.216.refs_3_.refs_0_), channel_id=1, source_target_pairs={{0,4},{2,6},{4,0},{6,2},{1,5},{3,7},{5,1},{7,3},{8,12},{10,14},{12... | collective-permute-start | bytes 393224 | tf_op jit(solution)/shard_map/ppermute | solution.py:576
  66.6 1.8 %collective-permute-start.23 = (bf16[96,512]{1,0:T(8,128)(2,1)S(1)}, bf16[96,512]{1,0:T(8,128)(2,1)S(1)}, u32[]{:S(2)}, u32[]{:S(2)}) collective-permute-start(bf16[96,512]{1,0:T(8,128)(2,1)S(1)} %get-tuple-element.193.refs_3_), channel_id=1, source_target_pairs={{0,8},{1,17},{2,10},{3,19},{4,12},{5,21},{6,14},{7,23},{8,0},{9,25... | collective-permute-start | bytes 294920 | tf_op jit(solution)/shard_map/ppermute | solution.py:584
  68.5 1.7 %collective-permute-start.26 = (bf16[256,512]{1,0:T(8,128)(2,1)S(1)}, bf16[256,512]{1,0:T(8,128)(2,1)S(1)}, u32[]{:S(2)}, u32[]{:S(2)}) collective-permute-start(bf16[256,512]{1,0:T(8,128)(2,1)S(1)} %shard_map.218.refs_3_.refs_0_), channel_id=1, source_target_pairs={{0,16},{1,9},{2,18},{3,11},{4,20},{5,13},{6,22},{7,15},{8,24},{9,1... | collective-permute-start | bytes 786440 | tf_op jit(solution)/shard_map/ppermute | solution.py:584
  70.1 2.2 %collective-permute-done.23.refs_1_ = bf16[96,512]{1,0:T(8,128)(2,1)S(1)} collective-permute-done((bf16[96,512]{1,0:T(8,128)(2,1)S(1)}, bf16[96,512]{1,0:T(8,128)(2,1)S(1)}, u32[]{:S(2)}, u32[]{:S(2)}) %collective-permute-start.23) | collective-permute-done | bytes 98336 | tf_op jit(solution)/shard_map/ppermute | solution.py:584
  72.4 2.0 %collective-permute-start.25 = (bf16[64,512]{1,0:T(8,128)(2,1)S(1)}, bf16[64,512]{1,0:T(8,128)(2,1)S(1)}, u32[]{:S(2)}, u32[]{:S(2)}) collective-permute-start(bf16[64,512]{1,0:T(8,128)(2,1)S(1)} %get-tuple-element.195.refs_3_), channel_id=1, source_target_pairs={{0,2},{2,0},{4,6},{6,4},{1,3},{3,1},{5,7},{7,5},{8,10},{10,8},{12,... | collective-permute-start | bytes 196616 | tf_op jit(solution)/shard_map/ppermute | solution.py:576
  74.5 0.1 collective-permute-start.29
  74.6 0.3 collective-permute-done.26.refs_1_
  75.0 1.5 %collective-permute-start.31 = (bf16[512,512]{1,0:T(8,128)(2,1)S(1)}, bf16[512,512]{1,0:T(8,128)(2,1)S(1)}, u32[]{:S(2)}, u32[]{:S(2)}) collective-permute-start(bf16[512,512]{1,0:T(8,128)(2,1)S(1)} %shard_map.221.refs_3_.refs_0_), channel_id=1, source_target_pairs={{0,8},{1,17},{2,10},{3,19},{4,12},{5,21},{6,14},{7,23},{8,0},{9,25... | collective-permute-start | bytes 1572872 | tf_op jit(solution)/shard_map/ppermute | solution.py:584
  76.5 1.0 collective-permute-done.25.refs_1_
  77.5 1.4 %collective-permute-start.28 = (bf16[48,512]{1,0:T(8,128)(2,1)S(1)}, bf16[48,512]{1,0:T(8,128)(2,1)S(1)}, u32[]{:S(2)}, u32[]{:S(2)}) collective-permute-start(bf16[48,512]{1,0:T(8,128)(2,1)S(1)} %get-tuple-element.197.refs_3_), channel_id=1, source_target_pairs={{0,4},{2,6},{4,0},{6,2},{1,5},{3,7},{5,1},{7,3},{8,12},{10,14},{12... | collective-permute-start | bytes 147464 | tf_op jit(solution)/shard_map/ppermute | solution.py:576
  78.9 1.0 %collective-permute-done.29.refs_1_ = bf16[128,512]{1,0:T(8,128)(2,1)S(1)} collective-permute-done((bf16[128,512]{1,0:T(8,128)(2,1)S(1)}, bf16[128,512]{1,0:T(8,128)(2,1)S(1)}, u32[]{:S(2)}, u32[]{:S(2)}) %collective-permute-start.29) | collective-permute-done | bytes 131104 | tf_op jit(solution)/shard_map/ppermute | solution.py:576
  80.0 1.5 %collective-permute-start.33 = (bf16[256,512]{1,0:T(8,128)(2,1)S(1)}, bf16[256,512]{1,0:T(8,128)(2,1)S(1)}, u32[]{:S(2)}, u32[]{:S(2)}) collective-permute-start(bf16[256,512]{1,0:T(8,128)(2,1)S(1)} %shard_map.223.refs_3_.refs_0_), channel_id=1, source_target_pairs={{0,8},{1,17},{2,10},{3,19},{4,12},{5,21},{6,14},{7,23},{8,0},{9,25... | collective-permute-start | bytes 786440 | tf_op jit(solution)/shard_map/ppermute | solution.py:584
  81.5 1.0 %collective-permute-done.28.refs_1_ = bf16[48,512]{1,0:T(8,128)(2,1)S(1)} collective-permute-done((bf16[48,512]{1,0:T(8,128)(2,1)S(1)}, bf16[48,512]{1,0:T(8,128)(2,1)S(1)}, u32[]{:S(2)}, u32[]{:S(2)}) %collective-permute-start.28) | collective-permute-done | bytes 49184 | tf_op jit(solution)/shard_map/ppermute | solution.py:576
  82.6 2.2 %collective-permute-start.30 = (bf16[48,512]{1,0:T(8,128)(2,1)S(1)}, bf16[48,512]{1,0:T(8,128)(2,1)S(1)}, u32[]{:S(2)}, u32[]{:S(2)}) collective-permute-start(bf16[48,512]{1,0:T(8,128)(2,1)S(1)} %shard_map.224.refs_3_.refs_0_), channel_id=1, source_target_pairs={{0,8},{1,17},{2,10},{3,19},{4,12},{5,21},{6,14},{7,23},{8,0},{9,25... | collective-permute-start | bytes 147464 | tf_op jit(solution)/shard_map/ppermute | solution.py:584
  85.0 1.5 %shard_map.226 = (f32[8,128]{1,0:T(8,128)S(1)}, f32[512,2048]{1,0:T(8,128)}, f32[2048,512]{1,0:T(8,128)}) custom-call(bf16[1024,512]{1,0:T(8,128)(2,1)S(1)} %shard_map.225.refs_0_.refs_2_, s32[8,128]{1,0:T(8,128)S(1)} %get-tuple-element.127.refs_13_.refs_5_.refs_8_.refs_2_.refs_9_.refs_6_.refs_1_, bf16[1024,512]{1,0:T(8,128)(2,1)S(1)} %shard_map.225.refs_0_.refs_2_), custom_call_target="tpu_custom_call" | custom-call | flops 1 | bytes 1024 | tf_op jit(solution)/shard_map/pallas_call | solution.py:161
  86.4 0.6 collective-permute-done.33.refs_1_
  87.1 1.8 %collective-permute-start.35 = (bf16[512,512]{1,0:T(8,128)(2,1)S(1)}, bf16[512,512]{1,0:T(8,128)(2,1)S(1)}, u32[]{:S(2)}, u32[]{:S(2)}) collective-permute-start(bf16[512,512]{1,0:T(8,128)(2,1)S(1)} %shard_map.227.refs_2_.refs_0_), channel_id=1, source_target_pairs={{0,16},{1,9},{2,18},{3,11},{4,20},{5,13},{6,22},{7,15},{8,24},{9,1... | collective-permute-start | bytes 1572872 | tf_op jit(solution)/shard_map/ppermute | solution.py:584
  88.9 1.5 %shard_map.228 = (f32[8,128]{1,0:T(8,128)S(1)}, f32[512,2048]{1,0:T(8,128)}, f32[2048,512]{1,0:T(8,128)}) custom-call(bf16[1024,512]{1,0:T(8,128)(2,1)S(1)} %collective-permute-done.32.refs_0_, s32[8,128]{1,0:T(8,128)S(1)} %get-tuple-element.127.refs_13_.refs_5_.refs_8_.refs_2_.refs_9_.refs_6_.refs_1_, ...), custom_call_target="tpu_custom_call", output_to_operand_aliasing={{1}: (3, {}), {2}: (4, {})} | custom-call | flops 1 | bytes 1024 | tf_op jit(solution)/shard_map/pallas_call | solution.py:161
  90.4 0.3 collective-permute-start.34
  90.8 5.6 %collective-permute-done.35.refs_1_ = bf16[512,512]{1,0:T(8,128)(2,1)S(1)} collective-permute-done((bf16[512,512]{1,0:T(8,128)(2,1)S(1)}, bf16[512,512]{1,0:T(8,128)(2,1)S(1)}, u32[]{:S(2)}, u32[]{:S(2)}) %collective-permute-start.35) | collective-permute-done | bytes 524320 | tf_op jit(solution)/shard_map/ppermute | solution.py:584
  96.5 1.5 %shard_map.231 = (f32[8,128]{1,0:T(8,128)S(1)}, f32[512,2048]{1,0:T(8,128)}, f32[2048,512]{1,0:T(8,128)}) custom-call(bf16[1024,512]{1,0:T(8,128)(2,1)S(1)} %shard_map.230.refs_0_.refs_2_, s32[8,128]{1,0:T(8,128)S(1)} %get-tuple-element.127.refs_13_.refs_5_.refs_8_.refs_2_.refs_9_.refs_6_.refs_1_, ...), custom_call_target="tpu_custom_call", output_to_operand_aliasing={{1}: (3, {}), {2}: (4, {})} | custom-call | flops 1 | bytes 1024 | tf_op jit(solution)/shard_map/pallas_call | solution.py:161
  98.1 0.6 collective-permute-start.36
  98.6 0.5 collective-permute-done.37.refs_0_
  99.2 1.5 %shard_map.233 = (f32[8,128]{1,0:T(8,128)S(1)}, f32[512,2048]{1,0:T(8,128)}, f32[2048,512]{1,0:T(8,128)}) custom-call(bf16[1024,512]{1,0:T(8,128)(2,1)S(1)} %collective-permute-done.37.refs_0_, s32[8,128]{1,0:T(8,128)S(1)} %get-tuple-element.127.refs_13_.refs_5_.refs_8_.refs_2_.refs_9_.refs_6_.refs_1_, ...), custom_call_target="tpu_custom_call", output_to_operand_aliasing={{1}: (3, {}), {2}: (4, {})} | custom-call | flops 1 | bytes 1024 | tf_op jit(solution)/shard_map/pallas_call | solution.py:161
  100.7 0.9 shard_map.234
  (58 shorter events, 1.7 us)
Async XLA Ops:
  1.5 12.0 %collective-permute-start.1 = (bf16[64,512]{1,0:T(8,128)(2,1)S(1)}, bf16[64,512]{1,0:T(8,128)(2,1)S(1)}, u32[]{:S(2)}, u32[]{:S(2)}) collective-permute-start(bf16[64,512]{1,0:T(8,128)(2,1)S(1)} %fusion), channel_id=1, source_target_pairs={{0,4},{2,6},{4,0},{6,2},{1,5},{3,7},{5,1},{7,3},{8,12},{10,14},{12... | collective-permute-start | bytes 196616 | tf_op jit(solution)/shard_map/ppermute | solution.py:557
  5.6 7.9 %collective-permute-start = (bf16[64,512]{1,0:T(8,128)(2,1)S(1)}, bf16[64,512]{1,0:T(8,128)(2,1)S(1)}, u32[]{:S(2)}, u32[]{:S(2)}) collective-permute-start(bf16[64,512]{1,0:T(8,128)(2,1)S(1)} %fusion), channel_id=1, source_target_pairs={{0,2},{2,0},{4,6},{6,4},{1,3},{3,1},{5,7},{7,5},{8,10},{10,8},{12,... | collective-permute-start | bytes 196616 | tf_op jit(solution)/shard_map/ppermute | solution.py:557
  7.2 6.4 %collective-permute-start.2 = (bf16[64,512]{1,0:T(8,128)(2,1)S(1)}, bf16[64,512]{1,0:T(8,128)(2,1)S(1)}, u32[]{:S(2)}, u32[]{:S(2)}) collective-permute-start(bf16[64,512]{1,0:T(8,128)(2,1)S(1)} %fusion), channel_id=1, source_target_pairs={{0,6},{2,4},{4,2},{6,0},{1,7},{3,5},{5,3},{7,1},{8,14},{10,12},{12... | collective-permute-start | bytes 196616 | tf_op jit(solution)/shard_map/ppermute | solution.py:557
  10.9 4.2 %copy-start = (bf16[2048,512]{1,0:T(8,128)(2,1)}, bf16[2048,512]{1,0:T(8,128)(2,1)S(1)}, u32[]{:S(2)}) copy-start(bf16[2048,512]{1,0:T(8,128)(2,1)S(1)} %get-tuple-element.114.refs_1_) | copy-start | bytes 6291460
  13.6 1.5 %collective-permute-start.3 = (bf16[192,512]{1,0:T(8,128)(2,1)S(1)}, bf16[192,512]{1,0:T(8,128)(2,1)S(1)}, u32[]{:S(2)}, u32[]{:S(2)}) collective-permute-start(bf16[192,512]{1,0:T(8,128)(2,1)S(1)} %shard_map.197.refs_0_.refs_14_), channel_id=1, source_target_pairs={{0,1},{1,0},{2,3},{3,2},{4,5},{5,4},{6,7},{7,6},{8,9},{9,8},{10,11... | collective-permute-start | bytes 589832 | tf_op jit(solution)/shard_map/ppermute | solution.py:557
  21.3 7.7 %collective-permute-start.4 = (bf16[256,512]{1,0:T(8,128)(2,1)S(1)}, bf16[256,512]{1,0:T(8,128)(2,1)S(1)}, u32[]{:S(2)}, u32[]{:S(2)}) collective-permute-start(bf16[256,512]{1,0:T(8,128)(2,1)S(1)} %get-tuple-element.141), channel_id=1, source_target_pairs={{0,1},{1,0},{2,3},{3,2},{4,5},{5,4},{6,7},{7,6},{8,9},{9,8},{10,11... | collective-permute-start | bytes 786440 | tf_op jit(solution)/shard_map/ppermute | solution.py:557
  21.6 7.5 %collective-permute-start.5 = (bf16[256,512]{1,0:T(8,128)(2,1)S(1)}, bf16[256,512]{1,0:T(8,128)(2,1)S(1)}, u32[]{:S(2)}, u32[]{:S(2)}) collective-permute-start(bf16[256,512]{1,0:T(8,128)(2,1)S(1)} %get-tuple-element.142), channel_id=1, source_target_pairs={{0,1},{1,0},{2,3},{3,2},{4,5},{5,4},{6,7},{7,6},{8,9},{9,8},{10,11... | collective-permute-start | bytes 786440 | tf_op jit(solution)/shard_map/ppermute | solution.py:557
  25.3 3.8 %collective-permute-start.6 = (bf16[256,512]{1,0:T(8,128)(2,1)S(1)}, bf16[256,512]{1,0:T(8,128)(2,1)S(1)}, u32[]{:S(2)}, u32[]{:S(2)}) collective-permute-start(bf16[256,512]{1,0:T(8,128)(2,1)S(1)} %get-tuple-element.143), channel_id=1, source_target_pairs={{0,1},{1,0},{2,3},{3,2},{4,5},{5,4},{6,7},{7,6},{8,9},{9,8},{10,11... | collective-permute-start | bytes 786440 | tf_op jit(solution)/shard_map/ppermute | solution.py:557
  25.5 3.6 %collective-permute-start.7 = (bf16[256,512]{1,0:T(8,128)(2,1)S(1)}, bf16[256,512]{1,0:T(8,128)(2,1)S(1)}, u32[]{:S(2)}, u32[]{:S(2)}) collective-permute-start(bf16[256,512]{1,0:T(8,128)(2,1)S(1)} %get-tuple-element.144), channel_id=1, source_target_pairs={{0,1},{1,0},{2,3},{3,2},{4,5},{5,4},{6,7},{7,6},{8,9},{9,8},{10,11... | collective-permute-start | bytes 786440 | tf_op jit(solution)/shard_map/ppermute | solution.py:557
  29.5 9.3 %collective-permute-start.8 = (bf16[512,512]{1,0:T(8,128)(2,1)S(1)}, bf16[512,512]{1,0:T(8,128)(2,1)S(1)}, u32[]{:S(2)}, u32[]{:S(2)}) collective-permute-start(bf16[512,512]{1,0:T(8,128)(2,1)S(1)} %get-tuple-element.146.refs_6_), channel_id=1, source_target_pairs={{0,8},{1,17},{2,10},{3,19},{4,12},{5,21},{6,14},{7,23},{8,0},{9,25... | collective-permute-start | bytes 1572872 | tf_op jit(solution)/shard_map/ppermute | solution.py:584
  31.3 9.5 %collective-permute-start.10 = (bf16[256,512]{1,0:T(8,128)(2,1)S(1)}, bf16[256,512]{1,0:T(8,128)(2,1)S(1)}, u32[]{:S(2)}, u32[]{:S(2)}) collective-permute-start(bf16[256,512]{1,0:T(8,128)(2,1)S(1)} %get-tuple-element.164), channel_id=1, source_target_pairs={{0,1},{1,0},{2,3},{3,2},{4,5},{5,4},{6,7},{7,6},{8,9},{9,8},{10,11... | collective-permute-start | bytes 786440 | tf_op jit(solution)/shard_map/ppermute | solution.py:557
  31.3 9.5 %collective-permute-start.11 = (bf16[256,512]{1,0:T(8,128)(2,1)S(1)}, bf16[256,512]{1,0:T(8,128)(2,1)S(1)}, u32[]{:S(2)}, u32[]{:S(2)}) collective-permute-start(bf16[256,512]{1,0:T(8,128)(2,1)S(1)} %get-tuple-element.165), channel_id=1, source_target_pairs={{0,1},{1,0},{2,3},{3,2},{4,5},{5,4},{6,7},{7,6},{8,9},{9,8},{10,11... | collective-permute-start | bytes 786440 | tf_op jit(solution)/shard_map/ppermute | solution.py:557
  35.0 5.7 %collective-permute-start.12 = (bf16[256,512]{1,0:T(8,128)(2,1)S(1)}, bf16[256,512]{1,0:T(8,128)(2,1)S(1)}, u32[]{:S(2)}, u32[]{:S(2)}) collective-permute-start(bf16[256,512]{1,0:T(8,128)(2,1)S(1)} %get-tuple-element.166), channel_id=1, source_target_pairs={{0,1},{1,0},{2,3},{3,2},{4,5},{5,4},{6,7},{7,6},{8,9},{9,8},{10,11... | collective-permute-start | bytes 786440 | tf_op jit(solution)/shard_map/ppermute | solution.py:557
  35.1 5.7 %collective-permute-start.13 = (bf16[256,512]{1,0:T(8,128)(2,1)S(1)}, bf16[256,512]{1,0:T(8,128)(2,1)S(1)}, u32[]{:S(2)}, u32[]{:S(2)}) collective-permute-start(bf16[256,512]{1,0:T(8,128)(2,1)S(1)} %get-tuple-element.167), channel_id=1, source_target_pairs={{0,1},{1,0},{2,3},{3,2},{4,5},{5,4},{6,7},{7,6},{8,9},{9,8},{10,11... | collective-permute-start | bytes 786440 | tf_op jit(solution)/shard_map/ppermute | solution.py:557
  39.0 6.4 %collective-permute-start.9 = (bf16[256,512]{1,0:T(8,128)(2,1)S(1)}, bf16[256,512]{1,0:T(8,128)(2,1)S(1)}, u32[]{:S(2)}, u32[]{:S(2)}) collective-permute-start(bf16[256,512]{1,0:T(8,128)(2,1)S(1)} %get-tuple-element.156.refs_9_), channel_id=1, source_target_pairs={{0,16},{1,9},{2,18},{3,11},{4,20},{5,13},{6,22},{7,15},{8,24},{9,1... | collective-permute-start | bytes 786440 | tf_op jit(solution)/shard_map/ppermute | solution.py:584
  41.1 9.9 %collective-permute-start.15 = (bf16[512,512]{1,0:T(8,128)(2,1)S(1)}, bf16[512,512]{1,0:T(8,128)(2,1)S(1)}, u32[]{:S(2)}, u32[]{:S(2)}) collective-permute-start(bf16[512,512]{1,0:T(8,128)(2,1)S(1)} %get-tuple-element.168.refs_12_), channel_id=1, source_target_pairs={{0,16},{1,9},{2,18},{3,11},{4,20},{5,13},{6,22},{7,15},{8,24},{9,1... | collective-permute-start | bytes 1572872 | tf_op jit(solution)/shard_map/ppermute | solution.py:584
  45.5 7.4 %collective-permute-start.14 = (bf16[128,512]{1,0:T(8,128)(2,1)S(1)}, bf16[128,512]{1,0:T(8,128)(2,1)S(1)}, u32[]{:S(2)}, u32[]{:S(2)}) collective-permute-start(bf16[128,512]{1,0:T(8,128)(2,1)S(1)} %get-tuple-element.171.refs_10_), channel_id=1, source_target_pairs={{0,2},{2,0},{4,6},{6,4},{1,3},{3,1},{5,7},{7,5},{8,10},{10,8},{12,... | collective-permute-start | bytes 393224 | tf_op jit(solution)/shard_map/ppermute | solution.py:576
  49.4 11.1 %collective-permute-start.16 = (bf16[128,512]{1,0:T(8,128)(2,1)S(1)}, bf16[128,512]{1,0:T(8,128)(2,1)S(1)}, u32[]{:S(2)}, u32[]{:S(2)}) collective-permute-start(bf16[128,512]{1,0:T(8,128)(2,1)S(1)} %get-tuple-element.183), channel_id=1, source_target_pairs={{0,1},{1,0},{2,3},{3,2},{4,5},{5,4},{6,7},{7,6},{8,9},{9,8},{10,11... | collective-permute-start | bytes 393224 | tf_op jit(solution)/shard_map/ppermute | solution.py:557
  49.4 11.1 %collective-permute-start.17 = (bf16[128,512]{1,0:T(8,128)(2,1)S(1)}, bf16[128,512]{1,0:T(8,128)(2,1)S(1)}, u32[]{:S(2)}, u32[]{:S(2)}) collective-permute-start(bf16[128,512]{1,0:T(8,128)(2,1)S(1)} %get-tuple-element.184), channel_id=1, source_target_pairs={{0,1},{1,0},{2,3},{3,2},{4,5},{5,4},{6,7},{7,6},{8,9},{9,8},{10,11... | collective-permute-start | bytes 393224 | tf_op jit(solution)/shard_map/ppermute | solution.py:557
  49.9 10.6 %collective-permute-start.18 = (bf16[128,512]{1,0:T(8,128)(2,1)S(1)}, bf16[128,512]{1,0:T(8,128)(2,1)S(1)}, u32[]{:S(2)}, u32[]{:S(2)}) collective-permute-start(bf16[128,512]{1,0:T(8,128)(2,1)S(1)} %get-tuple-element.185), channel_id=1, source_target_pairs={{0,1},{1,0},{2,3},{3,2},{4,5},{5,4},{6,7},{7,6},{8,9},{9,8},{10,11... | collective-permute-start | bytes 393224 | tf_op jit(solution)/shard_map/ppermute | solution.py:557
  51.2 7.3 %collective-permute-start.19 = (bf16[256,512]{1,0:T(8,128)(2,1)S(1)}, bf16[256,512]{1,0:T(8,128)(2,1)S(1)}, u32[]{:S(2)}, u32[]{:S(2)}) collective-permute-start(bf16[256,512]{1,0:T(8,128)(2,1)S(1)} %get-tuple-element.178.refs_3_), channel_id=1, source_target_pairs={{0,8},{1,17},{2,10},{3,19},{4,12},{5,21},{6,14},{7,23},{8,0},{9,25... | collective-permute-start | bytes 786440 | tf_op jit(solution)/shard_map/ppermute | solution.py:584
  52.9 2.4 %copy-start.1 = (bf16[2048,512]{1,0:T(8,128)(2,1)S(1)}, bf16[2048,512]{1,0:T(8,128)(2,1)}, u32[]{:S(2)}) copy-start(bf16[2048,512]{1,0:T(8,128)(2,1)} %copy-done) | copy-start | bytes 6291460
  52.9 9.3 %collective-permute-start.22 = (bf16[128,512]{1,0:T(8,128)(2,1)S(1)}, bf16[128,512]{1,0:T(8,128)(2,1)S(1)}, u32[]{:S(2)}, u32[]{:S(2)}) collective-permute-start(bf16[128,512]{1,0:T(8,128)(2,1)S(1)} %shard_map.211.refs_6_.refs_0_), channel_id=1, source_target_pairs={{0,4},{2,6},{4,0},{6,2},{1,5},{3,7},{5,1},{7,3},{8,12},{10,14},{12... | collective-permute-start | bytes 393224 | tf_op jit(solution)/shard_map/ppermute | solution.py:576
  58.6 6.2 %collective-permute-start.21 = (bf16[128,512]{1,0:T(8,128)(2,1)S(1)}, bf16[128,512]{1,0:T(8,128)(2,1)S(1)}, u32[]{:S(2)}, u32[]{:S(2)}) collective-permute-start(bf16[128,512]{1,0:T(8,128)(2,1)S(1)} %get-tuple-element.188.refs_7_), channel_id=1, source_target_pairs={{0,2},{2,0},{4,6},{6,4},{1,3},{3,1},{5,7},{7,5},{8,10},{10,8},{12,... | collective-permute-start | bytes 393224 | tf_op jit(solution)/shard_map/ppermute | solution.py:576
  60.7 5.9 %collective-permute-start.20 = (bf16[192,512]{1,0:T(8,128)(2,1)S(1)}, bf16[192,512]{1,0:T(8,128)(2,1)S(1)}, u32[]{:S(2)}, u32[]{:S(2)}) collective-permute-start(bf16[192,512]{1,0:T(8,128)(2,1)S(1)} %get-tuple-element.190.refs_3_), channel_id=1, source_target_pairs={{0,16},{1,9},{2,18},{3,11},{4,20},{5,13},{6,22},{7,15},{8,24},{9,1... | collective-permute-start | bytes 589832 | tf_op jit(solution)/shard_map/ppermute | solution.py:584
  62.3 6.1 %collective-permute-start.24 = (bf16[128,512]{1,0:T(8,128)(2,1)S(1)}, bf16[128,512]{1,0:T(8,128)(2,1)S(1)}, u32[]{:S(2)}, u32[]{:S(2)}) collective-permute-start(bf16[128,512]{1,0:T(8,128)(2,1)S(1)} %shard_map.215.refs_3_.refs_0_), channel_id=1, source_target_pairs={{0,2},{2,0},{4,6},{6,4},{1,3},{3,1},{5,7},{7,5},{8,10},{10,8},{12,... | collective-permute-start | bytes 393224 | tf_op jit(solution)/shard_map/ppermute | solution.py:576
  64.8 9.7 %collective-permute-start.27 = (bf16[128,512]{1,0:T(8,128)(2,1)S(1)}, bf16[128,512]{1,0:T(8,128)(2,1)S(1)}, u32[]{:S(2)}, u32[]{:S(2)}) collective-permute-start(bf16[128,512]{1,0:T(8,128)(2,1)S(1)} %shard_map.216.refs_3_.refs_0_), channel_id=1, source_target_pairs={{0,4},{2,6},{4,0},{6,2},{1,5},{3,7},{5,1},{7,3},{8,12},{10,14},{12... | collective-permute-start | bytes 393224 | tf_op jit(solution)/shard_map/ppermute | solution.py:576
  66.6 5.7 %collective-permute-start.23 = (bf16[96,512]{1,0:T(8,128)(2,1)S(1)}, bf16[96,512]{1,0:T(8,128)(2,1)S(1)}, u32[]{:S(2)}, u32[]{:S(2)}) collective-permute-start(bf16[96,512]{1,0:T(8,128)(2,1)S(1)} %get-tuple-element.193.refs_3_), channel_id=1, source_target_pairs={{0,8},{1,17},{2,10},{3,19},{4,12},{5,21},{6,14},{7,23},{8,0},{9,25... | collective-permute-start | bytes 294920 | tf_op jit(solution)/shard_map/ppermute | solution.py:584
  68.5 6.4 %collective-permute-start.26 = (bf16[256,512]{1,0:T(8,128)(2,1)S(1)}, bf16[256,512]{1,0:T(8,128)(2,1)S(1)}, u32[]{:S(2)}, u32[]{:S(2)}) collective-permute-start(bf16[256,512]{1,0:T(8,128)(2,1)S(1)} %shard_map.218.refs_3_.refs_0_), channel_id=1, source_target_pairs={{0,16},{1,9},{2,18},{3,11},{4,20},{5,13},{6,22},{7,15},{8,24},{9,1... | collective-permute-start | bytes 786440 | tf_op jit(solution)/shard_map/ppermute | solution.py:584
  72.4 5.0 %collective-permute-start.25 = (bf16[64,512]{1,0:T(8,128)(2,1)S(1)}, bf16[64,512]{1,0:T(8,128)(2,1)S(1)}, u32[]{:S(2)}, u32[]{:S(2)}) collective-permute-start(bf16[64,512]{1,0:T(8,128)(2,1)S(1)} %get-tuple-element.195.refs_3_), channel_id=1, source_target_pairs={{0,2},{2,0},{4,6},{6,4},{1,3},{3,1},{5,7},{7,5},{8,10},{10,8},{12,... | collective-permute-start | bytes 196616 | tf_op jit(solution)/shard_map/ppermute | solution.py:576
  74.5 5.4 %collective-permute-start.29 = (bf16[128,512]{1,0:T(8,128)(2,1)S(1)}, bf16[128,512]{1,0:T(8,128)(2,1)S(1)}, u32[]{:S(2)}, u32[]{:S(2)}) collective-permute-start(bf16[128,512]{1,0:T(8,128)(2,1)S(1)} %shard_map.220.refs_3_.refs_0_), channel_id=1, source_target_pairs={{0,2},{2,0},{4,6},{6,4},{1,3},{3,1},{5,7},{7,5},{8,10},{10,8},{12,... | collective-permute-start | bytes 393224 | tf_op jit(solution)/shard_map/ppermute | solution.py:576
  75.0 9.8 %collective-permute-start.31 = (bf16[512,512]{1,0:T(8,128)(2,1)S(1)}, bf16[512,512]{1,0:T(8,128)(2,1)S(1)}, u32[]{:S(2)}, u32[]{:S(2)}) collective-permute-start(bf16[512,512]{1,0:T(8,128)(2,1)S(1)} %shard_map.221.refs_3_.refs_0_), channel_id=1, source_target_pairs={{0,8},{1,17},{2,10},{3,19},{4,12},{5,21},{6,14},{7,23},{8,0},{9,25... | collective-permute-start | bytes 1572872 | tf_op jit(solution)/shard_map/ppermute | solution.py:584
  77.5 5.1 %collective-permute-start.28 = (bf16[48,512]{1,0:T(8,128)(2,1)S(1)}, bf16[48,512]{1,0:T(8,128)(2,1)S(1)}, u32[]{:S(2)}, u32[]{:S(2)}) collective-permute-start(bf16[48,512]{1,0:T(8,128)(2,1)S(1)} %get-tuple-element.197.refs_3_), channel_id=1, source_target_pairs={{0,4},{2,6},{4,0},{6,2},{1,5},{3,7},{5,1},{7,3},{8,12},{10,14},{12... | collective-permute-start | bytes 147464 | tf_op jit(solution)/shard_map/ppermute | solution.py:576
  80.0 7.0 %collective-permute-start.33 = (bf16[256,512]{1,0:T(8,128)(2,1)S(1)}, bf16[256,512]{1,0:T(8,128)(2,1)S(1)}, u32[]{:S(2)}, u32[]{:S(2)}) collective-permute-start(bf16[256,512]{1,0:T(8,128)(2,1)S(1)} %shard_map.223.refs_3_.refs_0_), channel_id=1, source_target_pairs={{0,8},{1,17},{2,10},{3,19},{4,12},{5,21},{6,14},{7,23},{8,0},{9,25... | collective-permute-start | bytes 786440 | tf_op jit(solution)/shard_map/ppermute | solution.py:584
  82.6 7.8 %collective-permute-start.30 = (bf16[48,512]{1,0:T(8,128)(2,1)S(1)}, bf16[48,512]{1,0:T(8,128)(2,1)S(1)}, u32[]{:S(2)}, u32[]{:S(2)}) collective-permute-start(bf16[48,512]{1,0:T(8,128)(2,1)S(1)} %shard_map.224.refs_3_.refs_0_), channel_id=1, source_target_pairs={{0,8},{1,17},{2,10},{3,19},{4,12},{5,21},{6,14},{7,23},{8,0},{9,25... | collective-permute-start | bytes 147464 | tf_op jit(solution)/shard_map/ppermute | solution.py:584
  84.9 4.0 %collective-permute-start.32 = (bf16[1024,512]{1,0:T(8,128)(2,1)S(1)}, bf16[1024,512]{1,0:T(8,128)(2,1)S(1)}, u32[]{:S(2)}, u32[]{:S(2)}) collective-permute-start(bf16[1024,512]{1,0:T(8,128)(2,1)S(1)} %shard_map.225.refs_0_.refs_2_), channel_id=1, source_target_pairs={{0,1},{1,0},{2,3},{3,2},{4,5},{5,4},{6,7},{7,6},{8,9},{9,8},{10,11... | collective-permute-start | bytes 3145736 | tf_op jit(solution)/shard_map/ppermute | solution.py:557
  87.1 9.2 %collective-permute-start.35 = (bf16[512,512]{1,0:T(8,128)(2,1)S(1)}, bf16[512,512]{1,0:T(8,128)(2,1)S(1)}, u32[]{:S(2)}, u32[]{:S(2)}) collective-permute-start(bf16[512,512]{1,0:T(8,128)(2,1)S(1)} %shard_map.227.refs_2_.refs_0_), channel_id=1, source_target_pairs={{0,16},{1,9},{2,18},{3,11},{4,20},{5,13},{6,22},{7,15},{8,24},{9,1... | collective-permute-start | bytes 1572872 | tf_op jit(solution)/shard_map/ppermute | solution.py:584
  90.4 7.6 %collective-permute-start.34 = (bf16[96,512]{1,0:T(8,128)(2,1)S(1)}, bf16[96,512]{1,0:T(8,128)(2,1)S(1)}, u32[]{:S(2)}, u32[]{:S(2)}) collective-permute-start(bf16[96,512]{1,0:T(8,128)(2,1)S(1)} %shard_map.229.refs_3_.refs_0_), channel_id=1, source_target_pairs={{0,16},{1,9},{2,18},{3,11},{4,20},{5,13},{6,22},{7,15},{8,24},{9,1... | collective-permute-start | bytes 294920 | tf_op jit(solution)/shard_map/ppermute | solution.py:584
  96.5 2.7 %collective-permute-start.37 = (bf16[1024,512]{1,0:T(8,128)(2,1)S(1)}, bf16[1024,512]{1,0:T(8,128)(2,1)S(1)}, u32[]{:S(2)}, u32[]{:S(2)}) collective-permute-start(bf16[1024,512]{1,0:T(8,128)(2,1)S(1)} %shard_map.230.refs_0_.refs_2_), channel_id=1, source_target_pairs={{0,1},{1,0},{2,3},{3,2},{4,5},{5,4},{6,7},{7,6},{8,9},{9,8},{10,11... | collective-permute-start | bytes 3145736 | tf_op jit(solution)/shard_map/ppermute | solution.py:557
  98.1 2.6 %collective-permute-start.36 = (bf16[192,512]{1,0:T(8,128)(2,1)S(1)}, bf16[192,512]{1,0:T(8,128)(2,1)S(1)}, u32[]{:S(2)}, u32[]{:S(2)}) collective-permute-start(bf16[192,512]{1,0:T(8,128)(2,1)S(1)} %shard_map.232.refs_2_.refs_0_), channel_id=1, source_target_pairs={{0,1},{1,0},{2,3},{3,2},{4,5},{5,4},{6,7},{7,6},{8,9},{9,8},{10,11... | collective-permute-start | bytes 589832 | tf_op jit(solution)/shard_map/ppermute | solution.py:557

commit v5 on v4

--- a/solution.py
+++ b/solution.py
@@ -12,14 +12,13 @@
 MASKED = -1e30
 BAND = 128
 ROWS = 256
-PIECE = 256
+PIECE = 512
 AXES = ("dp", "expert", "tok")
 GLUE = 23 * 10**9
-COPIES = 8
 WORK = 1
 ORDER = (
     "f", "A", "f", "a", "B", "n", "a", "b", "h", "a", "r", "b", "a", "o", "b", "t", "a", "b", "t",
-    "a", "t", "b", "a", "t", "b", "t", "a", "1", "b", "2", "t", "b", "3", "t", "4", "T",
+    "a", "t", "b", "a", "t", "b", "t", "b", "1", "t", "2", "t", "3", "T",
 )
 
 
@@ -79,7 +78,7 @@
 
     def call(
         self, kernel, operands, outs, fetched=(), scalars=(), scratch=(), room=2 << 20, weight=WORK,
-        sent=(), aliased=(), kept=(), numbers=(), delayed=0,
+        sent=(), aliased=(), kept=(), numbers=(), delayed=0, copies=8,
     ):
         n, f, s = len(operands), len(fetched) + len(kept), len(scalars)
         late = () if self.last is None else (self.last,)
@@ -155,7 +154,7 @@
         if f:
             extra.append(pltpu.SemaphoreType.DMA((f,)))
         if h:
-            extra.append(pltpu.SemaphoreType.DMA((COPIES,)))
+            extra.append(pltpu.SemaphoreType.DMA((copies,)))
         if numbers:
             extra += [pltpu.SMEM(numbers[0].shape, jnp.int32), pltpu.SemaphoreType.DMA((1,))]
         results = pl.pallas_call(
@@ -191,15 +190,12 @@
     spots_wait, xn_ref, kv_ref, kvt_ref, gates_ref, gt_ref, small_ref, sent_keep, gains_keep, keyid_ref,
     place_ref,
 ):
-    ln_ref, x_ref = ln_wait(), x_wait()
-    length = x_ref.shape[0]
+    ln_ref, ln_two_ref, sent_ref = ln_wait(), ln_two_wait(), sent_wait()
     gain = ln_ref[...]
     gains_keep[0:1, :] = gain
-    for start in range(0, length, ROWS):
-        rows = pl.ds(start, ROWS)
-        normalized, _ = normalize(x_ref[rows, :].astype(F32))
-        xn_ref[rows, :] = (normalized * gain).astype(BF)
-    normed = xn_ref[...]
+    gains_keep[1:2, :] = ln_two_ref[...]
+    sent_keep[...] = sent_ref[...].astype(F32)
+    column_ids(sent_keep, keyid_ref)
     wkv_ref, wr_ref, ids_ref = wkv_wait(), wr_wait(), ids_wait()
     pair = wkv_ref.shape[1]
     experts = wr_ref.shape[0]
@@ -207,6 +203,16 @@
     small_ref[pair:, :] = jnp.concatenate(
         [wr_ref[...].astype(F32), jnp.zeros((16 - experts, wr_ref.shape[1]), F32)], axis=0
     ).astype(BF)
+    spots_ref = spots_wait()
+    for i in range(spots_ref.shape[0]):
+        place_ref[i : i + 1, :] = jnp.full((1, place_ref.shape[1]), spots_ref[i], jnp.int32)
+    x_ref = x_wait()
+    length = x_ref.shape[0]
+    for start in range(0, length, ROWS):
+        rows = pl.ds(start, ROWS)
+        normalized, _ = normalize(x_ref[rows, :].astype(F32))
+        xn_ref[rows, :] = (normalized * gain).astype(BF)
+    normed = xn_ref[...]
     small = small_ref[...]
     both = nt(small, normed)
     kvt_ref[...] = both[:pair].astype(BF)
@@ -224,15 +230,8 @@
     total = functools.reduce(lambda a, b: a + b, raised)
     for route in range(choose):
         gates_ref[route : route + 1, :] = raised[route] / total
-    gains_keep[1:2, :] = ln_two_wait()[...]
-    sent_ref = sent_wait()
-    sent_keep[...] = sent_ref[...].astype(F32)
-    column_ids(sent_keep, keyid_ref)
     g_ref = g_wait()
     gt_ref[...] = g_ref[...].T
-    spots_ref = spots_wait()
-    for i in range(spots_ref.shape[0]):
-        place_ref[i : i + 1, :] = jnp.full((1, place_ref.shape[1]), spots_ref[i], jnp.int32)
 
 
 def upstream_kernel(g_ref, wout_ref, win_wait, ag_ref):
@@ -579,8 +578,11 @@
     for d in range(dp):
         for e in range(expert):
             for t in range(tok):
-                other = d ^ (1 << ((stage + t) % bits(dp)))
-                pairs.append(((d * expert + e) * tok + t, (other * expert + e) * tok + t))
+                if kind == "dp":
+                    there = (d ^ (1 << ((stage + t) % bits(dp)))) * expert + e
+                else:
+                    there = d * expert + (e ^ (1 << ((stage + t) % bits(expert))))
+                pairs.append(((d * expert + e) * tok + t, there * tok + t))
     return lax.ppermute(array, AXES, pairs)
 
 
@@ -616,8 +618,9 @@
 
 
 class Job:
-    def __init__(self, kind, views, key, row=0, count=0, each=0):
+    def __init__(self, kind, views, key, row=0, count=0, each=0, shared=False):
         self.kind, self.views, self.key, self.row = kind, views, key, row
+        self.shared = shared
         self.count, self.each = count, each
         rows = views[0].rows
         self.kept = rows // 2
@@ -742,8 +745,14 @@
                 others = exchange([send] * lax.axis_size("tok"), "tok")
             else:
                 others = [swap(send, key)]
+            more = []
+            if any(job.shared for job in jobs):
+                more = [exchange([a] * lax.axis_size("tok"), "tok") for a in (send, others[0])]
             for name, job, own, offset in zip(group, jobs, owns, offsets):
-                self.take(name, [own] + [View(other, offset, job.sent) for other in others])
+                views = [own] + [View(other, offset, job.sent) for other in others]
+                if job.shared:
+                    views = [views] + [[View(a, offset, job.sent) for a in same] for same in zip(*more)]
+                self.take(name, views)
 
     def finish(self, name):
         while name in self.walks:
@@ -763,16 +772,13 @@
         halved.append(key)
     for key in (order + experts)[len(halved) :]:
         views = yield Job("add", views, key)
-    views = [views]
-    for key in reversed(halved):
-        if len(views) == 1:
-            views = yield Job("add", views[0], key)
-        else:
-            views = yield Job("weave", views, key, place_row(before), count, each)
-            each *= 2
-        before = key
-    views = yield Job("weave", views, ("tok", 0), place_row(before), count, each)
-    return views
+    views = yield Job("add", views, halved[-1])
+    for before, key in zip(halved[:0:-1], halved[-2::-1]):
+        views = yield Job(
+            "weave", views, key, place_row(before), count, each, shared=key == order[0]
+        )
+        each *= 2
+    return views, order[0], count, each
 
 
 def tail_walk(views, experts, each, mirror):
@@ -800,36 +806,50 @@
     return views
 
 
-def place_part(line, place, view, turn, first, hidden, full, before):
-    rows, width = view.rows, view.array.shape[1]
-    many = hidden // width
-    block = rows // many
-
-    def kernel(part_ref, place_ref, _, wide_ref, send, gin_ref, gout_ref):
-        part = place_ref[0] ^ turn
-        for i in range(many):
-            span = slice(i * block, (i + 1) * block)
-            wide_ref[span, :] = part_ref[
-                view.start + i * block : view.start + (i + 1) * block, :
-            ].astype(F32)
-            column, at = first + i * width, part * block
-            to = pl.multiple_of(column + jnp.minimum(at, width - block), block)
-            row = pl.multiple_of(jnp.maximum(at - width, 0), block)
-            send(
-                wide_ref.at[span, :],
-                gout_ref.at[pl.ds(to, block), :],
-                gin_ref.at[pl.ds(row, block), column : column + width],
-                at < width,
-            )
+def place_parts(line, place, items, walk, first, width, full, before):
+    _, (_, phase), count, each = walk
+    peers, stages = lax.axis_size("tok"), bits(lax.axis_size("dp"))
+    share = 2 * width // peers
+    arrays = []
+    for view, _, _ in items:
+        if not any(view.array is a for a in arrays):
+            arrays.append(view.array)
+    n = len(arrays)
+
+    def kernel(*refs):
+        place_ref, _, wide_ref, send, gin_ref, gout_ref = refs[n:]
+        top = 0
+        for view, turn, far in items:
+            part_ref = refs[[view.array is a for a in arrays].index(True)]
+            part, bit = place_ref[0] ^ turn, place_ref[place_row(("dp", (phase + turn) % stages))]
+            if far:
+                bit = 1 - bit
+            for i in range(count):
+                span = slice(top, top + each)
+                top = top + each
+                wide_ref[span, :] = part_ref[
+                    view.start + i * each : view.start + (i + 1) * each, :
+                ].astype(F32)
+                base = 2 * i * each
+                column, at = first + base // share * width, part * share + base % share + bit * each
+                to = pl.multiple_of(column + jnp.minimum(at, width - each), each)
+                across = pl.multiple_of(jnp.maximum(at - width, 0), each)
+                send(
+                    wide_ref.at[span, :],
+                    gout_ref.at[pl.ds(to, each), :],
+                    gin_ref.at[pl.ds(across, each), column : column + width],
+                    at < width,
+                )
 
     _, *grads = line.call(
         kernel,
-        (view.array,),
+        arrays,
         (),
         scalars=(place,),
-        scratch=(sds((rows, width), F32),),
+        scratch=(sds((len(items) * count * each, width), F32),),
         sent=(sds((width, full), F32), sds((full, width), F32)),
         aliased=before,
+        copies=len(items) * count,
     )
     return tuple(grads)
 
@@ -1039,25 +1059,28 @@
             room=6 << 20,
         )
 
-    def place_one(name, turn):
-        if turn == 0:
-            made[name] = chains.finish(name)
-        views = made[name][:1] if turn == 0 else made[name][1:]
-        for view in views:
-            made["both"] = place_part(
-                line, place, view, turn, *spans[name], full, made.get("both", ())
-            )
-            turn += 1
+    def place_some(name, wanted):
+        walk = chains.finish(name)
+        items = [
+            (views[far], turn, far)
+            for far in (0, 1)
+            for turn, views in enumerate(walk[0])
+            if wanted(turn > 0, far == 1)
+        ]
+        made["both"] = place_parts(
+            line, place, items, walk, spans[name][0], width, full, made.get("both", ())
+        )
 
     def last():
         made["t"] = place_tail(line, place, chains.finish("t"), experts, head, misc)
 
     made = {}
     acts = {"f": ffn, "n": hidden, "h": heads_back, "r": rows_back, "o": out, "T": last}
-    for i, name in enumerate("abc"):
-        acts[name.upper()] = functools.partial(ffn, name, i % 2)
-        acts[str(2 * i + 1)] = functools.partial(place_one, name, 0)
-        acts[str(2 * i + 2)] = functools.partial(place_one, name, 1)
+    for i, name in enumerate("ab"):
+        acts[name.upper()] = functools.partial(ffn, name, i)
+    acts["1"] = lambda: place_some("a", lambda other, far: True)
+    acts["2"] = lambda: place_some("b", lambda other, far: not (other and far))
+    acts["3"] = lambda: place_some("b", lambda other, far: other and far)
     for word in ORDER:
         if word in acts:
             acts[word]()

time: 102 us -> 100 us (0.980)
  starting transfers between devices: 38.1 us -> 35.8 us
  waiting for transfers between devices: 17.7 us -> 19.9 us
  Pallas kernels: 43.7 us -> 42.4 us
    ppermute x12, waiting for transfers between devices: 10.5 us -> 12 us  [swap(): return lax.ppermute(array, AXES, pairs)]
    pallas_call x40 -> x37, Pallas kernels: 43.7 us -> 42.4 us  [call(): pl.pallas_call(wrapped, out_shape=outs + list(sent), in_specs=[pl.BlockSp...]
    ppermute x18 -> x16, starting transfers between devices: 9.33 us -> 8.23 us  [exchange(): lax.ppermute(parts[k], axis, [(i, i ^ k) for i in range(size)])]
  transfers between devices with their start and end apart: 38 -> 36, of which waited for: 12 -> 13; matrix products, arithmetic and copies ran while one was open for 0% -> 0% of each run, Pallas kernels for 36% -> 35%
where the time goes in v5:
time: 100 us
  Pallas kernels  42.4 us (42%)
  starting transfers between devices  35.8 us (36%)
  waiting for transfers between devices  19.9 us (20%)
  between operations  1 us (1%)
    pallas_call x37, Pallas kernels, call(): pl.pallas_call(wrapped, out_shape=outs + list(sent), in_specs=[pl.BlockSp...  42.4 us
    ppermute x12, starting transfers between devices, swap(): return lax.ppermute(array, AXES, pairs)  17.4 us
    ppermute x12, waiting for transfers between devices, swap(): return lax.ppermute(array, AXES, pairs)  12 us
    ppermute x8, starting transfers between devices, swap(): lax.ppermute(array, 'expert', [(i, i ^ 1 << stage) for i in range(size)])  10.2 us
    ppermute x16, starting transfers between devices, exchange(): lax.ppermute(parts[k], axis, [(i, i ^ k) for i in range(size)])  8.23 us
    ppermute x8, waiting for transfers between devices, swap(): lax.ppermute(array, 'expert', [(i, i ^ 1 << stage) for i in range(size)])  6.17 us
  transfers between devices with their start and end apart: 36, of which 13 were waited for; matrix products, arithmetic and copies ran while one was open for 0% of the time, Pallas kernels for 35%

profile of v5, /device:TPU:0, one launch (start us, length us, event | category | flops | bytes accessed | tf_op | source)
XLA Modules:
  0.0 100.0 jit_solution(2882386925258076759)
XLA Ops:
  0.6 0.9 fusion
  1.5 4.1 %collective-permute-start.1 = (bf16[64,512]{1,0:T(8,128)(2,1)S(1)}, bf16[64,512]{1,0:T(8,128)(2,1)S(1)}, u32[]{:S(2)}, u32[]{:S(2)}) collective-permute-start(bf16[64,512]{1,0:T(8,128)(2,1)S(1)} %fusion), channel_id=1, source_target_pairs={{0,4},{2,6},{4,0},{6,2},{1,5},{3,7},{5,1},{7,3},{8,12},{10,14},{12... | collective-permute-start | bytes 196616 | tf_op jit(solution)/shard_map/ppermute | solution.py:556
  5.6 1.6 %collective-permute-start = (bf16[64,512]{1,0:T(8,128)(2,1)S(1)}, bf16[64,512]{1,0:T(8,128)(2,1)S(1)}, u32[]{:S(2)}, u32[]{:S(2)}) collective-permute-start(bf16[64,512]{1,0:T(8,128)(2,1)S(1)} %fusion), channel_id=1, source_target_pairs={{0,2},{2,0},{4,6},{6,4},{1,3},{3,1},{5,7},{7,5},{8,10},{10,8},{12,... | collective-permute-start | bytes 196616 | tf_op jit(solution)/shard_map/ppermute | solution.py:556
  7.2 0.1 stack.27.refs_11_.refs_12_
  7.3 3.2 %shard_map.195 = (bf16[1024,512]{1,0:T(8,128)(2,1)S(1)}, bf16[1024,128]{1,0:T(8,128)(2,1)S(1)}, bf16[128,1024]{1,0:T(8,128)(2,1)S(1)}, f32[2,1024]{1,0:T(2,128)S...) custom-call(f32[1,512]{1,0:T(1,128)} %bitcast.24, ...), custom_call_target="tpu_custom_call" | custom-call | flops 1 | bytes 1024 | tf_op jit(solution)/shard_map/pallas_call | solution.py:160
  10.5 2.6 %shard_map.196 = (bf16[1024,2048]{1,0:T(8,128)(2,1)S(1)}, bf16[512,2048]{1,0:T(8,128)(2,1)S(1)}) custom-call(bf16[1024,512]{1,0:T(8,128)(2,1)S(1)} %get-tuple-element.102.refs_0_.refs_1_, bf16[2048,512]{1,0:T(8,128)(2,1)S(1)} %get-tuple-element.103.refs_1_, bf16[512,2048]{1,0:T(8,128)(2,1)} %refs_2_.1, f32[1,1024]{1,0:T(1,128)S(1)} %get-tuple-element.104.refs_3_.refs_8_.refs_10_), custom_call_target="tpu_custom_call" | custom-call | flops 1 | bytes 1024 | tf_op jit(solution)/shard_map/pallas_call | solution.py:160
  13.1 0.1 collective-permute-done.2.refs_2_
  13.4 1.4 %collective-permute-done.3.refs_1_ = bf16[192,512]{1,0:T(8,128)(2,1)S(1)} collective-permute-done((bf16[192,512]{1,0:T(8,128)(2,1)S(1)}, bf16[192,512]{1,0:T(8,128)(2,1)S(1)}, u32[]{:S(2)}, u32[]{:S(2)}) %collective-permute-start.3) | collective-permute-done | bytes 196640 | tf_op jit(solution)/shard_map/ppermute | solution.py:556
  14.8 3.0 %shard_map.198 = (bf16[256,512]{1,0:T(8,128)(2,1)S(1)}, bf16[256,512]{1,0:T(8,128)(2,1)S(1)}, bf16[64,2048]{1,0:T(8,128)(2,1)S(1)}, bf16[64,2048]{1,0:T(8,128)(2...) custom-call(bf16[192,512]{1,0:T(8,128)(2,1)S(1)} %shard_map.197.refs, ...), custom_call_target="tpu_custom_call" | custom-call | flops 1 | bytes 1024 | tf_op jit(solution)/shard_map/pallas_call | solution.py:160
  17.8 3.2 %shard_map.199 = (bf16[1024,512]{1,0:T(8,128)(2,1)S(1)}, bf16[1024,512]{1,0:T(8,128)(2,1)S(1)}, bf16[512,512]{1,0:T(8,128)(2,1)S(1)}, bf16[512,512]{1,0:T(8,128)(2,1)S(1)}) custom-call(bf16[1024,512]{1,0:T(8,128)(2,1)S(1)} %get-tuple-element.118.refs_0_, bf16[512,1024]{1,0:T(8,128)(2,1)S(1)} %get-tuple-element.119.refs_1_, ...), custom_call_target="tpu_custom_call" | custom-call | flops 1 | bytes 1024 | tf_op jit(solution)/shard_map/pallas_call | solution.py:160
  21.0 0.2 collective-permute-start.4
  21.2 3.4 %shard_map.200 = (bf16[1024,512]{1,0:T(8,128)(2,1)S(1)}, bf16[1024,512]{1,0:T(8,128)(2,1)S(1)}, bf16[512,512]{1,0:T(8,128)(2,1)S(1)}, bf16[512,512]{1,0:T(8,128)(2,1)S(1)}) custom-call(bf16[1024,512]{1,0:T(8,128)(2,1)S(1)} %get-tuple-element.118.refs_0_, bf16[512,1024]{1,0:T(8,128)(2,1)S(1)} %get-tuple-element.119.refs_1_, ...), custom_call_target="tpu_custom_call" | custom-call | flops 1 | bytes 1024 | tf_op jit(solution)/shard_map/pallas_call | solution.py:160
  24.6 0.4 collective-permute-start.5
  25.1 3.2 %shard_map.201 = (bf16[1024,512]{1,0:T(8,128)(2,1)S(1)}, bf16[1024,512]{1,0:T(8,128)(2,1)S(1)}, bf16[512,512]{1,0:T(8,128)(2,1)S(1)}, bf16[512,512]{1,0:T(8,128)(2,1)S(1)}) custom-call(bf16[1024,512]{1,0:T(8,128)(2,1)S(1)} %get-tuple-element.118.refs_0_, bf16[512,1024]{1,0:T(8,128)(2,1)S(1)} %get-tuple-element.119.refs_1_, ...), custom_call_target="tpu_custom_call" | custom-call | flops 1 | bytes 1024 | tf_op jit(solution)/shard_map/pallas_call | solution.py:160
  28.3 0.5 shard_map.202
  28.8 1.6 %collective-permute-start.6 = (bf16[512,512]{1,0:T(8,128)(2,1)S(1)}, bf16[512,512]{1,0:T(8,128)(2,1)S(1)}, u32[]{:S(2)}, u32[]{:S(2)}) collective-permute-start(bf16[512,512]{1,0:T(8,128)(2,1)S(1)} %get-tuple-element.131.refs_6_), channel_id=1, source_target_pairs={{0,8},{1,17},{2,10},{3,19},{4,12},{5,21},{6,14},{7,23},{8,0},{9,25... | collective-permute-start | bytes 1572872 | tf_op jit(solution)/shard_map/ppermute | solution.py:586
  30.4 3.2 %shard_map.203 = (bf16[1024,512]{1,0:T(8,128)(2,1)S(1)}, bf16[1024,512]{1,0:T(8,128)(2,1)S(1)}, bf16[512,512]{1,0:T(8,128)(2,1)S(1)}, bf16[512,512]{1,0:T(8,128)(2,1)S(1)}) custom-call(bf16[1024,512]{1,0:T(8,128)(2,1)S(1)} %get-tuple-element.118.refs_0_, bf16[512,1024]{1,0:T(8,128)(2,1)S(1)} %get-tuple-element.119.refs_1_, ...), custom_call_target="tpu_custom_call" | custom-call | flops 1 | bytes 1024 | tf_op jit(solution)/shard_map/pallas_call | solution.py:160
  33.6 0.6 collective-permute-start.9
  34.2 3.2 %shard_map.204 = (f32[1024,512]{1,0:T(8,128)S(1)}, bf16[1024,512]{1,0:T(8,128)(2,1)S(1)}, f32[1,512]{1,0:T(1,128)S(1)}) custom-call(f32[1024,512]{1,0:T(8,128)S(1)} %get-tuple-element.117.refs_0_, bf16[1024,512]{1,0:T(8,128)(2,1)S(1)} %get-tuple-element.102.refs_0_.refs_1_, bf16[512,2048]{1,0:T(8,128)(2,1)S(1)} %get-tuple-element.105.refs_3_.refs_4_.refs_2_, ...), custom_call_target="tpu_custom_call" | custom-call | flops 1 | bytes 1024 | tf_op jit(solution)/shard_map/pallas_call | solution.py:160
  37.4 0.6 collective-permute-done.6.refs_1_
  38.0 0.2 shard_map.205
  38.2 1.7 %collective-permute-start.7 = (bf16[256,512]{1,0:T(8,128)(2,1)S(1)}, bf16[256,512]{1,0:T(8,128)(2,1)S(1)}, u32[]{:S(2)}, u32[]{:S(2)}) collective-permute-start(bf16[256,512]{1,0:T(8,128)(2,1)S(1)} %get-tuple-element.141.refs_5_), channel_id=1, source_target_pairs={{0,16},{1,9},{2,18},{3,11},{4,20},{5,13},{6,22},{7,15},{8,24},{9,1... | collective-permute-start | bytes 786440 | tf_op jit(solution)/shard_map/ppermute | solution.py:586
  39.9 0.5 shard_map.206
  40.4 0.5 collective-permute-start.11
  40.9 3.1 %shard_map.207 = (bf16[400,1024]{1,0:T(8,128)(2,1)S(1)}, bf16[256,512]{1,0:T(8,128)(2,1)S(1)}) custom-call(bf16[1024,128]{1,0:T(8,128)(2,1)S(1)} %get-tuple-element.107.refs_3_.refs_0_, bf16[128,1024]{1,0:T(8,128)(2,1)S(1)} %get-tuple-element.108.refs_4_.refs_1_, f32[2,1024]{1,0:T(2,128)S(1)} %get-tuple-element.109.refs_5_.refs_2_, ...), custom_call_target="tpu_custom_call" | custom-call | flops 1 | bytes 1024 | tf_op jit(solution)/shard_map/pallas_call | solution.py:160
  44.0 0.7 collective-permute-done.7.refs_1_
  44.7 0.1 shard_map.208
  44.8 0.8 collective-permute-start.10
  45.6 2.9 %shard_map.209 = (bf16[128,512]{1,0:T(8,128)(2,1)S(1)}, bf16[128,512]{1,0:T(8,128)(2,1)S(1)}, bf16[128,512]{1,0:T(8,128)(2,1)S(1)}, bf16[128,512]{1,0:T(8,128)(2...) custom-call(bf16[400,1024]{1,0:T(8,128)(2,1)S(1)} %get-tuple-element.154.refs_0_, ...), custom_call_target="tpu_custom_call" | custom-call | flops 1 | bytes 1024 | tf_op jit(solution)/shard_map/pallas_call | solution.py:160
  48.6 0.5 collective-permute-start.13
  49.2 1.1 %collective-permute-done.11.refs_1_ = bf16[512,512]{1,0:T(8,128)(2,1)S(1)} collective-permute-done((bf16[512,512]{1,0:T(8,128)(2,1)S(1)}, bf16[512,512]{1,0:T(8,128)(2,1)S(1)}, u32[]{:S(2)}, u32[]{:S(2)}) %collective-permute-start.11) | collective-permute-done | bytes 524320 | tf_op jit(solution)/shard_map/ppermute | solution.py:586
  50.3 0.2 shard_map.210
  50.5 1.6 %collective-permute-start.15 = (bf16[256,512]{1,0:T(8,128)(2,1)S(1)}, bf16[256,512]{1,0:T(8,128)(2,1)S(1)}, u32[]{:S(2)}, u32[]{:S(2)}) collective-permute-start(bf16[256,512]{1,0:T(8,128)(2,1)S(1)} %get-tuple-element.159.refs_3_), channel_id=1, source_target_pairs={{0,8},{1,17},{2,10},{3,19},{4,12},{5,21},{6,14},{7,23},{8,0},{9,25... | collective-permute-start | bytes 786440 | tf_op jit(solution)/shard_map/ppermute | solution.py:586
  52.2 2.4 %collective-permute-start.18 = (bf16[128,512]{1,0:T(8,128)(2,1)S(1)}, bf16[128,512]{1,0:T(8,128)(2,1)S(1)}, u32[]{:S(2)}, u32[]{:S(2)}) collective-permute-start(bf16[128,512]{1,0:T(8,128)(2,1)S(1)} %shard_map.211.refs_6_.refs_0_), channel_id=1, source_target_pairs={{0,4},{2,6},{4,0},{6,2},{1,5},{3,7},{5,1},{7,3},{8,12},{10,14},{12... | collective-permute-start | bytes 393224 | tf_op jit(solution)/shard_map/ppermute | solution.py:575
  54.6 3.1 %shard_map.212 = (f32[8,128]{1,0:T(8,128)S(1)}, bf16[1024,512]{1,0:T(8,128)(2,1)}) custom-call(f32[1024,512]{1,0:T(8,128)S(1)} %get-tuple-element.117.refs_0_, bf16[2048,512]{1,0:T(8,128)(2,1)S(1)} %copy-done.1, bf16[1024,512]{1,0:T(8,128)(2,1)S(1)} %get-tuple-element.123.refs_2_, bf16[1024,512]{1,0:T(8,128)(2,1)S(1)} %get-tuple-element.125.refs_3_, ...), custom_call_target="tpu_custom_call" | custom-call | flops 1 | bytes 1024 | tf_op jit(solution)/shard_map/pallas_call | solution.py:160
  57.7 0.1 shard_map.213
  57.8 1.9 %collective-permute-start.17 = (bf16[128,512]{1,0:T(8,128)(2,1)S(1)}, bf16[128,512]{1,0:T(8,128)(2,1)S(1)}, u32[]{:S(2)}, u32[]{:S(2)}) collective-permute-start(bf16[128,512]{1,0:T(8,128)(2,1)S(1)} %get-tuple-element.169.refs_7_), channel_id=1, source_target_pairs={{0,2},{2,0},{4,6},{6,4},{1,3},{3,1},{5,7},{7,5},{8,10},{10,8},{12,... | collective-permute-start | bytes 393224 | tf_op jit(solution)/shard_map/ppermute | solution.py:575
  59.7 0.1 shard_map.214
  59.9 1.6 %collective-permute-start.16 = (bf16[192,512]{1,0:T(8,128)(2,1)S(1)}, bf16[192,512]{1,0:T(8,128)(2,1)S(1)}, u32[]{:S(2)}, u32[]{:S(2)}) collective-permute-start(bf16[192,512]{1,0:T(8,128)(2,1)S(1)} %get-tuple-element.171.refs_3_), channel_id=1, source_target_pairs={{0,16},{1,9},{2,18},{3,11},{4,20},{5,13},{6,22},{7,15},{8,24},{9,1... | collective-permute-start | bytes 589832 | tf_op jit(solution)/shard_map/ppermute | solution.py:586
  61.5 0.3 collective-permute-start.20
  61.8 2.2 %collective-permute-done.17.refs_1_ = bf16[128,512]{1,0:T(8,128)(2,1)S(1)} collective-permute-done((bf16[128,512]{1,0:T(8,128)(2,1)S(1)}, bf16[128,512]{1,0:T(8,128)(2,1)S(1)}, u32[]{:S(2)}, u32[]{:S(2)}) %collective-permute-start.17) | collective-permute-done | bytes 131104 | tf_op jit(solution)/shard_map/ppermute | solution.py:575
  64.0 1.9 %collective-permute-start.23 = (bf16[128,512]{1,0:T(8,128)(2,1)S(1)}, bf16[128,512]{1,0:T(8,128)(2,1)S(1)}, u32[]{:S(2)}, u32[]{:S(2)}) collective-permute-start(bf16[128,512]{1,0:T(8,128)(2,1)S(1)} %shard_map.216.refs_3_.refs_0_), channel_id=1, source_target_pairs={{0,4},{2,6},{4,0},{6,2},{1,5},{3,7},{5,1},{7,3},{8,12},{10,14},{12... | collective-permute-start | bytes 393224 | tf_op jit(solution)/shard_map/ppermute | solution.py:575
  66.0 0.1 shard_map.217
  66.0 1.6 %collective-permute-start.19 = (bf16[96,512]{1,0:T(8,128)(2,1)S(1)}, bf16[96,512]{1,0:T(8,128)(2,1)S(1)}, u32[]{:S(2)}, u32[]{:S(2)}) collective-permute-start(bf16[96,512]{1,0:T(8,128)(2,1)S(1)} %get-tuple-element.174.refs_3_), channel_id=1, source_target_pairs={{0,8},{1,17},{2,10},{3,19},{4,12},{5,21},{6,14},{7,23},{8,0},{9,25... | collective-permute-start | bytes 294920 | tf_op jit(solution)/shard_map/ppermute | solution.py:586
  67.7 1.6 %collective-permute-start.22 = (bf16[256,512]{1,0:T(8,128)(2,1)S(1)}, bf16[256,512]{1,0:T(8,128)(2,1)S(1)}, u32[]{:S(2)}, u32[]{:S(2)}) collective-permute-start(bf16[256,512]{1,0:T(8,128)(2,1)S(1)} %shard_map.218.refs_3_.refs_0_), channel_id=1, source_target_pairs={{0,16},{1,9},{2,18},{3,11},{4,20},{5,13},{6,22},{7,15},{8,24},{9,1... | collective-permute-start | bytes 786440 | tf_op jit(solution)/shard_map/ppermute | solution.py:586
  69.3 2.5 %collective-permute-done.19.refs_1_ = bf16[96,512]{1,0:T(8,128)(2,1)S(1)} collective-permute-done((bf16[96,512]{1,0:T(8,128)(2,1)S(1)}, bf16[96,512]{1,0:T(8,128)(2,1)S(1)}, u32[]{:S(2)}, u32[]{:S(2)}) %collective-permute-start.19) | collective-permute-done | bytes 98336 | tf_op jit(solution)/shard_map/ppermute | solution.py:586
  71.9 1.8 %collective-permute-start.21 = (bf16[64,512]{1,0:T(8,128)(2,1)S(1)}, bf16[64,512]{1,0:T(8,128)(2,1)S(1)}, u32[]{:S(2)}, u32[]{:S(2)}) collective-permute-start(bf16[64,512]{1,0:T(8,128)(2,1)S(1)} %get-tuple-element.176.refs_3_), channel_id=1, source_target_pairs={{0,2},{2,0},{4,6},{6,4},{1,3},{3,1},{5,7},{7,5},{8,10},{10,8},{12,... | collective-permute-start | bytes 196616 | tf_op jit(solution)/shard_map/ppermute | solution.py:575
  73.7 0.3 collective-permute-start.25
  74.2 1.5 %collective-permute-start.28 = (bf16[512,512]{1,0:T(8,128)(2,1)S(1)}, bf16[512,512]{1,0:T(8,128)(2,1)S(1)}, u32[]{:S(2)}, u32[]{:S(2)}) collective-permute-start(bf16[512,512]{1,0:T(8,128)(2,1)S(1)} %shard_map.221.refs_3_.refs_0_), channel_id=1, source_target_pairs={{0,8},{1,17},{2,10},{3,19},{4,12},{5,21},{6,14},{7,23},{8,0},{9,25... | collective-permute-start | bytes 1572872 | tf_op jit(solution)/shard_map/ppermute | solution.py:586
  75.7 1.1 %collective-permute-done.21.refs_1_ = bf16[64,512]{1,0:T(8,128)(2,1)S(1)} collective-permute-done((bf16[64,512]{1,0:T(8,128)(2,1)S(1)}, bf16[64,512]{1,0:T(8,128)(2,1)S(1)}, u32[]{:S(2)}, u32[]{:S(2)}) %collective-permute-start.21) | collective-permute-done | bytes 65568 | tf_op jit(solution)/shard_map/ppermute | solution.py:575
  76.9 0.8 collective-permute-start.24
  77.6 1.1 %collective-permute-done.25.refs_1_ = bf16[128,512]{1,0:T(8,128)(2,1)S(1)} collective-permute-done((bf16[128,512]{1,0:T(8,128)(2,1)S(1)}, bf16[128,512]{1,0:T(8,128)(2,1)S(1)}, u32[]{:S(2)}, u32[]{:S(2)}) %collective-permute-start.25) | collective-permute-done | bytes 131104 | tf_op jit(solution)/shard_map/ppermute | solution.py:575
  78.8 1.4 %collective-permute-start.30 = (bf16[256,512]{1,0:T(8,128)(2,1)S(1)}, bf16[256,512]{1,0:T(8,128)(2,1)S(1)}, u32[]{:S(2)}, u32[]{:S(2)}) collective-permute-start(bf16[256,512]{1,0:T(8,128)(2,1)S(1)} %shard_map.223.refs_3_.refs_0_), channel_id=1, source_target_pairs={{0,8},{1,17},{2,10},{3,19},{4,12},{5,21},{6,14},{7,23},{8,0},{9,25... | collective-permute-start | bytes 786440 | tf_op jit(solution)/shard_map/ppermute | solution.py:586
  80.2 1.7 %collective-permute-done.24.refs_1_ = bf16[48,512]{1,0:T(8,128)(2,1)S(1)} collective-permute-done((bf16[48,512]{1,0:T(8,128)(2,1)S(1)}, bf16[48,512]{1,0:T(8,128)(2,1)S(1)}, u32[]{:S(2)}, u32[]{:S(2)}) %collective-permute-start.24) | collective-permute-done | bytes 49184 | tf_op jit(solution)/shard_map/ppermute | solution.py:575
  81.9 2.1 %collective-permute-start.26 = (bf16[48,512]{1,0:T(8,128)(2,1)S(1)}, bf16[48,512]{1,0:T(8,128)(2,1)S(1)}, u32[]{:S(2)}, u32[]{:S(2)}) collective-permute-start(bf16[48,512]{1,0:T(8,128)(2,1)S(1)} %shard_map.224.refs_3_.refs_0_), channel_id=1, source_target_pairs={{0,8},{1,17},{2,10},{3,19},{4,12},{5,21},{6,14},{7,23},{8,0},{9,25... | collective-permute-start | bytes 147464 | tf_op jit(solution)/shard_map/ppermute | solution.py:586
  84.0 2.2 %collective-permute-done.30.refs_1_ = bf16[256,512]{1,0:T(8,128)(2,1)S(1)} collective-permute-done((bf16[256,512]{1,0:T(8,128)(2,1)S(1)}, bf16[256,512]{1,0:T(8,128)(2,1)S(1)}, u32[]{:S(2)}, u32[]{:S(2)}) %collective-permute-start.30) | collective-permute-done | bytes 262176 | tf_op jit(solution)/shard_map/ppermute | solution.py:586
  86.3 1.8 %collective-permute-start.33 = (bf16[512,512]{1,0:T(8,128)(2,1)S(1)}, bf16[512,512]{1,0:T(8,128)(2,1)S(1)}, u32[]{:S(2)}, u32[]{:S(2)}) collective-permute-start(bf16[512,512]{1,0:T(8,128)(2,1)S(1)} %shard_map.225.refs_5_.refs_0_), channel_id=1, source_target_pairs={{0,16},{1,9},{2,18},{3,11},{4,20},{5,13},{6,22},{7,15},{8,24},{9,1... | collective-permute-start | bytes 1572872 | tf_op jit(solution)/shard_map/ppermute | solution.py:586
  88.2 2.1 %shard_map.226 = (f32[8,128]{1,0:T(8,128)S(1)}, f32[512,2048]{1,0:T(8,128)}, f32[2048,512]{1,0:T(8,128)}) custom-call(bf16[512,512]{1,0:T(8,128)(2,1)S(1)} %shard_map.221.refs_3_.refs_0_, bf16[512,512]{1,0:T(8,128)(2,1)S(1)} %collective-permute-done.27.refs_1_, bf16[512,512]{1,0:T(8,128)(2,1)S(1)} %collective-permute-done.28.refs_2_, ...), custom_call_target="tpu_custom_call" | custom-call | flops 1 | bytes 1024 | tf_op jit(solution)/shard_map/pallas_call | solution.py:160
  90.4 0.3 collective-permute-start.31
  90.7 4.9 %collective-permute-done.33.refs_2_ = bf16[512,512]{1,0:T(8,128)(2,1)S(1)} collective-permute-done((bf16[512,512]{1,0:T(8,128)(2,1)S(1)}, bf16[512,512]{1,0:T(8,128)(2,1)S(1)}, u32[]{:S(2)}, u32[]{:S(2)}) %collective-permute-start.33) | collective-permute-done | bytes 524320 | tf_op jit(solution)/shard_map/ppermute | solution.py:586
  95.6 1.8 %shard_map.228 = (f32[8,128]{1,0:T(8,128)S(1)}, f32[512,2048]{1,0:T(8,128)}, f32[2048,512]{1,0:T(8,128)}) custom-call(bf16[512,512]{1,0:T(8,128)(2,1)S(1)} %shard_map.225.refs_5_.refs_0_, bf16[512,512]{1,0:T(8,128)(2,1)S(1)} %collective-permute-done.32.refs_1_, ...), custom_call_target="tpu_custom_call", output_to_operand_aliasing={{1}: (5, {}), {2}: (6, {})} | custom-call | flops 1 | bytes 1024 | tf_op jit(solution)/shard_map/pallas_call | solution.py:160
  97.4 0.6 collective-permute-start.34
  98.0 1.0 %shard_map.230 = (f32[8,128]{1,0:T(8,128)S(1)}, f32[512,2048]{1,0:T(8,128)}, f32[2048,512]{1,0:T(8,128)}) custom-call(bf16[512,512]{1,0:T(8,128)(2,1)S(1)} %collective-permute-done.35.refs_0_, s32[8,128]{1,0:T(8,128)S(1)} %get-tuple-element.116.refs_13_.refs_5_.refs_4_.refs_2_.refs_9_.refs_6_.refs_3_.refs_1_, ...), custom_call_target="tpu_custom_call", output_to_operand_aliasing={{1}: (3, {}), {2}: (4, {})} | custom-call | flops 1 | bytes 1024 | tf_op jit(solution)/shard_map/pallas_call | solution.py:160
  99.1 0.9 shard_map.231
  (51 shorter events, 1.0 us)
Async XLA Ops:
  1.5 11.6 %collective-permute-start.1 = (bf16[64,512]{1,0:T(8,128)(2,1)S(1)}, bf16[64,512]{1,0:T(8,128)(2,1)S(1)}, u32[]{:S(2)}, u32[]{:S(2)}) collective-permute-start(bf16[64,512]{1,0:T(8,128)(2,1)S(1)} %fusion), channel_id=1, source_target_pairs={{0,4},{2,6},{4,0},{6,2},{1,5},{3,7},{5,1},{7,3},{8,12},{10,14},{12... | collective-permute-start | bytes 196616 | tf_op jit(solution)/shard_map/ppermute | solution.py:556
  5.6 7.5 %collective-permute-start = (bf16[64,512]{1,0:T(8,128)(2,1)S(1)}, bf16[64,512]{1,0:T(8,128)(2,1)S(1)}, u32[]{:S(2)}, u32[]{:S(2)}) collective-permute-start(bf16[64,512]{1,0:T(8,128)(2,1)S(1)} %fusion), channel_id=1, source_target_pairs={{0,2},{2,0},{4,6},{6,4},{1,3},{3,1},{5,7},{7,5},{8,10},{10,8},{12,... | collective-permute-start | bytes 196616 | tf_op jit(solution)/shard_map/ppermute | solution.py:556
  7.2 6.1 %collective-permute-start.2 = (bf16[64,512]{1,0:T(8,128)(2,1)S(1)}, bf16[64,512]{1,0:T(8,128)(2,1)S(1)}, u32[]{:S(2)}, u32[]{:S(2)}) collective-permute-start(bf16[64,512]{1,0:T(8,128)(2,1)S(1)} %fusion), channel_id=1, source_target_pairs={{0,6},{2,4},{4,2},{6,0},{1,7},{3,5},{5,3},{7,1},{8,14},{10,12},{12... | collective-permute-start | bytes 196616 | tf_op jit(solution)/shard_map/ppermute | solution.py:556
  10.5 4.3 %copy-start = (bf16[2048,512]{1,0:T(8,128)(2,1)}, bf16[2048,512]{1,0:T(8,128)(2,1)S(1)}, u32[]{:S(2)}) copy-start(bf16[2048,512]{1,0:T(8,128)(2,1)S(1)} %get-tuple-element.103.refs_1_) | copy-start | bytes 6291460
  13.3 1.5 %collective-permute-start.3 = (bf16[192,512]{1,0:T(8,128)(2,1)S(1)}, bf16[192,512]{1,0:T(8,128)(2,1)S(1)}, u32[]{:S(2)}, u32[]{:S(2)}) collective-permute-start(bf16[192,512]{1,0:T(8,128)(2,1)S(1)} %shard_map.197.refs_0_.refs_14_), channel_id=1, source_target_pairs={{0,1},{1,0},{2,3},{3,2},{4,5},{5,4},{6,7},{7,6},{8,9},{9,8},{10,11... | collective-permute-start | bytes 589832 | tf_op jit(solution)/shard_map/ppermute | solution.py:556
  21.0 7.2 %collective-permute-start.4 = (bf16[512,512]{1,0:T(8,128)(2,1)S(1)}, bf16[512,512]{1,0:T(8,128)(2,1)S(1)}, u32[]{:S(2)}, u32[]{:S(2)}) collective-permute-start(bf16[512,512]{1,0:T(8,128)(2,1)S(1)} %get-tuple-element.128), channel_id=1, source_target_pairs={{0,1},{1,0},{2,3},{3,2},{4,5},{5,4},{6,7},{7,6},{8,9},{9,8},{10,11... | collective-permute-start | bytes 1572872 | tf_op jit(solution)/shard_map/ppermute | solution.py:556
  24.6 3.7 %collective-permute-start.5 = (bf16[512,512]{1,0:T(8,128)(2,1)S(1)}, bf16[512,512]{1,0:T(8,128)(2,1)S(1)}, u32[]{:S(2)}, u32[]{:S(2)}) collective-permute-start(bf16[512,512]{1,0:T(8,128)(2,1)S(1)} %get-tuple-element.129), channel_id=1, source_target_pairs={{0,1},{1,0},{2,3},{3,2},{4,5},{5,4},{6,7},{7,6},{8,9},{9,8},{10,11... | collective-permute-start | bytes 1572872 | tf_op jit(solution)/shard_map/ppermute | solution.py:556
  28.8 9.2 %collective-permute-start.6 = (bf16[512,512]{1,0:T(8,128)(2,1)S(1)}, bf16[512,512]{1,0:T(8,128)(2,1)S(1)}, u32[]{:S(2)}, u32[]{:S(2)}) collective-permute-start(bf16[512,512]{1,0:T(8,128)(2,1)S(1)} %get-tuple-element.131.refs_6_), channel_id=1, source_target_pairs={{0,8},{1,17},{2,10},{3,19},{4,12},{5,21},{6,14},{7,23},{8,0},{9,25... | collective-permute-start | bytes 1572872 | tf_op jit(solution)/shard_map/ppermute | solution.py:586
  30.4 9.5 %collective-permute-start.8 = (bf16[512,512]{1,0:T(8,128)(2,1)S(1)}, bf16[512,512]{1,0:T(8,128)(2,1)S(1)}, u32[]{:S(2)}, u32[]{:S(2)}) collective-permute-start(bf16[512,512]{1,0:T(8,128)(2,1)S(1)} %get-tuple-element.147), channel_id=1, source_target_pairs={{0,1},{1,0},{2,3},{3,2},{4,5},{5,4},{6,7},{7,6},{8,9},{9,8},{10,11... | collective-permute-start | bytes 1572872 | tf_op jit(solution)/shard_map/ppermute | solution.py:556
  33.6 6.3 %collective-permute-start.9 = (bf16[512,512]{1,0:T(8,128)(2,1)S(1)}, bf16[512,512]{1,0:T(8,128)(2,1)S(1)}, u32[]{:S(2)}, u32[]{:S(2)}) collective-permute-start(bf16[512,512]{1,0:T(8,128)(2,1)S(1)} %get-tuple-element.148), channel_id=1, source_target_pairs={{0,1},{1,0},{2,3},{3,2},{4,5},{5,4},{6,7},{7,6},{8,9},{9,8},{10,11... | collective-permute-start | bytes 1572872 | tf_op jit(solution)/shard_map/ppermute | solution.py:556
  38.2 6.4 %collective-permute-start.7 = (bf16[256,512]{1,0:T(8,128)(2,1)S(1)}, bf16[256,512]{1,0:T(8,128)(2,1)S(1)}, u32[]{:S(2)}, u32[]{:S(2)}) collective-permute-start(bf16[256,512]{1,0:T(8,128)(2,1)S(1)} %get-tuple-element.141.refs_5_), channel_id=1, source_target_pairs={{0,16},{1,9},{2,18},{3,11},{4,20},{5,13},{6,22},{7,15},{8,24},{9,1... | collective-permute-start | bytes 786440 | tf_op jit(solution)/shard_map/ppermute | solution.py:586
  40.4 9.9 %collective-permute-start.11 = (bf16[512,512]{1,0:T(8,128)(2,1)S(1)}, bf16[512,512]{1,0:T(8,128)(2,1)S(1)}, u32[]{:S(2)}, u32[]{:S(2)}) collective-permute-start(bf16[512,512]{1,0:T(8,128)(2,1)S(1)} %get-tuple-element.149.refs_12_), channel_id=1, source_target_pairs={{0,16},{1,9},{2,18},{3,11},{4,20},{5,13},{6,22},{7,15},{8,24},{9,1... | collective-permute-start | bytes 1572872 | tf_op jit(solution)/shard_map/ppermute | solution.py:586
  44.8 7.4 %collective-permute-start.10 = (bf16[128,512]{1,0:T(8,128)(2,1)S(1)}, bf16[128,512]{1,0:T(8,128)(2,1)S(1)}, u32[]{:S(2)}, u32[]{:S(2)}) collective-permute-start(bf16[128,512]{1,0:T(8,128)(2,1)S(1)} %get-tuple-element.152.refs_10_), channel_id=1, source_target_pairs={{0,2},{2,0},{4,6},{6,4},{1,3},{3,1},{5,7},{7,5},{8,10},{10,8},{12,... | collective-permute-start | bytes 393224 | tf_op jit(solution)/shard_map/ppermute | solution.py:575
  48.5 11.2 %collective-permute-start.12 = (bf16[128,512]{1,0:T(8,128)(2,1)S(1)}, bf16[128,512]{1,0:T(8,128)(2,1)S(1)}, u32[]{:S(2)}, u32[]{:S(2)}) collective-permute-start(bf16[128,512]{1,0:T(8,128)(2,1)S(1)} %get-tuple-element.164), channel_id=1, source_target_pairs={{0,1},{1,0},{2,3},{3,2},{4,5},{5,4},{6,7},{7,6},{8,9},{9,8},{10,11... | collective-permute-start | bytes 393224 | tf_op jit(solution)/shard_map/ppermute | solution.py:556
  48.6 11.1 %collective-permute-start.13 = (bf16[128,512]{1,0:T(8,128)(2,1)S(1)}, bf16[128,512]{1,0:T(8,128)(2,1)S(1)}, u32[]{:S(2)}, u32[]{:S(2)}) collective-permute-start(bf16[128,512]{1,0:T(8,128)(2,1)S(1)} %get-tuple-element.165), channel_id=1, source_target_pairs={{0,1},{1,0},{2,3},{3,2},{4,5},{5,4},{6,7},{7,6},{8,9},{9,8},{10,11... | collective-permute-start | bytes 393224 | tf_op jit(solution)/shard_map/ppermute | solution.py:556
  49.1 10.6 %collective-permute-start.14 = (bf16[128,512]{1,0:T(8,128)(2,1)S(1)}, bf16[128,512]{1,0:T(8,128)(2,1)S(1)}, u32[]{:S(2)}, u32[]{:S(2)}) collective-permute-start(bf16[128,512]{1,0:T(8,128)(2,1)S(1)} %get-tuple-element.166), channel_id=1, source_target_pairs={{0,1},{1,0},{2,3},{3,2},{4,5},{5,4},{6,7},{7,6},{8,9},{9,8},{10,11... | collective-permute-start | bytes 393224 | tf_op jit(solution)/shard_map/ppermute | solution.py:556
  50.5 7.2 %collective-permute-start.15 = (bf16[256,512]{1,0:T(8,128)(2,1)S(1)}, bf16[256,512]{1,0:T(8,128)(2,1)S(1)}, u32[]{:S(2)}, u32[]{:S(2)}) collective-permute-start(bf16[256,512]{1,0:T(8,128)(2,1)S(1)} %get-tuple-element.159.refs_3_), channel_id=1, source_target_pairs={{0,8},{1,17},{2,10},{3,19},{4,12},{5,21},{6,14},{7,23},{8,0},{9,25... | collective-permute-start | bytes 786440 | tf_op jit(solution)/shard_map/ppermute | solution.py:586
  52.1 2.4 %copy-start.1 = (bf16[2048,512]{1,0:T(8,128)(2,1)S(1)}, bf16[2048,512]{1,0:T(8,128)(2,1)}, u32[]{:S(2)}) copy-start(bf16[2048,512]{1,0:T(8,128)(2,1)} %copy-done) | copy-start | bytes 6291460
  52.2 9.3 %collective-permute-start.18 = (bf16[128,512]{1,0:T(8,128)(2,1)S(1)}, bf16[128,512]{1,0:T(8,128)(2,1)S(1)}, u32[]{:S(2)}, u32[]{:S(2)}) collective-permute-start(bf16[128,512]{1,0:T(8,128)(2,1)S(1)} %shard_map.211.refs_6_.refs_0_), channel_id=1, source_target_pairs={{0,4},{2,6},{4,0},{6,2},{1,5},{3,7},{5,1},{7,3},{8,12},{10,14},{12... | collective-permute-start | bytes 393224 | tf_op jit(solution)/shard_map/ppermute | solution.py:575
  57.8 6.2 %collective-permute-start.17 = (bf16[128,512]{1,0:T(8,128)(2,1)S(1)}, bf16[128,512]{1,0:T(8,128)(2,1)S(1)}, u32[]{:S(2)}, u32[]{:S(2)}) collective-permute-start(bf16[128,512]{1,0:T(8,128)(2,1)S(1)} %get-tuple-element.169.refs_7_), channel_id=1, source_target_pairs={{0,2},{2,0},{4,6},{6,4},{1,3},{3,1},{5,7},{7,5},{8,10},{10,8},{12,... | collective-permute-start | bytes 393224 | tf_op jit(solution)/shard_map/ppermute | solution.py:575
  59.9 6.1 %collective-permute-start.16 = (bf16[192,512]{1,0:T(8,128)(2,1)S(1)}, bf16[192,512]{1,0:T(8,128)(2,1)S(1)}, u32[]{:S(2)}, u32[]{:S(2)}) collective-permute-start(bf16[192,512]{1,0:T(8,128)(2,1)S(1)} %get-tuple-element.171.refs_3_), channel_id=1, source_target_pairs={{0,16},{1,9},{2,18},{3,11},{4,20},{5,13},{6,22},{7,15},{8,24},{9,1... | collective-permute-start | bytes 589832 | tf_op jit(solution)/shard_map/ppermute | solution.py:586
  61.5 6.1 %collective-permute-start.20 = (bf16[128,512]{1,0:T(8,128)(2,1)S(1)}, bf16[128,512]{1,0:T(8,128)(2,1)S(1)}, u32[]{:S(2)}, u32[]{:S(2)}) collective-permute-start(bf16[128,512]{1,0:T(8,128)(2,1)S(1)} %shard_map.215.refs_3_.refs_0_), channel_id=1, source_target_pairs={{0,2},{2,0},{4,6},{6,4},{1,3},{3,1},{5,7},{7,5},{8,10},{10,8},{12,... | collective-permute-start | bytes 393224 | tf_op jit(solution)/shard_map/ppermute | solution.py:575
  64.0 9.7 %collective-permute-start.23 = (bf16[128,512]{1,0:T(8,128)(2,1)S(1)}, bf16[128,512]{1,0:T(8,128)(2,1)S(1)}, u32[]{:S(2)}, u32[]{:S(2)}) collective-permute-start(bf16[128,512]{1,0:T(8,128)(2,1)S(1)} %shard_map.216.refs_3_.refs_0_), channel_id=1, source_target_pairs={{0,4},{2,6},{4,0},{6,2},{1,5},{3,7},{5,1},{7,3},{8,12},{10,14},{12... | collective-permute-start | bytes 393224 | tf_op jit(solution)/shard_map/ppermute | solution.py:575
  66.0 5.8 %collective-permute-start.19 = (bf16[96,512]{1,0:T(8,128)(2,1)S(1)}, bf16[96,512]{1,0:T(8,128)(2,1)S(1)}, u32[]{:S(2)}, u32[]{:S(2)}) collective-permute-start(bf16[96,512]{1,0:T(8,128)(2,1)S(1)} %get-tuple-element.174.refs_3_), channel_id=1, source_target_pairs={{0,8},{1,17},{2,10},{3,19},{4,12},{5,21},{6,14},{7,23},{8,0},{9,25... | collective-permute-start | bytes 294920 | tf_op jit(solution)/shard_map/ppermute | solution.py:586
  67.7 6.4 %collective-permute-start.22 = (bf16[256,512]{1,0:T(8,128)(2,1)S(1)}, bf16[256,512]{1,0:T(8,128)(2,1)S(1)}, u32[]{:S(2)}, u32[]{:S(2)}) collective-permute-start(bf16[256,512]{1,0:T(8,128)(2,1)S(1)} %shard_map.218.refs_3_.refs_0_), channel_id=1, source_target_pairs={{0,16},{1,9},{2,18},{3,11},{4,20},{5,13},{6,22},{7,15},{8,24},{9,1... | collective-permute-start | bytes 786440 | tf_op jit(solution)/shard_map/ppermute | solution.py:586
  71.9 4.9 %collective-permute-start.21 = (bf16[64,512]{1,0:T(8,128)(2,1)S(1)}, bf16[64,512]{1,0:T(8,128)(2,1)S(1)}, u32[]{:S(2)}, u32[]{:S(2)}) collective-permute-start(bf16[64,512]{1,0:T(8,128)(2,1)S(1)} %get-tuple-element.176.refs_3_), channel_id=1, source_target_pairs={{0,2},{2,0},{4,6},{6,4},{1,3},{3,1},{5,7},{7,5},{8,10},{10,8},{12,... | collective-permute-start | bytes 196616 | tf_op jit(solution)/shard_map/ppermute | solution.py:575
  73.7 5.0 %collective-permute-start.25 = (bf16[128,512]{1,0:T(8,128)(2,1)S(1)}, bf16[128,512]{1,0:T(8,128)(2,1)S(1)}, u32[]{:S(2)}, u32[]{:S(2)}) collective-permute-start(bf16[128,512]{1,0:T(8,128)(2,1)S(1)} %shard_map.220.refs_3_.refs_0_), channel_id=1, source_target_pairs={{0,2},{2,0},{4,6},{6,4},{1,3},{3,1},{5,7},{7,5},{8,10},{10,8},{12,... | collective-permute-start | bytes 393224 | tf_op jit(solution)/shard_map/ppermute | solution.py:575
  74.2 9.8 %collective-permute-start.28 = (bf16[512,512]{1,0:T(8,128)(2,1)S(1)}, bf16[512,512]{1,0:T(8,128)(2,1)S(1)}, u32[]{:S(2)}, u32[]{:S(2)}) collective-permute-start(bf16[512,512]{1,0:T(8,128)(2,1)S(1)} %shard_map.221.refs_3_.refs_0_), channel_id=1, source_target_pairs={{0,8},{1,17},{2,10},{3,19},{4,12},{5,21},{6,14},{7,23},{8,0},{9,25... | collective-permute-start | bytes 1572872 | tf_op jit(solution)/shard_map/ppermute | solution.py:586
  75.7 12.5 %collective-permute-start.27 = (bf16[512,512]{1,0:T(8,128)(2,1)S(1)}, bf16[512,512]{1,0:T(8,128)(2,1)S(1)}, u32[]{:S(2)}, u32[]{:S(2)}) collective-permute-start(bf16[512,512]{1,0:T(8,128)(2,1)S(1)} %shard_map.221.refs_3_.refs_0_), channel_id=1, source_target_pairs={{0,1},{1,0},{2,3},{3,2},{4,5},{5,4},{6,7},{7,6},{8,9},{9,8},{10,11... | collective-permute-start | bytes 1572872 | tf_op jit(solution)/shard_map/ppermute | solution.py:556
  76.9 5.1 %collective-permute-start.24 = (bf16[48,512]{1,0:T(8,128)(2,1)S(1)}, bf16[48,512]{1,0:T(8,128)(2,1)S(1)}, u32[]{:S(2)}, u32[]{:S(2)}) collective-permute-start(bf16[48,512]{1,0:T(8,128)(2,1)S(1)} %get-tuple-element.178.refs_3_), channel_id=1, source_target_pairs={{0,4},{2,6},{4,0},{6,2},{1,5},{3,7},{5,1},{7,3},{8,12},{10,14},{12... | collective-permute-start | bytes 147464 | tf_op jit(solution)/shard_map/ppermute | solution.py:575
  78.8 7.4 %collective-permute-start.30 = (bf16[256,512]{1,0:T(8,128)(2,1)S(1)}, bf16[256,512]{1,0:T(8,128)(2,1)S(1)}, u32[]{:S(2)}, u32[]{:S(2)}) collective-permute-start(bf16[256,512]{1,0:T(8,128)(2,1)S(1)} %shard_map.223.refs_3_.refs_0_), channel_id=1, source_target_pairs={{0,8},{1,17},{2,10},{3,19},{4,12},{5,21},{6,14},{7,23},{8,0},{9,25... | collective-permute-start | bytes 786440 | tf_op jit(solution)/shard_map/ppermute | solution.py:586
  81.9 8.4 %collective-permute-start.26 = (bf16[48,512]{1,0:T(8,128)(2,1)S(1)}, bf16[48,512]{1,0:T(8,128)(2,1)S(1)}, u32[]{:S(2)}, u32[]{:S(2)}) collective-permute-start(bf16[48,512]{1,0:T(8,128)(2,1)S(1)} %shard_map.224.refs_3_.refs_0_), channel_id=1, source_target_pairs={{0,8},{1,17},{2,10},{3,19},{4,12},{5,21},{6,14},{7,23},{8,0},{9,25... | collective-permute-start | bytes 147464 | tf_op jit(solution)/shard_map/ppermute | solution.py:586
  84.0 4.2 %collective-permute-start.29 = (bf16[512,512]{1,0:T(8,128)(2,1)S(1)}, bf16[512,512]{1,0:T(8,128)(2,1)S(1)}, u32[]{:S(2)}, u32[]{:S(2)}) collective-permute-start(bf16[512,512]{1,0:T(8,128)(2,1)S(1)} %collective-permute-done.28.refs_2_), channel_id=1, source_target_pairs={{0,1},{1,0},{2,3},{3,2},{4,5},{5,4},{6,7},{7,6},{8,9},{9,8},{10,11... | collective-permute-start | bytes 1572872 | tf_op jit(solution)/shard_map/ppermute | solution.py:556
  86.3 9.2 %collective-permute-start.33 = (bf16[512,512]{1,0:T(8,128)(2,1)S(1)}, bf16[512,512]{1,0:T(8,128)(2,1)S(1)}, u32[]{:S(2)}, u32[]{:S(2)}) collective-permute-start(bf16[512,512]{1,0:T(8,128)(2,1)S(1)} %shard_map.225.refs_5_.refs_0_), channel_id=1, source_target_pairs={{0,16},{1,9},{2,18},{3,11},{4,20},{5,13},{6,22},{7,15},{8,24},{9,1... | collective-permute-start | bytes 1572872 | tf_op jit(solution)/shard_map/ppermute | solution.py:586
  88.2 7.4 %collective-permute-start.32 = (bf16[512,512]{1,0:T(8,128)(2,1)S(1)}, bf16[512,512]{1,0:T(8,128)(2,1)S(1)}, u32[]{:S(2)}, u32[]{:S(2)}) collective-permute-start(bf16[512,512]{1,0:T(8,128)(2,1)S(1)} %shard_map.225.refs_5_.refs_0_), channel_id=1, source_target_pairs={{0,1},{1,0},{2,3},{3,2},{4,5},{5,4},{6,7},{7,6},{8,9},{9,8},{10,11... | collective-permute-start | bytes 1572872 | tf_op jit(solution)/shard_map/ppermute | solution.py:556
  90.4 7.0 %collective-permute-start.31 = (bf16[96,512]{1,0:T(8,128)(2,1)S(1)}, bf16[96,512]{1,0:T(8,128)(2,1)S(1)}, u32[]{:S(2)}, u32[]{:S(2)}) collective-permute-start(bf16[96,512]{1,0:T(8,128)(2,1)S(1)} %shard_map.227.refs_4_.refs_0_), channel_id=1, source_target_pairs={{0,16},{1,9},{2,18},{3,11},{4,20},{5,13},{6,22},{7,15},{8,24},{9,1... | collective-permute-start | bytes 294920 | tf_op jit(solution)/shard_map/ppermute | solution.py:586
  95.6 2.4 %collective-permute-start.35 = (bf16[512,512]{1,0:T(8,128)(2,1)S(1)}, bf16[512,512]{1,0:T(8,128)(2,1)S(1)}, u32[]{:S(2)}, u32[]{:S(2)}) collective-permute-start(bf16[512,512]{1,0:T(8,128)(2,1)S(1)} %collective-permute-done.33.refs_2_), channel_id=1, source_target_pairs={{0,1},{1,0},{2,3},{3,2},{4,5},{5,4},{6,7},{7,6},{8,9},{9,8},{10,11... | collective-permute-start | bytes 1572872 | tf_op jit(solution)/shard_map/ppermute | solution.py:556
  97.4 1.6 %collective-permute-start.34 = (bf16[192,512]{1,0:T(8,128)(2,1)S(1)}, bf16[192,512]{1,0:T(8,128)(2,1)S(1)}, u32[]{:S(2)}, u32[]{:S(2)}) collective-permute-start(bf16[192,512]{1,0:T(8,128)(2,1)S(1)} %shard_map.229.refs_2_.refs_0_), channel_id=1, source_target_pairs={{0,1},{1,0},{2,3},{3,2},{4,5},{5,4},{6,7},{7,6},{8,9},{9,8},{10,11... | collective-permute-start | bytes 589832 | tf_op jit(solution)/shard_map/ppermute | solution.py:556

commit v6 on v5

--- a/solution.py
+++ b/solution.py
@@ -15,10 +15,10 @@
 PIECE = 512
 AXES = ("dp", "expert", "tok")
 GLUE = 23 * 10**9
-WORK = 1
+WORK = 0 * 10**9 + 1
 ORDER = (
-    "f", "A", "f", "a", "B", "n", "a", "b", "h", "a", "r", "b", "a", "o", "b", "t", "a", "b", "t",
-    "a", "t", "b", "a", "t", "b", "t", "b", "1", "t", "2", "t", "3", "T",
+    "f", "A", "f", "a", "B", "n", "a", "b", "h", "a", "r", "b", "a", "o", "b", "t", "a", "b", "a",
+    "t", "b", "a", "t", "b", "t", "b", "1", "t", "2", "t", "3", "T",
 )
 
 
@@ -783,24 +783,18 @@
 
 def tail_walk(views, experts, each, mirror):
     stages = bits(lax.axis_size("dp"))
-    order = [("dp", (s + mirror) % 2) for s in range(stages)]
-    halves = each >> stages >= 16
-    for key in order if halves else ():
-        views = yield Job("halve", views, key, place_row(key), experts, each)
+    first, *others = [("dp", (s + mirror) % stages) for s in range(stages)]
+    halves = each >= 32
+    if halves:
+        views = yield Job("halve", views, first, place_row(first), experts, each)
         each //= 2
     for stage in range(bits(experts)):
         key = ("expert", stage)
         views = yield Job("pick", views, key, place_row(key), experts >> stage, each)
-    before = None
-    for key in reversed(order):
-        if before is None or not halves:
-            views = yield Job("add", views, key)
-        else:
-            views = yield Job("weave", views, key, place_row(before), 1, each)
-            each *= 2
-        before = key
+    for key in [*others, first]:
+        views = yield Job("add", views, key)
     if halves:
-        views = yield Job("weave", views, ("tok", 0), place_row(before), 1, each)
+        views = yield Job("weave", views, ("tok", 0), place_row(first), 1, each)
     else:
         views = yield Job("add", views, ("tok", 0))
     return views

time: 100 us -> 99.3 us (level)
    ppermute x12 -> x11, waiting for transfers between devices: 12 us -> 7.95 us  [swap(): return lax.ppermute(array, AXES, pairs)]
    ppermute x8, waiting for transfers between devices: 6.17 us -> 9.51 us  [swap(): lax.ppermute(array, 'expert', [(i, i ^ 1 << stage) for i in range(size)])]
    ppermute x12 -> x11, starting transfers between devices: 17.4 us -> 16.3 us  [swap(): return lax.ppermute(array, AXES, pairs)]
    pallas_call x37 -> x36, Pallas kernels: 42.4 us -> 42.3 us  [call(): pl.pallas_call(wrapped, out_shape=outs + list(sent), in_specs=[pl.BlockSp...]
  transfers between devices with their start and end apart: 36 -> 35, of which waited for: 13 -> 12; matrix products, arithmetic and copies ran while one was open for 0% -> 0% of each run, Pallas kernels for 35% -> 35%
where the time goes in v6:
time: 99.3 us; the launch traced here: 99.1 us
  Pallas kernels  42.3 us (43%)
  starting transfers between devices  35.8 us (36%)
  waiting for transfers between devices  19.1 us (19%)
    pallas_call x36, Pallas kernels, call(): pl.pallas_call(wrapped, out_shape=outs + list(sent), in_specs=[pl.BlockSp...  42.3 us
    ppermute x11, starting transfers between devices, swap(): return lax.ppermute(array, AXES, pairs)  16.3 us
    ppermute x8, starting transfers between devices, swap(): lax.ppermute(array, 'expert', [(i, i ^ 1 << stage) for i in range(size)])  11.2 us
    ppermute x8, waiting for transfers between devices, swap(): lax.ppermute(array, 'expert', [(i, i ^ 1 << stage) for i in range(size)])  9.51 us
    ppermute x16, starting transfers between devices, exchange(): lax.ppermute(parts[k], axis, [(i, i ^ k) for i in range(size)])  8.23 us
    ppermute x11, waiting for transfers between devices, swap(): return lax.ppermute(array, AXES, pairs)  7.95 us
  transfers between devices with their start and end apart: 35, of which 12 were waited for; matrix products, arithmetic and copies ran while one was open for 0% of the time, Pallas kernels for 35%

profile of v6, /device:TPU:0, one launch (start us, length us, event | category | flops | bytes accessed | tf_op | source)
XLA Modules:
  0.0 99.1 jit_solution(14654937008745311465)
XLA Ops:
  0.6 0.9 fusion
  1.5 4.1 %collective-permute-start.1 = (bf16[64,512]{1,0:T(8,128)(2,1)S(1)}, bf16[64,512]{1,0:T(8,128)(2,1)S(1)}, u32[]{:S(2)}, u32[]{:S(2)}) collective-permute-start(bf16[64,512]{1,0:T(8,128)(2,1)S(1)} %fusion), channel_id=1, source_target_pairs={{0,4},{2,6},{4,0},{6,2},{1,5},{3,7},{5,1},{7,3},{8,12},{10,14},{12... | collective-permute-start | bytes 196616 | tf_op jit(solution)/shard_map/ppermute | solution.py:556
  5.6 1.6 %collective-permute-start = (bf16[64,512]{1,0:T(8,128)(2,1)S(1)}, bf16[64,512]{1,0:T(8,128)(2,1)S(1)}, u32[]{:S(2)}, u32[]{:S(2)}) collective-permute-start(bf16[64,512]{1,0:T(8,128)(2,1)S(1)} %fusion), channel_id=1, source_target_pairs={{0,2},{2,0},{4,6},{6,4},{1,3},{3,1},{5,7},{7,5},{8,10},{10,8},{12,... | collective-permute-start | bytes 196616 | tf_op jit(solution)/shard_map/ppermute | solution.py:556
  7.2 0.1 stack.27.refs_11_.refs_12_
  7.3 3.2 %shard_map.195 = (bf16[1024,512]{1,0:T(8,128)(2,1)S(1)}, bf16[1024,128]{1,0:T(8,128)(2,1)S(1)}, bf16[128,1024]{1,0:T(8,128)(2,1)S(1)}, f32[2,1024]{1,0:T(2,128)S...) custom-call(f32[1,512]{1,0:T(1,128)} %bitcast.24, ...), custom_call_target="tpu_custom_call" | custom-call | flops 1 | bytes 1024 | tf_op jit(solution)/shard_map/pallas_call | solution.py:160
  10.5 2.6 %shard_map.196 = (bf16[1024,2048]{1,0:T(8,128)(2,1)S(1)}, bf16[512,2048]{1,0:T(8,128)(2,1)S(1)}) custom-call(bf16[1024,512]{1,0:T(8,128)(2,1)S(1)} %get-tuple-element.100.refs_0_.refs_1_, bf16[2048,512]{1,0:T(8,128)(2,1)S(1)} %get-tuple-element.101.refs_1_, bf16[512,2048]{1,0:T(8,128)(2,1)} %refs_2_.1, f32[1,1024]{1,0:T(1,128)S(1)} %get-tuple-element.102.refs_3_.refs_8_.refs_10_), custom_call_target="tpu_custom_call" | custom-call | flops 1 | bytes 1024 | tf_op jit(solution)/shard_map/pallas_call | solution.py:160
  13.1 0.1 collective-permute-done.2.refs_2_
  13.4 1.4 %collective-permute-done.3.refs_1_ = bf16[192,512]{1,0:T(8,128)(2,1)S(1)} collective-permute-done((bf16[192,512]{1,0:T(8,128)(2,1)S(1)}, bf16[192,512]{1,0:T(8,128)(2,1)S(1)}, u32[]{:S(2)}, u32[]{:S(2)}) %collective-permute-start.3) | collective-permute-done | bytes 196640 | tf_op jit(solution)/shard_map/ppermute | solution.py:556
  14.8 3.0 %shard_map.198 = (bf16[256,512]{1,0:T(8,128)(2,1)S(1)}, bf16[256,512]{1,0:T(8,128)(2,1)S(1)}, bf16[64,2048]{1,0:T(8,128)(2,1)S(1)}, bf16[64,2048]{1,0:T(8,128)(2...) custom-call(bf16[192,512]{1,0:T(8,128)(2,1)S(1)} %shard_map.197.refs, ...), custom_call_target="tpu_custom_call" | custom-call | flops 1 | bytes 1024 | tf_op jit(solution)/shard_map/pallas_call | solution.py:160
  17.8 3.2 %shard_map.199 = (bf16[1024,512]{1,0:T(8,128)(2,1)S(1)}, bf16[1024,512]{1,0:T(8,128)(2,1)S(1)}, bf16[512,512]{1,0:T(8,128)(2,1)S(1)}, bf16[512,512]{1,0:T(8,128)(2,1)S(1)}) custom-call(bf16[1024,512]{1,0:T(8,128)(2,1)S(1)} %get-tuple-element.116.refs_0_, bf16[512,1024]{1,0:T(8,128)(2,1)S(1)} %get-tuple-element.117.refs_1_, ...), custom_call_target="tpu_custom_call" | custom-call | flops 1 | bytes 1024 | tf_op jit(solution)/shard_map/pallas_call | solution.py:160
  21.0 0.2 collective-permute-start.4
  21.2 3.4 %shard_map.200 = (bf16[1024,512]{1,0:T(8,128)(2,1)S(1)}, bf16[1024,512]{1,0:T(8,128)(2,1)S(1)}, bf16[512,512]{1,0:T(8,128)(2,1)S(1)}, bf16[512,512]{1,0:T(8,128)(2,1)S(1)}) custom-call(bf16[1024,512]{1,0:T(8,128)(2,1)S(1)} %get-tuple-element.116.refs_0_, bf16[512,1024]{1,0:T(8,128)(2,1)S(1)} %get-tuple-element.117.refs_1_, ...), custom_call_target="tpu_custom_call" | custom-call | flops 1 | bytes 1024 | tf_op jit(solution)/shard_map/pallas_call | solution.py:160
  24.6 0.4 collective-permute-start.5
  25.1 3.2 %shard_map.201 = (bf16[1024,512]{1,0:T(8,128)(2,1)S(1)}, bf16[1024,512]{1,0:T(8,128)(2,1)S(1)}, bf16[512,512]{1,0:T(8,128)(2,1)S(1)}, bf16[512,512]{1,0:T(8,128)(2,1)S(1)}) custom-call(bf16[1024,512]{1,0:T(8,128)(2,1)S(1)} %get-tuple-element.116.refs_0_, bf16[512,1024]{1,0:T(8,128)(2,1)S(1)} %get-tuple-element.117.refs_1_, ...), custom_call_target="tpu_custom_call" | custom-call | flops 1 | bytes 1024 | tf_op jit(solution)/shard_map/pallas_call | solution.py:160
  28.3 0.5 shard_map.202
  28.8 1.6 %collective-permute-start.6 = (bf16[512,512]{1,0:T(8,128)(2,1)S(1)}, bf16[512,512]{1,0:T(8,128)(2,1)S(1)}, u32[]{:S(2)}, u32[]{:S(2)}) collective-permute-start(bf16[512,512]{1,0:T(8,128)(2,1)S(1)} %get-tuple-element.129.refs_6_), channel_id=1, source_target_pairs={{0,8},{1,17},{2,10},{3,19},{4,12},{5,21},{6,14},{7,23},{8,0},{9,25... | collective-permute-start | bytes 1572872 | tf_op jit(solution)/shard_map/ppermute | solution.py:586
  30.4 3.2 %shard_map.203 = (bf16[1024,512]{1,0:T(8,128)(2,1)S(1)}, bf16[1024,512]{1,0:T(8,128)(2,1)S(1)}, bf16[512,512]{1,0:T(8,128)(2,1)S(1)}, bf16[512,512]{1,0:T(8,128)(2,1)S(1)}) custom-call(bf16[1024,512]{1,0:T(8,128)(2,1)S(1)} %get-tuple-element.116.refs_0_, bf16[512,1024]{1,0:T(8,128)(2,1)S(1)} %get-tuple-element.117.refs_1_, ...), custom_call_target="tpu_custom_call" | custom-call | flops 1 | bytes 1024 | tf_op jit(solution)/shard_map/pallas_call | solution.py:160
  33.6 0.6 collective-permute-start.9
  34.2 3.2 %shard_map.204 = (f32[1024,512]{1,0:T(8,128)S(1)}, bf16[1024,512]{1,0:T(8,128)(2,1)S(1)}, f32[1,512]{1,0:T(1,128)S(1)}) custom-call(f32[1024,512]{1,0:T(8,128)S(1)} %get-tuple-element.115.refs_0_, bf16[1024,512]{1,0:T(8,128)(2,1)S(1)} %get-tuple-element.100.refs_0_.refs_1_, bf16[512,2048]{1,0:T(8,128)(2,1)S(1)} %get-tuple-element.103.refs_3_.refs_4_.refs_2_, ...), custom_call_target="tpu_custom_call" | custom-call | flops 1 | bytes 1024 | tf_op jit(solution)/shard_map/pallas_call | solution.py:160
  37.4 0.6 collective-permute-done.6.refs_1_
  38.0 0.2 shard_map.205
  38.2 1.7 %collective-permute-start.7 = (bf16[256,512]{1,0:T(8,128)(2,1)S(1)}, bf16[256,512]{1,0:T(8,128)(2,1)S(1)}, u32[]{:S(2)}, u32[]{:S(2)}) collective-permute-start(bf16[256,512]{1,0:T(8,128)(2,1)S(1)} %get-tuple-element.139.refs_5_), channel_id=1, source_target_pairs={{0,16},{1,9},{2,18},{3,11},{4,20},{5,13},{6,22},{7,15},{8,24},{9,1... | collective-permute-start | bytes 786440 | tf_op jit(solution)/shard_map/ppermute | solution.py:586
  39.9 0.5 shard_map.206
  40.4 0.5 collective-permute-start.11
  40.9 3.1 %shard_map.207 = (bf16[400,1024]{1,0:T(8,128)(2,1)S(1)}, bf16[256,512]{1,0:T(8,128)(2,1)S(1)}) custom-call(bf16[1024,128]{1,0:T(8,128)(2,1)S(1)} %get-tuple-element.105.refs_3_.refs_0_, bf16[128,1024]{1,0:T(8,128)(2,1)S(1)} %get-tuple-element.106.refs_4_.refs_1_, f32[2,1024]{1,0:T(2,128)S(1)} %get-tuple-element.107.refs_5_.refs_2_, ...), custom_call_target="tpu_custom_call" | custom-call | flops 1 | bytes 1024 | tf_op jit(solution)/shard_map/pallas_call | solution.py:160
  44.0 0.7 collective-permute-done.7.refs_1_
  44.7 0.1 shard_map.208
  44.8 0.8 collective-permute-start.10
  45.6 2.9 %shard_map.209 = (bf16[128,512]{1,0:T(8,128)(2,1)S(1)}, bf16[128,512]{1,0:T(8,128)(2,1)S(1)}, bf16[128,512]{1,0:T(8,128)(2,1)S(1)}, bf16[128,512]{1,0:T(8,128)(2...) custom-call(bf16[400,1024]{1,0:T(8,128)(2,1)S(1)} %get-tuple-element.152.refs_0_, ...), custom_call_target="tpu_custom_call" | custom-call | flops 1 | bytes 1024 | tf_op jit(solution)/shard_map/pallas_call | solution.py:160
  48.5 0.1 collective-permute-start.12
  48.6 0.5 collective-permute-start.13
  49.1 0.1 collective-permute-start.14
  49.2 1.1 %collective-permute-done.11.refs_1_ = bf16[512,512]{1,0:T(8,128)(2,1)S(1)} collective-permute-done((bf16[512,512]{1,0:T(8,128)(2,1)S(1)}, bf16[512,512]{1,0:T(8,128)(2,1)S(1)}, u32[]{:S(2)}, u32[]{:S(2)}) %collective-permute-start.11) | collective-permute-done | bytes 524320 | tf_op jit(solution)/shard_map/ppermute | solution.py:586
  50.3 0.2 shard_map.210
  50.5 1.6 %collective-permute-start.15 = (bf16[256,512]{1,0:T(8,128)(2,1)S(1)}, bf16[256,512]{1,0:T(8,128)(2,1)S(1)}, u32[]{:S(2)}, u32[]{:S(2)}) collective-permute-start(bf16[256,512]{1,0:T(8,128)(2,1)S(1)} %get-tuple-element.157.refs_3_), channel_id=1, source_target_pairs={{0,8},{1,17},{2,10},{3,19},{4,12},{5,21},{6,14},{7,23},{8,0},{9,25... | collective-permute-start | bytes 786440 | tf_op jit(solution)/shard_map/ppermute | solution.py:586
  52.2 2.4 %collective-permute-start.17 = (bf16[128,512]{1,0:T(8,128)(2,1)S(1)}, bf16[128,512]{1,0:T(8,128)(2,1)S(1)}, u32[]{:S(2)}, u32[]{:S(2)}) collective-permute-start(bf16[128,512]{1,0:T(8,128)(2,1)S(1)} %shard_map.211.refs_6_.refs_0_), channel_id=1, source_target_pairs={{0,4},{2,6},{4,0},{6,2},{1,5},{3,7},{5,1},{7,3},{8,12},{10,14},{12... | collective-permute-start | bytes 393224 | tf_op jit(solution)/shard_map/ppermute | solution.py:575
  54.6 3.1 %shard_map.212 = (f32[8,128]{1,0:T(8,128)S(1)}, bf16[1024,512]{1,0:T(8,128)(2,1)}) custom-call(f32[1024,512]{1,0:T(8,128)S(1)} %get-tuple-element.115.refs_0_, bf16[2048,512]{1,0:T(8,128)(2,1)S(1)} %copy-done.1, bf16[1024,512]{1,0:T(8,128)(2,1)S(1)} %get-tuple-element.121.refs_2_, bf16[1024,512]{1,0:T(8,128)(2,1)S(1)} %get-tuple-element.123.refs_3_, ...), custom_call_target="tpu_custom_call" | custom-call | flops 1 | bytes 1024 | tf_op jit(solution)/shard_map/pallas_call | solution.py:160
  57.7 0.1 shard_map.213
  57.8 1.9 %collective-permute-start.19 = (bf16[128,512]{1,0:T(8,128)(2,1)S(1)}, bf16[128,512]{1,0:T(8,128)(2,1)S(1)}, u32[]{:S(2)}, u32[]{:S(2)}) collective-permute-start(bf16[128,512]{1,0:T(8,128)(2,1)S(1)} %get-tuple-element.167.refs_7_), channel_id=1, source_target_pairs={{0,2},{2,0},{4,6},{6,4},{1,3},{3,1},{5,7},{7,5},{8,10},{10,8},{12,... | collective-permute-start | bytes 393224 | tf_op jit(solution)/shard_map/ppermute | solution.py:575
  59.7 0.1 shard_map.214
  59.9 1.6 %collective-permute-start.16 = (bf16[192,512]{1,0:T(8,128)(2,1)S(1)}, bf16[192,512]{1,0:T(8,128)(2,1)S(1)}, u32[]{:S(2)}, u32[]{:S(2)}) collective-permute-start(bf16[192,512]{1,0:T(8,128)(2,1)S(1)} %get-tuple-element.169.refs_3_), channel_id=1, source_target_pairs={{0,16},{1,9},{2,18},{3,11},{4,20},{5,13},{6,22},{7,15},{8,24},{9,1... | collective-permute-start | bytes 589832 | tf_op jit(solution)/shard_map/ppermute | solution.py:586
  61.5 0.3 collective-permute-start.18
  61.8 2.2 %collective-permute-done.19.refs_1_ = bf16[128,512]{1,0:T(8,128)(2,1)S(1)} collective-permute-done((bf16[128,512]{1,0:T(8,128)(2,1)S(1)}, bf16[128,512]{1,0:T(8,128)(2,1)S(1)}, u32[]{:S(2)}, u32[]{:S(2)}) %collective-permute-start.19) | collective-permute-done | bytes 131104 | tf_op jit(solution)/shard_map/ppermute | solution.py:575
  64.0 1.9 %collective-permute-start.22 = (bf16[128,512]{1,0:T(8,128)(2,1)S(1)}, bf16[128,512]{1,0:T(8,128)(2,1)S(1)}, u32[]{:S(2)}, u32[]{:S(2)}) collective-permute-start(bf16[128,512]{1,0:T(8,128)(2,1)S(1)} %shard_map.216.refs_3_.refs_0_), channel_id=1, source_target_pairs={{0,4},{2,6},{4,0},{6,2},{1,5},{3,7},{5,1},{7,3},{8,12},{10,14},{12... | collective-permute-start | bytes 393224 | tf_op jit(solution)/shard_map/ppermute | solution.py:575
  66.0 0.8 collective-permute-done.18.refs_1_
  66.8 1.8 %collective-permute-start.21 = (bf16[256,512]{1,0:T(8,128)(2,1)S(1)}, bf16[256,512]{1,0:T(8,128)(2,1)S(1)}, u32[]{:S(2)}, u32[]{:S(2)}) collective-permute-start(bf16[256,512]{1,0:T(8,128)(2,1)S(1)} %shard_map.217.refs_3_.refs_0_), channel_id=1, source_target_pairs={{0,16},{1,9},{2,18},{3,11},{4,20},{5,13},{6,22},{7,15},{8,24},{9,1... | collective-permute-start | bytes 786440 | tf_op jit(solution)/shard_map/ppermute | solution.py:586
  68.6 0.1 shard_map.218
  68.7 1.2 %collective-permute-start.20 = (bf16[128,512]{1,0:T(8,128)(2,1)S(1)}, bf16[128,512]{1,0:T(8,128)(2,1)S(1)}, u32[]{:S(2)}, u32[]{:S(2)}) collective-permute-start(bf16[128,512]{1,0:T(8,128)(2,1)S(1)} %get-tuple-element.172.refs_3_), channel_id=1, source_target_pairs={{0,2},{2,0},{4,6},{6,4},{1,3},{3,1},{5,7},{7,5},{8,10},{10,8},{12,... | collective-permute-start | bytes 393224 | tf_op jit(solution)/shard_map/ppermute | solution.py:575
  69.9 2.7 %collective-permute-done.22.refs_1_ = bf16[128,512]{1,0:T(8,128)(2,1)S(1)} collective-permute-done((bf16[128,512]{1,0:T(8,128)(2,1)S(1)}, bf16[128,512]{1,0:T(8,128)(2,1)S(1)}, u32[]{:S(2)}, u32[]{:S(2)}) %collective-permute-start.22) | collective-permute-done | bytes 131104 | tf_op jit(solution)/shard_map/ppermute | solution.py:575
  72.7 0.6 collective-permute-done.21.refs_1_
  73.4 1.6 %collective-permute-start.27 = (bf16[512,512]{1,0:T(8,128)(2,1)S(1)}, bf16[512,512]{1,0:T(8,128)(2,1)S(1)}, u32[]{:S(2)}, u32[]{:S(2)}) collective-permute-start(bf16[512,512]{1,0:T(8,128)(2,1)S(1)} %shard_map.220.refs_3_.refs_0_), channel_id=1, source_target_pairs={{0,8},{1,17},{2,10},{3,19},{4,12},{5,21},{6,14},{7,23},{8,0},{9,25... | collective-permute-start | bytes 1572872 | tf_op jit(solution)/shard_map/ppermute | solution.py:586
  75.0 2.7 %collective-permute-start.23 = (bf16[96,512]{1,0:T(8,128)(2,1)S(1)}, bf16[96,512]{1,0:T(8,128)(2,1)S(1)}, u32[]{:S(2)}, u32[]{:S(2)}) collective-permute-start(bf16[96,512]{1,0:T(8,128)(2,1)S(1)} %get-tuple-element.174.refs_3_), channel_id=1, source_target_pairs={{0,4},{2,6},{4,0},{6,2},{1,5},{3,7},{5,1},{7,3},{8,12},{10,14},{12... | collective-permute-start | bytes 294920 | tf_op jit(solution)/shard_map/ppermute | solution.py:575
  77.7 1.8 %collective-permute-start.29 = (bf16[256,512]{1,0:T(8,128)(2,1)S(1)}, bf16[256,512]{1,0:T(8,128)(2,1)S(1)}, u32[]{:S(2)}, u32[]{:S(2)}) collective-permute-start(bf16[256,512]{1,0:T(8,128)(2,1)S(1)} %shard_map.222.refs_3_.refs_0_), channel_id=1, source_target_pairs={{0,8},{1,17},{2,10},{3,19},{4,12},{5,21},{6,14},{7,23},{8,0},{9,25... | collective-permute-start | bytes 786440 | tf_op jit(solution)/shard_map/ppermute | solution.py:586
  79.5 3.7 %collective-permute-done.23.refs_1_ = bf16[96,512]{1,0:T(8,128)(2,1)S(1)} collective-permute-done((bf16[96,512]{1,0:T(8,128)(2,1)S(1)}, bf16[96,512]{1,0:T(8,128)(2,1)S(1)}, u32[]{:S(2)}, u32[]{:S(2)}) %collective-permute-start.23) | collective-permute-done | bytes 98336 | tf_op jit(solution)/shard_map/ppermute | solution.py:575
  83.3 1.5 %collective-permute-start.25 = (bf16[96,512]{1,0:T(8,128)(2,1)S(1)}, bf16[96,512]{1,0:T(8,128)(2,1)S(1)}, u32[]{:S(2)}, u32[]{:S(2)}) collective-permute-start(bf16[96,512]{1,0:T(8,128)(2,1)S(1)} %shard_map.223.refs_3_.refs_0_), channel_id=1, source_target_pairs={{0,8},{1,17},{2,10},{3,19},{4,12},{5,21},{6,14},{7,23},{8,0},{9,25... | collective-permute-start | bytes 294920 | tf_op jit(solution)/shard_map/ppermute | solution.py:586
  84.7 0.7 collective-permute-done.29.refs_1_
  85.5 1.8 %collective-permute-start.32 = (bf16[512,512]{1,0:T(8,128)(2,1)S(1)}, bf16[512,512]{1,0:T(8,128)(2,1)S(1)}, u32[]{:S(2)}, u32[]{:S(2)}) collective-permute-start(bf16[512,512]{1,0:T(8,128)(2,1)S(1)} %shard_map.224.refs_5_.refs_0_), channel_id=1, source_target_pairs={{0,16},{1,9},{2,18},{3,11},{4,20},{5,13},{6,22},{7,15},{8,24},{9,1... | collective-permute-start | bytes 1572872 | tf_op jit(solution)/shard_map/ppermute | solution.py:586
  87.3 2.1 %shard_map.225 = (f32[8,128]{1,0:T(8,128)S(1)}, f32[512,2048]{1,0:T(8,128)}, f32[2048,512]{1,0:T(8,128)}) custom-call(bf16[512,512]{1,0:T(8,128)(2,1)S(1)} %shard_map.220.refs_3_.refs_0_, bf16[512,512]{1,0:T(8,128)(2,1)S(1)} %collective-permute-done.26.refs_1_, bf16[512,512]{1,0:T(8,128)(2,1)S(1)} %collective-permute-done.27.refs_2_, ...), custom_call_target="tpu_custom_call" | custom-call | flops 1 | bytes 1024 | tf_op jit(solution)/shard_map/pallas_call | solution.py:160
  89.5 0.9 collective-permute-start.30
  90.4 4.3 %collective-permute-done.32.refs_2_ = bf16[512,512]{1,0:T(8,128)(2,1)S(1)} collective-permute-done((bf16[512,512]{1,0:T(8,128)(2,1)S(1)}, bf16[512,512]{1,0:T(8,128)(2,1)S(1)}, u32[]{:S(2)}, u32[]{:S(2)}) %collective-permute-start.32) | collective-permute-done | bytes 524320 | tf_op jit(solution)/shard_map/ppermute | solution.py:586
  94.7 1.8 %shard_map.227 = (f32[8,128]{1,0:T(8,128)S(1)}, f32[512,2048]{1,0:T(8,128)}, f32[2048,512]{1,0:T(8,128)}) custom-call(bf16[512,512]{1,0:T(8,128)(2,1)S(1)} %shard_map.224.refs_5_.refs_0_, bf16[512,512]{1,0:T(8,128)(2,1)S(1)} %collective-permute-done.31.refs_1_, ...), custom_call_target="tpu_custom_call", output_to_operand_aliasing={{1}: (5, {}), {2}: (6, {})} | custom-call | flops 1 | bytes 1024 | tf_op jit(solution)/shard_map/pallas_call | solution.py:160
  96.6 0.6 collective-permute-start.33
  97.1 1.0 %shard_map.229 = (f32[8,128]{1,0:T(8,128)S(1)}, f32[512,2048]{1,0:T(8,128)}, f32[2048,512]{1,0:T(8,128)}) custom-call(bf16[512,512]{1,0:T(8,128)(2,1)S(1)} %collective-permute-done.34.refs_0_, s32[8,128]{1,0:T(8,128)S(1)} %get-tuple-element.114.refs_13_.refs_5_.refs_4_.refs_2_.refs_9_.refs_6_.refs_3_.refs_1_, ...), custom_call_target="tpu_custom_call", output_to_operand_aliasing={{1}: (3, {}), {2}: (4, {})} | custom-call | flops 1 | bytes 1024 | tf_op jit(solution)/shard_map/pallas_call | solution.py:160
  98.2 0.9 shard_map.230
  (48 shorter events, 0.8 us)
Async XLA Ops:
  1.5 11.6 %collective-permute-start.1 = (bf16[64,512]{1,0:T(8,128)(2,1)S(1)}, bf16[64,512]{1,0:T(8,128)(2,1)S(1)}, u32[]{:S(2)}, u32[]{:S(2)}) collective-permute-start(bf16[64,512]{1,0:T(8,128)(2,1)S(1)} %fusion), channel_id=1, source_target_pairs={{0,4},{2,6},{4,0},{6,2},{1,5},{3,7},{5,1},{7,3},{8,12},{10,14},{12... | collective-permute-start | bytes 196616 | tf_op jit(solution)/shard_map/ppermute | solution.py:556
  5.6 7.5 %collective-permute-start = (bf16[64,512]{1,0:T(8,128)(2,1)S(1)}, bf16[64,512]{1,0:T(8,128)(2,1)S(1)}, u32[]{:S(2)}, u32[]{:S(2)}) collective-permute-start(bf16[64,512]{1,0:T(8,128)(2,1)S(1)} %fusion), channel_id=1, source_target_pairs={{0,2},{2,0},{4,6},{6,4},{1,3},{3,1},{5,7},{7,5},{8,10},{10,8},{12,... | collective-permute-start | bytes 196616 | tf_op jit(solution)/shard_map/ppermute | solution.py:556
  7.2 6.1 %collective-permute-start.2 = (bf16[64,512]{1,0:T(8,128)(2,1)S(1)}, bf16[64,512]{1,0:T(8,128)(2,1)S(1)}, u32[]{:S(2)}, u32[]{:S(2)}) collective-permute-start(bf16[64,512]{1,0:T(8,128)(2,1)S(1)} %fusion), channel_id=1, source_target_pairs={{0,6},{2,4},{4,2},{6,0},{1,7},{3,5},{5,3},{7,1},{8,14},{10,12},{12... | collective-permute-start | bytes 196616 | tf_op jit(solution)/shard_map/ppermute | solution.py:556
  10.5 4.3 %copy-start = (bf16[2048,512]{1,0:T(8,128)(2,1)}, bf16[2048,512]{1,0:T(8,128)(2,1)S(1)}, u32[]{:S(2)}) copy-start(bf16[2048,512]{1,0:T(8,128)(2,1)S(1)} %get-tuple-element.101.refs_1_) | copy-start | bytes 6291460
  13.3 1.5 %collective-permute-start.3 = (bf16[192,512]{1,0:T(8,128)(2,1)S(1)}, bf16[192,512]{1,0:T(8,128)(2,1)S(1)}, u32[]{:S(2)}, u32[]{:S(2)}) collective-permute-start(bf16[192,512]{1,0:T(8,128)(2,1)S(1)} %shard_map.197.refs_0_.refs_14_), channel_id=1, source_target_pairs={{0,1},{1,0},{2,3},{3,2},{4,5},{5,4},{6,7},{7,6},{8,9},{9,8},{10,11... | collective-permute-start | bytes 589832 | tf_op jit(solution)/shard_map/ppermute | solution.py:556
  21.0 7.2 %collective-permute-start.4 = (bf16[512,512]{1,0:T(8,128)(2,1)S(1)}, bf16[512,512]{1,0:T(8,128)(2,1)S(1)}, u32[]{:S(2)}, u32[]{:S(2)}) collective-permute-start(bf16[512,512]{1,0:T(8,128)(2,1)S(1)} %get-tuple-element.126), channel_id=1, source_target_pairs={{0,1},{1,0},{2,3},{3,2},{4,5},{5,4},{6,7},{7,6},{8,9},{9,8},{10,11... | collective-permute-start | bytes 1572872 | tf_op jit(solution)/shard_map/ppermute | solution.py:556
  24.6 3.7 %collective-permute-start.5 = (bf16[512,512]{1,0:T(8,128)(2,1)S(1)}, bf16[512,512]{1,0:T(8,128)(2,1)S(1)}, u32[]{:S(2)}, u32[]{:S(2)}) collective-permute-start(bf16[512,512]{1,0:T(8,128)(2,1)S(1)} %get-tuple-element.127), channel_id=1, source_target_pairs={{0,1},{1,0},{2,3},{3,2},{4,5},{5,4},{6,7},{7,6},{8,9},{9,8},{10,11... | collective-permute-start | bytes 1572872 | tf_op jit(solution)/shard_map/ppermute | solution.py:556
  28.8 9.2 %collective-permute-start.6 = (bf16[512,512]{1,0:T(8,128)(2,1)S(1)}, bf16[512,512]{1,0:T(8,128)(2,1)S(1)}, u32[]{:S(2)}, u32[]{:S(2)}) collective-permute-start(bf16[512,512]{1,0:T(8,128)(2,1)S(1)} %get-tuple-element.129.refs_6_), channel_id=1, source_target_pairs={{0,8},{1,17},{2,10},{3,19},{4,12},{5,21},{6,14},{7,23},{8,0},{9,25... | collective-permute-start | bytes 1572872 | tf_op jit(solution)/shard_map/ppermute | solution.py:586
  30.4 9.5 %collective-permute-start.8 = (bf16[512,512]{1,0:T(8,128)(2,1)S(1)}, bf16[512,512]{1,0:T(8,128)(2,1)S(1)}, u32[]{:S(2)}, u32[]{:S(2)}) collective-permute-start(bf16[512,512]{1,0:T(8,128)(2,1)S(1)} %get-tuple-element.145), channel_id=1, source_target_pairs={{0,1},{1,0},{2,3},{3,2},{4,5},{5,4},{6,7},{7,6},{8,9},{9,8},{10,11... | collective-permute-start | bytes 1572872 | tf_op jit(solution)/shard_map/ppermute | solution.py:556
  33.6 6.3 %collective-permute-start.9 = (bf16[512,512]{1,0:T(8,128)(2,1)S(1)}, bf16[512,512]{1,0:T(8,128)(2,1)S(1)}, u32[]{:S(2)}, u32[]{:S(2)}) collective-permute-start(bf16[512,512]{1,0:T(8,128)(2,1)S(1)} %get-tuple-element.146), channel_id=1, source_target_pairs={{0,1},{1,0},{2,3},{3,2},{4,5},{5,4},{6,7},{7,6},{8,9},{9,8},{10,11... | collective-permute-start | bytes 1572872 | tf_op jit(solution)/shard_map/ppermute | solution.py:556
  38.2 6.4 %collective-permute-start.7 = (bf16[256,512]{1,0:T(8,128)(2,1)S(1)}, bf16[256,512]{1,0:T(8,128)(2,1)S(1)}, u32[]{:S(2)}, u32[]{:S(2)}) collective-permute-start(bf16[256,512]{1,0:T(8,128)(2,1)S(1)} %get-tuple-element.139.refs_5_), channel_id=1, source_target_pairs={{0,16},{1,9},{2,18},{3,11},{4,20},{5,13},{6,22},{7,15},{8,24},{9,1... | collective-permute-start | bytes 786440 | tf_op jit(solution)/shard_map/ppermute | solution.py:586
  40.4 9.9 %collective-permute-start.11 = (bf16[512,512]{1,0:T(8,128)(2,1)S(1)}, bf16[512,512]{1,0:T(8,128)(2,1)S(1)}, u32[]{:S(2)}, u32[]{:S(2)}) collective-permute-start(bf16[512,512]{1,0:T(8,128)(2,1)S(1)} %get-tuple-element.147.refs_12_), channel_id=1, source_target_pairs={{0,16},{1,9},{2,18},{3,11},{4,20},{5,13},{6,22},{7,15},{8,24},{9,1... | collective-permute-start | bytes 1572872 | tf_op jit(solution)/shard_map/ppermute | solution.py:586
  44.8 7.4 %collective-permute-start.10 = (bf16[128,512]{1,0:T(8,128)(2,1)S(1)}, bf16[128,512]{1,0:T(8,128)(2,1)S(1)}, u32[]{:S(2)}, u32[]{:S(2)}) collective-permute-start(bf16[128,512]{1,0:T(8,128)(2,1)S(1)} %get-tuple-element.150.refs_10_), channel_id=1, source_target_pairs={{0,2},{2,0},{4,6},{6,4},{1,3},{3,1},{5,7},{7,5},{8,10},{10,8},{12,... | collective-permute-start | bytes 393224 | tf_op jit(solution)/shard_map/ppermute | solution.py:575
  48.5 11.2 %collective-permute-start.12 = (bf16[128,512]{1,0:T(8,128)(2,1)S(1)}, bf16[128,512]{1,0:T(8,128)(2,1)S(1)}, u32[]{:S(2)}, u32[]{:S(2)}) collective-permute-start(bf16[128,512]{1,0:T(8,128)(2,1)S(1)} %get-tuple-element.162), channel_id=1, source_target_pairs={{0,1},{1,0},{2,3},{3,2},{4,5},{5,4},{6,7},{7,6},{8,9},{9,8},{10,11... | collective-permute-start | bytes 393224 | tf_op jit(solution)/shard_map/ppermute | solution.py:556
  48.6 11.1 %collective-permute-start.13 = (bf16[128,512]{1,0:T(8,128)(2,1)S(1)}, bf16[128,512]{1,0:T(8,128)(2,1)S(1)}, u32[]{:S(2)}, u32[]{:S(2)}) collective-permute-start(bf16[128,512]{1,0:T(8,128)(2,1)S(1)} %get-tuple-element.163), channel_id=1, source_target_pairs={{0,1},{1,0},{2,3},{3,2},{4,5},{5,4},{6,7},{7,6},{8,9},{9,8},{10,11... | collective-permute-start | bytes 393224 | tf_op jit(solution)/shard_map/ppermute | solution.py:556
  49.1 10.6 %collective-permute-start.14 = (bf16[128,512]{1,0:T(8,128)(2,1)S(1)}, bf16[128,512]{1,0:T(8,128)(2,1)S(1)}, u32[]{:S(2)}, u32[]{:S(2)}) collective-permute-start(bf16[128,512]{1,0:T(8,128)(2,1)S(1)} %get-tuple-element.164), channel_id=1, source_target_pairs={{0,1},{1,0},{2,3},{3,2},{4,5},{5,4},{6,7},{7,6},{8,9},{9,8},{10,11... | collective-permute-start | bytes 393224 | tf_op jit(solution)/shard_map/ppermute | solution.py:556
  50.5 7.2 %collective-permute-start.15 = (bf16[256,512]{1,0:T(8,128)(2,1)S(1)}, bf16[256,512]{1,0:T(8,128)(2,1)S(1)}, u32[]{:S(2)}, u32[]{:S(2)}) collective-permute-start(bf16[256,512]{1,0:T(8,128)(2,1)S(1)} %get-tuple-element.157.refs_3_), channel_id=1, source_target_pairs={{0,8},{1,17},{2,10},{3,19},{4,12},{5,21},{6,14},{7,23},{8,0},{9,25... | collective-permute-start | bytes 786440 | tf_op jit(solution)/shard_map/ppermute | solution.py:586
  52.1 2.4 %copy-start.1 = (bf16[2048,512]{1,0:T(8,128)(2,1)S(1)}, bf16[2048,512]{1,0:T(8,128)(2,1)}, u32[]{:S(2)}) copy-start(bf16[2048,512]{1,0:T(8,128)(2,1)} %copy-done) | copy-start | bytes 6291460
  52.2 9.3 %collective-permute-start.17 = (bf16[128,512]{1,0:T(8,128)(2,1)S(1)}, bf16[128,512]{1,0:T(8,128)(2,1)S(1)}, u32[]{:S(2)}, u32[]{:S(2)}) collective-permute-start(bf16[128,512]{1,0:T(8,128)(2,1)S(1)} %shard_map.211.refs_6_.refs_0_), channel_id=1, source_target_pairs={{0,4},{2,6},{4,0},{6,2},{1,5},{3,7},{5,1},{7,3},{8,12},{10,14},{12... | collective-permute-start | bytes 393224 | tf_op jit(solution)/shard_map/ppermute | solution.py:575
  57.8 6.2 %collective-permute-start.19 = (bf16[128,512]{1,0:T(8,128)(2,1)S(1)}, bf16[128,512]{1,0:T(8,128)(2,1)S(1)}, u32[]{:S(2)}, u32[]{:S(2)}) collective-permute-start(bf16[128,512]{1,0:T(8,128)(2,1)S(1)} %get-tuple-element.167.refs_7_), channel_id=1, source_target_pairs={{0,2},{2,0},{4,6},{6,4},{1,3},{3,1},{5,7},{7,5},{8,10},{10,8},{12,... | collective-permute-start | bytes 393224 | tf_op jit(solution)/shard_map/ppermute | solution.py:575
  59.9 8.8 %collective-permute-start.16 = (bf16[192,512]{1,0:T(8,128)(2,1)S(1)}, bf16[192,512]{1,0:T(8,128)(2,1)S(1)}, u32[]{:S(2)}, u32[]{:S(2)}) collective-permute-start(bf16[192,512]{1,0:T(8,128)(2,1)S(1)} %get-tuple-element.169.refs_3_), channel_id=1, source_target_pairs={{0,16},{1,9},{2,18},{3,11},{4,20},{5,13},{6,22},{7,15},{8,24},{9,1... | collective-permute-start | bytes 589832 | tf_op jit(solution)/shard_map/ppermute | solution.py:586
  61.5 5.3 %collective-permute-start.18 = (bf16[128,512]{1,0:T(8,128)(2,1)S(1)}, bf16[128,512]{1,0:T(8,128)(2,1)S(1)}, u32[]{:S(2)}, u32[]{:S(2)}) collective-permute-start(bf16[128,512]{1,0:T(8,128)(2,1)S(1)} %shard_map.215.refs_3_.refs_0_), channel_id=1, source_target_pairs={{0,2},{2,0},{4,6},{6,4},{1,3},{3,1},{5,7},{7,5},{8,10},{10,8},{12,... | collective-permute-start | bytes 393224 | tf_op jit(solution)/shard_map/ppermute | solution.py:575
  64.0 8.6 %collective-permute-start.22 = (bf16[128,512]{1,0:T(8,128)(2,1)S(1)}, bf16[128,512]{1,0:T(8,128)(2,1)S(1)}, u32[]{:S(2)}, u32[]{:S(2)}) collective-permute-start(bf16[128,512]{1,0:T(8,128)(2,1)S(1)} %shard_map.216.refs_3_.refs_0_), channel_id=1, source_target_pairs={{0,4},{2,6},{4,0},{6,2},{1,5},{3,7},{5,1},{7,3},{8,12},{10,14},{12... | collective-permute-start | bytes 393224 | tf_op jit(solution)/shard_map/ppermute | solution.py:575
  66.8 6.4 %collective-permute-start.21 = (bf16[256,512]{1,0:T(8,128)(2,1)S(1)}, bf16[256,512]{1,0:T(8,128)(2,1)S(1)}, u32[]{:S(2)}, u32[]{:S(2)}) collective-permute-start(bf16[256,512]{1,0:T(8,128)(2,1)S(1)} %shard_map.217.refs_3_.refs_0_), channel_id=1, source_target_pairs={{0,16},{1,9},{2,18},{3,11},{4,20},{5,13},{6,22},{7,15},{8,24},{9,1... | collective-permute-start | bytes 786440 | tf_op jit(solution)/shard_map/ppermute | solution.py:586
  68.7 6.2 %collective-permute-start.20 = (bf16[128,512]{1,0:T(8,128)(2,1)S(1)}, bf16[128,512]{1,0:T(8,128)(2,1)S(1)}, u32[]{:S(2)}, u32[]{:S(2)}) collective-permute-start(bf16[128,512]{1,0:T(8,128)(2,1)S(1)} %get-tuple-element.172.refs_3_), channel_id=1, source_target_pairs={{0,2},{2,0},{4,6},{6,4},{1,3},{3,1},{5,7},{7,5},{8,10},{10,8},{12,... | collective-permute-start | bytes 393224 | tf_op jit(solution)/shard_map/ppermute | solution.py:575
  72.6 5.0 %collective-permute-start.24 = (bf16[128,512]{1,0:T(8,128)(2,1)S(1)}, bf16[128,512]{1,0:T(8,128)(2,1)S(1)}, u32[]{:S(2)}, u32[]{:S(2)}) collective-permute-start(bf16[128,512]{1,0:T(8,128)(2,1)S(1)} %shard_map.219.refs_3_.refs_0_), channel_id=1, source_target_pairs={{0,2},{2,0},{4,6},{6,4},{1,3},{3,1},{5,7},{7,5},{8,10},{10,8},{12,... | collective-permute-start | bytes 393224 | tf_op jit(solution)/shard_map/ppermute | solution.py:575
  73.4 11.4 %collective-permute-start.27 = (bf16[512,512]{1,0:T(8,128)(2,1)S(1)}, bf16[512,512]{1,0:T(8,128)(2,1)S(1)}, u32[]{:S(2)}, u32[]{:S(2)}) collective-permute-start(bf16[512,512]{1,0:T(8,128)(2,1)S(1)} %shard_map.220.refs_3_.refs_0_), channel_id=1, source_target_pairs={{0,8},{1,17},{2,10},{3,19},{4,12},{5,21},{6,14},{7,23},{8,0},{9,25... | collective-permute-start | bytes 1572872 | tf_op jit(solution)/shard_map/ppermute | solution.py:586
  74.9 12.4 %collective-permute-start.26 = (bf16[512,512]{1,0:T(8,128)(2,1)S(1)}, bf16[512,512]{1,0:T(8,128)(2,1)S(1)}, u32[]{:S(2)}, u32[]{:S(2)}) collective-permute-start(bf16[512,512]{1,0:T(8,128)(2,1)S(1)} %shard_map.220.refs_3_.refs_0_), channel_id=1, source_target_pairs={{0,1},{1,0},{2,3},{3,2},{4,5},{5,4},{6,7},{7,6},{8,9},{9,8},{10,11... | collective-permute-start | bytes 1572872 | tf_op jit(solution)/shard_map/ppermute | solution.py:556
  75.0 8.3 %collective-permute-start.23 = (bf16[96,512]{1,0:T(8,128)(2,1)S(1)}, bf16[96,512]{1,0:T(8,128)(2,1)S(1)}, u32[]{:S(2)}, u32[]{:S(2)}) collective-permute-start(bf16[96,512]{1,0:T(8,128)(2,1)S(1)} %get-tuple-element.174.refs_3_), channel_id=1, source_target_pairs={{0,4},{2,6},{4,0},{6,2},{1,5},{3,7},{5,1},{7,3},{8,12},{10,14},{12... | collective-permute-start | bytes 294920 | tf_op jit(solution)/shard_map/ppermute | solution.py:575
  77.7 7.7 %collective-permute-start.29 = (bf16[256,512]{1,0:T(8,128)(2,1)S(1)}, bf16[256,512]{1,0:T(8,128)(2,1)S(1)}, u32[]{:S(2)}, u32[]{:S(2)}) collective-permute-start(bf16[256,512]{1,0:T(8,128)(2,1)S(1)} %shard_map.222.refs_3_.refs_0_), channel_id=1, source_target_pairs={{0,8},{1,17},{2,10},{3,19},{4,12},{5,21},{6,14},{7,23},{8,0},{9,25... | collective-permute-start | bytes 786440 | tf_op jit(solution)/shard_map/ppermute | solution.py:586
  83.3 6.2 %collective-permute-start.25 = (bf16[96,512]{1,0:T(8,128)(2,1)S(1)}, bf16[96,512]{1,0:T(8,128)(2,1)S(1)}, u32[]{:S(2)}, u32[]{:S(2)}) collective-permute-start(bf16[96,512]{1,0:T(8,128)(2,1)S(1)} %shard_map.223.refs_3_.refs_0_), channel_id=1, source_target_pairs={{0,8},{1,17},{2,10},{3,19},{4,12},{5,21},{6,14},{7,23},{8,0},{9,25... | collective-permute-start | bytes 294920 | tf_op jit(solution)/shard_map/ppermute | solution.py:586
  84.7 2.6 %collective-permute-start.28 = (bf16[512,512]{1,0:T(8,128)(2,1)S(1)}, bf16[512,512]{1,0:T(8,128)(2,1)S(1)}, u32[]{:S(2)}, u32[]{:S(2)}) collective-permute-start(bf16[512,512]{1,0:T(8,128)(2,1)S(1)} %collective-permute-done.27.refs_2_), channel_id=1, source_target_pairs={{0,1},{1,0},{2,3},{3,2},{4,5},{5,4},{6,7},{7,6},{8,9},{9,8},{10,11... | collective-permute-start | bytes 1572872 | tf_op jit(solution)/shard_map/ppermute | solution.py:556
  85.5 9.2 %collective-permute-start.32 = (bf16[512,512]{1,0:T(8,128)(2,1)S(1)}, bf16[512,512]{1,0:T(8,128)(2,1)S(1)}, u32[]{:S(2)}, u32[]{:S(2)}) collective-permute-start(bf16[512,512]{1,0:T(8,128)(2,1)S(1)} %shard_map.224.refs_5_.refs_0_), channel_id=1, source_target_pairs={{0,16},{1,9},{2,18},{3,11},{4,20},{5,13},{6,22},{7,15},{8,24},{9,1... | collective-permute-start | bytes 1572872 | tf_op jit(solution)/shard_map/ppermute | solution.py:586
  87.3 7.4 %collective-permute-start.31 = (bf16[512,512]{1,0:T(8,128)(2,1)S(1)}, bf16[512,512]{1,0:T(8,128)(2,1)S(1)}, u32[]{:S(2)}, u32[]{:S(2)}) collective-permute-start(bf16[512,512]{1,0:T(8,128)(2,1)S(1)} %shard_map.224.refs_5_.refs_0_), channel_id=1, source_target_pairs={{0,1},{1,0},{2,3},{3,2},{4,5},{5,4},{6,7},{7,6},{8,9},{9,8},{10,11... | collective-permute-start | bytes 1572872 | tf_op jit(solution)/shard_map/ppermute | solution.py:556
  89.5 7.0 %collective-permute-start.30 = (bf16[96,512]{1,0:T(8,128)(2,1)S(1)}, bf16[96,512]{1,0:T(8,128)(2,1)S(1)}, u32[]{:S(2)}, u32[]{:S(2)}) collective-permute-start(bf16[96,512]{1,0:T(8,128)(2,1)S(1)} %shard_map.226.refs_4_.refs_0_), channel_id=1, source_target_pairs={{0,16},{1,9},{2,18},{3,11},{4,20},{5,13},{6,22},{7,15},{8,24},{9,1... | collective-permute-start | bytes 294920 | tf_op jit(solution)/shard_map/ppermute | solution.py:586
  94.7 2.4 %collective-permute-start.34 = (bf16[512,512]{1,0:T(8,128)(2,1)S(1)}, bf16[512,512]{1,0:T(8,128)(2,1)S(1)}, u32[]{:S(2)}, u32[]{:S(2)}) collective-permute-start(bf16[512,512]{1,0:T(8,128)(2,1)S(1)} %collective-permute-done.32.refs_2_), channel_id=1, source_target_pairs={{0,1},{1,0},{2,3},{3,2},{4,5},{5,4},{6,7},{7,6},{8,9},{9,8},{10,11... | collective-permute-start | bytes 1572872 | tf_op jit(solution)/shard_map/ppermute | solution.py:556
  96.6 1.6 %collective-permute-start.33 = (bf16[192,512]{1,0:T(8,128)(2,1)S(1)}, bf16[192,512]{1,0:T(8,128)(2,1)S(1)}, u32[]{:S(2)}, u32[]{:S(2)}) collective-permute-start(bf16[192,512]{1,0:T(8,128)(2,1)S(1)} %shard_map.228.refs_2_.refs_0_), channel_id=1, source_target_pairs={{0,1},{1,0},{2,3},{3,2},{4,5},{5,4},{6,7},{7,6},{8,9},{9,8},{10,11... | collective-permute-start | bytes 589832 | tf_op jit(solution)/shard_map/ppermute | solution.py:556

commit v7 on v6

--- a/solution.py
+++ b/solution.py
@@ -1073,8 +1073,8 @@
     for i, name in enumerate("ab"):
         acts[name.upper()] = functools.partial(ffn, name, i)
     acts["1"] = lambda: place_some("a", lambda other, far: True)
-    acts["2"] = lambda: place_some("b", lambda other, far: not (other and far))
-    acts["3"] = lambda: place_some("b", lambda other, far: other and far)
+    acts["2"] = lambda: place_some("b", lambda other, far: not far)
+    acts["3"] = lambda: place_some("b", lambda other, far: far)
     for word in ORDER:
         if word in acts:
             acts[word]()

time: 99.3 us -> 99.3 us (level)
  no operation moved by 1% of the time
where the time goes in v7:
time: 99.3 us; the launch traced here: 99.1 us
  Pallas kernels  42.3 us (43%)
  starting transfers between devices  35.8 us (36%)
  waiting for transfers between devices  19.1 us (19%)
  between operations  1 us (1%)
    pallas_call x36, Pallas kernels, call(): pl.pallas_call(wrapped, out_shape=outs + list(sent), in_specs=[pl.BlockSp...  42.3 us
    ppermute x11, starting transfers between devices, swap(): return lax.ppermute(array, AXES, pairs)  16.3 us
    ppermute x8, starting transfers between devices, swap(): lax.ppermute(array, 'expert', [(i, i ^ 1 << stage) for i in range(size)])  11.2 us
    ppermute x8, waiting for transfers between devices, swap(): lax.ppermute(array, 'expert', [(i, i ^ 1 << stage) for i in range(size)])  9.51 us
    ppermute x16, starting transfers between devices, exchange(): lax.ppermute(parts[k], axis, [(i, i ^ k) for i in range(size)])  8.23 us
    ppermute x11, waiting for transfers between devices, swap(): return lax.ppermute(array, AXES, pairs)  7.95 us
  transfers between devices with their start and end apart: 35, of which 12 were waited for; matrix products, arithmetic and copies ran while one was open for 0% of the time, Pallas kernels for 35%

profile of v7, /device:TPU:0, one launch (start us, length us, event | category | flops | bytes accessed | tf_op | source)
XLA Modules:
  0.0 99.1 jit_solution(13690761494761770295)
XLA Ops:
  0.6 0.9 fusion
  1.5 4.1 %collective-permute-start.1 = (bf16[64,512]{1,0:T(8,128)(2,1)S(1)}, bf16[64,512]{1,0:T(8,128)(2,1)S(1)}, u32[]{:S(2)}, u32[]{:S(2)}) collective-permute-start(bf16[64,512]{1,0:T(8,128)(2,1)S(1)} %fusion), channel_id=1, source_target_pairs={{0,4},{2,6},{4,0},{6,2},{1,5},{3,7},{5,1},{7,3},{8,12},{10,14},{12... | collective-permute-start | bytes 196616 | tf_op jit(solution)/shard_map/ppermute | solution.py:556
  5.6 1.6 %collective-permute-start = (bf16[64,512]{1,0:T(8,128)(2,1)S(1)}, bf16[64,512]{1,0:T(8,128)(2,1)S(1)}, u32[]{:S(2)}, u32[]{:S(2)}) collective-permute-start(bf16[64,512]{1,0:T(8,128)(2,1)S(1)} %fusion), channel_id=1, source_target_pairs={{0,2},{2,0},{4,6},{6,4},{1,3},{3,1},{5,7},{7,5},{8,10},{10,8},{12,... | collective-permute-start | bytes 196616 | tf_op jit(solution)/shard_map/ppermute | solution.py:556
  7.2 0.1 stack.27.refs_11_.refs_12_
  7.3 3.2 %shard_map.195 = (bf16[1024,512]{1,0:T(8,128)(2,1)S(1)}, bf16[1024,128]{1,0:T(8,128)(2,1)S(1)}, bf16[128,1024]{1,0:T(8,128)(2,1)S(1)}, f32[2,1024]{1,0:T(2,128)S...) custom-call(f32[1,512]{1,0:T(1,128)} %bitcast.24, ...), custom_call_target="tpu_custom_call" | custom-call | flops 1 | bytes 1024 | tf_op jit(solution)/shard_map/pallas_call | solution.py:160
  10.5 2.6 %shard_map.196 = (bf16[1024,2048]{1,0:T(8,128)(2,1)S(1)}, bf16[512,2048]{1,0:T(8,128)(2,1)S(1)}) custom-call(bf16[1024,512]{1,0:T(8,128)(2,1)S(1)} %get-tuple-element.100.refs_0_.refs_1_, bf16[2048,512]{1,0:T(8,128)(2,1)S(1)} %get-tuple-element.101.refs_1_, bf16[512,2048]{1,0:T(8,128)(2,1)} %refs_2_.1, f32[1,1024]{1,0:T(1,128)S(1)} %get-tuple-element.102.refs_3_.refs_8_.refs_10_), custom_call_target="tpu_custom_call" | custom-call | flops 1 | bytes 1024 | tf_op jit(solution)/shard_map/pallas_call | solution.py:160
  13.1 0.1 collective-permute-done.2.refs_2_
  13.3 0.1 collective-permute-start.3
  13.4 1.4 %collective-permute-done.3.refs_1_ = bf16[192,512]{1,0:T(8,128)(2,1)S(1)} collective-permute-done((bf16[192,512]{1,0:T(8,128)(2,1)S(1)}, bf16[192,512]{1,0:T(8,128)(2,1)S(1)}, u32[]{:S(2)}, u32[]{:S(2)}) %collective-permute-start.3) | collective-permute-done | bytes 196640 | tf_op jit(solution)/shard_map/ppermute | solution.py:556
  14.8 3.0 %shard_map.198 = (bf16[256,512]{1,0:T(8,128)(2,1)S(1)}, bf16[256,512]{1,0:T(8,128)(2,1)S(1)}, bf16[64,2048]{1,0:T(8,128)(2,1)S(1)}, bf16[64,2048]{1,0:T(8,128)(2...) custom-call(bf16[192,512]{1,0:T(8,128)(2,1)S(1)} %shard_map.197.refs, ...), custom_call_target="tpu_custom_call" | custom-call | flops 1 | bytes 1024 | tf_op jit(solution)/shard_map/pallas_call | solution.py:160
  17.8 3.2 %shard_map.199 = (bf16[1024,512]{1,0:T(8,128)(2,1)S(1)}, bf16[1024,512]{1,0:T(8,128)(2,1)S(1)}, bf16[512,512]{1,0:T(8,128)(2,1)S(1)}, bf16[512,512]{1,0:T(8,128)(2,1)S(1)}) custom-call(bf16[1024,512]{1,0:T(8,128)(2,1)S(1)} %get-tuple-element.116.refs_0_, bf16[512,1024]{1,0:T(8,128)(2,1)S(1)} %get-tuple-element.117.refs_1_, ...), custom_call_target="tpu_custom_call" | custom-call | flops 1 | bytes 1024 | tf_op jit(solution)/shard_map/pallas_call | solution.py:160
  21.0 0.2 collective-permute-start.4
  21.2 3.4 %shard_map.200 = (bf16[1024,512]{1,0:T(8,128)(2,1)S(1)}, bf16[1024,512]{1,0:T(8,128)(2,1)S(1)}, bf16[512,512]{1,0:T(8,128)(2,1)S(1)}, bf16[512,512]{1,0:T(8,128)(2,1)S(1)}) custom-call(bf16[1024,512]{1,0:T(8,128)(2,1)S(1)} %get-tuple-element.116.refs_0_, bf16[512,1024]{1,0:T(8,128)(2,1)S(1)} %get-tuple-element.117.refs_1_, ...), custom_call_target="tpu_custom_call" | custom-call | flops 1 | bytes 1024 | tf_op jit(solution)/shard_map/pallas_call | solution.py:160
  24.6 0.4 collective-permute-start.5
  25.1 3.2 %shard_map.201 = (bf16[1024,512]{1,0:T(8,128)(2,1)S(1)}, bf16[1024,512]{1,0:T(8,128)(2,1)S(1)}, bf16[512,512]{1,0:T(8,128)(2,1)S(1)}, bf16[512,512]{1,0:T(8,128)(2,1)S(1)}) custom-call(bf16[1024,512]{1,0:T(8,128)(2,1)S(1)} %get-tuple-element.116.refs_0_, bf16[512,1024]{1,0:T(8,128)(2,1)S(1)} %get-tuple-element.117.refs_1_, ...), custom_call_target="tpu_custom_call" | custom-call | flops 1 | bytes 1024 | tf_op jit(solution)/shard_map/pallas_call | solution.py:160
  28.3 0.5 shard_map.202
  28.8 1.6 %collective-permute-start.6 = (bf16[512,512]{1,0:T(8,128)(2,1)S(1)}, bf16[512,512]{1,0:T(8,128)(2,1)S(1)}, u32[]{:S(2)}, u32[]{:S(2)}) collective-permute-start(bf16[512,512]{1,0:T(8,128)(2,1)S(1)} %get-tuple-element.129.refs_6_), channel_id=1, source_target_pairs={{0,8},{1,17},{2,10},{3,19},{4,12},{5,21},{6,14},{7,23},{8,0},{9,25... | collective-permute-start | bytes 1572872 | tf_op jit(solution)/shard_map/ppermute | solution.py:586
  30.4 3.2 %shard_map.203 = (bf16[1024,512]{1,0:T(8,128)(2,1)S(1)}, bf16[1024,512]{1,0:T(8,128)(2,1)S(1)}, bf16[512,512]{1,0:T(8,128)(2,1)S(1)}, bf16[512,512]{1,0:T(8,128)(2,1)S(1)}) custom-call(bf16[1024,512]{1,0:T(8,128)(2,1)S(1)} %get-tuple-element.116.refs_0_, bf16[512,1024]{1,0:T(8,128)(2,1)S(1)} %get-tuple-element.117.refs_1_, ...), custom_call_target="tpu_custom_call" | custom-call | flops 1 | bytes 1024 | tf_op jit(solution)/shard_map/pallas_call | solution.py:160
  33.6 0.6 collective-permute-start.9
  34.2 3.2 %shard_map.204 = (f32[1024,512]{1,0:T(8,128)S(1)}, bf16[1024,512]{1,0:T(8,128)(2,1)S(1)}, f32[1,512]{1,0:T(1,128)S(1)}) custom-call(f32[1024,512]{1,0:T(8,128)S(1)} %get-tuple-element.115.refs_0_, bf16[1024,512]{1,0:T(8,128)(2,1)S(1)} %get-tuple-element.100.refs_0_.refs_1_, bf16[512,2048]{1,0:T(8,128)(2,1)S(1)} %get-tuple-element.103.refs_3_.refs_4_.refs_2_, ...), custom_call_target="tpu_custom_call" | custom-call | flops 1 | bytes 1024 | tf_op jit(solution)/shard_map/pallas_call | solution.py:160
  37.4 0.6 collective-permute-done.6.refs_1_
  38.0 0.2 shard_map.205
  38.2 1.7 %collective-permute-start.7 = (bf16[256,512]{1,0:T(8,128)(2,1)S(1)}, bf16[256,512]{1,0:T(8,128)(2,1)S(1)}, u32[]{:S(2)}, u32[]{:S(2)}) collective-permute-start(bf16[256,512]{1,0:T(8,128)(2,1)S(1)} %get-tuple-element.139.refs_5_), channel_id=1, source_target_pairs={{0,16},{1,9},{2,18},{3,11},{4,20},{5,13},{6,22},{7,15},{8,24},{9,1... | collective-permute-start | bytes 786440 | tf_op jit(solution)/shard_map/ppermute | solution.py:586
  39.9 0.5 shard_map.206
  40.4 0.5 collective-permute-start.11
  40.9 3.1 %shard_map.207 = (bf16[400,1024]{1,0:T(8,128)(2,1)S(1)}, bf16[256,512]{1,0:T(8,128)(2,1)S(1)}) custom-call(bf16[1024,128]{1,0:T(8,128)(2,1)S(1)} %get-tuple-element.105.refs_3_.refs_0_, bf16[128,1024]{1,0:T(8,128)(2,1)S(1)} %get-tuple-element.106.refs_4_.refs_1_, f32[2,1024]{1,0:T(2,128)S(1)} %get-tuple-element.107.refs_5_.refs_2_, ...), custom_call_target="tpu_custom_call" | custom-call | flops 1 | bytes 1024 | tf_op jit(solution)/shard_map/pallas_call | solution.py:160
  44.0 0.7 collective-permute-done.7.refs_1_
  44.7 0.1 shard_map.208
  44.8 0.8 collective-permute-start.10
  45.6 2.9 %shard_map.209 = (bf16[128,512]{1,0:T(8,128)(2,1)S(1)}, bf16[128,512]{1,0:T(8,128)(2,1)S(1)}, bf16[128,512]{1,0:T(8,128)(2,1)S(1)}, bf16[128,512]{1,0:T(8,128)(2...) custom-call(bf16[400,1024]{1,0:T(8,128)(2,1)S(1)} %get-tuple-element.152.refs_0_, ...), custom_call_target="tpu_custom_call" | custom-call | flops 1 | bytes 1024 | tf_op jit(solution)/shard_map/pallas_call | solution.py:160
  48.6 0.5 collective-permute-start.13
  49.1 0.1 collective-permute-start.14
  49.2 1.1 %collective-permute-done.11.refs_1_ = bf16[512,512]{1,0:T(8,128)(2,1)S(1)} collective-permute-done((bf16[512,512]{1,0:T(8,128)(2,1)S(1)}, bf16[512,512]{1,0:T(8,128)(2,1)S(1)}, u32[]{:S(2)}, u32[]{:S(2)}) %collective-permute-start.11) | collective-permute-done | bytes 524320 | tf_op jit(solution)/shard_map/ppermute | solution.py:586
  50.3 0.2 shard_map.210
  50.5 1.6 %collective-permute-start.15 = (bf16[256,512]{1,0:T(8,128)(2,1)S(1)}, bf16[256,512]{1,0:T(8,128)(2,1)S(1)}, u32[]{:S(2)}, u32[]{:S(2)}) collective-permute-start(bf16[256,512]{1,0:T(8,128)(2,1)S(1)} %get-tuple-element.157.refs_3_), channel_id=1, source_target_pairs={{0,8},{1,17},{2,10},{3,19},{4,12},{5,21},{6,14},{7,23},{8,0},{9,25... | collective-permute-start | bytes 786440 | tf_op jit(solution)/shard_map/ppermute | solution.py:586
  52.2 2.4 %collective-permute-start.17 = (bf16[128,512]{1,0:T(8,128)(2,1)S(1)}, bf16[128,512]{1,0:T(8,128)(2,1)S(1)}, u32[]{:S(2)}, u32[]{:S(2)}) collective-permute-start(bf16[128,512]{1,0:T(8,128)(2,1)S(1)} %shard_map.211.refs_6_.refs_0_), channel_id=1, source_target_pairs={{0,4},{2,6},{4,0},{6,2},{1,5},{3,7},{5,1},{7,3},{8,12},{10,14},{12... | collective-permute-start | bytes 393224 | tf_op jit(solution)/shard_map/ppermute | solution.py:575
  54.6 3.1 %shard_map.212 = (f32[8,128]{1,0:T(8,128)S(1)}, bf16[1024,512]{1,0:T(8,128)(2,1)}) custom-call(f32[1024,512]{1,0:T(8,128)S(1)} %get-tuple-element.115.refs_0_, bf16[2048,512]{1,0:T(8,128)(2,1)S(1)} %copy-done.1, bf16[1024,512]{1,0:T(8,128)(2,1)S(1)} %get-tuple-element.121.refs_2_, bf16[1024,512]{1,0:T(8,128)(2,1)S(1)} %get-tuple-element.123.refs_3_, ...), custom_call_target="tpu_custom_call" | custom-call | flops 1 | bytes 1024 | tf_op jit(solution)/shard_map/pallas_call | solution.py:160
  57.7 0.1 shard_map.213
  57.8 1.9 %collective-permute-start.19 = (bf16[128,512]{1,0:T(8,128)(2,1)S(1)}, bf16[128,512]{1,0:T(8,128)(2,1)S(1)}, u32[]{:S(2)}, u32[]{:S(2)}) collective-permute-start(bf16[128,512]{1,0:T(8,128)(2,1)S(1)} %get-tuple-element.167.refs_7_), channel_id=1, source_target_pairs={{0,2},{2,0},{4,6},{6,4},{1,3},{3,1},{5,7},{7,5},{8,10},{10,8},{12,... | collective-permute-start | bytes 393224 | tf_op jit(solution)/shard_map/ppermute | solution.py:575
  59.7 0.1 shard_map.214
  59.9 1.6 %collective-permute-start.16 = (bf16[192,512]{1,0:T(8,128)(2,1)S(1)}, bf16[192,512]{1,0:T(8,128)(2,1)S(1)}, u32[]{:S(2)}, u32[]{:S(2)}) collective-permute-start(bf16[192,512]{1,0:T(8,128)(2,1)S(1)} %get-tuple-element.169.refs_3_), channel_id=1, source_target_pairs={{0,16},{1,9},{2,18},{3,11},{4,20},{5,13},{6,22},{7,15},{8,24},{9,1... | collective-permute-start | bytes 589832 | tf_op jit(solution)/shard_map/ppermute | solution.py:586
  61.5 0.3 collective-permute-start.18
  61.8 2.2 %collective-permute-done.19.refs_1_ = bf16[128,512]{1,0:T(8,128)(2,1)S(1)} collective-permute-done((bf16[128,512]{1,0:T(8,128)(2,1)S(1)}, bf16[128,512]{1,0:T(8,128)(2,1)S(1)}, u32[]{:S(2)}, u32[]{:S(2)}) %collective-permute-start.19) | collective-permute-done | bytes 131104 | tf_op jit(solution)/shard_map/ppermute | solution.py:575
  64.0 1.9 %collective-permute-start.22 = (bf16[128,512]{1,0:T(8,128)(2,1)S(1)}, bf16[128,512]{1,0:T(8,128)(2,1)S(1)}, u32[]{:S(2)}, u32[]{:S(2)}) collective-permute-start(bf16[128,512]{1,0:T(8,128)(2,1)S(1)} %shard_map.216.refs_3_.refs_0_), channel_id=1, source_target_pairs={{0,4},{2,6},{4,0},{6,2},{1,5},{3,7},{5,1},{7,3},{8,12},{10,14},{12... | collective-permute-start | bytes 393224 | tf_op jit(solution)/shard_map/ppermute | solution.py:575
  66.0 0.8 collective-permute-done.18.refs_1_
  66.8 1.8 %collective-permute-start.21 = (bf16[256,512]{1,0:T(8,128)(2,1)S(1)}, bf16[256,512]{1,0:T(8,128)(2,1)S(1)}, u32[]{:S(2)}, u32[]{:S(2)}) collective-permute-start(bf16[256,512]{1,0:T(8,128)(2,1)S(1)} %shard_map.217.refs_3_.refs_0_), channel_id=1, source_target_pairs={{0,16},{1,9},{2,18},{3,11},{4,20},{5,13},{6,22},{7,15},{8,24},{9,1... | collective-permute-start | bytes 786440 | tf_op jit(solution)/shard_map/ppermute | solution.py:586
  68.6 0.1 shard_map.218
  68.7 1.2 %collective-permute-start.20 = (bf16[128,512]{1,0:T(8,128)(2,1)S(1)}, bf16[128,512]{1,0:T(8,128)(2,1)S(1)}, u32[]{:S(2)}, u32[]{:S(2)}) collective-permute-start(bf16[128,512]{1,0:T(8,128)(2,1)S(1)} %get-tuple-element.172.refs_3_), channel_id=1, source_target_pairs={{0,2},{2,0},{4,6},{6,4},{1,3},{3,1},{5,7},{7,5},{8,10},{10,8},{12,... | collective-permute-start | bytes 393224 | tf_op jit(solution)/shard_map/ppermute | solution.py:575
  69.9 2.7 %collective-permute-done.22.refs_1_ = bf16[128,512]{1,0:T(8,128)(2,1)S(1)} collective-permute-done((bf16[128,512]{1,0:T(8,128)(2,1)S(1)}, bf16[128,512]{1,0:T(8,128)(2,1)S(1)}, u32[]{:S(2)}, u32[]{:S(2)}) %collective-permute-start.22) | collective-permute-done | bytes 131104 | tf_op jit(solution)/shard_map/ppermute | solution.py:575
  72.7 0.6 collective-permute-done.21.refs_1_
  73.4 1.6 %collective-permute-start.27 = (bf16[512,512]{1,0:T(8,128)(2,1)S(1)}, bf16[512,512]{1,0:T(8,128)(2,1)S(1)}, u32[]{:S(2)}, u32[]{:S(2)}) collective-permute-start(bf16[512,512]{1,0:T(8,128)(2,1)S(1)} %shard_map.220.refs_3_.refs_0_), channel_id=1, source_target_pairs={{0,8},{1,17},{2,10},{3,19},{4,12},{5,21},{6,14},{7,23},{8,0},{9,25... | collective-permute-start | bytes 1572872 | tf_op jit(solution)/shard_map/ppermute | solution.py:586
  75.0 2.7 %collective-permute-start.23 = (bf16[96,512]{1,0:T(8,128)(2,1)S(1)}, bf16[96,512]{1,0:T(8,128)(2,1)S(1)}, u32[]{:S(2)}, u32[]{:S(2)}) collective-permute-start(bf16[96,512]{1,0:T(8,128)(2,1)S(1)} %get-tuple-element.174.refs_3_), channel_id=1, source_target_pairs={{0,4},{2,6},{4,0},{6,2},{1,5},{3,7},{5,1},{7,3},{8,12},{10,14},{12... | collective-permute-start | bytes 294920 | tf_op jit(solution)/shard_map/ppermute | solution.py:575
  77.7 1.8 %collective-permute-start.29 = (bf16[256,512]{1,0:T(8,128)(2,1)S(1)}, bf16[256,512]{1,0:T(8,128)(2,1)S(1)}, u32[]{:S(2)}, u32[]{:S(2)}) collective-permute-start(bf16[256,512]{1,0:T(8,128)(2,1)S(1)} %shard_map.222.refs_3_.refs_0_), channel_id=1, source_target_pairs={{0,8},{1,17},{2,10},{3,19},{4,12},{5,21},{6,14},{7,23},{8,0},{9,25... | collective-permute-start | bytes 786440 | tf_op jit(solution)/shard_map/ppermute | solution.py:586
  79.5 3.7 %collective-permute-done.23.refs_1_ = bf16[96,512]{1,0:T(8,128)(2,1)S(1)} collective-permute-done((bf16[96,512]{1,0:T(8,128)(2,1)S(1)}, bf16[96,512]{1,0:T(8,128)(2,1)S(1)}, u32[]{:S(2)}, u32[]{:S(2)}) %collective-permute-start.23) | collective-permute-done | bytes 98336 | tf_op jit(solution)/shard_map/ppermute | solution.py:575
  83.3 1.5 %collective-permute-start.25 = (bf16[96,512]{1,0:T(8,128)(2,1)S(1)}, bf16[96,512]{1,0:T(8,128)(2,1)S(1)}, u32[]{:S(2)}, u32[]{:S(2)}) collective-permute-start(bf16[96,512]{1,0:T(8,128)(2,1)S(1)} %shard_map.223.refs_3_.refs_0_), channel_id=1, source_target_pairs={{0,8},{1,17},{2,10},{3,19},{4,12},{5,21},{6,14},{7,23},{8,0},{9,25... | collective-permute-start | bytes 294920 | tf_op jit(solution)/shard_map/ppermute | solution.py:586
  84.7 0.7 collective-permute-done.29.refs_1_
  85.5 1.8 %collective-permute-start.33 = (bf16[512,512]{1,0:T(8,128)(2,1)S(1)}, bf16[512,512]{1,0:T(8,128)(2,1)S(1)}, u32[]{:S(2)}, u32[]{:S(2)}) collective-permute-start(bf16[512,512]{1,0:T(8,128)(2,1)S(1)} %shard_map.224.refs_5_.refs_0_), channel_id=1, source_target_pairs={{0,16},{1,9},{2,18},{3,11},{4,20},{5,13},{6,22},{7,15},{8,24},{9,1... | collective-permute-start | bytes 1572872 | tf_op jit(solution)/shard_map/ppermute | solution.py:586
  87.3 2.1 %shard_map.225 = (f32[8,128]{1,0:T(8,128)S(1)}, f32[512,2048]{1,0:T(8,128)}, f32[2048,512]{1,0:T(8,128)}) custom-call(bf16[512,512]{1,0:T(8,128)(2,1)S(1)} %shard_map.220.refs_3_.refs_0_, bf16[512,512]{1,0:T(8,128)(2,1)S(1)} %collective-permute-done.26.refs_1_, bf16[512,512]{1,0:T(8,128)(2,1)S(1)} %collective-permute-done.27.refs_2_, ...), custom_call_target="tpu_custom_call" | custom-call | flops 1 | bytes 1024 | tf_op jit(solution)/shard_map/pallas_call | solution.py:160
  89.5 0.9 collective-permute-start.30
  90.4 4.3 %collective-permute-done.33.refs_0_ = bf16[512,512]{1,0:T(8,128)(2,1)S(1)} collective-permute-done((bf16[512,512]{1,0:T(8,128)(2,1)S(1)}, bf16[512,512]{1,0:T(8,128)(2,1)S(1)}, u32[]{:S(2)}, u32[]{:S(2)}) %collective-permute-start.33) | collective-permute-done | bytes 524320 | tf_op jit(solution)/shard_map/ppermute | solution.py:586
  94.7 1.4 %shard_map.227 = (f32[8,128]{1,0:T(8,128)S(1)}, f32[512,2048]{1,0:T(8,128)}, f32[2048,512]{1,0:T(8,128)}) custom-call(bf16[512,512]{1,0:T(8,128)(2,1)S(1)} %shard_map.224.refs_5_.refs_0_, bf16[512,512]{1,0:T(8,128)(2,1)S(1)} %collective-permute-done.31.refs_1_, ...), custom_call_target="tpu_custom_call", output_to_operand_aliasing={{1}: (4, {}), {2}: (5, {})} | custom-call | flops 1 | bytes 1024 | tf_op jit(solution)/shard_map/pallas_call | solution.py:160
  96.2 0.6 collective-permute-start.32
  96.8 1.4 %shard_map.229 = (f32[8,128]{1,0:T(8,128)S(1)}, f32[512,2048]{1,0:T(8,128)}, f32[2048,512]{1,0:T(8,128)}) custom-call(bf16[512,512]{1,0:T(8,128)(2,1)S(1)} %collective-permute-done.33.refs_0_, bf16[512,512]{1,0:T(8,128)(2,1)S(1)} %collective-permute-done.34.refs_1_, ...), custom_call_target="tpu_custom_call", output_to_operand_aliasing={{1}: (4, {}), {2}: (5, {})} | custom-call | flops 1 | bytes 1024 | tf_op jit(solution)/shard_map/pallas_call | solution.py:160
  98.2 0.9 shard_map.230
  (48 shorter events, 0.8 us)
Async XLA Ops:
  1.5 11.6 %collective-permute-start.1 = (bf16[64,512]{1,0:T(8,128)(2,1)S(1)}, bf16[64,512]{1,0:T(8,128)(2,1)S(1)}, u32[]{:S(2)}, u32[]{:S(2)}) collective-permute-start(bf16[64,512]{1,0:T(8,128)(2,1)S(1)} %fusion), channel_id=1, source_target_pairs={{0,4},{2,6},{4,0},{6,2},{1,5},{3,7},{5,1},{7,3},{8,12},{10,14},{12... | collective-permute-start | bytes 196616 | tf_op jit(solution)/shard_map/ppermute | solution.py:556
  5.6 7.5 %collective-permute-start = (bf16[64,512]{1,0:T(8,128)(2,1)S(1)}, bf16[64,512]{1,0:T(8,128)(2,1)S(1)}, u32[]{:S(2)}, u32[]{:S(2)}) collective-permute-start(bf16[64,512]{1,0:T(8,128)(2,1)S(1)} %fusion), channel_id=1, source_target_pairs={{0,2},{2,0},{4,6},{6,4},{1,3},{3,1},{5,7},{7,5},{8,10},{10,8},{12,... | collective-permute-start | bytes 196616 | tf_op jit(solution)/shard_map/ppermute | solution.py:556
  7.2 6.1 %collective-permute-start.2 = (bf16[64,512]{1,0:T(8,128)(2,1)S(1)}, bf16[64,512]{1,0:T(8,128)(2,1)S(1)}, u32[]{:S(2)}, u32[]{:S(2)}) collective-permute-start(bf16[64,512]{1,0:T(8,128)(2,1)S(1)} %fusion), channel_id=1, source_target_pairs={{0,6},{2,4},{4,2},{6,0},{1,7},{3,5},{5,3},{7,1},{8,14},{10,12},{12... | collective-permute-start | bytes 196616 | tf_op jit(solution)/shard_map/ppermute | solution.py:556
  10.5 4.3 %copy-start = (bf16[2048,512]{1,0:T(8,128)(2,1)}, bf16[2048,512]{1,0:T(8,128)(2,1)S(1)}, u32[]{:S(2)}) copy-start(bf16[2048,512]{1,0:T(8,128)(2,1)S(1)} %get-tuple-element.101.refs_1_) | copy-start | bytes 6291460
  13.3 1.5 %collective-permute-start.3 = (bf16[192,512]{1,0:T(8,128)(2,1)S(1)}, bf16[192,512]{1,0:T(8,128)(2,1)S(1)}, u32[]{:S(2)}, u32[]{:S(2)}) collective-permute-start(bf16[192,512]{1,0:T(8,128)(2,1)S(1)} %shard_map.197.refs_0_.refs_14_), channel_id=1, source_target_pairs={{0,1},{1,0},{2,3},{3,2},{4,5},{5,4},{6,7},{7,6},{8,9},{9,8},{10,11... | collective-permute-start | bytes 589832 | tf_op jit(solution)/shard_map/ppermute | solution.py:556
  21.0 7.2 %collective-permute-start.4 = (bf16[512,512]{1,0:T(8,128)(2,1)S(1)}, bf16[512,512]{1,0:T(8,128)(2,1)S(1)}, u32[]{:S(2)}, u32[]{:S(2)}) collective-permute-start(bf16[512,512]{1,0:T(8,128)(2,1)S(1)} %get-tuple-element.126), channel_id=1, source_target_pairs={{0,1},{1,0},{2,3},{3,2},{4,5},{5,4},{6,7},{7,6},{8,9},{9,8},{10,11... | collective-permute-start | bytes 1572872 | tf_op jit(solution)/shard_map/ppermute | solution.py:556
  24.6 3.7 %collective-permute-start.5 = (bf16[512,512]{1,0:T(8,128)(2,1)S(1)}, bf16[512,512]{1,0:T(8,128)(2,1)S(1)}, u32[]{:S(2)}, u32[]{:S(2)}) collective-permute-start(bf16[512,512]{1,0:T(8,128)(2,1)S(1)} %get-tuple-element.127), channel_id=1, source_target_pairs={{0,1},{1,0},{2,3},{3,2},{4,5},{5,4},{6,7},{7,6},{8,9},{9,8},{10,11... | collective-permute-start | bytes 1572872 | tf_op jit(solution)/shard_map/ppermute | solution.py:556
  28.8 9.2 %collective-permute-start.6 = (bf16[512,512]{1,0:T(8,128)(2,1)S(1)}, bf16[512,512]{1,0:T(8,128)(2,1)S(1)}, u32[]{:S(2)}, u32[]{:S(2)}) collective-permute-start(bf16[512,512]{1,0:T(8,128)(2,1)S(1)} %get-tuple-element.129.refs_6_), channel_id=1, source_target_pairs={{0,8},{1,17},{2,10},{3,19},{4,12},{5,21},{6,14},{7,23},{8,0},{9,25... | collective-permute-start | bytes 1572872 | tf_op jit(solution)/shard_map/ppermute | solution.py:586
  30.4 9.5 %collective-permute-start.8 = (bf16[512,512]{1,0:T(8,128)(2,1)S(1)}, bf16[512,512]{1,0:T(8,128)(2,1)S(1)}, u32[]{:S(2)}, u32[]{:S(2)}) collective-permute-start(bf16[512,512]{1,0:T(8,128)(2,1)S(1)} %get-tuple-element.145), channel_id=1, source_target_pairs={{0,1},{1,0},{2,3},{3,2},{4,5},{5,4},{6,7},{7,6},{8,9},{9,8},{10,11... | collective-permute-start | bytes 1572872 | tf_op jit(solution)/shard_map/ppermute | solution.py:556
  33.6 6.3 %collective-permute-start.9 = (bf16[512,512]{1,0:T(8,128)(2,1)S(1)}, bf16[512,512]{1,0:T(8,128)(2,1)S(1)}, u32[]{:S(2)}, u32[]{:S(2)}) collective-permute-start(bf16[512,512]{1,0:T(8,128)(2,1)S(1)} %get-tuple-element.146), channel_id=1, source_target_pairs={{0,1},{1,0},{2,3},{3,2},{4,5},{5,4},{6,7},{7,6},{8,9},{9,8},{10,11... | collective-permute-start | bytes 1572872 | tf_op jit(solution)/shard_map/ppermute | solution.py:556
  38.2 6.4 %collective-permute-start.7 = (bf16[256,512]{1,0:T(8,128)(2,1)S(1)}, bf16[256,512]{1,0:T(8,128)(2,1)S(1)}, u32[]{:S(2)}, u32[]{:S(2)}) collective-permute-start(bf16[256,512]{1,0:T(8,128)(2,1)S(1)} %get-tuple-element.139.refs_5_), channel_id=1, source_target_pairs={{0,16},{1,9},{2,18},{3,11},{4,20},{5,13},{6,22},{7,15},{8,24},{9,1... | collective-permute-start | bytes 786440 | tf_op jit(solution)/shard_map/ppermute | solution.py:586
  40.4 9.9 %collective-permute-start.11 = (bf16[512,512]{1,0:T(8,128)(2,1)S(1)}, bf16[512,512]{1,0:T(8,128)(2,1)S(1)}, u32[]{:S(2)}, u32[]{:S(2)}) collective-permute-start(bf16[512,512]{1,0:T(8,128)(2,1)S(1)} %get-tuple-element.147.refs_12_), channel_id=1, source_target_pairs={{0,16},{1,9},{2,18},{3,11},{4,20},{5,13},{6,22},{7,15},{8,24},{9,1... | collective-permute-start | bytes 1572872 | tf_op jit(solution)/shard_map/ppermute | solution.py:586
  44.8 7.4 %collective-permute-start.10 = (bf16[128,512]{1,0:T(8,128)(2,1)S(1)}, bf16[128,512]{1,0:T(8,128)(2,1)S(1)}, u32[]{:S(2)}, u32[]{:S(2)}) collective-permute-start(bf16[128,512]{1,0:T(8,128)(2,1)S(1)} %get-tuple-element.150.refs_10_), channel_id=1, source_target_pairs={{0,2},{2,0},{4,6},{6,4},{1,3},{3,1},{5,7},{7,5},{8,10},{10,8},{12,... | collective-permute-start | bytes 393224 | tf_op jit(solution)/shard_map/ppermute | solution.py:575
  48.5 11.2 %collective-permute-start.12 = (bf16[128,512]{1,0:T(8,128)(2,1)S(1)}, bf16[128,512]{1,0:T(8,128)(2,1)S(1)}, u32[]{:S(2)}, u32[]{:S(2)}) collective-permute-start(bf16[128,512]{1,0:T(8,128)(2,1)S(1)} %get-tuple-element.162), channel_id=1, source_target_pairs={{0,1},{1,0},{2,3},{3,2},{4,5},{5,4},{6,7},{7,6},{8,9},{9,8},{10,11... | collective-permute-start | bytes 393224 | tf_op jit(solution)/shard_map/ppermute | solution.py:556
  48.6 11.1 %collective-permute-start.13 = (bf16[128,512]{1,0:T(8,128)(2,1)S(1)}, bf16[128,512]{1,0:T(8,128)(2,1)S(1)}, u32[]{:S(2)}, u32[]{:S(2)}) collective-permute-start(bf16[128,512]{1,0:T(8,128)(2,1)S(1)} %get-tuple-element.163), channel_id=1, source_target_pairs={{0,1},{1,0},{2,3},{3,2},{4,5},{5,4},{6,7},{7,6},{8,9},{9,8},{10,11... | collective-permute-start | bytes 393224 | tf_op jit(solution)/shard_map/ppermute | solution.py:556
  49.1 10.6 %collective-permute-start.14 = (bf16[128,512]{1,0:T(8,128)(2,1)S(1)}, bf16[128,512]{1,0:T(8,128)(2,1)S(1)}, u32[]{:S(2)}, u32[]{:S(2)}) collective-permute-start(bf16[128,512]{1,0:T(8,128)(2,1)S(1)} %get-tuple-element.164), channel_id=1, source_target_pairs={{0,1},{1,0},{2,3},{3,2},{4,5},{5,4},{6,7},{7,6},{8,9},{9,8},{10,11... | collective-permute-start | bytes 393224 | tf_op jit(solution)/shard_map/ppermute | solution.py:556
  50.5 7.2 %collective-permute-start.15 = (bf16[256,512]{1,0:T(8,128)(2,1)S(1)}, bf16[256,512]{1,0:T(8,128)(2,1)S(1)}, u32[]{:S(2)}, u32[]{:S(2)}) collective-permute-start(bf16[256,512]{1,0:T(8,128)(2,1)S(1)} %get-tuple-element.157.refs_3_), channel_id=1, source_target_pairs={{0,8},{1,17},{2,10},{3,19},{4,12},{5,21},{6,14},{7,23},{8,0},{9,25... | collective-permute-start | bytes 786440 | tf_op jit(solution)/shard_map/ppermute | solution.py:586
  52.1 2.4 %copy-start.1 = (bf16[2048,512]{1,0:T(8,128)(2,1)S(1)}, bf16[2048,512]{1,0:T(8,128)(2,1)}, u32[]{:S(2)}) copy-start(bf16[2048,512]{1,0:T(8,128)(2,1)} %copy-done) | copy-start | bytes 6291460
  52.2 9.3 %collective-permute-start.17 = (bf16[128,512]{1,0:T(8,128)(2,1)S(1)}, bf16[128,512]{1,0:T(8,128)(2,1)S(1)}, u32[]{:S(2)}, u32[]{:S(2)}) collective-permute-start(bf16[128,512]{1,0:T(8,128)(2,1)S(1)} %shard_map.211.refs_6_.refs_0_), channel_id=1, source_target_pairs={{0,4},{2,6},{4,0},{6,2},{1,5},{3,7},{5,1},{7,3},{8,12},{10,14},{12... | collective-permute-start | bytes 393224 | tf_op jit(solution)/shard_map/ppermute | solution.py:575
  57.8 6.2 %collective-permute-start.19 = (bf16[128,512]{1,0:T(8,128)(2,1)S(1)}, bf16[128,512]{1,0:T(8,128)(2,1)S(1)}, u32[]{:S(2)}, u32[]{:S(2)}) collective-permute-start(bf16[128,512]{1,0:T(8,128)(2,1)S(1)} %get-tuple-element.167.refs_7_), channel_id=1, source_target_pairs={{0,2},{2,0},{4,6},{6,4},{1,3},{3,1},{5,7},{7,5},{8,10},{10,8},{12,... | collective-permute-start | bytes 393224 | tf_op jit(solution)/shard_map/ppermute | solution.py:575
  59.9 8.8 %collective-permute-start.16 = (bf16[192,512]{1,0:T(8,128)(2,1)S(1)}, bf16[192,512]{1,0:T(8,128)(2,1)S(1)}, u32[]{:S(2)}, u32[]{:S(2)}) collective-permute-start(bf16[192,512]{1,0:T(8,128)(2,1)S(1)} %get-tuple-element.169.refs_3_), channel_id=1, source_target_pairs={{0,16},{1,9},{2,18},{3,11},{4,20},{5,13},{6,22},{7,15},{8,24},{9,1... | collective-permute-start | bytes 589832 | tf_op jit(solution)/shard_map/ppermute | solution.py:586
  61.5 5.3 %collective-permute-start.18 = (bf16[128,512]{1,0:T(8,128)(2,1)S(1)}, bf16[128,512]{1,0:T(8,128)(2,1)S(1)}, u32[]{:S(2)}, u32[]{:S(2)}) collective-permute-start(bf16[128,512]{1,0:T(8,128)(2,1)S(1)} %shard_map.215.refs_3_.refs_0_), channel_id=1, source_target_pairs={{0,2},{2,0},{4,6},{6,4},{1,3},{3,1},{5,7},{7,5},{8,10},{10,8},{12,... | collective-permute-start | bytes 393224 | tf_op jit(solution)/shard_map/ppermute | solution.py:575
  64.0 8.6 %collective-permute-start.22 = (bf16[128,512]{1,0:T(8,128)(2,1)S(1)}, bf16[128,512]{1,0:T(8,128)(2,1)S(1)}, u32[]{:S(2)}, u32[]{:S(2)}) collective-permute-start(bf16[128,512]{1,0:T(8,128)(2,1)S(1)} %shard_map.216.refs_3_.refs_0_), channel_id=1, source_target_pairs={{0,4},{2,6},{4,0},{6,2},{1,5},{3,7},{5,1},{7,3},{8,12},{10,14},{12... | collective-permute-start | bytes 393224 | tf_op jit(solution)/shard_map/ppermute | solution.py:575
  66.8 6.4 %collective-permute-start.21 = (bf16[256,512]{1,0:T(8,128)(2,1)S(1)}, bf16[256,512]{1,0:T(8,128)(2,1)S(1)}, u32[]{:S(2)}, u32[]{:S(2)}) collective-permute-start(bf16[256,512]{1,0:T(8,128)(2,1)S(1)} %shard_map.217.refs_3_.refs_0_), channel_id=1, source_target_pairs={{0,16},{1,9},{2,18},{3,11},{4,20},{5,13},{6,22},{7,15},{8,24},{9,1... | collective-permute-start | bytes 786440 | tf_op jit(solution)/shard_map/ppermute | solution.py:586
  68.7 6.2 %collective-permute-start.20 = (bf16[128,512]{1,0:T(8,128)(2,1)S(1)}, bf16[128,512]{1,0:T(8,128)(2,1)S(1)}, u32[]{:S(2)}, u32[]{:S(2)}) collective-permute-start(bf16[128,512]{1,0:T(8,128)(2,1)S(1)} %get-tuple-element.172.refs_3_), channel_id=1, source_target_pairs={{0,2},{2,0},{4,6},{6,4},{1,3},{3,1},{5,7},{7,5},{8,10},{10,8},{12,... | collective-permute-start | bytes 393224 | tf_op jit(solution)/shard_map/ppermute | solution.py:575
  72.6 5.0 %collective-permute-start.24 = (bf16[128,512]{1,0:T(8,128)(2,1)S(1)}, bf16[128,512]{1,0:T(8,128)(2,1)S(1)}, u32[]{:S(2)}, u32[]{:S(2)}) collective-permute-start(bf16[128,512]{1,0:T(8,128)(2,1)S(1)} %shard_map.219.refs_3_.refs_0_), channel_id=1, source_target_pairs={{0,2},{2,0},{4,6},{6,4},{1,3},{3,1},{5,7},{7,5},{8,10},{10,8},{12,... | collective-permute-start | bytes 393224 | tf_op jit(solution)/shard_map/ppermute | solution.py:575
  73.4 11.4 %collective-permute-start.27 = (bf16[512,512]{1,0:T(8,128)(2,1)S(1)}, bf16[512,512]{1,0:T(8,128)(2,1)S(1)}, u32[]{:S(2)}, u32[]{:S(2)}) collective-permute-start(bf16[512,512]{1,0:T(8,128)(2,1)S(1)} %shard_map.220.refs_3_.refs_0_), channel_id=1, source_target_pairs={{0,8},{1,17},{2,10},{3,19},{4,12},{5,21},{6,14},{7,23},{8,0},{9,25... | collective-permute-start | bytes 1572872 | tf_op jit(solution)/shard_map/ppermute | solution.py:586
  74.9 12.4 %collective-permute-start.26 = (bf16[512,512]{1,0:T(8,128)(2,1)S(1)}, bf16[512,512]{1,0:T(8,128)(2,1)S(1)}, u32[]{:S(2)}, u32[]{:S(2)}) collective-permute-start(bf16[512,512]{1,0:T(8,128)(2,1)S(1)} %shard_map.220.refs_3_.refs_0_), channel_id=1, source_target_pairs={{0,1},{1,0},{2,3},{3,2},{4,5},{5,4},{6,7},{7,6},{8,9},{9,8},{10,11... | collective-permute-start | bytes 1572872 | tf_op jit(solution)/shard_map/ppermute | solution.py:556
  75.0 8.3 %collective-permute-start.23 = (bf16[96,512]{1,0:T(8,128)(2,1)S(1)}, bf16[96,512]{1,0:T(8,128)(2,1)S(1)}, u32[]{:S(2)}, u32[]{:S(2)}) collective-permute-start(bf16[96,512]{1,0:T(8,128)(2,1)S(1)} %get-tuple-element.174.refs_3_), channel_id=1, source_target_pairs={{0,4},{2,6},{4,0},{6,2},{1,5},{3,7},{5,1},{7,3},{8,12},{10,14},{12... | collective-permute-start | bytes 294920 | tf_op jit(solution)/shard_map/ppermute | solution.py:575
  77.7 7.7 %collective-permute-start.29 = (bf16[256,512]{1,0:T(8,128)(2,1)S(1)}, bf16[256,512]{1,0:T(8,128)(2,1)S(1)}, u32[]{:S(2)}, u32[]{:S(2)}) collective-permute-start(bf16[256,512]{1,0:T(8,128)(2,1)S(1)} %shard_map.222.refs_3_.refs_0_), channel_id=1, source_target_pairs={{0,8},{1,17},{2,10},{3,19},{4,12},{5,21},{6,14},{7,23},{8,0},{9,25... | collective-permute-start | bytes 786440 | tf_op jit(solution)/shard_map/ppermute | solution.py:586
  83.3 6.2 %collective-permute-start.25 = (bf16[96,512]{1,0:T(8,128)(2,1)S(1)}, bf16[96,512]{1,0:T(8,128)(2,1)S(1)}, u32[]{:S(2)}, u32[]{:S(2)}) collective-permute-start(bf16[96,512]{1,0:T(8,128)(2,1)S(1)} %shard_map.223.refs_3_.refs_0_), channel_id=1, source_target_pairs={{0,8},{1,17},{2,10},{3,19},{4,12},{5,21},{6,14},{7,23},{8,0},{9,25... | collective-permute-start | bytes 294920 | tf_op jit(solution)/shard_map/ppermute | solution.py:586
  84.7 2.6 %collective-permute-start.28 = (bf16[512,512]{1,0:T(8,128)(2,1)S(1)}, bf16[512,512]{1,0:T(8,128)(2,1)S(1)}, u32[]{:S(2)}, u32[]{:S(2)}) collective-permute-start(bf16[512,512]{1,0:T(8,128)(2,1)S(1)} %collective-permute-done.27.refs_2_), channel_id=1, source_target_pairs={{0,1},{1,0},{2,3},{3,2},{4,5},{5,4},{6,7},{7,6},{8,9},{9,8},{10,11... | collective-permute-start | bytes 1572872 | tf_op jit(solution)/shard_map/ppermute | solution.py:556
  85.5 9.2 %collective-permute-start.33 = (bf16[512,512]{1,0:T(8,128)(2,1)S(1)}, bf16[512,512]{1,0:T(8,128)(2,1)S(1)}, u32[]{:S(2)}, u32[]{:S(2)}) collective-permute-start(bf16[512,512]{1,0:T(8,128)(2,1)S(1)} %shard_map.224.refs_5_.refs_0_), channel_id=1, source_target_pairs={{0,16},{1,9},{2,18},{3,11},{4,20},{5,13},{6,22},{7,15},{8,24},{9,1... | collective-permute-start | bytes 1572872 | tf_op jit(solution)/shard_map/ppermute | solution.py:586
  87.3 7.4 %collective-permute-start.31 = (bf16[512,512]{1,0:T(8,128)(2,1)S(1)}, bf16[512,512]{1,0:T(8,128)(2,1)S(1)}, u32[]{:S(2)}, u32[]{:S(2)}) collective-permute-start(bf16[512,512]{1,0:T(8,128)(2,1)S(1)} %shard_map.224.refs_5_.refs_0_), channel_id=1, source_target_pairs={{0,1},{1,0},{2,3},{3,2},{4,5},{5,4},{6,7},{7,6},{8,9},{9,8},{10,11... | collective-permute-start | bytes 1572872 | tf_op jit(solution)/shard_map/ppermute | solution.py:556
  89.5 6.7 %collective-permute-start.30 = (bf16[96,512]{1,0:T(8,128)(2,1)S(1)}, bf16[96,512]{1,0:T(8,128)(2,1)S(1)}, u32[]{:S(2)}, u32[]{:S(2)}) collective-permute-start(bf16[96,512]{1,0:T(8,128)(2,1)S(1)} %shard_map.226.refs_3_.refs_0_), channel_id=1, source_target_pairs={{0,16},{1,9},{2,18},{3,11},{4,20},{5,13},{6,22},{7,15},{8,24},{9,1... | collective-permute-start | bytes 294920 | tf_op jit(solution)/shard_map/ppermute | solution.py:586
  94.7 2.0 %collective-permute-start.34 = (bf16[512,512]{1,0:T(8,128)(2,1)S(1)}, bf16[512,512]{1,0:T(8,128)(2,1)S(1)}, u32[]{:S(2)}, u32[]{:S(2)}) collective-permute-start(bf16[512,512]{1,0:T(8,128)(2,1)S(1)} %collective-permute-done.33.refs_0_), channel_id=1, source_target_pairs={{0,1},{1,0},{2,3},{3,2},{4,5},{5,4},{6,7},{7,6},{8,9},{9,8},{10,11... | collective-permute-start | bytes 1572872 | tf_op jit(solution)/shard_map/ppermute | solution.py:556
  96.2 2.0 %collective-permute-start.32 = (bf16[192,512]{1,0:T(8,128)(2,1)S(1)}, bf16[192,512]{1,0:T(8,128)(2,1)S(1)}, u32[]{:S(2)}, u32[]{:S(2)}) collective-permute-start(bf16[192,512]{1,0:T(8,128)(2,1)S(1)} %shard_map.228.refs_3_.refs_0_), channel_id=1, source_target_pairs={{0,1},{1,0},{2,3},{3,2},{4,5},{5,4},{6,7},{7,6},{8,9},{9,8},{10,11... | collective-permute-start | bytes 589832 | tf_op jit(solution)/shard_map/ppermute | solution.py:556
